TPU v7x, 32 devices: a whole 2x2x4 slice. The times are simulated.
32 devices in a mesh: dp: 16 (over z, x, core), fsdp: 2 (over y).
Axes of the slice: x: 2, y: 2, z: 4, core: 2. Of those that a mesh axis runs over, the one named last changes fastest.
Arguments:
- enc_tokens: bfloat16 [32768, 768], P(('dp', 'fsdp')), may hold values from -6 to 6
- dec_tokens: bfloat16 [8192, 768], P(('dp', 'fsdp')), may hold values from -6 to 6
- enc_segments: int32 [32768], P(('dp', 'fsdp')), may hold values from -1 to 15, as said below
- dec_segments: int32 [8192], P(('dp', 'fsdp')), may hold values from -1 to 15, as said below
- enc_upstream: bfloat16 [32768, 768], P(('dp', 'fsdp')), may hold values from -6 to 6
- dec_upstream: bfloat16 [8192, 768], P(('dp', 'fsdp')), may hold values from -6 to 6
- encoder_query: bfloat16 [768, 768], P('fsdp'), may hold values from -0.0546875 to 0.0546875
- encoder_keyval: bfloat16 [768, 1536], P('fsdp'), may hold values from -0.21875 to 0.21875
- encoder_proj: bfloat16 [768, 768], P('fsdp'), may hold values from -0.625 to 0.625
- encoder_inner: bfloat16 [768, 3072], P('fsdp'), may hold values from -0.21875 to 0.21875
- encoder_outer: bfloat16 [3072, 768], P('fsdp'), may hold values from -0.109375 to 0.109375
- encoder_gains: bfloat16 [768, 2], P('fsdp'), may hold values from 0.5 to 1.5
- encoder_table: bfloat16 [32, 12], P('fsdp'), may hold values from -4 to 4
- decoder_query: bfloat16 [768, 768], P('fsdp'), may hold values from -0.0546875 to 0.0546875
- decoder_keyval: bfloat16 [768, 1536], P('fsdp'), may hold values from -0.21875 to 0.21875
- decoder_proj: bfloat16 [768, 768], P('fsdp'), may hold values from -0.625 to 0.625
- cross_query: bfloat16 [768, 768], P('fsdp'), may hold values from -0.0390625 to 0.0390625
- cross_keyval: bfloat16 [768, 1536], P('fsdp'), may hold values from -0.21875 to 0.21875
- cross_proj: bfloat16 [768, 768], P('fsdp'), may hold values from -0.625 to 0.625
- decoder_inner: bfloat16 [768, 3072], P('fsdp'), may hold values from -0.21875 to 0.21875
- decoder_outer: bfloat16 [3072, 768], P('fsdp'), may hold values from -0.109375 to 0.109375
- decoder_gains: bfloat16 [768, 3], P('fsdp'), may hold values from 0.5 to 1.5
- decoder_table: bfloat16 [32, 12], P('fsdp'), may hold values from -4 to 4
Outputs:
- enc_result: bfloat16 [32768, 768], P(('dp', 'fsdp'))
- dec_result: bfloat16 [8192, 768], P(('dp', 'fsdp'))
- enc_tokens_grad: float32 [32768, 768], P(('dp', 'fsdp'))
- dec_tokens_grad: float32 [8192, 768], P(('dp', 'fsdp'))
- encoder_query_grad: float32 [768, 768], P(('dp', 'fsdp'))
- encoder_keyval_grad: float32 [768, 1536], P(('dp', 'fsdp'))
- encoder_proj_grad: float32 [768, 768], P(('dp', 'fsdp'))
- encoder_inner_grad: float32 [768, 3072], P(('dp', 'fsdp'))
- encoder_outer_grad: float32 [3072, 768], P(('dp', 'fsdp'))
- encoder_gains_grad: float32 [768, 2], P(('dp', 'fsdp'))
- encoder_table_grad: float32 [32, 12], replicated
- decoder_query_grad: float32 [768, 768], P(('dp', 'fsdp'))
- decoder_keyval_grad: float32 [768, 1536], P(('dp', 'fsdp'))
- decoder_proj_grad: float32 [768, 768], P(('dp', 'fsdp'))
- cross_query_grad: float32 [768, 768], P(('dp', 'fsdp'))
- cross_keyval_grad: float32 [768, 1536], P(('dp', 'fsdp'))
- cross_proj_grad: float32 [768, 768], P(('dp', 'fsdp'))
- decoder_inner_grad: float32 [768, 3072], P(('dp', 'fsdp'))
- decoder_outer_grad: float32 [3072, 768], P(('dp', 'fsdp'))
- decoder_gains_grad: float32 [768, 3], P(('dp', 'fsdp'))
- decoder_table_grad: float32 [32, 12], replicated
Inputs may be any that keep to these rules, and one draw needn't show every extreme that they name: `enc_segments`: in each block of 1024 rows (the rows of one device) the sequences stand whole and back to back from the block's first row, numbered 0, 1, 2, ... in order, at most 16 of them, followed by padding rows marked -1; every block ends with at least one padding row. `dec_segments`: in each block of 256 rows the decoder targets of the same device's sequences stand back to back from the block's first row, with the same numbers in the same order, each sequence with one row or more, followed by padding rows marked -1.
All inputs are finite; a program needn't handle non-finite values.
Results may differ from a plain program's by a relative error of at most 0.025.
The roundings to bfloat16 on the way count: a program that leaves them out, or rounds other values in their place, can miss the bound.
Values may be sent and summed in bfloat16 or wider, within the bound.
A program may use at most 384 MiB of HBM per device.

v0:
```python
import math

import jax
import jax.numpy as jnp
from jax import lax
from jax.sharding import PartitionSpec as P

H = 12
HD = 64
NB = 32


EPSILON = 1e-06
MASKED = -1e30
ENC_EDGES = (12, 16, 23, 32, 46, 64, 91)
DEC_EDGES = tuple((math.ceil(16 * 2 ** (3 * power / 16)) for power in range(1, 16)))


def encoder_bucket(query_places, key_places):
    distance = query_places[:, None] - key_places[None, :]
    reach = jnp.abs(distance)
    farther = 8 + sum(((reach >= threshold).astype(jnp.int32) for threshold in ENC_EDGES))
    return jnp.where(reach < 8, reach, farther) + 16 * (distance < 0).astype(jnp.int32)


def decoder_bucket(query_places, key_places):
    ahead = jnp.maximum(query_places[:, None] - key_places[None, :], 0)
    farther = 16 + sum(((ahead >= threshold).astype(jnp.int32) for threshold in DEC_EDGES))
    return jnp.where(ahead < 16, ahead, farther)


def product(former, latter):
    return jnp.dot(former, latter, preferred_element_type=jnp.float32)


def transpose_product(former, latter):
    return lax.dot_general(
        former, latter, (((0,), (0,)), ((), ())), preferred_element_type=jnp.float32
    )


def product_transposed(former, latter):
    return lax.dot_general(
        former, latter, (((1,), (1,)), ((), ())), preferred_element_type=jnp.float32
    )


def smooth_gate(value):
    return jax.nn.gelu(value, approximate=True)


def norm_forward(stream, norm_gain):
    return (
        stream * lax.rsqrt(jnp.mean(stream * stream, axis=-1, keepdims=True) + EPSILON) * norm_gain
    )


def norm_backward(stream, norm_gain, gradient):
    outcome, pullback = jax.vjp(norm_forward, stream, norm_gain)
    return pullback(gradient)


def split_heads(matrix):
    return matrix.reshape(matrix.shape[0], H, HD)


def bucket_table(bucket):
    return (bucket[..., None] == jnp.arange(NB, dtype=jnp.int32)).astype(jnp.float32)


def block_scores(query_block, key_heads, table_t, bucket, allowed):
    scores = jnp.einsum("qhd,khd->hqk", query_block, key_heads, preferred_element_type=jnp.float32)
    onehot = None
    if table_t is not None:
        onehot = bucket_table(bucket)
        scores = scores + jnp.einsum(
            "qkb,hb->hqk", onehot, table_t, precision=lax.Precision.HIGHEST
        )
    return (jnp.where(allowed[None], scores, MASKED), onehot)


def attend_forward(queries, key_heads, value_heads, table_t, layout):
    row_count = queries.shape[0]
    block_rows = min(512, row_count)
    block_count = row_count // block_rows

    def one_block(block_index):
        offset = block_index * block_rows
        query_block = lax.dynamic_slice_in_dim(queries, offset, block_rows, 0)
        bucket, allowed = layout(offset, block_rows)
        scores, onehot = block_scores(query_block, key_heads, table_t, bucket, allowed)
        highest = jnp.max(scores, axis=-1, keepdims=True)
        exponent = jnp.exp(scores - highest)
        summed = jnp.sum(exponent, axis=-1, keepdims=True)
        weights = (exponent / summed).astype(jnp.bfloat16)
        mixture = jnp.einsum(
            "hqk,khd->qhd", weights, value_heads, preferred_element_type=jnp.float32
        )
        return (mixture.astype(jnp.bfloat16), (highest + jnp.log(summed))[..., 0])

    mixture, logsum = lax.map(one_block, jnp.arange(block_count, dtype=jnp.int32))
    return (mixture.reshape(row_count, H * HD), logsum)


def attend_backward(queries, key_heads, value_heads, table_t, layout, logsum, dmixture):
    row_count = queries.shape[0]
    block_rows = min(512, row_count)
    block_count = row_count // block_rows
    dheads = split_heads(dmixture)

    def one_block(running, element):
        dkeys, dvalues, dtable = running
        block_index, logsum_block = element
        offset = block_index * block_rows
        query_block = lax.dynamic_slice_in_dim(queries, offset, block_rows, 0)
        dmix_block = lax.dynamic_slice_in_dim(dheads, offset, block_rows, 0)
        bucket, allowed = layout(offset, block_rows)
        scores, onehot = block_scores(query_block, key_heads, table_t, bucket, allowed)
        weights = jnp.exp(scores - logsum_block[..., None])
        dweights = jnp.einsum(
            "qhd,khd->hqk", dmix_block, value_heads, preferred_element_type=jnp.float32
        )
        dscores = weights * (dweights - jnp.sum(weights * dweights, axis=-1, keepdims=True))
        if table_t is not None:
            dtable = dtable + jnp.einsum(
                "hqk,qkb->bh", dscores, onehot, precision=lax.Precision.HIGHEST
            )
        dscores_low = dscores.astype(jnp.bfloat16)
        dquery = jnp.einsum(
            "hqk,khd->qhd", dscores_low, key_heads, preferred_element_type=jnp.float32
        )
        dkeys = dkeys + jnp.einsum(
            "hqk,qhd->khd", dscores_low, query_block, preferred_element_type=jnp.float32
        )
        dvalues = dvalues + jnp.einsum(
            "hqk,qhd->khd",
            weights.astype(jnp.bfloat16),
            dmix_block,
            preferred_element_type=jnp.float32,
        )
        return ((dkeys, dvalues, dtable), dquery)

    initial = (
        jnp.zeros(key_heads.shape, jnp.float32),
        jnp.zeros(value_heads.shape, jnp.float32),
        jnp.zeros((NB, H), jnp.float32),
    )
    (dkeys, dvalues, dtable), dquery = lax.scan(
        one_block, initial, (jnp.arange(block_count, dtype=jnp.int32), logsum)
    )
    features = H * HD
    return (
        dquery.reshape(row_count, features),
        dkeys.reshape(-1, features),
        dvalues.reshape(-1, features),
        dtable,
    )


def attention_forward(stream, norm_gain, wquery, wkeyval, wproj, table_t, layout, memory):
    normed = norm_forward(stream, norm_gain).astype(jnp.bfloat16)
    queries = product(normed, wquery).astype(jnp.bfloat16)
    source = normed if memory is None else memory
    keyval = product(source, wkeyval).astype(jnp.bfloat16)
    features = queries.shape[1]
    mixture, logsum = attend_forward(
        split_heads(queries),
        split_heads(keyval[:, :features]),
        split_heads(keyval[:, features:]),
        table_t,
        layout,
    )
    return (stream + product(mixture, wproj), (normed, queries, keyval, mixture, logsum))


def attention_backward(
    stream, norm_gain, wquery, wkeyval, wproj, table_t, layout, memory, stored, gradient
):
    normed, queries, keyval, mixture, logsum = stored
    features = queries.shape[1]
    gradient_low = gradient.astype(jnp.bfloat16)
    project_grad = transpose_product(mixture, gradient_low)
    dmixture = product_transposed(gradient_low, wproj).astype(jnp.bfloat16)
    dquery, dkeys, dvalues, dtable = attend_backward(
        split_heads(queries),
        split_heads(keyval[:, :features]),
        split_heads(keyval[:, features:]),
        table_t,
        layout,
        logsum,
        dmixture,
    )
    dquery_low = dquery.astype(jnp.bfloat16)
    dkeyval_low = jnp.concatenate([dkeys, dvalues], axis=1).astype(jnp.bfloat16)
    source = normed if memory is None else memory
    query_grad = transpose_product(normed, dquery_low)
    keyval_grad = transpose_product(source, dkeyval_low)
    dnormed = product_transposed(dquery_low, wquery)
    dsource = product_transposed(dkeyval_low, wkeyval)
    if memory is None:
        dnormed = dnormed + dsource
        dsource = None
    dstream, dgain = norm_backward(stream, norm_gain, dnormed)
    return (gradient + dstream, dgain, query_grad, keyval_grad, project_grad, dtable, dsource)


def feed_forward(stream, norm_gain, winner, wouter):
    normed = norm_forward(stream, norm_gain).astype(jnp.bfloat16)
    before = product(normed, winner)
    hidden = smooth_gate(before).astype(jnp.bfloat16)
    return (stream + product(hidden, wouter), (normed, before, hidden))


def feed_backward(stream, norm_gain, winner, wouter, stored, gradient):
    normed, before, hidden = stored
    gradient_low = gradient.astype(jnp.bfloat16)
    outer_grad = transpose_product(hidden, gradient_low)
    dhidden = product_transposed(gradient_low, wouter)
    gate_value, gate_pullback = jax.vjp(smooth_gate, before)
    dbefore = gate_pullback(dhidden)[0].astype(jnp.bfloat16)
    inner_grad = transpose_product(normed, dbefore)
    dnormed = product_transposed(dbefore, winner)
    dstream, dgain = norm_backward(stream, norm_gain, dnormed)
    return (gradient + dstream, dgain, inner_grad, outer_grad)


def encoder_forward(stream, layer_weights, layout):
    wquery, wkeyval, wproj, winner, wouter, gains, table = layer_weights
    gain_cols = gains.astype(jnp.float32)
    table_t = table.astype(jnp.float32).T
    middle, self_stored = attention_forward(
        stream, gain_cols[:, 0], wquery, wkeyval, wproj, table_t, layout, None
    )
    result, ffn_stored = feed_forward(middle, gain_cols[:, 1], winner, wouter)
    return (result, (middle, self_stored, ffn_stored))


def encoder_backward(stream, layer_weights, layout, stored, gradient):
    wquery, wkeyval, wproj, winner, wouter, gains, table = layer_weights
    gain_cols = gains.astype(jnp.float32)
    table_t = table.astype(jnp.float32).T
    middle, self_stored, ffn_stored = stored
    gradient, gain_ffn, inner_grad, outer_grad = feed_backward(
        middle, gain_cols[:, 1], winner, wouter, ffn_stored, gradient
    )
    gradient, gain_self, query_grad, keyval_grad, project_grad, table_grad, unused = (
        attention_backward(
            stream,
            gain_cols[:, 0],
            wquery,
            wkeyval,
            wproj,
            table_t,
            layout,
            None,
            self_stored,
            gradient,
        )
    )
    gains_grad = jnp.stack([gain_self, gain_ffn], axis=1)
    return (
        gradient,
        (query_grad, keyval_grad, project_grad, inner_grad, outer_grad, gains_grad),
        table_grad,
    )


def decoder_forward(stream, layer_weights, self_layout, cross_layout, memory):
    wquery, wkeyval, wproj, cquery, ckeyval, cproj, winner, wouter, gains, table = layer_weights
    gain_cols = gains.astype(jnp.float32)
    table_t = table.astype(jnp.float32).T
    after_self, self_stored = attention_forward(
        stream, gain_cols[:, 0], wquery, wkeyval, wproj, table_t, self_layout, None
    )
    after_cross, cross_stored = attention_forward(
        after_self, gain_cols[:, 1], cquery, ckeyval, cproj, None, cross_layout, memory
    )
    result, ffn_stored = feed_forward(after_cross, gain_cols[:, 2], winner, wouter)
    return (result, (after_self, after_cross, self_stored, cross_stored, ffn_stored))


def decoder_backward(stream, layer_weights, self_layout, cross_layout, memory, stored, gradient):
    wquery, wkeyval, wproj, cquery, ckeyval, cproj, winner, wouter, gains, table = layer_weights
    gain_cols = gains.astype(jnp.float32)
    table_t = table.astype(jnp.float32).T
    after_self, after_cross, self_stored, cross_stored, ffn_stored = stored
    gradient, gain_ffn, inner_grad, outer_grad = feed_backward(
        after_cross, gain_cols[:, 2], winner, wouter, ffn_stored, gradient
    )
    gradient, gain_cross, cquery_grad, ckeyval_grad, cproject_grad, unused, memory_grad = (
        attention_backward(
            after_self,
            gain_cols[:, 1],
            cquery,
            ckeyval,
            cproj,
            None,
            cross_layout,
            memory,
            cross_stored,
            gradient,
        )
    )
    gradient, gain_self, query_grad, keyval_grad, project_grad, table_grad, unused = (
        attention_backward(
            stream,
            gain_cols[:, 0],
            wquery,
            wkeyval,
            wproj,
            table_t,
            self_layout,
            None,
            self_stored,
            gradient,
        )
    )
    gains_grad = jnp.stack([gain_self, gain_cross, gain_ffn], axis=1)
    grads = (
        query_grad,
        keyval_grad,
        project_grad,
        cquery_grad,
        ckeyval_grad,
        cproject_grad,
        inner_grad,
        outer_grad,
        gains_grad,
    )
    return (gradient, grads, table_grad, memory_grad)


def body(
    enc_tokens,
    dec_tokens,
    enc_segments,
    dec_segments,
    enc_upstream,
    dec_upstream,
    encoder_query,
    encoder_keyval,
    encoder_proj,
    encoder_inner,
    encoder_outer,
    encoder_gains,
    encoder_table,
    decoder_query,
    decoder_keyval,
    decoder_proj,
    cross_query,
    cross_keyval,
    cross_proj,
    decoder_inner,
    decoder_outer,
    decoder_gains,
    decoder_table,
):
    enc_places = jnp.arange(enc_tokens.shape[0], dtype=jnp.int32)
    dec_places = jnp.arange(dec_tokens.shape[0], dtype=jnp.int32)

    def enc_layout(offset, length):
        places = offset + jnp.arange(length, dtype=jnp.int32)
        labels = lax.dynamic_slice_in_dim(enc_segments, offset, length, 0)
        return (encoder_bucket(places, enc_places), labels[:, None] == enc_segments[None, :])

    def self_layout(offset, length):
        places = offset + jnp.arange(length, dtype=jnp.int32)
        allowed = (dec_segments[:, None] == dec_segments[None, :]) & (
            dec_places[None, :] <= places[:, None]
        )
        return (decoder_bucket(places, dec_places), allowed)

    def cross_layout(offset, length):
        return (None, dec_segments[:, None] == enc_segments[None, :])

    enc_set = (
        lax.all_gather(encoder_query, "fsdp", axis=0, tiled=True),
        lax.all_gather(encoder_keyval, "fsdp", axis=0, tiled=True),
        lax.all_gather(encoder_proj, "fsdp", axis=0, tiled=True),
        lax.all_gather(encoder_inner, "fsdp", axis=0, tiled=True),
        lax.all_gather(encoder_outer, "fsdp", axis=0, tiled=True),
        lax.all_gather(encoder_gains, "fsdp", axis=0, tiled=True),
        lax.all_gather(encoder_table, "fsdp", axis=0, tiled=True),
    )
    enc_stream = enc_tokens.astype(jnp.float32)
    enc_final, enc_stored = encoder_forward(enc_stream, enc_set, enc_layout)
    memory = enc_final.astype(jnp.bfloat16)
    dec_set = (
        lax.all_gather(decoder_query, "fsdp", axis=0, tiled=True),
        lax.all_gather(decoder_keyval, "fsdp", axis=0, tiled=True),
        lax.all_gather(decoder_proj, "fsdp", axis=0, tiled=True),
        lax.all_gather(cross_query, "fsdp", axis=0, tiled=True),
        lax.all_gather(cross_keyval, "fsdp", axis=0, tiled=True),
        lax.all_gather(cross_proj, "fsdp", axis=0, tiled=True),
        lax.all_gather(decoder_inner, "fsdp", axis=0, tiled=True),
        lax.all_gather(decoder_outer, "fsdp", axis=0, tiled=True),
        lax.all_gather(decoder_gains, "fsdp", axis=0, tiled=True),
        lax.all_gather(decoder_table, "fsdp", axis=0, tiled=True),
    )
    dec_stream = dec_tokens.astype(jnp.float32)
    dec_final, dec_stored = decoder_forward(dec_stream, dec_set, self_layout, cross_layout, memory)
    dec_live = (dec_segments >= 0).astype(jnp.float32)[:, None]
    dec_gradient, dec_grads, dec_table_grad, memory_grad = decoder_backward(
        dec_stream,
        dec_set,
        self_layout,
        cross_layout,
        memory,
        dec_stored,
        dec_upstream.astype(jnp.float32) * dec_live,
    )
    enc_set = (
        lax.all_gather(encoder_query, "fsdp", axis=0, tiled=True),
        lax.all_gather(encoder_keyval, "fsdp", axis=0, tiled=True),
        lax.all_gather(encoder_proj, "fsdp", axis=0, tiled=True),
        lax.all_gather(encoder_inner, "fsdp", axis=0, tiled=True),
        lax.all_gather(encoder_outer, "fsdp", axis=0, tiled=True),
        lax.all_gather(encoder_gains, "fsdp", axis=0, tiled=True),
        lax.all_gather(encoder_table, "fsdp", axis=0, tiled=True),
    )
    enc_again_final, enc_stored = encoder_forward(enc_stream, enc_set, enc_layout)
    enc_live = (enc_segments >= 0).astype(jnp.float32)[:, None]
    enc_gradient, enc_grads, enc_table_grad = encoder_backward(
        enc_stream,
        enc_set,
        enc_layout,
        enc_stored,
        enc_upstream.astype(jnp.float32) * enc_live + memory_grad,
    )
    shares = (
        lax.psum_scatter(enc_grads[0], ("dp", "fsdp"), scatter_dimension=0, tiled=True),
        lax.psum_scatter(enc_grads[1], ("dp", "fsdp"), scatter_dimension=0, tiled=True),
        lax.psum_scatter(enc_grads[2], ("dp", "fsdp"), scatter_dimension=0, tiled=True),
        lax.psum_scatter(enc_grads[3], ("dp", "fsdp"), scatter_dimension=0, tiled=True),
        lax.psum_scatter(enc_grads[4], ("dp", "fsdp"), scatter_dimension=0, tiled=True),
        lax.psum_scatter(enc_grads[5], ("dp", "fsdp"), scatter_dimension=0, tiled=True),
        lax.psum_scatter(dec_grads[0], ("dp", "fsdp"), scatter_dimension=0, tiled=True),
        lax.psum_scatter(dec_grads[1], ("dp", "fsdp"), scatter_dimension=0, tiled=True),
        lax.psum_scatter(dec_grads[2], ("dp", "fsdp"), scatter_dimension=0, tiled=True),
        lax.psum_scatter(dec_grads[3], ("dp", "fsdp"), scatter_dimension=0, tiled=True),
        lax.psum_scatter(dec_grads[4], ("dp", "fsdp"), scatter_dimension=0, tiled=True),
        lax.psum_scatter(dec_grads[5], ("dp", "fsdp"), scatter_dimension=0, tiled=True),
        lax.psum_scatter(dec_grads[6], ("dp", "fsdp"), scatter_dimension=0, tiled=True),
        lax.psum_scatter(dec_grads[7], ("dp", "fsdp"), scatter_dimension=0, tiled=True),
        lax.psum_scatter(dec_grads[8], ("dp", "fsdp"), scatter_dimension=0, tiled=True),
    )
    enc_shares = tuple(shares[:6])
    dec_shares = tuple(shares[6:])
    table_shares = lax.psum((enc_table_grad, dec_table_grad), ("dp", "fsdp"))
    return (
        (memory, dec_final.astype(jnp.bfloat16), enc_gradient, dec_gradient)
        + tuple(enc_shares)
        + (table_shares[0],)
        + tuple(dec_shares)
        + (table_shares[1],)
    )


def solution(mesh):
    in_specs = (
        P(("dp", "fsdp"), None),
        P(("dp", "fsdp"), None),
        P(("dp", "fsdp")),
        P(("dp", "fsdp")),
        P(("dp", "fsdp"), None),
        P(("dp", "fsdp"), None),
        P("fsdp", None),
        P("fsdp", None),
        P("fsdp", None),
        P("fsdp", None),
        P("fsdp", None),
        P("fsdp", None),
        P("fsdp", None),
        P("fsdp", None),
        P("fsdp", None),
        P("fsdp", None),
        P("fsdp", None),
        P("fsdp", None),
        P("fsdp", None),
        P("fsdp", None),
        P("fsdp", None),
        P("fsdp", None),
        P("fsdp", None),
    )
    out_specs = (
        P(("dp", "fsdp"), None),
        P(("dp", "fsdp"), None),
        P(("dp", "fsdp"), None),
        P(("dp", "fsdp"), None),
        P(("dp", "fsdp"), None),
        P(("dp", "fsdp"), None),
        P(("dp", "fsdp"), None),
        P(("dp", "fsdp"), None),
        P(("dp", "fsdp"), None),
        P(("dp", "fsdp"), None),
        P(),
        P(("dp", "fsdp"), None),
        P(("dp", "fsdp"), None),
        P(("dp", "fsdp"), None),
        P(("dp", "fsdp"), None),
        P(("dp", "fsdp"), None),
        P(("dp", "fsdp"), None),
        P(("dp", "fsdp"), None),
        P(("dp", "fsdp"), None),
        P(("dp", "fsdp"), None),
        P(),
    )
    return jax.shard_map(body, mesh=mesh, in_specs=in_specs, out_specs=out_specs, check_vma=False)
```

profile of v0, /device:TPU:0, one launch (start us, length us, event | category | flops | bytes accessed | tf_op | source)
XLA Modules:
  0.0 2398.7 jit_solution(16198302836555184641)
XLA Ops:
  50.9 8.7 all-gather.14.cloned.1.call-done
  63.6 33.6 %all-gather.24.cloned.1.call-done = bf16[768,1536]{1,0:T(8,128)(2,1)} async-done(((bf16[384,1536]{1,0:T(8,128)(2,1)}), bf16[768,1536]{1,0:T(8,128)(2,1)}) %all-gather.24.cloned.1.call-update) | async-done | bytes 2359312 | tf_op jit(solution)/shard_map/all_gather | solution.py:390
  101.7 33.0 %all-gather.16.cloned.1.call-done = bf16[768,1536]{1,0:T(8,128)(2,1)} async-done(((bf16[384,1536]{1,0:T(8,128)(2,1)}), bf16[768,1536]{1,0:T(8,128)(2,1)}) %all-gather.16.cloned.1.call-update) | async-done | bytes 2359312 | tf_op jit(solution)/shard_map/all_gather | solution.py:378
  144.7 204.2 %while.9 = (s32[]{:T(128)}, bf16[2,512,12,64]{1,3,2,0:T(8,128)(2,1)}, s32[2]{0:T(128)S(1)}, s32[1024]{0:T(1024)S(1)}, bf16[1024,12,64]{0,2,1:T(8,128)(2,1)}, /*i...) while((s32[]{:T(128)}, ...), condition=%wide.region_4.5_spmd.clone, body=%wide.region_1.4_spmd.clone.sunk | while | flops 4102955520 | bytes 167313120 | solution.py:101
  148.9 23.7 fusion.375
  172.5 28.3 %fusion.376 = f32[12,512,1024]{2,1,0:T(8,128)} fusion(f32[512,1024,12]{1,2,0:T(8,128)} %fusion.375, pred[512,1024]{1,0:T(8,128)(4,1)S(1)} %broadcast_compare_fusion.7, bf16[1024,12,64]{0,2,1:T(8,128)(2,1)S(1)} %get-tuple-element.863, bf16[1024,12,64]{0,2,1:T(8,128)(2,1)S(1)} %copy-done.2, s32[]{:T(128)S(6)} %select_n.137), kind=kOutput, calls=%fused_computation.8.clone.1 | convolution fusion | flops 817889280 | bytes 53215236 | tf_op jit(solution)/shard_map/while/body/eval_jaxpr/qhd,khd->hqk/dot_general | solution.py:72
  200.9 21.5 fusion.377
  222.3 25.4 %fusion.378 = bf16[2,512,12,64]{1,3,2,0:T(8,128)(2,1)} fusion(bf16[2,512,12,64]{1,3,2,0:T(8,128)(2,1)} %get-tuple-element.847, s32[]{:T(128)S(6)} %copy.201, bf16[1024,12,64]{0,2,1:T(8,128)(2,1)S(1)} %get-tuple-element.865, f32[12,512]{1,0:T(8,128)S(1)} %fusion.377, f32[12,512,1024]{2,1,0:T(8,128)} %fusion.376), kind=kOutput, calls=%fused_computation.26.clone.1 | convolution fusion | flops 824581120 | bytes 52715524 | tf_op jit(solution)/shard_map/while/body/eval_jaxpr/hqk,khd->qhd/dot_general | solution.py:96
  251.6 23.7 fusion.375
  275.2 28.0 %fusion.376 = f32[12,512,1024]{2,1,0:T(8,128)} fusion(f32[512,1024,12]{1,2,0:T(8,128)} %fusion.375, pred[512,1024]{1,0:T(8,128)(4,1)S(1)} %broadcast_compare_fusion.7, bf16[1024,12,64]{0,2,1:T(8,128)(2,1)S(1)} %get-tuple-element.863, bf16[1024,12,64]{0,2,1:T(8,128)(2,1)S(1)} %copy-done.2, s32[]{:T(128)S(6)} %select_n.137), kind=kOutput, calls=%fused_computation.8.clone.1 | convolution fusion | flops 817889280 | bytes 53215236 | tf_op jit(solution)/shard_map/while/body/eval_jaxpr/qhd,khd->hqk/dot_general | solution.py:72
  303.2 19.9 fusion.377
  323.2 25.5 %fusion.378 = bf16[2,512,12,64]{1,3,2,0:T(8,128)(2,1)} fusion(bf16[2,512,12,64]{1,3,2,0:T(8,128)(2,1)} %get-tuple-element.847, s32[]{:T(128)S(6)} %copy.201, bf16[1024,12,64]{0,2,1:T(8,128)(2,1)S(1)} %get-tuple-element.865, f32[12,512]{1,0:T(8,128)S(1)} %fusion.377, f32[12,512,1024]{2,1,0:T(8,128)} %fusion.376), kind=kOutput, calls=%fused_computation.26.clone.1 | convolution fusion | flops 824581120 | bytes 52715524 | tf_op jit(solution)/shard_map/while/body/eval_jaxpr/hqk,khd->qhd/dot_general | solution.py:96
  372.1 17.8 add_convert_fusion
  418.8 43.2 %all-gather.36.cloned.1.call-done = bf16[768,3072]{1,0:T(8,128)(2,1)} async-done(((bf16[384,3072]{1,0:T(8,128)(2,1)}), bf16[768,3072]{1,0:T(8,128)(2,1)}) %all-gather.36.cloned.1.call-update) | async-done | bytes 4718608 | tf_op jit(solution)/shard_map/all_gather | solution.py:395
  467.6 58.6 %all-gather.38.cloned.1.call-done = bf16[3072,768]{1,0:T(8,128)(2,1)} async-done(((bf16[1536,768]{1,0:T(8,128)(2,1)}), bf16[3072,768]{1,0:T(8,128)(2,1)}) %all-gather.38.cloned.1.call-update) | async-done | bytes 4718608 | tf_op jit(solution)/shard_map/all_gather | solution.py:396
  542.5 12.0 multiply_reduce_fusion.1
  556.1 6.8 multiply_convert_fusion.1
  569.6 158.3 %while.10 = (s32[]{:T(128)}, bf16[2,512,12,64]{1,3,2,0:T(8,128)(2,1)}, f32[2,12,512]{2,1,0:T(8,128)}, s32[2]{0:T(128)S(1)}, s32[1024]{0:T(1024)S(1)}, /*index=5*...) while((s32[]{:T(128)}, ...), condition=%wide.region_18.19_spmd.clone, body=%wide.region_15.18_spmd.clone.sunk | while | flops 4109232640 | bytes 154902288 | solution.py:101
  573.7 23.7 fusion.383
  597.3 28.6 %fusion.384 = (f32[12,512]{1,0:T(8,128)S(1)}, f32[12,512,1024]{2,1,0:T(8,128)}) fusion(f32[512,1024,12]{1,2,0:T(8,128)} %fusion.383, bf16[1024,12,64]{0,2,1:T(8,128)(2,1)S(1)} %get-tuple-element.902, bf16[1024,12,64]{0,2,1:T(8,128)(2,1)S(1)} %copy-done.3, s32[]{:T(128)S(6)} %select_n.139, pred[512,1024]{1,0:T(8,128)(4,1)S(1)} %broadcast_compare_fusion.8), kind=kOutput, calls=%fused_computation.346.clone.1 | convolution fusion | flops 824174592 | bytes 53239812 | tf_op jit(solution)/shard_map/while/body/eval_jaxpr/qhd,khd->hqk/dot_general | solution.py:72
  626.0 11.0 fusion.385
  637.0 10.4 fusion.386
  652.4 23.7 fusion.383
  676.1 28.8 %fusion.384 = (f32[12,512]{1,0:T(8,128)S(1)}, f32[12,512,1024]{2,1,0:T(8,128)}) fusion(f32[512,1024,12]{1,2,0:T(8,128)} %fusion.383, bf16[1024,12,64]{0,2,1:T(8,128)(2,1)S(1)} %get-tuple-element.902, bf16[1024,12,64]{0,2,1:T(8,128)(2,1)S(1)} %copy-done.3, s32[]{:T(128)S(6)} %select_n.139, pred[512,1024]{1,0:T(8,128)(4,1)S(1)} %broadcast_compare_fusion.8), kind=kOutput, calls=%fused_computation.346.clone.1 | convolution fusion | flops 824174592 | bytes 53239812 | tf_op jit(solution)/shard_map/while/body/eval_jaxpr/qhd,khd->hqk/dot_general | solution.py:72
  704.9 11.1 fusion.385
  716.0 10.4 fusion.386
  744.6 7.6 fusion.146
  752.4 8.5 fusion.235
  766.9 16.8 fusion.96
  783.7 10.1 multiply_reduce_fusion.2
  804.6 472.4 %while.11 = (s32[]{:T(128)}, f32[1024,12,64]{0,2,1:T(8,128)}, f32[1024,12,64]{0,2,1:T(8,128)}, f32[32,12]{0,1:T(8,128)S(1)}, bf16[2,512,12,64]{1,3,2,0:T(8,128)(...) while((s32[]{:T(128)}, f32[1024,12,64]{0,2,1:T(8,128)}, ...), condition=%wide.region_23.24_spmd.clone, body=%wide.region_21.23_spmd.clone.sunk | while | flops 8973184000 | bytes 459451456 | solution.py:148
  816.6 10.2 fusion.398
  826.8 23.7 fusion.400
  850.5 30.6 %copy.193 = f32[512,1024,12]{1,0,2:T(8,128)} copy(f32[512,1024,12]{0,2,1:T(8,128)} %fusion.400) | data formatting | bytes 50331648 | tf_op jit(solution)/shard_map/while/body/eval_jaxpr/qkb,hb->hqk/dot_general | solution.py:76
  881.1 27.1 %multiply_reduce_fusion.14 = (f32[12,512]{1,0:T(8,128)S(1)}, f32[12,512,1024]{2,1,0:T(8,128)}) fusion(f32[12,512,1024]{2,1,0:T(8,128)} %fusion.398, f32[12,512]{1,0:T(8,128)S(1)} %dynamic-slice_bitcast_fusion.2, f32[512,1024,12]{1,0,2:T(8,128)} %copy.193, bf16[1024,12,64]{0,2,1:T(8,128)(2,1)S(1)} %get-tuple-element.951, ...), kind=kOutput, calls=%fused_computation.73.clone.1 | convolution fusion | flops 836757504 | bytes 78430208 | tf_op jit(solution)/shard_map/while/body/eval_jaxpr/qhd,khd->hqk/dot_general | solution.py:72
  908.3 26.0 %subtract_multiply_fusion.3 = f32[12,512,1024]{2,1,0:T(8,128)} fusion(f32[12,512,1024]{2,1,0:T(8,128)} %get-tuple-element.832, f32[12,512,1024]{2,1,0:T(8,128)} %fusion.398, f32[12,512]{1,0:T(8,128)S(1)} %get-tuple-element.833), kind=kLoop, calls=%fused_computation.72.clone.1 | loop fusion | flops 12582912 | bytes 75522048 | tf_op jit(solution)/shard_map/while/body/eval_jaxpr/mul | solution.py:123
  934.3 12.2 bitcast_add_fusion.9
  946.5 11.4 bitcast_dynamic-update-slice_fusion.5
  957.9 12.1 bitcast_add_fusion.8
  970.0 30.8 %copy.194 = f32[12,512,1024]{1,0,2:T(8,128)} copy(f32[12,512,1024]{2,1,0:T(8,128)} %subtract_multiply_fusion.3) | data formatting | bytes 50331648 | tf_op jit(solution)/shard_map/while/body/eval_jaxpr/mul | solution.py:123
  1000.8 38.9 %fusion.401 = f32[32,12]{0,1:T(8,128)S(1)} fusion(f32[12,512,1024]{1,0,2:T(8,128)} %copy.194, s32[512,1024]{0,1:T(8,128)} %copy-done, f32[32,12]{0,1:T(8,128)S(1)} %get-tuple-element.929, pred[]{:T(512)S(6)} %compare.3), kind=kOutput, calls=%fused_computation.96.clone.1 | convolution fusion | flops 2432697088 | bytes 27266048 | tf_op jit(solution)/shard_map/while/body/eval_jaxpr/hqk,qkb->bh/dot_general | solution.py:125
  1045.2 10.2 fusion.398
  1055.4 23.7 fusion.400
  1079.2 30.4 %copy.193 = f32[512,1024,12]{1,0,2:T(8,128)} copy(f32[512,1024,12]{0,2,1:T(8,128)} %fusion.400) | data formatting | bytes 50331648 | tf_op jit(solution)/shard_map/while/body/eval_jaxpr/qkb,hb->hqk/dot_general | solution.py:76
  1109.5 26.7 %multiply_reduce_fusion.14 = (f32[12,512]{1,0:T(8,128)S(1)}, f32[12,512,1024]{2,1,0:T(8,128)}) fusion(f32[12,512,1024]{2,1,0:T(8,128)} %fusion.398, f32[12,512]{1,0:T(8,128)S(1)} %dynamic-slice_bitcast_fusion.2, f32[512,1024,12]{1,0,2:T(8,128)} %copy.193, bf16[1024,12,64]{0,2,1:T(8,128)(2,1)S(1)} %get-tuple-element.951, ...), kind=kOutput, calls=%fused_computation.73.clone.1 | convolution fusion | flops 836757504 | bytes 78430208 | tf_op jit(solution)/shard_map/while/body/eval_jaxpr/qhd,khd->hqk/dot_general | solution.py:72
  1136.2 25.7 %subtract_multiply_fusion.3 = f32[12,512,1024]{2,1,0:T(8,128)} fusion(f32[12,512,1024]{2,1,0:T(8,128)} %get-tuple-element.832, f32[12,512,1024]{2,1,0:T(8,128)} %fusion.398, f32[12,512]{1,0:T(8,128)S(1)} %get-tuple-element.833), kind=kLoop, calls=%fused_computation.72.clone.1 | loop fusion | flops 12582912 | bytes 75522048 | tf_op jit(solution)/shard_map/while/body/eval_jaxpr/mul | solution.py:123
  1162.0 13.1 bitcast_add_fusion.9
  1175.1 11.3 bitcast_dynamic-update-slice_fusion.5
  1186.4 13.0 bitcast_add_fusion.8
  1199.4 30.8 %copy.194 = f32[12,512,1024]{1,0,2:T(8,128)} copy(f32[12,512,1024]{2,1,0:T(8,128)} %subtract_multiply_fusion.3) | data formatting | bytes 50331648 | tf_op jit(solution)/shard_map/while/body/eval_jaxpr/mul | solution.py:123
  1230.2 38.9 %fusion.401 = f32[32,12]{0,1:T(8,128)S(1)} fusion(f32[12,512,1024]{1,0,2:T(8,128)} %copy.194, s32[512,1024]{0,1:T(8,128)} %copy-done, f32[32,12]{0,1:T(8,128)S(1)} %get-tuple-element.929, pred[]{:T(512)S(6)} %compare.3), kind=kOutput, calls=%fused_computation.96.clone.1 | convolution fusion | flops 2432697088 | bytes 27266048 | tf_op jit(solution)/shard_map/while/body/eval_jaxpr/hqk,qkb->bh/dot_general | solution.py:125
  1296.2 7.2 fusion.141
  1324.7 7.0 fusion.203
  1339.5 10.4 fusion.234
  1351.3 13.6 fusion.113
  1391.6 40.1 %all-reduce.2 = (f32[768,2]{0,1:T(2,128)S(1)}, f32[32,12]{0,1:T(8,128)}, f32[768,3]{0,1:T(4,128)S(1)}, f32[32,12]{0,1:T(8,128)}) all-reduce(f32[768,2]{0,1:T(2,128)S(1)} %pad_maximum_fusion.10, f32[32,12]{0,1:T(8,128)S(1)} %copy-done.89, f32[768,3]{0,1:T(4,128)S(1)} %pad_maximum_fusion.9, ...), channel_id=7, replica_groups=mesh['dp'=16,'fsdp'=2] {'dp','fsdp'}, use_global_device_ids=true, to_apply=%region_35.36.clone | all-reduce | flops 4608 | bytes 36864
  1440.1 48.3 %reduce-scatter.26.cloned.1.call-done = f32[24,768]{1,0:T(8,128)} async-done(((f32[768,768]{1,0:T(8,128)}), f32[24,768]{1,0:T(8,128)}) %reduce-scatter.26.cloned.1.call-update) | async-done | bytes 73744 | tf_op jit(solution)/shard_map/reduce_scatter | solution.py:437
  1488.4 111.9 %reduce-scatter.34.cloned.1.call-done = f32[24,1536]{1,0:T(8,128)} async-done(((f32[768,1536]{1,0:T(8,128)}), f32[24,1536]{1,0:T(8,128)}) %reduce-scatter.34.cloned.1.call-update) | async-done | bytes 147472 | tf_op jit(solution)/shard_map/reduce_scatter | solution.py:441
  1600.3 113.0 %reduce-scatter.18.cloned.1.call-done = f32[24,1536]{1,0:T(8,128)} async-done(((f32[768,1536]{1,0:T(8,128)}), f32[24,1536]{1,0:T(8,128)}) %reduce-scatter.18.cloned.1.call-update) | async-done | bytes 147472 | tf_op jit(solution)/shard_map/reduce_scatter | solution.py:432
  1713.3 112.2 %reduce-scatter.28.cloned.1.call-done = f32[24,1536]{1,0:T(8,128)} async-done(((f32[768,1536]{1,0:T(8,128)}), f32[24,1536]{1,0:T(8,128)}) %reduce-scatter.28.cloned.1.call-update) | async-done | bytes 147472 | tf_op jit(solution)/shard_map/reduce_scatter | solution.py:438
  1825.5 142.1 %reduce-scatter.40.cloned.1.call-done = f32[96,768]{1,0:T(8,128)} async-done(((f32[3072,768]{1,0:T(8,128)}), f32[96,768]{1,0:T(8,128)}) %reduce-scatter.40.cloned.1.call-update) | async-done | bytes 294928 | tf_op jit(solution)/shard_map/reduce_scatter | solution.py:444
  1967.6 140.9 %reduce-scatter.38.cloned.1.call-done = f32[24,3072]{1,0:T(8,128)} async-done(((f32[768,3072]{1,0:T(8,128)}), f32[24,3072]{1,0:T(8,128)}) %reduce-scatter.38.cloned.1.call-update) | async-done | bytes 294928 | tf_op jit(solution)/shard_map/reduce_scatter | solution.py:443
  2108.6 142.1 %reduce-scatter.22.cloned.1.call-done = f32[24,3072]{1,0:T(8,128)} async-done(((f32[768,3072]{1,0:T(8,128)}), f32[24,3072]{1,0:T(8,128)}) %reduce-scatter.22.cloned.1.call-update) | async-done | bytes 294928 | tf_op jit(solution)/shard_map/reduce_scatter | solution.py:434
  2250.7 140.9 %reduce-scatter.24.cloned.1.call-done = f32[96,768]{1,0:T(8,128)} async-done(((f32[3072,768]{1,0:T(8,128)}), f32[96,768]{1,0:T(8,128)}) %reduce-scatter.24.cloned.1.call-update) | async-done | bytes 294928 | tf_op jit(solution)/shard_map/reduce_scatter | solution.py:435
  (544 shorter events, 285.7 us)
Async XLA Ops:
  7.2 41.0 %all-gather.26.cloned.1.call-start = ((), (), s32[]{:S(2)}) async-start(), calls=%async_computation.19 | async-start | bytes 1769472 | tf_op jit(solution)/shard_map/all_gather | solution.py:389
  7.9 51.7 %all-gather.14.cloned.1.call-start = ((), (), s32[]{:S(2)}) async-start(), calls=%async_computation.13 | async-start | bytes 1769472 | tf_op jit(solution)/shard_map/all_gather | solution.py:377
  8.7 88.6 %all-gather.24.cloned.1.call-start = ((), (), s32[]{:S(2)}) async-start(), calls=%async_computation.18 | async-start | bytes 3538944 | tf_op jit(solution)/shard_map/all_gather | solution.py:390
  9.4 125.3 %all-gather.16.cloned.1.call-start = ((), (), s32[]{:S(2)}) async-start(), calls=%async_computation.14 | async-start | bytes 3538944 | tf_op jit(solution)/shard_map/all_gather | solution.py:378
  10.0 343.5 %all-gather.18.cloned.1.call-start = ((), (), s32[]{:S(2)}) async-start(), calls=%async_computation.15 | async-start | bytes 1769472 | tf_op jit(solution)/shard_map/all_gather | solution.py:379
  10.6 354.6 %all-gather.28.cloned.1.call-start = ((), (), s32[]{:S(2)}) async-start(), calls=%async_computation.20 | async-start | bytes 1769472 | tf_op jit(solution)/shard_map/all_gather | solution.py:391
  11.2 357.9 %all-gather.32.cloned.1.call-start = ((), (), s32[]{:S(2)}) async-start(), calls=%async_computation.22 | async-start | bytes 1769472 | tf_op jit(solution)/shard_map/all_gather | solution.py:392
  11.9 360.2 %all-gather.20.cloned.1.call-start = ((), (), s32[]{:S(2)}) async-start(), calls=%async_computation.16 | async-start | bytes 7077888 | tf_op jit(solution)/shard_map/all_gather | solution.py:380
  12.7 359.4 %all-gather.22.cloned.1.call-start = ((), (), s32[]{:S(2)}) async-start(), calls=%async_computation.17 | async-start | bytes 7077888 | tf_op jit(solution)/shard_map/all_gather | solution.py:381
  13.4 376.5 %all-gather.30.cloned.1.call-start = ((), (), s32[]{:S(2)}) async-start(), calls=%async_computation.21 | async-start | bytes 3538944 | tf_op jit(solution)/shard_map/all_gather | solution.py:393
  14.0 11.8 copy-start.136
  14.0 16.8 copy-start.132
  14.0 21.2 copy-start.133
  14.0 401.7 %all-gather.34.cloned.1.call-start = ((), (), s32[]{:S(2)}) async-start(), calls=%async_computation.23 | async-start | bytes 1769472 | tf_op jit(solution)/shard_map/all_gather | solution.py:394
  14.8 447.2 %all-gather.36.cloned.1.call-start = ((), (), s32[]{:S(2)}) async-start(), calls=%async_computation.24 | async-start | bytes 7077888 | tf_op jit(solution)/shard_map/all_gather | solution.py:395
  15.4 510.8 %all-gather.38.cloned.1.call-start = ((), (), s32[]{:S(2)}) async-start(), calls=%async_computation.25 | async-start | bytes 7077888 | tf_op jit(solution)/shard_map/all_gather | solution.py:396
  16.1 1423.9 %reduce-scatter.36.cloned.1.call-start = ((), (), s32[]{:S(2)}) async-start(), calls=%async_computation.36 | async-start | bytes 2433024 | tf_op jit(solution)/shard_map/reduce_scatter | solution.py:442
  19.3 25.3 %copy-start.60 = (s32[256,256]{0,1:T(8,128)}, s32[256,256]{0,1:T(8,128)S(1)}, u32[]{:S(2)}) copy-start(s32[256,256]{0,1:T(8,128)S(1)} %compare_select_fusion.3) | copy-start | bytes 786436
  20.0 77.3 %copy-start.107 = (f32[256]{0:T(256)}, f32[256]{0:T(256)S(1)}, u32[]{:S(2)}) copy-start(f32[256]{0:T(256)S(1)} %fusion.212) | copy-start | bytes 3076
  25.9 108.9 %copy-start.113 = (f32[768]{0:T(1024)}, f32[768]{0:T(1024)S(1)}, u32[]{:S(2)}) copy-start(f32[768]{0:T(1024)S(1)} %get-tuple-element.545) | copy-start | bytes 9220
  30.9 66.4 %copy-start.93 = (f32[768]{0:T(1024)}, f32[768]{0:T(1024)S(1)}, u32[]{:S(2)}) copy-start(f32[768]{0:T(1024)S(1)} %get-tuple-element.543) | copy-start | bytes 9220
  41.3 93.4 %copy-start.17 = (bf16[1024,768]{0,1:T(8,128)(2,1)}, bf16[1024,768]{0,1:T(8,128)(2,1)S(1)}, u32[]{:S(2)}) copy-start(bf16[1024,768]{0,1:T(8,128)(2,1)S(1)} %copy.131) | copy-start | bytes 4718596
  41.7 93.0 %copy-start.118 = (f32[1024]{0:T(1024)}, f32[1024]{0:T(1024)S(1)}, u32[]{:S(2)}) copy-start(f32[1024]{0:T(1024)S(1)} %fusion.210) | copy-start | bytes 12292
  148.9 23.7 copy-start.2
  251.6 23.7 copy-start.2
  415.7 46.2 %copy-start.80 = (f32[768]{0:T(1024)S(1)}, f32[768]{0:T(1024)}, u32[]{:S(2)}) copy-start(f32[768]{0:T(1024)} %get-tuple-element.541) | copy-start | bytes 9220
  418.8 115.9 %copy-start.103 = (f32[256]{0:T(256)}, f32[256]{0:T(256)S(1)}, u32[]{:S(2)}) copy-start(f32[256]{0:T(256)S(1)} %fusion.214) | copy-start | bytes 3076
  461.9 64.2 %copy-start.128 = (f32[256]{0:T(256)S(1)}, f32[256]{0:T(256)}, u32[]{:S(2)}) copy-start(f32[256]{0:T(256)} %compare_convert_fusion.1) | copy-start | bytes 3076
  537.7 902.3 %reduce-scatter.32.cloned.1.call-start = ((), (), s32[]{:S(2)}) async-start(), calls=%async_computation.34 | async-start | bytes 2433024 | tf_op jit(solution)/shard_map/reduce_scatter | solution.py:440
  540.6 13.9 copy-start.91
  542.5 12.0 slice-start
  542.5 12.0 slice-start.1
  542.5 13.5 slice-start.2
  568.3 871.8 %reduce-scatter.30.cloned.1.call-start = ((), (), s32[]{:S(2)}) async-start(), calls=%async_computation.33 | async-start | bytes 2433024 | tf_op jit(solution)/shard_map/reduce_scatter | solution.py:439
  573.7 23.7 copy-start.3
  626.0 11.1 copy-start.38
  652.4 23.7 copy-start.3
  704.8 11.1 copy-start.38
  735.0 58.8 %copy-start.85 = (f32[1024]{0:T(1024)}, f32[1024]{0:T(1024)S(1)}, u32[]{:S(2)}) copy-start(f32[1024]{0:T(1024)S(1)} %fusion.211) | copy-start | bytes 12292
  752.3 687.8 %reduce-scatter.20.cloned.1.call-start = ((), (), s32[]{:S(2)}) async-start(), calls=%async_computation.28 | async-start | bytes 2433024 | tf_op jit(solution)/shard_map/reduce_scatter | solution.py:433
  766.9 16.8 copy-start.29
  799.4 640.6 %reduce-scatter.16.cloned.1.call-start = ((), (), s32[]{:S(2)}) async-start(), calls=%async_computation.26 | async-start | bytes 2433024 | tf_op jit(solution)/shard_map/reduce_scatter | solution.py:431
  811.1 15.7 copy-start.58
  816.6 10.2 copy-start
  908.3 26.0 %copy-start.11 = (bf16[1024,12,64]{0,2,1:T(8,128)(2,1)S(1)}, bf16[1024,12,64]{0,2,1:T(8,128)(2,1)}, u32[]{:S(2)}) copy-start(bf16[1024,12,64]{0,2,1:T(8,128)(2,1)} %get-tuple-element.954) | copy-start | bytes 4718596 | tf_op jit(solution)/shard_map/while
  946.5 11.4 copy-start.4
  1000.8 38.9 %copy-start.59 = (s32[1024]{0:T(1024)S(1)}, s32[1024]{0:T(1024)}, u32[]{:S(2)}) copy-start(s32[1024]{0:T(1024)} %copy-done.58) | copy-start | bytes 12292 | tf_op jit(solution)/shard_map/while
  1000.8 38.9 %copy-start.142 = (s32[2]{0:T(128)S(1)}, s32[2]{0:T(128)}, u32[]{:S(2)}) copy-start(s32[2]{0:T(128)} %copy-done.141) | copy-start | bytes 28 | tf_op jit(solution)/shard_map/while
  1039.7 15.7 copy-start.58
  1045.2 10.2 copy-start
  1136.2 25.7 %copy-start.11 = (bf16[1024,12,64]{0,2,1:T(8,128)(2,1)S(1)}, bf16[1024,12,64]{0,2,1:T(8,128)(2,1)}, u32[]{:S(2)}) copy-start(bf16[1024,12,64]{0,2,1:T(8,128)(2,1)} %get-tuple-element.954) | copy-start | bytes 4718596 | tf_op jit(solution)/shard_map/while
  1175.1 11.3 copy-start.4
  1230.2 38.9 %copy-start.59 = (s32[1024]{0:T(1024)S(1)}, s32[1024]{0:T(1024)}, u32[]{:S(2)}) copy-start(s32[1024]{0:T(1024)} %copy-done.58) | copy-start | bytes 12292 | tf_op jit(solution)/shard_map/while
  1230.2 38.9 %copy-start.142 = (s32[2]{0:T(128)S(1)}, s32[2]{0:T(128)}, u32[]{:S(2)}) copy-start(s32[2]{0:T(128)} %copy-done.141) | copy-start | bytes 28 | tf_op jit(solution)/shard_map/while
  1284.6 203.8 %reduce-scatter.26.cloned.1.call-start = ((), (), s32[]{:S(2)}) async-start(), calls=%async_computation.31 | async-start | bytes 2433024 | tf_op jit(solution)/shard_map/reduce_scatter | solution.py:437
  1296.2 304.1 %reduce-scatter.34.cloned.1.call-start = ((), (), s32[]{:S(2)}) async-start(), calls=%async_computation.35 | async-start | bytes 4866048 | tf_op jit(solution)/shard_map/reduce_scatter | solution.py:441
  1303.5 409.8 %reduce-scatter.18.cloned.1.call-start = ((), (), s32[]{:S(2)}) async-start(), calls=%async_computation.27 | async-start | bytes 4866048 | tf_op jit(solution)/shard_map/reduce_scatter | solution.py:432
  1315.3 510.2 %reduce-scatter.28.cloned.1.call-start = ((), (), s32[]{:S(2)}) async-start(), calls=%async_computation.32 | async-start | bytes 4866048 | tf_op jit(solution)/shard_map/reduce_scatter | solution.py:438
  1322.8 644.8 %reduce-scatter.40.cloned.1.call-start = ((), (), s32[]{:S(2)}) async-start(), calls=%async_computation.38 | async-start | bytes 9732096 | tf_op jit(solution)/shard_map/reduce_scatter | solution.py:444
  1331.7 776.9 %reduce-scatter.38.cloned.1.call-start = ((), (), s32[]{:S(2)}) async-start(), calls=%async_computation.37 | async-start | bytes 9732096 | tf_op jit(solution)/shard_map/reduce_scatter | solution.py:443
  1338.8 911.9 %reduce-scatter.22.cloned.1.call-start = ((), (), s32[]{:S(2)}) async-start(), calls=%async_computation.29 | async-start | bytes 9732096 | tf_op jit(solution)/shard_map/reduce_scatter | solution.py:434
  1349.9 1041.8 %reduce-scatter.24.cloned.1.call-start = ((), (), s32[]{:S(2)}) async-start(), calls=%async_computation.30 | async-start | bytes 9732096 | tf_op jit(solution)/shard_map/reduce_scatter | solution.py:435
  1386.2 46.7 %copy-start.131 = (f32[256]{0:T(256)S(1)}, f32[256]{0:T(256)}, u32[]{:S(2)}) copy-start(f32[256]{0:T(256)} %copy-done.130) | copy-start | bytes 3076
  1386.2 46.7 %copy-start.31 = (f32[256,768]{1,0:T(8,128)S(1)}, f32[256,768]{1,0:T(8,128)}, u32[]{:S(2)}) copy-start(f32[256,768]{1,0:T(8,128)} %copy-done.30) | copy-start | bytes 2359300
  (121 other events, 446.1 us)
Sparse Core Ops, SparseCore 0:
  9.6 25.6 all-gather.25
  36.8 22.7 all-gather.13
  61.1 36.0 all-gather.23
  98.6 36.0 all-gather.15
  136.1 22.7 all-gather.17
  160.3 22.7 all-gather.27
  184.7 22.7 all-gather.31
  209.1 62.6 all-gather.19
  273.3 62.6 all-gather.21
  337.4 36.0 all-gather.29
  375.0 22.7 all-gather.33
  399.2 62.6 all-gather.35
  463.5 62.6 all-gather.37
  537.8 98.8 reduce-scatter.35
  643.3 98.0 reduce-scatter.31
  752.4 98.8 reduce-scatter.29
  857.8 98.0 reduce-scatter.19
  1284.8 98.8 reduce-scatter.15
  1390.3 98.0 reduce-scatter.25
  1494.3 105.9 reduce-scatter.33
  1607.3 105.9 reduce-scatter.17
  1719.4 106.1 reduce-scatter.27
  1833.0 134.6 reduce-scatter.39
  1974.0 134.5 reduce-scatter.37
  2116.0 134.6 reduce-scatter.21
  2257.0 134.5 reduce-scatter.23
where the time goes:
time: 2410 us; the launch traced here: 2400 us
  waiting for transfers between devices  1140 us (47%)
  matrix products  808 us (34%)
  local copies, waits for them, and re-layouts  198 us (8%)
  other arithmetic  160 us (7%)
  blocking collectives  58.3 us (2%)
    dot_general x8, matrix products, block_scores(): jnp.einsum('qhd,khd->hqk', query_block, key_heads, preferred_element_type...  173 us
    dot_general x7, matrix products, block_scores(): jnp.einsum('qkb,hb->hqk', onehot, table_t, precision=lax.Precision.HIGHEST)  146 us
    reduce_scatter x1, waiting for transfers between devices, body(): lax.psum_scatter(dec_grads[7], ('dp', 'fsdp'), scatter_dimension=0, tiled...  142 us
    reduce_scatter x1, waiting for transfers between devices, body(): lax.psum_scatter(enc_grads[3], ('dp', 'fsdp'), scatter_dimension=0, tiled...  142 us
    reduce_scatter x1, waiting for transfers between devices, body(): lax.psum_scatter(enc_grads[4], ('dp', 'fsdp'), scatter_dimension=0, tiled...  141 us
    reduce_scatter x1, waiting for transfers between devices, body(): lax.psum_scatter(dec_grads[6], ('dp', 'fsdp'), scatter_dimension=0, tiled...  141 us
    reduce_scatter x1, waiting for transfers between devices, body(): lax.psum_scatter(enc_grads[1], ('dp', 'fsdp'), scatter_dimension=0, tiled...  113 us
    reduce_scatter x1, waiting for transfers between devices, body(): lax.psum_scatter(dec_grads[1], ('dp', 'fsdp'), scatter_dimension=0, tiled...  112 us
  transfers between devices with their start and end apart: 26, of which 13 were waited for; matrix products, arithmetic and copies ran while one was open for 47% of the time, Pallas kernels for 0%

commit v1 on v0

v1 whole, which is shorter than its diff:
```python
import functools
import math

import jax
import jax.numpy as jnp
from jax import lax
from jax.experimental import pallas as pl
from jax.experimental.pallas import tpu as pltpu
from jax.sharding import PartitionSpec as P

H = 12
HD = 64
NB = 32
TILE = 128
BAND = 5
EPSILON = 1e-06
MASKED = -1e30
ENC_EDGES = (12, 16, 23, 32, 46, 64, 91)
DEC_EDGES = tuple((math.ceil(16 * 2 ** (3 * power / 16)) for power in range(1, 16)))
PADDING_LABEL = 1 << 20


def encoder_bucket(distance):
    reach = jnp.abs(distance)
    farther = 8 + sum(((reach >= threshold).astype(jnp.int32) for threshold in ENC_EDGES))
    return jnp.where(reach < 8, reach, farther) + 16 * (distance < 0).astype(jnp.int32)


def decoder_bucket(distance):
    ahead = jnp.maximum(distance, 0)
    farther = 16 + sum(((ahead >= threshold).astype(jnp.int32) for threshold in DEC_EDGES))
    return jnp.where(ahead < 16, ahead, farther)


def band_onehot(bucket_of):
    shape = (NB, BAND, TILE, TILE)
    step = lax.broadcasted_iota(jnp.int32, shape, 1) - 2
    key = lax.broadcasted_iota(jnp.int32, shape, 2)
    query = lax.broadcasted_iota(jnp.int32, shape, 3)
    bucket = bucket_of(step * TILE + query - key)
    return (bucket == lax.broadcasted_iota(jnp.int32, shape, 0)).reshape(NB, BAND * TILE * TILE)


def band_bias(table, bucket_of):
    onehot = band_onehot(bucket_of).astype(jnp.bfloat16)
    flat = lax.dot_general(
        table, onehot, (((0,), (0,)), ((), ())), preferred_element_type=jnp.float32
    )
    return flat.reshape(H, BAND, TILE, TILE)


def band_table_grad(band, bucket_of):
    onehot = band_onehot(bucket_of).astype(jnp.float32)
    return lax.dot_general(
        onehot,
        band.reshape(H, BAND * TILE * TILE),
        (((1,), (1,)), ((), ())),
        precision=lax.Precision.HIGHEST,
        preferred_element_type=jnp.float32,
    )


def key_bounds(query_labels, key_labels, query_rows, key_rows):
    queries = jnp.where(query_labels < 0, PADDING_LABEL, query_labels).reshape(-1, query_rows)
    keys = jnp.where(key_labels < 0, PADDING_LABEL, key_labels)
    first = jnp.sum((keys[None, :] < queries[:, :1]).astype(jnp.int32), axis=1)
    last = jnp.sum((keys[None, :] <= queries[:, -1:]).astype(jnp.int32), axis=1)
    return jnp.stack([first // key_rows, (last + key_rows - 1) // key_rows])


def fold_rows(value, combine):
    rows = value.shape[0]
    while rows > 8:
        rows //= 2
        value = combine(value[:rows], value[rows:])
    return value


def head_parts(block):
    lane = lax.broadcasted_iota(jnp.int32, block.shape, 1)
    zero = jnp.zeros_like(block)
    return (jnp.where(lane < HD, block, zero), jnp.where(lane < HD, zero, block))


def flip(value):
    return value.astype(jnp.float32).T


def band_index(query_tile, key_tile):
    return jnp.clip(query_tile - key_tile, -2, 2) + 2


def tile_mask(spec, key_tile, query_block, segk_ref, segq_ref):
    rows, lanes = spec["kb"], spec["qb"]
    start = pl.multiple_of(key_tile * rows, rows)
    labels = segk_ref[pl.ds(start, rows), :]
    labels = jnp.concatenate([labels] * (lanes // TILE), axis=1)
    mask = labels == segq_ref[...]
    if spec["causal"]:
        key = lax.broadcasted_iota(jnp.int32, (rows, lanes), 0) + key_tile * rows
        query = lax.broadcasted_iota(jnp.int32, (rows, lanes), 1) + query_block * lanes
        mask = mask & (key <= query)
    return mask


def tile_bias(spec, head, key_tile, query_block, bias_ref):
    rows, lanes = spec["kb"] // TILE, spec["qb"] // TILE
    return jnp.concatenate(
        [
            jnp.concatenate(
                [
                    bias_ref[
                        head, band_index(query_block * lanes + lane, key_tile * rows + row)
                    ]
                    for lane in range(lanes)
                ],
                axis=1,
            )
            for row in range(rows)
        ],
        axis=0,
    )


def dot_rows(former, latter):
    return lax.dot_general(
        former, latter, (((1,), (1,)), ((), ())), preferred_element_type=jnp.float32
    )


def dot_plain(former, latter):
    return jnp.dot(former, latter, preferred_element_type=jnp.float32)


def forward_kernel(spec, bounds_ref, q_ref, k_ref, v_ref, segq_ref, segk_ref, *rest):
    bias_ref, rest = (rest[0], rest[1:]) if spec["bias"] else (None, rest)
    o_ref, lse_ref, score_ref, vt_ref = rest
    kb, qb = spec["kb"], spec["qb"]
    block = pl.program_id(1)

    @pl.when(block == 0)
    def _():
        vt_ref[...] = flip(v_ref[...]).astype(jnp.bfloat16)

    parts = head_parts(q_ref[...])
    first, last = bounds_ref[0, block], bounds_ref[1, block]

    def score(tile, highest):
        start = pl.multiple_of(tile * kb, kb)
        keys = k_ref[pl.ds(start, kb), :]
        mask = tile_mask(spec, tile, block, segk_ref, segq_ref)
        fresh = []
        for head in range(2):
            s = dot_rows(keys, parts[head])
            if spec["bias"]:
                s = s + tile_bias(spec, head, tile, block, bias_ref)
            s = jnp.where(mask, s, MASKED)
            score_ref[head, pl.ds(start, kb), :] = s
            fresh.append(jnp.maximum(highest[head], fold_rows(s, jnp.maximum)))
        return tuple(fresh)

    low = jnp.full((8, qb), MASKED, jnp.float32)
    highest = lax.fori_loop(first, last, score, (low, low))
    top = [jnp.max(value, axis=0, keepdims=True) for value in highest]

    def exponent(tile, summed):
        start = pl.multiple_of(tile * kb, kb)
        fresh = []
        for head in range(2):
            e = jnp.exp(score_ref[head, pl.ds(start, kb), :] - top[head])
            score_ref[head, pl.ds(start, kb), :] = e
            fresh.append(summed[head] + fold_rows(e, jnp.add))
        return tuple(fresh)

    none = jnp.zeros((8, qb), jnp.float32)
    summed = lax.fori_loop(first, last, exponent, (none, none))
    total = [jnp.sum(value, axis=0, keepdims=True) for value in summed]
    scale = [1.0 / value for value in total]

    def mix(tile, mixed):
        start = pl.multiple_of(tile * kb, kb)
        fresh = []
        for head in range(2):
            weights = (score_ref[head, pl.ds(start, kb), :] * scale[head]).astype(jnp.bfloat16)
            values = vt_ref[pl.ds(head * HD, HD), pl.ds(start, kb)]
            fresh.append(mixed[head] + dot_plain(values, weights))
        return tuple(fresh)

    nothing = jnp.zeros((HD, qb), jnp.float32)
    mixed = lax.fori_loop(first, last, mix, (nothing, nothing))
    o_ref[...] = flip(jnp.concatenate(mixed, axis=0)).astype(jnp.bfloat16)
    lse_ref[0] = jnp.concatenate(
        [top[head] + jnp.log(total[head]) for head in range(2)], axis=0
    )


def backward_kernel(
    spec, bounds_ref, q_ref, k_ref, v_ref, do_ref, lse_ref, segq_ref, segk_ref, *rest
):
    bias_ref, rest = (rest[0], rest[1:]) if spec["bias"] else (None, rest)
    dq_ref, dkv_ref, rest = rest[0], rest[1], rest[2:]
    band_ref, rest = (rest[0], rest[1:]) if spec["bias"] else (None, rest)
    p_ref, dp_ref, dk_ref, dv_ref, kt_ref = rest
    kb, qb = spec["kb"], spec["qb"]
    pair, block = pl.program_id(0), pl.program_id(1)

    @pl.when(block == 0)
    def _():
        kt_ref[...] = flip(k_ref[...]).astype(jnp.bfloat16)
        dk_ref[...] = jnp.zeros_like(dk_ref)
        dv_ref[...] = jnp.zeros_like(dv_ref)
        if spec["bias"]:
            band_ref[...] = jnp.zeros_like(band_ref)

    parts = head_parts(q_ref[...])
    dparts = head_parts(do_ref[...])
    lse = lse_ref[0]
    first, last = bounds_ref[0, block], bounds_ref[1, block]

    def weigh(tile, delta):
        start = pl.multiple_of(tile * kb, kb)
        keys = k_ref[pl.ds(start, kb), :]
        values = v_ref[pl.ds(start, kb), :]
        mask = tile_mask(spec, tile, block, segk_ref, segq_ref)
        fresh = []
        dvalues = dv_ref[pl.ds(start, kb), :]
        for head in range(2):
            s = dot_rows(keys, parts[head])
            if spec["bias"]:
                s = s + tile_bias(spec, head, tile, block, bias_ref)
            p = jnp.exp(jnp.where(mask, s, MASKED) - lse[head : head + 1])
            dp = dot_rows(values, dparts[head])
            p_ref[head, pl.ds(start, kb), :] = p
            dp_ref[head, pl.ds(start, kb), :] = dp
            fresh.append(delta[head] + fold_rows(p * dp, jnp.add))
            dvalues = dvalues + dot_plain(p.astype(jnp.bfloat16), dparts[head])
        dv_ref[pl.ds(start, kb), :] = dvalues
        return tuple(fresh)

    none = jnp.zeros((8, qb), jnp.float32)
    delta = lax.fori_loop(first, last, weigh, (none, none))
    delta = [jnp.sum(value, axis=0, keepdims=True) for value in delta]

    def pull(tile, dquery):
        start = pl.multiple_of(tile * kb, kb)
        fresh = []
        dkeys = dk_ref[pl.ds(start, kb), :]
        for head in range(2):
            ds = p_ref[head, pl.ds(start, kb), :] * (
                dp_ref[head, pl.ds(start, kb), :] - delta[head]
            )
            if spec["bias"]:
                rows, lanes = kb // TILE, qb // TILE
                for row in range(rows):
                    for lane in range(lanes):
                        index = band_index(block * lanes + lane, tile * rows + row)
                        band_ref[head, index] += ds[
                            row * TILE : (row + 1) * TILE, lane * TILE : (lane + 1) * TILE
                        ]
            low = ds.astype(jnp.bfloat16)
            dkeys = dkeys + dot_plain(low, parts[head])
            kt = kt_ref[pl.ds(head * HD, HD), pl.ds(start, kb)]
            fresh.append(dquery[head] + dot_plain(kt, low))
        dk_ref[pl.ds(start, kb), :] = dkeys
        return tuple(fresh)

    nothing = jnp.zeros((HD, qb), jnp.float32)
    dquery = lax.fori_loop(first, last, pull, (nothing, nothing))
    dq_ref[...] = flip(jnp.concatenate(dquery, axis=0)).astype(jnp.bfloat16)

    @pl.when(block == pl.num_programs(1) - 1)
    def _():
        column = pl.multiple_of(pair * 2 * HD, 2 * HD)
        dkv_ref[:, pl.ds(column, 2 * HD)] = dk_ref[...].astype(jnp.bfloat16)
        column = pl.multiple_of((pl.num_programs(0) + pair) * 2 * HD, 2 * HD)
        dkv_ref[:, pl.ds(column, 2 * HD)] = dv_ref[...].astype(jnp.bfloat16)


def attention_setup(queries, keyval, query_labels, key_labels, bias, causal):
    rows, keys = queries.shape[0], keyval.shape[0]
    qb, kb = min(256, rows), min(256, keys)
    spec = dict(qb=qb, kb=kb, causal=causal, bias=bias is not None)
    bounds = key_bounds(query_labels, key_labels, qb, kb)
    segq = query_labels[None, :]
    segk = jnp.broadcast_to(key_labels[:, None], (keys, TILE))
    pairs = H // 2
    in_specs = dict(
        q=pl.BlockSpec((qb, 2 * HD), lambda pair, block, bounds: (block, pair)),
        k=pl.BlockSpec((keys, 2 * HD), lambda pair, block, bounds: (0, pair)),
        v=pl.BlockSpec((keys, 2 * HD), lambda pair, block, bounds: (0, pairs + pair)),
        segq=pl.BlockSpec((1, qb), lambda pair, block, bounds: (0, block)),
        segk=pl.BlockSpec((keys, TILE), lambda pair, block, bounds: (0, 0)),
        lse=pl.BlockSpec((1, 2, qb), lambda pair, block, bounds: (pair, 0, block)),
        band=pl.BlockSpec(
            (2, BAND, TILE, TILE), lambda pair, block, bounds: (pair, 0, 0, 0)
        ),
        whole=pl.BlockSpec((keys, 4 * pairs * HD), lambda pair, block, bounds: (0, 0)),
    )
    return spec, bounds, segq, segk, in_specs, (pairs, rows // qb)


def attend_forward(queries, keyval, query_labels, key_labels, bias, causal):
    spec, bounds, segq, segk, specs, grid = attention_setup(
        queries, keyval, query_labels, key_labels, bias, causal
    )
    rows, keys = queries.shape[0], keyval.shape[0]
    work = H * rows * keys
    extra = ([specs["band"]], [bias]) if bias is not None else ([], [])
    return pl.pallas_call(
        functools.partial(forward_kernel, spec),
        out_shape=(
            jax.ShapeDtypeStruct((rows, H * HD), jnp.bfloat16),
            jax.ShapeDtypeStruct((H // 2, 2, rows), jnp.float32),
        ),
        grid_spec=pltpu.PrefetchScalarGridSpec(
            num_scalar_prefetch=1,
            grid=grid,
            in_specs=[specs["q"], specs["k"], specs["v"], specs["segq"], specs["segk"]]
            + extra[0],
            out_specs=[specs["q"], specs["lse"]],
            scratch_shapes=[
                pltpu.VMEM((2, keys, spec["qb"]), jnp.float32),
                pltpu.VMEM((2 * HD, keys), jnp.bfloat16),
            ],
        ),
        compiler_params=pltpu.CompilerParams(vmem_limit_bytes=40 << 20),
        cost_estimate=pl.CostEstimate(
            flops=16 * HD * work, transcendentals=work, bytes_accessed=8 << 20
        ),
    )(bounds, queries, keyval, keyval, segq, segk, *extra[1])


def attend_backward(queries, keyval, query_labels, key_labels, bias, causal, lse, dmixture):
    spec, bounds, segq, segk, specs, grid = attention_setup(
        queries, keyval, query_labels, key_labels, bias, causal
    )
    rows, keys = queries.shape[0], keyval.shape[0]
    work = H * rows * keys
    extra = ([specs["band"]], [bias]) if bias is not None else ([], [])
    band = (
        [jax.ShapeDtypeStruct((H, BAND, TILE, TILE), jnp.float32)] if bias is not None else []
    )
    out = pl.pallas_call(
        functools.partial(backward_kernel, spec),
        out_shape=[
            jax.ShapeDtypeStruct((rows, H * HD), jnp.bfloat16),
            jax.ShapeDtypeStruct((keys, 2 * H * HD), jnp.bfloat16),
        ]
        + band,
        grid_spec=pltpu.PrefetchScalarGridSpec(
            num_scalar_prefetch=1,
            grid=grid,
            in_specs=[
                specs["q"],
                specs["k"],
                specs["v"],
                specs["q"],
                specs["lse"],
                specs["segq"],
                specs["segk"],
            ]
            + extra[0],
            out_specs=[specs["q"], specs["whole"]] + extra[0],
            scratch_shapes=[
                pltpu.VMEM((2, keys, spec["qb"]), jnp.float32),
                pltpu.VMEM((2, keys, spec["qb"]), jnp.float32),
                pltpu.VMEM((keys, 2 * HD), jnp.float32),
                pltpu.VMEM((keys, 2 * HD), jnp.float32),
                pltpu.VMEM((2 * HD, keys), jnp.bfloat16),
            ],
        ),
        compiler_params=pltpu.CompilerParams(vmem_limit_bytes=48 << 20),
        cost_estimate=pl.CostEstimate(
            flops=40 * HD * work, transcendentals=work, bytes_accessed=16 << 20
        ),
    )(bounds, queries, keyval, keyval, dmixture, lse, segq, segk, *extra[1])
    return (out[0], out[1], out[2] if bias is not None else None)


def product(former, latter):
    return jnp.dot(former, latter, preferred_element_type=jnp.float32)


def transpose_product(former, latter):
    return lax.dot_general(
        former, latter, (((0,), (0,)), ((), ())), preferred_element_type=jnp.float32
    )


def product_transposed(former, latter):
    return lax.dot_general(
        former, latter, (((1,), (1,)), ((), ())), preferred_element_type=jnp.float32
    )


def smooth_gate(value):
    return jax.nn.gelu(value, approximate=True)


def norm_forward(stream, norm_gain):
    return (
        stream * lax.rsqrt(jnp.mean(stream * stream, axis=-1, keepdims=True) + EPSILON) * norm_gain
    )


def norm_backward(stream, norm_gain, gradient):
    outcome, pullback = jax.vjp(norm_forward, stream, norm_gain)
    return pullback(gradient)


def attention_forward(stream, norm_gain, wquery, wkeyval, wproj, layout, memory):
    normed = norm_forward(stream, norm_gain).astype(jnp.bfloat16)
    queries = product(normed, wquery).astype(jnp.bfloat16)
    source = normed if memory is None else memory
    keyval = product(source, wkeyval).astype(jnp.bfloat16)
    mixture, logsum = attend_forward(queries, keyval, *layout)
    return (stream + product(mixture, wproj), (normed, queries, keyval, mixture, logsum))


def attention_backward(stream, norm_gain, wquery, wkeyval, wproj, layout, memory, stored, gradient):
    normed, queries, keyval, mixture, logsum = stored
    gradient_low = gradient.astype(jnp.bfloat16)
    project_grad = transpose_product(mixture, gradient_low)
    dmixture = product_transposed(gradient_low, wproj).astype(jnp.bfloat16)
    dquery_low, dkeyval_low, band = attend_backward(queries, keyval, *layout, logsum, dmixture)
    source = normed if memory is None else memory
    query_grad = transpose_product(normed, dquery_low)
    keyval_grad = transpose_product(source, dkeyval_low)
    dnormed = product_transposed(dquery_low, wquery)
    dsource = product_transposed(dkeyval_low, wkeyval)
    if memory is None:
        dnormed = dnormed + dsource
        dsource = None
    dstream, dgain = norm_backward(stream, norm_gain, dnormed)
    return (gradient + dstream, dgain, query_grad, keyval_grad, project_grad, band, dsource)


def feed_forward(stream, norm_gain, winner, wouter):
    normed = norm_forward(stream, norm_gain).astype(jnp.bfloat16)
    before = product(normed, winner)
    hidden = smooth_gate(before).astype(jnp.bfloat16)
    return (stream + product(hidden, wouter), (normed, before, hidden))


def feed_backward(stream, norm_gain, winner, wouter, stored, gradient):
    normed, before, hidden = stored
    gradient_low = gradient.astype(jnp.bfloat16)
    outer_grad = transpose_product(hidden, gradient_low)
    dhidden = product_transposed(gradient_low, wouter)
    gate_value, gate_pullback = jax.vjp(smooth_gate, before)
    dbefore = gate_pullback(dhidden)[0].astype(jnp.bfloat16)
    inner_grad = transpose_product(normed, dbefore)
    dnormed = product_transposed(dbefore, winner)
    dstream, dgain = norm_backward(stream, norm_gain, dnormed)
    return (gradient + dstream, dgain, inner_grad, outer_grad)


def index_bits(devices):
    return devices.bit_length() - 1


def swap_pairs(devices, bit):
    return [(place, place ^ (1 << bit)) for place in range(devices)]


class Links:
    def __init__(self, mesh):
        self.sizes = dict(mesh.shape)
        self.bits = [("fsdp", bit) for bit in range(index_bits(self.sizes["fsdp"]))]
        self.bits += [("dp", bit) for bit in range(index_bits(self.sizes["dp"]))]

    def side(self, axis, bit):
        return (lax.axis_index(axis) >> bit) & 1

    def swap(self, value, axis, bit):
        return lax.ppermute(value, axis, swap_pairs(self.sizes[axis], bit))

    def gather(self, shard):
        rows, columns = shard.shape
        half = rows // 2
        core, place = self.side("dp", 0), lax.axis_index("fsdp")
        part = lax.dynamic_slice_in_dim(shard, core * half, half, 0)
        theirs = self.swap(part, "fsdp", 0)
        mate = self.swap(theirs, "dp", 0)
        whole = jnp.zeros((2 * rows, columns), shard.dtype)
        other = (1 - place) * rows
        whole = lax.dynamic_update_slice_in_dim(whole, shard, place * rows, 0)
        whole = lax.dynamic_update_slice_in_dim(whole, theirs, other + core * half, 0)
        return lax.dynamic_update_slice_in_dim(whole, mate, other + (1 - core) * half, 0)

    def gather_small(self, shard):
        other = self.swap(shard, "fsdp", 0)
        first = lax.axis_index("fsdp") == 0
        return jnp.concatenate(
            [jnp.where(first, shard, other), jnp.where(first, other, shard)], axis=0
        )

    def scatter(self, value, order, kept=jnp.bfloat16):
        rows, columns = value.shape
        shape = (2,) * len(self.bits) + (rows >> len(self.bits), columns)
        current = value.astype(kept).reshape(shape)
        left = list(reversed(self.bits))
        for step, key in enumerate(order):
            spot = left.index(key)
            side = self.side(*key)
            send = lax.dynamic_index_in_dim(current, 1 - side, spot, keepdims=False)
            mine = lax.dynamic_index_in_dim(current, side, spot, keepdims=False)
            arrived = self.swap(send, *key)
            current = mine.astype(jnp.float32) + arrived.astype(jnp.float32)
            if step < len(order) - 1:
                current = current.astype(kept)
            left.remove(key)
        return current

    def orders(self):
        core, row = ("dp", 0), ("fsdp", 0)
        rest = [key for key in self.bits if key not in (core, row)]
        across = rest[:1]
        return ([core] + across + [row] + rest[1:], [core, row] + rest)


def body(
    links,
    enc_tokens,
    dec_tokens,
    enc_segments,
    dec_segments,
    enc_upstream,
    dec_upstream,
    encoder_query,
    encoder_keyval,
    encoder_proj,
    encoder_inner,
    encoder_outer,
    encoder_gains,
    encoder_table,
    decoder_query,
    decoder_keyval,
    decoder_proj,
    cross_query,
    cross_keyval,
    cross_proj,
    decoder_inner,
    decoder_outer,
    decoder_gains,
    decoder_table,
):
    small = jnp.concatenate(
        [encoder_gains, decoder_gains]
        + [
            jnp.concatenate([encoder_table, decoder_table], axis=0).reshape(
                encoder_gains.shape[0], -1
            )
        ],
        axis=1,
    )
    small = links.gather_small(small)
    enc_gains = small[:, 0:2].astype(jnp.float32)
    dec_gains = small[:, 2:5].astype(jnp.float32)
    tables = small[:, 5:].reshape(2, 2, NB // 2, H)
    enc_bias = band_bias(tables[:, 0].reshape(NB, H), encoder_bucket)
    dec_bias = band_bias(tables[:, 1].reshape(NB, H), decoder_bucket)

    equery, ekeyval, eproj = (
        links.gather(w) for w in (encoder_query, encoder_keyval, encoder_proj)
    )
    einner, eouter = (links.gather(w) for w in (encoder_inner, encoder_outer))
    dquery, dkeyval, dproj = (
        links.gather(w) for w in (decoder_query, decoder_keyval, decoder_proj)
    )
    cquery, ckeyval, cproj = (links.gather(w) for w in (cross_query, cross_keyval, cross_proj))
    dinner, douter = (links.gather(w) for w in (decoder_inner, decoder_outer))

    enc_layout = (enc_segments, enc_segments, enc_bias, False)
    dec_layout = (dec_segments, dec_segments, dec_bias, True)
    cross_layout = (dec_segments, enc_segments, None, False)

    enc_stream = enc_tokens.astype(jnp.float32)
    enc_middle, enc_self = attention_forward(
        enc_stream, enc_gains[:, 0], equery, ekeyval, eproj, enc_layout, None
    )
    enc_final, enc_ffn = feed_forward(enc_middle, enc_gains[:, 1], einner, eouter)
    memory = enc_final.astype(jnp.bfloat16)

    dec_stream = dec_tokens.astype(jnp.float32)
    after_self, dec_self = attention_forward(
        dec_stream, dec_gains[:, 0], dquery, dkeyval, dproj, dec_layout, None
    )
    after_cross, dec_cross = attention_forward(
        after_self, dec_gains[:, 1], cquery, ckeyval, cproj, cross_layout, memory
    )
    dec_final, dec_ffn = feed_forward(after_cross, dec_gains[:, 2], dinner, douter)

    first, second = links.orders()

    dec_live = (dec_segments >= 0).astype(jnp.float32)[:, None]
    gradient = dec_upstream.astype(jnp.float32) * dec_live
    gradient, dgain_ffn, dinner_grad, douter_grad = feed_backward(
        after_cross, dec_gains[:, 2], dinner, douter, dec_ffn, gradient
    )
    dinner_share = links.scatter(dinner_grad, first)
    douter_share = links.scatter(douter_grad, second)
    gradient, dgain_cross, cquery_grad, ckeyval_grad, cproj_grad, _, memory_grad = (
        attention_backward(
            after_self,
            dec_gains[:, 1],
            cquery,
            ckeyval,
            cproj,
            cross_layout,
            memory,
            dec_cross,
            gradient,
        )
    )
    cproj_share = links.scatter(cproj_grad, first)
    cquery_share = links.scatter(cquery_grad, first)
    ckeyval_share = links.scatter(ckeyval_grad, second)
    dec_gradient, dgain_self, dquery_grad, dkeyval_grad, dproj_grad, dec_band, _ = (
        attention_backward(
            dec_stream,
            dec_gains[:, 0],
            dquery,
            dkeyval,
            dproj,
            dec_layout,
            None,
            dec_self,
            gradient,
        )
    )
    dproj_share = links.scatter(dproj_grad, first)
    dquery_share = links.scatter(dquery_grad, first)
    dkeyval_share = links.scatter(dkeyval_grad, second)

    enc_live = (enc_segments >= 0).astype(jnp.float32)[:, None]
    gradient = enc_upstream.astype(jnp.float32) * enc_live + memory_grad
    gradient, egain_ffn, einner_grad, eouter_grad = feed_backward(
        enc_middle, enc_gains[:, 1], einner, eouter, enc_ffn, gradient
    )
    einner_share = links.scatter(einner_grad, first)
    eouter_share = links.scatter(eouter_grad, second)
    enc_gradient, egain_self, equery_grad, ekeyval_grad, eproj_grad, enc_band, _ = (
        attention_backward(
            enc_stream,
            enc_gains[:, 0],
            equery,
            ekeyval,
            eproj,
            enc_layout,
            None,
            enc_self,
            gradient,
        )
    )
    eproj_share = links.scatter(eproj_grad, first)
    equery_share = links.scatter(equery_grad, first)
    ekeyval_share = links.scatter(ekeyval_grad, second)

    table_grads = jnp.concatenate(
        [
            band_table_grad(enc_band, encoder_bucket),
            band_table_grad(dec_band, decoder_bucket),
        ],
        axis=0,
    )
    columns = jnp.stack([egain_self, egain_ffn, dgain_self, dgain_cross, dgain_ffn], axis=1)
    wide = columns.shape[0]
    packed = jnp.concatenate(
        [columns, table_grads.reshape(wide, -1)], axis=1
    )
    packed = jnp.pad(packed, ((0, 0), (0, TILE - packed.shape[1])))
    small_share = links.scatter(packed, second, jnp.float32)
    tables_grad = lax.all_gather(small_share[:, 5:6], ("dp", "fsdp"), axis=0, tiled=True)
    tables_grad = tables_grad.reshape(2, NB, H)
    return (
        memory,
        dec_final.astype(jnp.bfloat16),
        enc_gradient,
        dec_gradient,
        equery_share,
        ekeyval_share,
        eproj_share,
        einner_share,
        eouter_share,
        small_share[:, 0:2],
        tables_grad[0],
        dquery_share,
        dkeyval_share,
        dproj_share,
        cquery_share,
        ckeyval_share,
        cproj_share,
        dinner_share,
        douter_share,
        small_share[:, 2:5],
        tables_grad[1],
    )


def solution(mesh):
    in_specs = (
        P(("dp", "fsdp"), None),
        P(("dp", "fsdp"), None),
        P(("dp", "fsdp")),
        P(("dp", "fsdp")),
        P(("dp", "fsdp"), None),
        P(("dp", "fsdp"), None),
        P("fsdp", None),
        P("fsdp", None),
        P("fsdp", None),
        P("fsdp", None),
        P("fsdp", None),
        P("fsdp", None),
        P("fsdp", None),
        P("fsdp", None),
        P("fsdp", None),
        P("fsdp", None),
        P("fsdp", None),
        P("fsdp", None),
        P("fsdp", None),
        P("fsdp", None),
        P("fsdp", None),
        P("fsdp", None),
        P("fsdp", None),
    )
    out_specs = (
        P(("dp", "fsdp"), None),
        P(("dp", "fsdp"), None),
        P(("dp", "fsdp"), None),
        P(("dp", "fsdp"), None),
        P(("dp", "fsdp"), None),
        P(("dp", "fsdp"), None),
        P(("dp", "fsdp"), None),
        P(("dp", "fsdp"), None),
        P(("dp", "fsdp"), None),
        P(("dp", "fsdp"), None),
        P(),
        P(("dp", "fsdp"), None),
        P(("dp", "fsdp"), None),
        P(("dp", "fsdp"), None),
        P(("dp", "fsdp"), None),
        P(("dp", "fsdp"), None),
        P(("dp", "fsdp"), None),
        P(("dp", "fsdp"), None),
        P(("dp", "fsdp"), None),
        P(("dp", "fsdp"), None),
        P(),
    )
    return jax.shard_map(
        functools.partial(body, Links(mesh)), mesh=mesh, in_specs=in_specs, out_specs=out_specs, check_vma=False)
```

time: 2410 us -> 1010 us (0.42)
  waiting for transfers between devices: 1140 us -> 320 us
  matrix products: 808 us -> 185 us
  Pallas kernels: 0 us -> 143 us
  other arithmetic: 160 us -> 48.6 us
  starting transfers between devices: 1.49 us -> 93.7 us
  local copies, waits for them, and re-layouts: 198 us -> 157 us
    reduce_scatter x13 -> x0, waiting for transfers between devices: 952 us -> none  [the longest x1 142 us: body(): lax.psum_scatter(dec_grads[7], ('dp', 'fsdp'), scatter_dimension=0, tiled...]
    dot_general x40 -> x4, matrix products: 606 us -> 27.1 us  [the longest x2 19.7 us: band_table_grad(): lax.dot_general(onehot, band.reshape(H, BAND * TILE * TILE), (((1,), (1,)...]
    ppermute x0 -> x97, waiting for transfers between devices: none -> 320 us  [swap(): return lax.ppermute(value, axis, swap_pairs(self.sizes[axis], bit))]
    all_gather x13 -> x0, waiting for transfers between devices: 177 us -> none  [the longest x1 58.6 us: body(): lax.all_gather(decoder_outer, 'fsdp', axis=0, tiled=True)]
    pallas_call x0 -> x6, Pallas kernels: none -> 143 us  [the longest x3 86.2 us: attend_backward(): pl.pallas_call(functools.partial(backward_kernel, spec), out_shape=[jax.S...]
    ppermute x0 -> x97, starting transfers between devices: none -> 93.7 us  [swap(): return lax.ppermute(value, axis, swap_pairs(self.sizes[axis], bit))]
    mul x2 -> x0, local copies, waits for them, and re-layouts: 61.6 us -> none  [one_block(): weights * (dweights - jnp.sum(weights * dweights, axis=-1, keepdims=True))]
    dot_general x2, local copies, waits for them, and re-layouts: 61 us -> 2.53 us  [band_bias(): lax.dot_general(table, onehot, (((0,), (0,)), ((), ())), preferred_elemen...]
  transfers between devices with their start and end apart: 26 -> 97, of which waited for: 13 -> 58; matrix products, arithmetic and copies ran while one was open for 47% -> 24% of each run, Pallas kernels for 0% -> 6%
where the time goes in v1:
time: 1010 us; the launch traced here: 998 us
  waiting for transfers between devices  320 us (32%)
  matrix products  185 us (18%)
  local copies, waits for them, and re-layouts  157 us (16%)
  Pallas kernels  143 us (14%)
  starting transfers between devices  93.7 us (9%)
  other arithmetic  48.6 us (5%)
  blocking collectives  40.9 us (4%)
  between operations  10.5 us (1%)
    ppermute x97, waiting for transfers between devices, swap(): return lax.ppermute(value, axis, swap_pairs(self.sizes[axis], bit))  320 us
    ppermute x97, starting transfers between devices, swap(): return lax.ppermute(value, axis, swap_pairs(self.sizes[axis], bit))  93.7 us
    pallas_call x3, Pallas kernels, attend_backward(): pl.pallas_call(functools.partial(backward_kernel, spec), out_shape=[jax.S...  86.2 us
    dot_general x13, matrix products, product_transposed(): lax.dot_general(former, latter, (((1,), (1,)), ((), ())), preferred_eleme...  60.8 us
    pallas_call x3, Pallas kernels, attend_forward(): pl.pallas_call(functools.partial(forward_kernel, spec), out_shape=(jax.Sh...  57.2 us
    dot_general x13, matrix products, transpose_product(): lax.dot_general(former, latter, (((0,), (0,)), ((), ())), preferred_eleme...  49.8 us
    dot_general x13, matrix products, product(): return jnp.dot(former, latter, preferred_element_type=jnp.float32)  46.7 us
    unnamed x1, blocking collectives  40.9 us
  transfers between devices with their start and end apart: 97, of which 58 were waited for; matrix products, arithmetic and copies ran while one was open for 24% of the time, Pallas kernels for 6%

profile of v1, /device:TPU:0, one launch (start us, length us, event | category | flops | bytes accessed | tf_op | source)
XLA Modules:
  0.0 998.1 jit_solution(4532418356554985991)
XLA Ops:
  76.8 4.0 fusion.37
  80.8 4.9 copy.275
  91.9 4.0 fusion.43
  112.1 6.3 collective-permute-done.15
  137.5 10.1 %collective-permute-done.19 = bf16[192,1536]{1,0:T(8,128)(2,1)} collective-permute-done((bf16[192,1536]{1,0:T(8,128)(2,1)S(1)}, bf16[192,1536]{1,0:T(8,128)(2,1)}, u32[]{:S(2)}, u32[]{:S(2)}) %collective-permute-start.19) | collective-permute-done | bytes 589856 | tf_op jit(solution)/shard_map/ppermute | solution.py:476
  160.0 5.5 shard_map.383
  168.2 10.1 %collective-permute-done.7 = bf16[192,3072]{1,0:T(8,128)(2,1)} collective-permute-done((bf16[192,3072]{1,0:T(8,128)(2,1)S(1)}, bf16[192,3072]{1,0:T(8,128)(2,1)}, u32[]{:S(2)}, u32[]{:S(2)}) %collective-permute-start.7) | collective-permute-done | bytes 1179680 | tf_op jit(solution)/shard_map/ppermute | solution.py:476
  179.2 4.8 convolution_convert_fusion.5.k_ref.v_ref
  184.0 19.6 %collective-permute-done.25 = bf16[768,768]{1,0:T(8,128)(2,1)} collective-permute-done((bf16[768,768]{1,0:T(8,128)(2,1)S(1)}, bf16[768,768]{1,0:T(8,128)(2,1)}, u32[]{:S(2)}, u32[]{:S(2)}) %collective-permute-start.25) | collective-permute-done | bytes 1179680 | tf_op jit(solution)/shard_map/ppermute | solution.py:476
  203.8 36.8 %shard_map.382 = (bf16[1024,768]{1,0:T(8,128)(2,1)S(1)}, f32[6,2,1024]{2,1,0:T(2,128)S(1)}) custom-call(s32[2,4]{1,0:T(2,128)S(1)} %pad_add_fusion.bounds_ref, bf16[1024,768]{1,0:T(8,128)(2,1)S(1)} %convolution_convert_fusion.11.q_ref, bf16[1024,1536]{1,0:T(8,128)(2,1)S(1)} %convolution_convert_fusion.5.k_ref.v_ref, ...), custom_call_target="tpu_custom_call" | custom-call | flops 12884901888 | bytes 8388608 | tf_op jit(solution)/shard_map/pallas_call | solution.py:309
  255.9 8.2 fusion.231
  266.5 10.6 %add_convert_fusion = bf16[1024,768]{0,1:T(8,128)(2,1)S(1)} fusion(f32[1024,768]{0,1:T(8,128)S(1)} %get-tuple-element.199, bf16[3072,768]{1,0:T(8,128)(2,1)} %constant_dynamic-update-slice_fusion.24, f32[1024,3072]{1,0:T(8,128)} %fusion.231), kind=kOutput, calls=%fused_computation.126 | convolution fusion | flops 4861722624 | bytes 22020096 | tf_op jit(solution)/shard_map/dot_general | solution.py:381
  280.1 14.8 %shard_map.384 = (bf16[256,768]{1,0:T(8,128)(2,1)S(1)}, f32[6,2,256]{2,1,0:T(2,128)S(1)}) custom-call(s32[2,1]{1,0:T(2,128)S(1)} %pad_add_fusion.2.bounds_ref, bf16[256,768]{1,0:T(8,128)(2,1)S(1)} %convolution_convert_fusion.20.q_ref, bf16[1024,1536]{1,0:T(8,128)(2,1)S(1)} %convolution_convert_fusion.4.k_ref.v_ref, ...), custom_call_target="tpu_custom_call" | custom-call | flops 3221225472 | bytes 8388608 | tf_op jit(solution)/shard_map/pallas_call | solution.py:309
  311.2 4.1 fusion.89
  319.3 20.8 %shard_map.385 = (bf16[256,768]{1,0:T(8,128)(2,1)S(1)}, bf16[1024,1536]{1,0:T(8,128)(2,1)S(1)}) custom-call(s32[2,1]{1,0:T(2,128)S(1)} %pad_add_fusion.2.bounds_ref, bf16[256,768]{1,0:T(8,128)(2,1)S(1)} %convolution_convert_fusion.20.q_ref, bf16[1024,1536]{1,0:T(8,128)(2,1)} %copy-done.16, bf16[1024,1536]{1,0:T(8,128)(2,1)} %copy-done.16, ...), custom_call_target="tpu_custom_call" | custom-call | flops 8053063680 | bytes 16777216 | tf_op jit(solution)/shard_map/pallas_call | solution.py:343
  340.2 6.1 fusion.101
  346.3 16.4 %fusion.6 = bf16[1024,3072]{1,0:T(8,128)(2,1)} fusion(f32[1024,3072]{1,0:T(8,128)} %fusion.231, bf16[1024,768]{0,1:T(8,128)(2,1)S(1)} %get-tuple-element.205, bf16[3072,768]{1,0:T(8,128)(2,1)} %constant_dynamic-update-slice_fusion.24), kind=kOutput, calls=%fused_computation.10 | convolution fusion | flops 4894752768 | bytes 25165824 | tf_op jit(solution)/shard_map/dot_general | solution.py:391
  362.8 9.2 multiply_reduce_fusion
  378.6 55.7 %shard_map.386 = (bf16[1024,768]{1,0:T(8,128)(2,1)S(1)}, bf16[1024,1536]{1,0:T(8,128)(2,1)}, f32[12,5,128,128]{3,2,1,0:T(8,128)}) custom-call(s32[2,4]{1,0:T(2,128)S(1)} %pad_add_fusion.bounds_ref, bf16[1024,768]{1,0:T(8,128)(2,1)S(1)} %copy-done.19, bf16[1024,1536]{1,0:T(8,128)(2,1)} %copy-done.17, bf16[1024,1536]{1,0:T(8,128)(2,1)} %copy-done.17, ...), custom_call_target="tpu_custom_call" | custom-call | flops 32212254720 | bytes 16777216 | tf_op jit(solution)/shard_map/pallas_call | solution.py:343
  434.3 7.0 fusion.243
  441.4 4.0 convolution_convert_fusion.7
  448.0 6.9 convolution_convert_fusion.1
  454.9 12.9 %convolution_convert_fusion = bf16[3072,768]{1,0:T(8,128)(2,1)} fusion(bf16[1024,768]{0,1:T(8,128)(2,1)S(1)} %copy-done.143, f32[1024,3072]{1,0:T(8,128)} %fusion.231), kind=kOutput, calls=%fused_computation.86 | convolution fusion | flops 4862509056 | bytes 18874368 | tf_op jit(solution)/shard_map/dot_general | solution.py:385
  472.0 9.7 shard_map.387
  489.8 4.1 convolution_convert_fusion.6
  499.1 4.5 convolution_convert_fusion.2
  511.9 3.9 copy.243
  533.9 10.7 %fusion.121 = f32[32,12]{0,1:T(8,128)S(1)} fusion(f32[12,5,128,128]{3,2,1,0:T(8,128)S(1)} %copy-done.139, s32[5]{0:T(128)S(1)} %copy-done.138), kind=kOutput, calls=%fused_computation.215 | convolution fusion | flops 511180800 | bytes 3933716 | tf_op jit(solution)/shard_map/dot_general | solution.py:54
  544.7 9.0 fusion.116
  559.7 5.3 constant_dynamic-slice_fusion.3
  568.0 16.0 %collective-permute-start.53 = (f32[2,2,2,24,128]{4,3,1,0,2:T(8,128)S(1)}, f32[2,2,2,24,128]{4,3,1,0,2:T(8,128)S(1)}, u32[]{:S(2)}, u32[]{:S(2)}) collective-permute-start(f32[2,2,2,24,128]{4,3,1,0,2:T(8,128)S(1)} %bitcast.581), channel_id=1, source_target_pairs={{0,1},{1,0},{2,3},{3,2},{4,5},{5,4},{6,7},{7,6},{8,9},{9,8},{10,11... | collective-permute-start | bytes 294920 | tf_op jit(solution)/shard_map/ppermute | solution.py:476
  615.0 40.9 %all-reduce.1 = f32[768]{0:T(1024)S(1)} all-reduce(f32[768]{0:T(1024)S(1)} %fusion.205), channel_id=1, replica_groups=mesh['dp'=16,'fsdp'=2] {'dp','fsdp'}, use_global_device_ids=true, to_apply=%add.1 | all-reduce | flops 768 | bytes 6144
  667.7 7.3 collective-permute-done.28
  677.1 4.2 collective-permute-done.38
  683.4 4.2 collective-permute-done.58
  689.8 4.2 collective-permute-done.68
  696.1 4.2 collective-permute-done.73
  700.3 5.7 collective-permute-done.83
  718.5 4.2 collective-permute-done.59
  725.2 4.1 collective-permute-done.69
  740.0 4.1 collective-permute-done.30
  744.4 4.1 collective-permute-done.40
  748.8 4.8 collective-permute-done.60
  753.6 4.7 collective-permute-done.70
  758.4 4.3 collective-permute-done.75
  762.7 4.3 collective-permute-done.85
  767.7 4.7 collective-permute-done.31
  773.2 4.0 collective-permute-done.41
  802.4 13.3 %collective-permute-done.33 = bf16[2,2,2,24,1536]{4,3,0,1,2:T(8,128)(2,1)S(1)} collective-permute-done((bf16[2,2,2,24,1536]{4,3,0,1,2:T(8,128)(2,1)S(1)}, bf16[2,2,2,24,1536]{4,3,0,1,2:T(8,128)(2,1)S(1)}, u32[]{:S(2)}, u32[]{:S(2)}) %collective-permute-start.33) | collective-permute-done | bytes 589856 | tf_op jit(solution)/shard_map/ppermute | solution.py:476
  817.2 11.1 %collective-permute-done.63 = bf16[2,2,2,24,1536]{4,3,0,1,2:T(8,128)(2,1)S(1)} collective-permute-done((bf16[2,2,2,24,1536]{4,3,0,1,2:T(8,128)(2,1)S(1)}, bf16[2,2,2,24,1536]{4,3,0,1,2:T(8,128)(2,1)S(1)}, u32[]{:S(2)}, u32[]{:S(2)}) %collective-permute-start.63) | collective-permute-done | bytes 589856 | tf_op jit(solution)/shard_map/ppermute | solution.py:476
  828.5 11.5 %collective-permute-done.78 = bf16[2,2,2,24,1536]{4,3,0,1,2:T(8,128)(2,1)S(1)} collective-permute-done((bf16[2,2,2,24,1536]{4,3,0,1,2:T(8,128)(2,1)S(1)}, bf16[2,2,2,24,1536]{4,3,0,1,2:T(8,128)(2,1)S(1)}, u32[]{:S(2)}, u32[]{:S(2)}) %collective-permute-start.78) | collective-permute-done | bytes 589856 | tf_op jit(solution)/shard_map/ppermute | solution.py:476
  841.6 6.5 collective-permute-done.34
  849.5 5.8 collective-permute-done.64
  856.8 5.3 collective-permute-done.79
  862.1 5.9 collective-permute-done.35
  868.3 4.8 collective-permute-done.65
  873.9 4.5 collective-permute-done.80
  879.4 6.2 collective-permute-done.36
  886.2 4.6 collective-permute-done.66
  891.5 4.6 collective-permute-done.81
  907.4 21.0 %collective-permute-done.43 = bf16[2,2,2,24,3072]{4,3,0,1,2:T(8,128)(2,1)S(1)} collective-permute-done((bf16[2,2,2,24,3072]{4,3,0,1,2:T(8,128)(2,1)S(1)}, bf16[2,2,2,24,3072]{4,3,0,1,2:T(8,128)(2,1)S(1)}, u32[]{:S(2)}, u32[]{:S(2)}) %collective-permute-start.43) | collective-permute-done | bytes 1179680 | tf_op jit(solution)/shard_map/ppermute | solution.py:476
  932.4 21.2 %collective-permute-done.88 = bf16[2,2,2,24,3072]{4,3,0,1,2:T(8,128)(2,1)S(1)} collective-permute-done((bf16[2,2,2,24,3072]{4,3,0,1,2:T(8,128)(2,1)S(1)}, bf16[2,2,2,24,3072]{4,3,0,1,2:T(8,128)(2,1)S(1)}, u32[]{:S(2)}, u32[]{:S(2)}) %collective-permute-start.88) | collective-permute-done | bytes 1179680 | tf_op jit(solution)/shard_map/ppermute | solution.py:476
  957.7 5.9 collective-permute-done.44
  979.9 7.0 collective-permute-done.90
  (808 shorter events, 388.4 us)
Async XLA Ops:
  2.5 99.6 %collective-permute-start.1 = (bf16[192,768]{1,0:T(8,128)(2,1)}, bf16[192,768]{1,0:T(8,128)(2,1)}, u32[]{:S(2)}, u32[]{:S(2)}) collective-permute-start(bf16[192,768]{1,0:T(8,128)(2,1)} %constant_dynamic-slice_fusion.56), channel_id=1, source_target_pairs={{0,1},{1,0},{2,3},{3,2},{4,5},{5,4},{6,7},{7,6},{8,9},{9,8},{10,11... | collective-permute-start | bytes 884744 | tf_op jit(solution)/shard_map/ppermute | solution.py:476
  7.0 84.5 %collective-permute-start = (bf16[384,6]{0,1:T(8,128)(2,1)S(1)}, bf16[384,6]{0,1:T(8,128)(2,1)S(1)}, u32[]{:S(2)}, u32[]{:S(2)}) collective-permute-start(bf16[384,6]{0,1:T(8,128)(2,1)S(1)} %pad_maximum_fusion.2), channel_id=1, source_target_pairs={{0,1},{1,0},{2,3},{3,2},{4,5},{5,4},{6,7},{7,6},{8,9},{9,8},{10,11... | collective-permute-start | bytes 13832 | tf_op jit(solution)/shard_map/ppermute | solution.py:476
  9.0 119.1 %collective-permute-start.3 = (bf16[192,1536]{1,0:T(8,128)(2,1)}, bf16[192,1536]{1,0:T(8,128)(2,1)}, u32[]{:S(2)}, u32[]{:S(2)}) collective-permute-start(bf16[192,1536]{1,0:T(8,128)(2,1)} %constant_dynamic-slice_fusion.55), channel_id=1, source_target_pairs={{0,1},{1,0},{2,3},{3,2},{4,5},{5,4},{6,7},{7,6},{8,9},{9,8},{10,11... | collective-permute-start | bytes 1769480 | tf_op jit(solution)/shard_map/ppermute | solution.py:476
  12.7 93.2 %collective-permute-start.5 = (bf16[192,768]{1,0:T(8,128)(2,1)}, bf16[192,768]{1,0:T(8,128)(2,1)}, u32[]{:S(2)}, u32[]{:S(2)}) collective-permute-start(bf16[192,768]{1,0:T(8,128)(2,1)} %constant_dynamic-slice_fusion.54), channel_id=1, source_target_pairs={{0,1},{1,0},{2,3},{3,2},{4,5},{5,4},{6,7},{7,6},{8,9},{9,8},{10,11... | collective-permute-start | bytes 884744 | tf_op jit(solution)/shard_map/ppermute | solution.py:476
  13.9 154.3 %collective-permute-start.9 = (bf16[768,768]{1,0:T(8,128)(2,1)}, bf16[768,768]{1,0:T(8,128)(2,1)}, u32[]{:S(2)}, u32[]{:S(2)}) collective-permute-start(bf16[768,768]{1,0:T(8,128)(2,1)} %constant_dynamic-slice_fusion.52), channel_id=1, source_target_pairs={{0,1},{1,0},{2,3},{3,2},{4,5},{5,4},{6,7},{7,6},{8,9},{9,8},{10,11... | collective-permute-start | bytes 3538952 | tf_op jit(solution)/shard_map/ppermute | solution.py:476
  91.6 17.5 %collective-permute-start.11 = (bf16[192,768]{1,0:T(8,128)(2,1)}, bf16[192,768]{1,0:T(8,128)(2,1)}, u32[]{:S(2)}, u32[]{:S(2)}) collective-permute-start(bf16[192,768]{1,0:T(8,128)(2,1)} %constant_dynamic-slice_fusion.51), channel_id=1, source_target_pairs={{0,1},{1,0},{2,3},{3,2},{4,5},{5,4},{6,7},{7,6},{8,9},{9,8},{10,11... | collective-permute-start | bytes 884744 | tf_op jit(solution)/shard_map/ppermute | solution.py:476
  102.1 10.0 %collective-permute-start.21 = (bf16[192,768]{1,0:T(8,128)(2,1)S(1)}, bf16[192,768]{1,0:T(8,128)(2,1)S(1)}, u32[]{:S(2)}, u32[]{:S(2)}) collective-permute-start(bf16[192,768]{1,0:T(8,128)(2,1)S(1)} %copy-done.114), channel_id=1, source_target_pairs={{0,1},{1,0},{2,3},{3,2},{4,5},{5,4},{6,7},{7,6},{8,9},{9,8},{10,11... | collective-permute-start | bytes 884744 | tf_op jit(solution)/shard_map/ppermute | solution.py:476
  105.9 12.5 %collective-permute-start.15 = (bf16[192,768]{1,0:T(8,128)(2,1)S(1)}, bf16[192,768]{1,0:T(8,128)(2,1)S(1)}, u32[]{:S(2)}, u32[]{:S(2)}) collective-permute-start(bf16[192,768]{1,0:T(8,128)(2,1)S(1)} %copy-done.113), channel_id=1, source_target_pairs={{0,1},{1,0},{2,3},{3,2},{4,5},{5,4},{6,7},{7,6},{8,9},{9,8},{10,11... | collective-permute-start | bytes 884744 | tf_op jit(solution)/shard_map/ppermute | solution.py:476
  109.0 15.7 %collective-permute-start.17 = (bf16[192,768]{1,0:T(8,128)(2,1)S(1)}, bf16[192,768]{1,0:T(8,128)(2,1)S(1)}, u32[]{:S(2)}, u32[]{:S(2)}) collective-permute-start(bf16[192,768]{1,0:T(8,128)(2,1)S(1)} %copy-done.115), channel_id=1, source_target_pairs={{0,1},{1,0},{2,3},{3,2},{4,5},{5,4},{6,7},{7,6},{8,9},{9,8},{10,11... | collective-permute-start | bytes 884744 | tf_op jit(solution)/shard_map/ppermute | solution.py:476
  112.1 15.3 %collective-permute-start.2 = (bf16[192,768]{1,0:T(8,128)(2,1)}, bf16[192,768]{1,0:T(8,128)(2,1)S(1)}, u32[]{:S(2)}, u32[]{:S(2)}) collective-permute-start(bf16[192,768]{1,0:T(8,128)(2,1)} %collective-permute-done.1), channel_id=1, source_target_pairs={{0,2},{2,0},{4,6},{6,4},{8,10},{10,8},{12,14},{14,12},{16,18},{18,... | collective-permute-start | bytes 884744 | tf_op jit(solution)/shard_map/ppermute | solution.py:476
  118.4 19.0 %collective-permute-start.13 = (bf16[192,1536]{1,0:T(8,128)(2,1)S(1)}, bf16[192,1536]{1,0:T(8,128)(2,1)S(1)}, u32[]{:S(2)}, u32[]{:S(2)}) collective-permute-start(bf16[192,1536]{1,0:T(8,128)(2,1)S(1)} %constant_dynamic-slice_fusion.50), channel_id=1, source_target_pairs={{0,1},{1,0},{2,3},{3,2},{4,5},{5,4},{6,7},{7,6},{8,9},{9,8},{10,11... | collective-permute-start | bytes 1769480 | tf_op jit(solution)/shard_map/ppermute | solution.py:476
  124.8 22.8 %collective-permute-start.19 = (bf16[192,1536]{1,0:T(8,128)(2,1)S(1)}, bf16[192,1536]{1,0:T(8,128)(2,1)}, u32[]{:S(2)}, u32[]{:S(2)}) collective-permute-start(bf16[192,1536]{1,0:T(8,128)(2,1)S(1)} %copy-done.109), channel_id=1, source_target_pairs={{0,1},{1,0},{2,3},{3,2},{4,5},{5,4},{6,7},{7,6},{8,9},{9,8},{10,11... | collective-permute-start | bytes 1769480 | tf_op jit(solution)/shard_map/ppermute | solution.py:476
  127.4 24.9 %collective-permute-start.6 = (bf16[192,768]{1,0:T(8,128)(2,1)}, bf16[192,768]{1,0:T(8,128)(2,1)S(1)}, u32[]{:S(2)}, u32[]{:S(2)}) collective-permute-start(bf16[192,768]{1,0:T(8,128)(2,1)} %collective-permute-done.5), channel_id=1, source_target_pairs={{0,2},{2,0},{4,6},{6,4},{8,10},{10,8},{12,14},{14,12},{16,18},{18,... | collective-permute-start | bytes 884744 | tf_op jit(solution)/shard_map/ppermute | solution.py:476
  128.2 21.3 %collective-permute-start.22 = (bf16[192,768]{1,0:T(8,128)(2,1)S(1)}, bf16[192,768]{1,0:T(8,128)(2,1)S(1)}, u32[]{:S(2)}, u32[]{:S(2)}) collective-permute-start(bf16[192,768]{1,0:T(8,128)(2,1)S(1)} %collective-permute-done.21), channel_id=1, source_target_pairs={{0,2},{2,0},{4,6},{6,4},{8,10},{10,8},{12,14},{14,12},{16,18},{18,... | collective-permute-start | bytes 884744 | tf_op jit(solution)/shard_map/ppermute | solution.py:476
  137.4 13.7 %collective-permute-start.16 = (bf16[192,768]{1,0:T(8,128)(2,1)S(1)}, bf16[192,768]{1,0:T(8,128)(2,1)S(1)}, u32[]{:S(2)}, u32[]{:S(2)}) collective-permute-start(bf16[192,768]{1,0:T(8,128)(2,1)S(1)} %collective-permute-done.15), channel_id=1, source_target_pairs={{0,2},{2,0},{4,6},{6,4},{8,10},{10,8},{12,14},{14,12},{16,18},{18,... | collective-permute-start | bytes 884744 | tf_op jit(solution)/shard_map/ppermute | solution.py:476
  149.5 28.9 %collective-permute-start.7 = (bf16[192,3072]{1,0:T(8,128)(2,1)S(1)}, bf16[192,3072]{1,0:T(8,128)(2,1)}, u32[]{:S(2)}, u32[]{:S(2)}) collective-permute-start(bf16[192,3072]{1,0:T(8,128)(2,1)S(1)} %copy-done.102), channel_id=1, source_target_pairs={{0,1},{1,0},{2,3},{3,2},{4,5},{5,4},{6,7},{7,6},{8,9},{9,8},{10,11... | collective-permute-start | bytes 3538952 | tf_op jit(solution)/shard_map/ppermute | solution.py:476
  151.1 52.5 %collective-permute-start.25 = (bf16[768,768]{1,0:T(8,128)(2,1)S(1)}, bf16[768,768]{1,0:T(8,128)(2,1)}, u32[]{:S(2)}, u32[]{:S(2)}) collective-permute-start(bf16[768,768]{1,0:T(8,128)(2,1)S(1)} %copy-done.103), channel_id=1, source_target_pairs={{0,1},{1,0},{2,3},{3,2},{4,5},{5,4},{6,7},{7,6},{8,9},{9,8},{10,11... | collective-permute-start | bytes 3538952 | tf_op jit(solution)/shard_map/ppermute | solution.py:476
  156.5 84.2 %collective-permute-start.23 = (bf16[192,3072]{1,0:T(8,128)(2,1)S(1)}, bf16[192,3072]{1,0:T(8,128)(2,1)}, u32[]{:S(2)}, u32[]{:S(2)}) collective-permute-start(bf16[192,3072]{1,0:T(8,128)(2,1)S(1)} %copy-done.104), channel_id=1, source_target_pairs={{0,1},{1,0},{2,3},{3,2},{4,5},{5,4},{6,7},{7,6},{8,9},{9,8},{10,11... | collective-permute-start | bytes 3538952 | tf_op jit(solution)/shard_map/ppermute | solution.py:476
  158.9 8.6 collective-permute-start.4
  167.6 76.6 %collective-permute-start.20 = (bf16[192,1536]{1,0:T(8,128)(2,1)}, bf16[192,1536]{1,0:T(8,128)(2,1)S(1)}, u32[]{:S(2)}, u32[]{:S(2)}) collective-permute-start(bf16[192,1536]{1,0:T(8,128)(2,1)} %collective-permute-done.19), channel_id=1, source_target_pairs={{0,2},{2,0},{4,6},{6,4},{8,10},{10,8},{12,14},{14,12},{16,18},{18,... | collective-permute-start | bytes 1769480 | tf_op jit(solution)/shard_map/ppermute | solution.py:476
  168.1 96.0 %collective-permute-start.10 = (bf16[768,768]{1,0:T(8,128)(2,1)}, bf16[768,768]{1,0:T(8,128)(2,1)}, u32[]{:S(2)}, u32[]{:S(2)}) collective-permute-start(bf16[768,768]{1,0:T(8,128)(2,1)} %collective-permute-done.9), channel_id=1, source_target_pairs={{0,2},{2,0},{4,6},{6,4},{8,10},{10,8},{12,14},{14,12},{16,18},{18,... | collective-permute-start | bytes 3538952 | tf_op jit(solution)/shard_map/ppermute | solution.py:476
  178.3 77.5 %collective-permute-start.8 = (bf16[192,3072]{1,0:T(8,128)(2,1)}, bf16[192,3072]{1,0:T(8,128)(2,1)S(1)}, u32[]{:S(2)}, u32[]{:S(2)}) collective-permute-start(bf16[192,3072]{1,0:T(8,128)(2,1)} %collective-permute-done.7), channel_id=1, source_target_pairs={{0,2},{2,0},{4,6},{6,4},{8,10},{10,8},{12,14},{14,12},{16,18},{18,... | collective-permute-start | bytes 3538952 | tf_op jit(solution)/shard_map/ppermute | solution.py:476
  203.6 102.5 %collective-permute-start.26 = (bf16[768,768]{1,0:T(8,128)(2,1)}, bf16[768,768]{1,0:T(8,128)(2,1)}, u32[]{:S(2)}, u32[]{:S(2)}) collective-permute-start(bf16[768,768]{1,0:T(8,128)(2,1)} %collective-permute-done.25), channel_id=1, source_target_pairs={{0,2},{2,0},{4,6},{6,4},{8,10},{10,8},{12,14},{14,12},{16,18},{18,... | collective-permute-start | bytes 3538952 | tf_op jit(solution)/shard_map/ppermute | solution.py:476
  240.7 59.0 %collective-permute-start.24 = (bf16[192,3072]{1,0:T(8,128)(2,1)}, bf16[192,3072]{1,0:T(8,128)(2,1)}, u32[]{:S(2)}, u32[]{:S(2)}) collective-permute-start(bf16[192,3072]{1,0:T(8,128)(2,1)} %collective-permute-done.23), channel_id=1, source_target_pairs={{0,2},{2,0},{4,6},{6,4},{8,10},{10,8},{12,14},{14,12},{16,18},{18,... | collective-permute-start | bytes 3538952 | tf_op jit(solution)/shard_map/ppermute | solution.py:476
  521.2 138.2 %collective-permute-start.27 = (bf16[2,2,2,2,24,768]{5,4,0,1,3,2:T(8,128)(2,1)}, bf16[2,2,2,2,24,768]{5,4,0,1,3,2:T(8,128)(2,1)}, u32[]{:S(2)}, u32[]{:S(2)}) collective-permute-start(bf16[2,2,2,2,24,768]{5,4,0,1,3,2:T(8,128)(2,1)} %bitcast.526), channel_id=1, source_target_pairs={{0,2},{2,0},{4,6},{6,4},{8,10},{10,8},{12,14},{14,12},{16,18},{18,... | collective-permute-start | bytes 1769480 | tf_op jit(solution)/shard_map/ppermute | solution.py:476
  523.8 273.5 %collective-permute-start.32 = (bf16[2,2,2,2,24,1536]{5,4,0,1,2,3:T(8,128)(2,1)}, bf16[2,2,2,2,24,1536]{5,4,0,1,2,3:T(8,128)(2,1)}, u32[]{:S(2)}, u32[]{:S(2)}) collective-permute-start(bf16[2,2,2,2,24,1536]{5,4,0,1,2,3:T(8,128)(2,1)} %bitcast.520), channel_id=1, source_target_pairs={{0,2},{2,0},{4,6},{6,4},{8,10},{10,8},{12,14},{14,12},{16,18},{18,... | collective-permute-start | bytes 3538952 | tf_op jit(solution)/shard_map/ppermute | solution.py:476
  526.0 134.8 %collective-permute-start.37 = (bf16[2,2,2,2,24,768]{5,4,0,1,3,2:T(8,128)(2,1)}, bf16[2,2,2,2,24,768]{5,4,0,1,3,2:T(8,128)(2,1)}, u32[]{:S(2)}, u32[]{:S(2)}) collective-permute-start(bf16[2,2,2,2,24,768]{5,4,0,1,3,2:T(8,128)(2,1)} %bitcast.525), channel_id=1, source_target_pairs={{0,2},{2,0},{4,6},{6,4},{8,10},{10,8},{12,14},{14,12},{16,18},{18,... | collective-permute-start | bytes 1769480 | tf_op jit(solution)/shard_map/ppermute | solution.py:476
  529.5 367.2 %collective-permute-start.42 = (bf16[2,2,2,2,24,3072]{5,4,0,1,3,2:T(8,128)(2,1)}, bf16[2,2,2,2,24,3072]{5,4,0,1,3,2:T(8,128)(2,1)}, u32[]{:S(2)}, u32[]{:S(2)}) collective-permute-start(bf16[2,2,2,2,24,3072]{5,4,0,1,3,2:T(8,128)(2,1)} %bitcast.517), channel_id=1, source_target_pairs={{0,2},{2,0},{4,6},{6,4},{8,10},{10,8},{12,14},{14,12},{16,18},{18,... | collective-permute-start | bytes 7077896 | tf_op jit(solution)/shard_map/ppermute | solution.py:476
  554.2 13.7 %collective-permute-start.52 = (f32[2,2,2,2,24,128]{5,4,3,2,1,0:T(8,128)S(1)}, f32[2,2,2,2,24,128]{5,4,3,2,1,0:T(8,128)S(1)}, u32[]{:S(2)}, u32[]{:S(2)}) collective-permute-start(f32[2,2,2,2,24,128]{5,4,3,2,1,0:T(8,128)S(1)} %dynamic-slice_bitcast_fusion.24), channel_id=1, source_target_pairs={{0,2},{2,0},{4,6},{6,4},{8,10},{10,8},{12,14},{14,12},{16,18},{18,... | collective-permute-start | bytes 589832 | tf_op jit(solution)/shard_map/ppermute | solution.py:476
  568.0 19.5 %collective-permute-start.53 = (f32[2,2,2,24,128]{4,3,1,0,2:T(8,128)S(1)}, f32[2,2,2,24,128]{4,3,1,0,2:T(8,128)S(1)}, u32[]{:S(2)}, u32[]{:S(2)}) collective-permute-start(f32[2,2,2,24,128]{4,3,1,0,2:T(8,128)S(1)} %bitcast.581), channel_id=1, source_target_pairs={{0,1},{1,0},{2,3},{3,2},{4,5},{5,4},{6,7},{7,6},{8,9},{9,8},{10,11... | collective-permute-start | bytes 294920 | tf_op jit(solution)/shard_map/ppermute | solution.py:476
  597.6 15.2 %collective-permute-start.56 = (f32[24,128]{0,1:T(8,128)}, f32[24,128]{0,1:T(8,128)}, u32[]{:S(2)}, u32[]{:S(2)}) collective-permute-start(f32[24,128]{0,1:T(8,128)} %bitcast.582), channel_id=1, source_target_pairs={{0,16},{2,18},{4,20},{6,22},{8,24},{10,26},{12,28},{14,30},{16,0},... | collective-permute-start | bytes 36872 | tf_op jit(solution)/shard_map/ppermute | solution.py:476
  612.8 49.8 %collective-permute-start.57 = (bf16[2,2,2,2,24,768]{5,4,0,1,3,2:T(8,128)(2,1)}, bf16[2,2,2,2,24,768]{5,4,0,1,3,2:T(8,128)(2,1)}, u32[]{:S(2)}, u32[]{:S(2)}) collective-permute-start(bf16[2,2,2,2,24,768]{5,4,0,1,3,2:T(8,128)(2,1)} %bitcast.580), channel_id=1, source_target_pairs={{0,2},{2,0},{4,6},{6,4},{8,10},{10,8},{12,14},{14,12},{16,18},{18,... | collective-permute-start | bytes 1769480 | tf_op jit(solution)/shard_map/ppermute | solution.py:476
  664.2 236.6 %collective-permute-start.47 = (bf16[2,2,2,2,96,768]{5,4,0,1,2,3:T(8,128)(2,1)S(1)}, bf16[2,2,2,2,96,768]{5,4,0,1,2,3:T(8,128)(2,1)S(1)}, u32[]{:S(2)}, u32[]{:S(2)}) collective-permute-start(bf16[2,2,2,2,96,768]{5,4,0,1,2,3:T(8,128)(2,1)S(1)} %bitcast.568), channel_id=1, source_target_pairs={{0,2},{2,0},{4,6},{6,4},{8,10},{10,8},{12,14},{14,12},{16,18},{18,... | collective-permute-start | bytes 7077896 | tf_op jit(solution)/shard_map/ppermute | solution.py:476
  664.8 10.1 %collective-permute-start.28 = (bf16[2,2,2,24,768]{4,3,0,1,2:T(8,128)(2,1)S(1)}, bf16[2,2,2,24,768]{4,3,0,1,2:T(8,128)(2,1)S(1)}, u32[]{:S(2)}, u32[]{:S(2)}) collective-permute-start(bf16[2,2,2,24,768]{4,3,0,1,2:T(8,128)(2,1)S(1)} %dynamic-slice_bitcast_fusion.23), channel_id=1, source_target_pairs={{0,4},{2,6},{4,0},{6,2},{8,12},{10,14},{12,8},{14,10},{16,20},{18,... | collective-permute-start | bytes 884744 | tf_op jit(solution)/shard_map/ppermute | solution.py:476
  667.3 14.0 %collective-permute-start.38 = (bf16[2,2,2,24,768]{4,3,0,1,2:T(8,128)(2,1)S(1)}, bf16[2,2,2,24,768]{4,3,0,1,2:T(8,128)(2,1)S(1)}, u32[]{:S(2)}, u32[]{:S(2)}) collective-permute-start(bf16[2,2,2,24,768]{4,3,0,1,2:T(8,128)(2,1)S(1)} %dynamic-slice_bitcast_fusion.21), channel_id=1, source_target_pairs={{0,4},{2,6},{4,0},{6,2},{8,12},{10,14},{12,8},{14,10},{16,20},{18,... | collective-permute-start | bytes 884744 | tf_op jit(solution)/shard_map/ppermute | solution.py:476
  675.0 12.6 %collective-permute-start.58 = (bf16[2,2,2,24,768]{4,3,0,1,2:T(8,128)(2,1)S(1)}, bf16[2,2,2,24,768]{4,3,0,1,2:T(8,128)(2,1)S(1)}, u32[]{:S(2)}, u32[]{:S(2)}) collective-permute-start(bf16[2,2,2,24,768]{4,3,0,1,2:T(8,128)(2,1)S(1)} %dynamic-slice_bitcast_fusion.18), channel_id=1, source_target_pairs={{0,4},{2,6},{4,0},{6,2},{8,12},{10,14},{12,8},{14,10},{16,20},{18,... | collective-permute-start | bytes 884744 | tf_op jit(solution)/shard_map/ppermute | solution.py:476
  681.3 12.6 %collective-permute-start.68 = (bf16[2,2,2,24,768]{4,3,0,1,2:T(8,128)(2,1)S(1)}, bf16[2,2,2,24,768]{4,3,0,1,2:T(8,128)(2,1)S(1)}, u32[]{:S(2)}, u32[]{:S(2)}) collective-permute-start(bf16[2,2,2,24,768]{4,3,0,1,2:T(8,128)(2,1)S(1)} %dynamic-slice_bitcast_fusion.16), channel_id=1, source_target_pairs={{0,4},{2,6},{4,0},{6,2},{8,12},{10,14},{12,8},{14,10},{16,20},{18,... | collective-permute-start | bytes 884744 | tf_op jit(solution)/shard_map/ppermute | solution.py:476
  687.6 12.6 %collective-permute-start.73 = (bf16[2,2,2,24,768]{4,3,0,1,2:T(8,128)(2,1)S(1)}, bf16[2,2,2,24,768]{4,3,0,1,2:T(8,128)(2,1)S(1)}, u32[]{:S(2)}, u32[]{:S(2)}) collective-permute-start(bf16[2,2,2,24,768]{4,3,0,1,2:T(8,128)(2,1)S(1)} %dynamic-slice_bitcast_fusion.15), channel_id=1, source_target_pairs={{0,4},{2,6},{4,0},{6,2},{8,12},{10,14},{12,8},{14,10},{16,20},{18,... | collective-permute-start | bytes 884744 | tf_op jit(solution)/shard_map/ppermute | solution.py:476
  693.9 12.1 %collective-permute-start.83 = (bf16[2,2,2,24,768]{4,3,0,1,2:T(8,128)(2,1)S(1)}, bf16[2,2,2,24,768]{4,3,0,1,2:T(8,128)(2,1)S(1)}, u32[]{:S(2)}, u32[]{:S(2)}) collective-permute-start(bf16[2,2,2,24,768]{4,3,0,1,2:T(8,128)(2,1)S(1)} %dynamic-slice_bitcast_fusion.13), channel_id=1, source_target_pairs={{0,4},{2,6},{4,0},{6,2},{8,12},{10,14},{12,8},{14,10},{16,20},{18,... | collective-permute-start | bytes 884744 | tf_op jit(solution)/shard_map/ppermute | solution.py:476
  700.2 99.2 %collective-permute-start.62 = (bf16[2,2,2,2,24,1536]{5,4,0,1,2,3:T(8,128)(2,1)S(1)}, bf16[2,2,2,2,24,1536]{5,4,0,1,2,3:T(8,128)(2,1)S(1)}, u32[]{:S(2)}, u32[]{:S(2)}) collective-permute-start(bf16[2,2,2,2,24,1536]{5,4,0,1,2,3:T(8,128)(2,1)S(1)} %bitcast.574), channel_id=1, source_target_pairs={{0,2},{2,0},{4,6},{6,4},{8,10},{10,8},{12,14},{14,12},{16,18},{18,... | collective-permute-start | bytes 3538952 | tf_op jit(solution)/shard_map/ppermute | solution.py:476
  797.3 105.8 %collective-permute-start.87 = (bf16[2,2,2,2,24,3072]{5,4,0,1,3,2:T(8,128)(2,1)S(1)}, bf16[2,2,2,2,24,3072]{5,4,0,1,3,2:T(8,128)(2,1)S(1)}, u32[]{:S(2)}, u32[]{:S(2)}) collective-permute-start(bf16[2,2,2,2,24,3072]{5,4,0,1,3,2:T(8,128)(2,1)S(1)} %bitcast.569), channel_id=1, source_target_pairs={{0,2},{2,0},{4,6},{6,4},{8,10},{10,8},{12,14},{14,12},{16,18},{18,... | collective-permute-start | bytes 7077896 | tf_op jit(solution)/shard_map/ppermute | solution.py:476
  799.5 16.3 %collective-permute-start.33 = (bf16[2,2,2,24,1536]{4,3,0,1,2:T(8,128)(2,1)S(1)}, bf16[2,2,2,24,1536]{4,3,0,1,2:T(8,128)(2,1)S(1)}, u32[]{:S(2)}, u32[]{:S(2)}) collective-permute-start(bf16[2,2,2,24,1536]{4,3,0,1,2:T(8,128)(2,1)S(1)} %dynamic-slice_bitcast_fusion.10), channel_id=1, source_target_pairs={{0,1},{1,0},{2,3},{3,2},{4,5},{5,4},{6,7},{7,6},{8,9},{9,8},{10,11... | collective-permute-start | bytes 1769480 | tf_op jit(solution)/shard_map/ppermute | solution.py:476
  801.2 27.1 %collective-permute-start.63 = (bf16[2,2,2,24,1536]{4,3,0,1,2:T(8,128)(2,1)S(1)}, bf16[2,2,2,24,1536]{4,3,0,1,2:T(8,128)(2,1)S(1)}, u32[]{:S(2)}, u32[]{:S(2)}) collective-permute-start(bf16[2,2,2,24,1536]{4,3,0,1,2:T(8,128)(2,1)S(1)} %dynamic-slice_bitcast_fusion.7), channel_id=1, source_target_pairs={{0,1},{1,0},{2,3},{3,2},{4,5},{5,4},{6,7},{7,6},{8,9},{9,8},{10,11... | collective-permute-start | bytes 1769480 | tf_op jit(solution)/shard_map/ppermute | solution.py:476
  815.7 24.3 %collective-permute-start.78 = (bf16[2,2,2,24,1536]{4,3,0,1,2:T(8,128)(2,1)S(1)}, bf16[2,2,2,24,1536]{4,3,0,1,2:T(8,128)(2,1)S(1)}, u32[]{:S(2)}, u32[]{:S(2)}) collective-permute-start(bf16[2,2,2,24,1536]{4,3,0,1,2:T(8,128)(2,1)S(1)} %dynamic-slice_bitcast_fusion.6), channel_id=1, source_target_pairs={{0,1},{1,0},{2,3},{3,2},{4,5},{5,4},{6,7},{7,6},{8,9},{9,8},{10,11... | collective-permute-start | bytes 1769480 | tf_op jit(solution)/shard_map/ppermute | solution.py:476
  828.4 77.3 %collective-permute-start.92 = (bf16[2,2,2,2,96,768]{5,4,0,1,2,3:T(8,128)(2,1)S(1)}, bf16[2,2,2,2,96,768]{5,4,0,1,2,3:T(8,128)(2,1)S(1)}, u32[]{:S(2)}, u32[]{:S(2)}) collective-permute-start(bf16[2,2,2,2,96,768]{5,4,0,1,2,3:T(8,128)(2,1)S(1)} %bitcast.567), channel_id=1, source_target_pairs={{0,2},{2,0},{4,6},{6,4},{8,10},{10,8},{12,14},{14,12},{16,18},{18,... | collective-permute-start | bytes 7077896 | tf_op jit(solution)/shard_map/ppermute | solution.py:476
  840.1 8.1 collective-permute-start.34
  848.1 7.2 collective-permute-start.64
  855.3 6.7 collective-permute-start.79
  878.3 7.2 collective-permute-start.36
  899.4 29.0 %collective-permute-start.43 = (bf16[2,2,2,24,3072]{4,3,0,1,2:T(8,128)(2,1)S(1)}, bf16[2,2,2,24,3072]{4,3,0,1,2:T(8,128)(2,1)S(1)}, u32[]{:S(2)}, u32[]{:S(2)}) collective-permute-start(bf16[2,2,2,24,3072]{4,3,0,1,2:T(8,128)(2,1)S(1)} %dynamic-slice_bitcast_fusion.3), channel_id=1, source_target_pairs={{0,4},{2,6},{4,0},{6,2},{8,12},{10,14},{12,8},{14,10},{16,20},{18,... | collective-permute-start | bytes 3538952 | tf_op jit(solution)/shard_map/ppermute | solution.py:476
  901.7 29.0 %collective-permute-start.48 = (bf16[2,2,2,96,768]{4,3,0,1,2:T(8,128)(2,1)S(1)}, bf16[2,2,2,96,768]{4,3,0,1,2:T(8,128)(2,1)S(1)}, u32[]{:S(2)}, u32[]{:S(2)}) collective-permute-start(bf16[2,2,2,96,768]{4,3,0,1,2:T(8,128)(2,1)S(1)} %dynamic-slice_bitcast_fusion.2), channel_id=1, source_target_pairs={{0,1},{1,0},{2,3},{3,2},{4,5},{5,4},{6,7},{7,6},{8,9},{9,8},{10,11... | collective-permute-start | bytes 3538952 | tf_op jit(solution)/shard_map/ppermute | solution.py:476
  904.3 49.3 %collective-permute-start.88 = (bf16[2,2,2,24,3072]{4,3,0,1,2:T(8,128)(2,1)S(1)}, bf16[2,2,2,24,3072]{4,3,0,1,2:T(8,128)(2,1)S(1)}, u32[]{:S(2)}, u32[]{:S(2)}) collective-permute-start(bf16[2,2,2,24,3072]{4,3,0,1,2:T(8,128)(2,1)S(1)} %dynamic-slice_bitcast_fusion.1), channel_id=1, source_target_pairs={{0,4},{2,6},{4,0},{6,2},{8,12},{10,14},{12,8},{14,10},{16,20},{18,... | collective-permute-start | bytes 3538952 | tf_op jit(solution)/shard_map/ppermute | solution.py:476
  906.7 49.3 %collective-permute-start.93 = (bf16[2,2,2,96,768]{4,3,0,1,2:T(8,128)(2,1)S(1)}, bf16[2,2,2,96,768]{4,3,0,1,2:T(8,128)(2,1)S(1)}, u32[]{:S(2)}, u32[]{:S(2)}) collective-permute-start(bf16[2,2,2,96,768]{4,3,0,1,2:T(8,128)(2,1)S(1)} %dynamic-slice_bitcast_fusion), channel_id=1, source_target_pairs={{0,1},{1,0},{2,3},{3,2},{4,5},{5,4},{6,7},{7,6},{8,9},{9,8},{10,11... | collective-permute-start | bytes 3538952 | tf_op jit(solution)/shard_map/ppermute | solution.py:476
  928.8 34.8 %collective-permute-start.44 = (bf16[2,2,24,3072]{3,2,0,1:T(8,128)(2,1)S(1)}, bf16[2,2,24,3072]{3,2,0,1:T(8,128)(2,1)S(1)}, u32[]{:S(2)}, u32[]{:S(2)}) collective-permute-start(bf16[2,2,24,3072]{3,2,0,1:T(8,128)(2,1)S(1)} %dynamic-slice_bitcast_fusion.9), channel_id=1, source_target_pairs={{0,1},{1,0},{2,3},{3,2},{4,5},{5,4},{6,7},{7,6},{8,9},{9,8},{10,11... | collective-permute-start | bytes 1769480 | tf_op jit(solution)/shard_map/ppermute | solution.py:476
  931.0 32.9 %collective-permute-start.49 = (bf16[2,2,96,768]{3,2,0,1:T(8,128)(2,1)S(1)}, bf16[2,2,96,768]{3,2,0,1:T(8,128)(2,1)S(1)}, u32[]{:S(2)}, u32[]{:S(2)}) collective-permute-start(bf16[2,2,96,768]{3,2,0,1:T(8,128)(2,1)S(1)} %dynamic-slice_bitcast_fusion.8), channel_id=1, source_target_pairs={{0,4},{2,6},{4,0},{6,2},{8,12},{10,14},{12,8},{14,10},{16,20},{18,... | collective-permute-start | bytes 1769480 | tf_op jit(solution)/shard_map/ppermute | solution.py:476
  954.1 15.9 %collective-permute-start.89 = (bf16[2,2,24,3072]{3,2,0,1:T(8,128)(2,1)S(1)}, bf16[2,2,24,3072]{3,2,0,1:T(8,128)(2,1)S(1)}, u32[]{:S(2)}, u32[]{:S(2)}) collective-permute-start(bf16[2,2,24,3072]{3,2,0,1:T(8,128)(2,1)S(1)} %dynamic-slice_bitcast_fusion.5), channel_id=1, source_target_pairs={{0,1},{1,0},{2,3},{3,2},{4,5},{5,4},{6,7},{7,6},{8,9},{9,8},{10,11... | collective-permute-start | bytes 1769480 | tf_op jit(solution)/shard_map/ppermute | solution.py:476
  956.3 13.9 %collective-permute-start.94 = (bf16[2,2,96,768]{3,2,0,1:T(8,128)(2,1)S(1)}, bf16[2,2,96,768]{3,2,0,1:T(8,128)(2,1)S(1)}, u32[]{:S(2)}, u32[]{:S(2)}) collective-permute-start(bf16[2,2,96,768]{3,2,0,1:T(8,128)(2,1)S(1)} %dynamic-slice_bitcast_fusion.4), channel_id=1, source_target_pairs={{0,4},{2,6},{4,0},{6,2},{8,12},{10,14},{12,8},{14,10},{16,20},{18,... | collective-permute-start | bytes 1769480 | tf_op jit(solution)/shard_map/ppermute | solution.py:476
  963.8 11.8 %collective-permute-start.45 = (bf16[2,24,3072]{2,1,0:T(8,128)(2,1)S(1)}, bf16[2,24,3072]{2,1,0:T(8,128)(2,1)S(1)}, u32[]{:S(2)}, u32[]{:S(2)}) collective-permute-start(bf16[2,24,3072]{2,1,0:T(8,128)(2,1)S(1)} %dynamic-slice_bitcast_fusion.20), channel_id=1, source_target_pairs={{0,8},{2,10},{4,12},{6,14},{8,0},{10,2},{12,4},{14,6},{16,24},{18,... | collective-permute-start | bytes 884744 | tf_op jit(solution)/shard_map/ppermute | solution.py:476
  964.1 14.9 %collective-permute-start.50 = (bf16[2,96,768]{2,1,0:T(8,128)(2,1)S(1)}, bf16[2,96,768]{2,1,0:T(8,128)(2,1)S(1)}, u32[]{:S(2)}, u32[]{:S(2)}) collective-permute-start(bf16[2,96,768]{2,1,0:T(8,128)(2,1)S(1)} %dynamic-slice_bitcast_fusion.19), channel_id=1, source_target_pairs={{0,8},{2,10},{4,12},{6,14},{8,0},{10,2},{12,4},{14,6},{16,24},{18,... | collective-permute-start | bytes 884744 | tf_op jit(solution)/shard_map/ppermute | solution.py:476
  970.2 16.8 %collective-permute-start.90 = (bf16[2,24,3072]{2,1,0:T(8,128)(2,1)S(1)}, bf16[2,24,3072]{2,1,0:T(8,128)(2,1)S(1)}, u32[]{:S(2)}, u32[]{:S(2)}) collective-permute-start(bf16[2,24,3072]{2,1,0:T(8,128)(2,1)S(1)} %dynamic-slice_bitcast_fusion.12), channel_id=1, source_target_pairs={{0,8},{2,10},{4,12},{6,14},{8,0},{10,2},{12,4},{14,6},{16,24},{18,... | collective-permute-start | bytes 884744 | tf_op jit(solution)/shard_map/ppermute | solution.py:476
  970.5 19.6 %collective-permute-start.95 = (bf16[2,96,768]{2,1,0:T(8,128)(2,1)S(1)}, bf16[2,96,768]{2,1,0:T(8,128)(2,1)S(1)}, u32[]{:S(2)}, u32[]{:S(2)}) collective-permute-start(bf16[2,96,768]{2,1,0:T(8,128)(2,1)S(1)} %dynamic-slice_bitcast_fusion.11), channel_id=1, source_target_pairs={{0,8},{2,10},{4,12},{6,14},{8,0},{10,2},{12,4},{14,6},{16,24},{18,... | collective-permute-start | bytes 884744 | tf_op jit(solution)/shard_map/ppermute | solution.py:476
  975.8 14.5 %collective-permute-start.46 = (bf16[24,3072]{1,0:T(8,128)(2,1)S(1)}, bf16[24,3072]{1,0:T(8,128)(2,1)S(1)}, u32[]{:S(2)}, u32[]{:S(2)}) collective-permute-start(bf16[24,3072]{1,0:T(8,128)(2,1)S(1)} %dynamic-slice_bitcast_fusion.34), channel_id=1, source_target_pairs={{0,16},{2,18},{4,20},{6,22},{8,24},{10,26},{12,28},{14,30},{16,0},... | collective-permute-start | bytes 442376 | tf_op jit(solution)/shard_map/ppermute | solution.py:476
  979.1 15.3 %collective-permute-start.51 = (bf16[96,768]{1,0:T(8,128)(2,1)S(1)}, bf16[96,768]{1,0:T(8,128)(2,1)S(1)}, u32[]{:S(2)}, u32[]{:S(2)}) collective-permute-start(bf16[96,768]{1,0:T(8,128)(2,1)S(1)} %dynamic-slice_bitcast_fusion.33), channel_id=1, source_target_pairs={{0,16},{2,18},{4,20},{6,22},{8,24},{10,26},{12,28},{14,30},{16,0},... | collective-permute-start | bytes 442376 | tf_op jit(solution)/shard_map/ppermute | solution.py:476
  987.0 6.7 collective-permute-start.91
  (194 other events, 2904.1 us)

commit v2 on v1

--- a/solution.py
+++ b/solution.py
@@ -92,7 +92,7 @@
 
 def tile_mask(spec, key_tile, query_block, segk_ref, segq_ref):
     rows, lanes = spec["kb"], spec["qb"]
-    start = pl.multiple_of(key_tile * rows, rows)
+    start = pl.multiple_of(key_tile * rows, rows) if spec["skip"] else key_tile * rows
     labels = segk_ref[pl.ds(start, rows), :]
     labels = jnp.concatenate([labels] * (lanes // TILE), axis=1)
     mask = labels == segq_ref[...]
@@ -132,66 +132,67 @@
     return jnp.dot(former, latter, preferred_element_type=jnp.float32)
 
 
+def for_counts(spec, first, last, run):
+    if not spec["skip"]:
+        run(0, spec["tiles"])
+        return
+    for count in range(1, spec["tiles"] + 1):
+        pl.when(last - first == count)(functools.partial(run, first, count))
+
+
 def forward_kernel(spec, bounds_ref, q_ref, k_ref, v_ref, segq_ref, segk_ref, *rest):
     bias_ref, rest = (rest[0], rest[1:]) if spec["bias"] else (None, rest)
     o_ref, lse_ref, score_ref, vt_ref = rest
-    kb, qb = spec["kb"], spec["qb"]
+    kb, qb, pairs = spec["kb"], spec["qb"], spec["pairs"]
     block = pl.program_id(1)
 
     @pl.when(block == 0)
     def _():
-        vt_ref[...] = flip(v_ref[...]).astype(jnp.bfloat16)
-
-    parts = head_parts(q_ref[...])
-    first, last = bounds_ref[0, block], bounds_ref[1, block]
-
-    def score(tile, highest):
-        start = pl.multiple_of(tile * kb, kb)
-        keys = k_ref[pl.ds(start, kb), :]
-        mask = tile_mask(spec, tile, block, segk_ref, segq_ref)
-        fresh = []
-        for head in range(2):
-            s = dot_rows(keys, parts[head])
-            if spec["bias"]:
-                s = s + tile_bias(spec, head, tile, block, bias_ref)
-            s = jnp.where(mask, s, MASKED)
-            score_ref[head, pl.ds(start, kb), :] = s
-            fresh.append(jnp.maximum(highest[head], fold_rows(s, jnp.maximum)))
-        return tuple(fresh)
-
-    low = jnp.full((8, qb), MASKED, jnp.float32)
-    highest = lax.fori_loop(first, last, score, (low, low))
-    top = [jnp.max(value, axis=0, keepdims=True) for value in highest]
-
-    def exponent(tile, summed):
-        start = pl.multiple_of(tile * kb, kb)
-        fresh = []
-        for head in range(2):
-            e = jnp.exp(score_ref[head, pl.ds(start, kb), :] - top[head])
-            score_ref[head, pl.ds(start, kb), :] = e
-            fresh.append(summed[head] + fold_rows(e, jnp.add))
-        return tuple(fresh)
-
-    none = jnp.zeros((8, qb), jnp.float32)
-    summed = lax.fori_loop(first, last, exponent, (none, none))
-    total = [jnp.sum(value, axis=0, keepdims=True) for value in summed]
-    scale = [1.0 / value for value in total]
-
-    def mix(tile, mixed):
-        start = pl.multiple_of(tile * kb, kb)
-        fresh = []
-        for head in range(2):
-            weights = (score_ref[head, pl.ds(start, kb), :] * scale[head]).astype(jnp.bfloat16)
-            values = vt_ref[pl.ds(head * HD, HD), pl.ds(start, kb)]
-            fresh.append(mixed[head] + dot_plain(values, weights))
-        return tuple(fresh)
-
-    nothing = jnp.zeros((HD, qb), jnp.float32)
-    mixed = lax.fori_loop(first, last, mix, (nothing, nothing))
-    o_ref[...] = flip(jnp.concatenate(mixed, axis=0)).astype(jnp.bfloat16)
-    lse_ref[0] = jnp.concatenate(
-        [top[head] + jnp.log(total[head]) for head in range(2)], axis=0
-    )
+        for pair in range(pairs):
+            span = slice(pair * 2 * HD, (pair + 1) * 2 * HD)
+            vt_ref[span, :] = flip(v_ref[:, span]).astype(jnp.bfloat16)
+
+    def run(first, count):
+        starts = [(first + tile) * kb for tile in range(count)]
+        if spec["skip"]:
+            starts = [pl.multiple_of(start, kb) for start in starts]
+        for pair in range(pairs):
+            span = slice(pair * 2 * HD, (pair + 1) * 2 * HD)
+            parts = head_parts(q_ref[:, span])
+            mixed, logsum = [], []
+            for head in range(2):
+                number = 2 * pair + head
+                top = None
+                for tile in range(count):
+                    s = dot_rows(k_ref[pl.ds(starts[tile], kb), span], parts[head])
+                    if spec["bias"]:
+                        s = s + tile_bias(spec, number, first + tile, block, bias_ref)
+                    mask = tile_mask(spec, first + tile, block, segk_ref, segq_ref)
+                    s = jnp.where(mask, s, MASKED)
+                    score_ref[number, tile] = s
+                    peak = fold_rows(s, jnp.maximum)
+                    top = peak if top is None else jnp.maximum(top, peak)
+                top = jnp.max(top, axis=0, keepdims=True)
+                total = None
+                for tile in range(count):
+                    e = jnp.exp(score_ref[number, tile] - top)
+                    score_ref[number, tile] = e
+                    part = fold_rows(e, jnp.add)
+                    total = part if total is None else total + part
+                total = jnp.sum(total, axis=0, keepdims=True)
+                scale = 1.0 / total
+                mix = None
+                for tile in range(count):
+                    weights = (score_ref[number, tile] * scale).astype(jnp.bfloat16)
+                    rows = slice(number * HD, (number + 1) * HD)
+                    part = dot_plain(vt_ref[rows, pl.ds(starts[tile], kb)], weights)
+                    mix = part if mix is None else mix + part
+                mixed.append(mix)
+                logsum.append(top + jnp.log(total))
+            o_ref[:, span] = flip(jnp.concatenate(mixed, axis=0)).astype(jnp.bfloat16)
+            lse_ref[pair] = jnp.concatenate(logsum, axis=0)
+
+    for_counts(spec, bounds_ref[0, block], bounds_ref[1, block], run)
 
 
 def backward_kernel(
@@ -201,106 +202,117 @@
     dq_ref, dkv_ref, rest = rest[0], rest[1], rest[2:]
     band_ref, rest = (rest[0], rest[1:]) if spec["bias"] else (None, rest)
     p_ref, dp_ref, dk_ref, dv_ref, kt_ref = rest
-    kb, qb = spec["kb"], spec["qb"]
-    pair, block = pl.program_id(0), pl.program_id(1)
+    kb, qb, pairs = spec["kb"], spec["qb"], spec["pairs"]
+    group, block = pl.program_id(0), pl.program_id(1)
 
     @pl.when(block == 0)
     def _():
-        kt_ref[...] = flip(k_ref[...]).astype(jnp.bfloat16)
+        for pair in range(pairs):
+            span = slice(pair * 2 * HD, (pair + 1) * 2 * HD)
+            kt_ref[span, :] = flip(k_ref[:, span]).astype(jnp.bfloat16)
         dk_ref[...] = jnp.zeros_like(dk_ref)
         dv_ref[...] = jnp.zeros_like(dv_ref)
         if spec["bias"]:
             band_ref[...] = jnp.zeros_like(band_ref)
 
-    parts = head_parts(q_ref[...])
-    dparts = head_parts(do_ref[...])
-    lse = lse_ref[0]
-    first, last = bounds_ref[0, block], bounds_ref[1, block]
-
-    def weigh(tile, delta):
-        start = pl.multiple_of(tile * kb, kb)
-        keys = k_ref[pl.ds(start, kb), :]
-        values = v_ref[pl.ds(start, kb), :]
-        mask = tile_mask(spec, tile, block, segk_ref, segq_ref)
-        fresh = []
-        dvalues = dv_ref[pl.ds(start, kb), :]
-        for head in range(2):
-            s = dot_rows(keys, parts[head])
-            if spec["bias"]:
-                s = s + tile_bias(spec, head, tile, block, bias_ref)
-            p = jnp.exp(jnp.where(mask, s, MASKED) - lse[head : head + 1])
-            dp = dot_rows(values, dparts[head])
-            p_ref[head, pl.ds(start, kb), :] = p
-            dp_ref[head, pl.ds(start, kb), :] = dp
-            fresh.append(delta[head] + fold_rows(p * dp, jnp.add))
-            dvalues = dvalues + dot_plain(p.astype(jnp.bfloat16), dparts[head])
-        dv_ref[pl.ds(start, kb), :] = dvalues
-        return tuple(fresh)
-
-    none = jnp.zeros((8, qb), jnp.float32)
-    delta = lax.fori_loop(first, last, weigh, (none, none))
-    delta = [jnp.sum(value, axis=0, keepdims=True) for value in delta]
-
-    def pull(tile, dquery):
-        start = pl.multiple_of(tile * kb, kb)
-        fresh = []
-        dkeys = dk_ref[pl.ds(start, kb), :]
-        for head in range(2):
-            ds = p_ref[head, pl.ds(start, kb), :] * (
-                dp_ref[head, pl.ds(start, kb), :] - delta[head]
-            )
-            if spec["bias"]:
-                rows, lanes = kb // TILE, qb // TILE
-                for row in range(rows):
-                    for lane in range(lanes):
-                        index = band_index(block * lanes + lane, tile * rows + row)
-                        band_ref[head, index] += ds[
-                            row * TILE : (row + 1) * TILE, lane * TILE : (lane + 1) * TILE
-                        ]
-            low = ds.astype(jnp.bfloat16)
-            dkeys = dkeys + dot_plain(low, parts[head])
-            kt = kt_ref[pl.ds(head * HD, HD), pl.ds(start, kb)]
-            fresh.append(dquery[head] + dot_plain(kt, low))
-        dk_ref[pl.ds(start, kb), :] = dkeys
-        return tuple(fresh)
-
-    nothing = jnp.zeros((HD, qb), jnp.float32)
-    dquery = lax.fori_loop(first, last, pull, (nothing, nothing))
-    dq_ref[...] = flip(jnp.concatenate(dquery, axis=0)).astype(jnp.bfloat16)
+    def run(first, count):
+        starts = [(first + tile) * kb for tile in range(count)]
+        if spec["skip"]:
+            starts = [pl.multiple_of(start, kb) for start in starts]
+        for pair in range(pairs):
+            span = slice(pair * 2 * HD, (pair + 1) * 2 * HD)
+            parts = head_parts(q_ref[:, span])
+            dparts = head_parts(do_ref[:, span])
+            lse = lse_ref[pair]
+            dquery = []
+            for head in range(2):
+                number = 2 * pair + head
+                delta = None
+                for tile in range(count):
+                    here = pl.ds(starts[tile], kb)
+                    s = dot_rows(k_ref[here, span], parts[head])
+                    if spec["bias"]:
+                        s = s + tile_bias(spec, number, first + tile, block, bias_ref)
+                    mask = tile_mask(spec, first + tile, block, segk_ref, segq_ref)
+                    p = jnp.exp(jnp.where(mask, s, MASKED) - lse[head : head + 1])
+                    dp = dot_rows(v_ref[here, span], dparts[head])
+                    p_ref[number, tile] = p
+                    dp_ref[number, tile] = dp
+                    part = fold_rows(p * dp, jnp.add)
+                    delta = part if delta is None else delta + part
+                    dv_ref[here, span] += dot_plain(p.astype(jnp.bfloat16), dparts[head])
+                delta = jnp.sum(delta, axis=0, keepdims=True)
+                mix = None
+                for tile in range(count):
+                    here = pl.ds(starts[tile], kb)
+                    ds = p_ref[number, tile] * (dp_ref[number, tile] - delta)
+                    if spec["bias"]:
+                        rows, lanes = kb // TILE, qb // TILE
+                        for row in range(rows):
+                            for lane in range(lanes):
+                                index = band_index(
+                                    block * lanes + lane, (first + tile) * rows + row
+                                )
+                                band_ref[number, index] += ds[
+                                    row * TILE : (row + 1) * TILE,
+                                    lane * TILE : (lane + 1) * TILE,
+                                ]
+                    low = ds.astype(jnp.bfloat16)
+                    dk_ref[here, span] += dot_plain(low, parts[head])
+                    rows = slice(number * HD, (number + 1) * HD)
+                    part = dot_plain(kt_ref[rows, here], low)
+                    mix = part if mix is None else mix + part
+                dquery.append(mix)
+            dq_ref[:, span] = flip(jnp.concatenate(dquery, axis=0)).astype(jnp.bfloat16)
+
+    for_counts(spec, bounds_ref[0, block], bounds_ref[1, block], run)
 
     @pl.when(block == pl.num_programs(1) - 1)
     def _():
-        column = pl.multiple_of(pair * 2 * HD, 2 * HD)
-        dkv_ref[:, pl.ds(column, 2 * HD)] = dk_ref[...].astype(jnp.bfloat16)
-        column = pl.multiple_of((pl.num_programs(0) + pair) * 2 * HD, 2 * HD)
-        dkv_ref[:, pl.ds(column, 2 * HD)] = dv_ref[...].astype(jnp.bfloat16)
+        width = pairs * 2 * HD
+        column = pl.multiple_of(group * width, width)
+        dkv_ref[:, pl.ds(column, width)] = dk_ref[...].astype(jnp.bfloat16)
+        column = pl.multiple_of((pl.num_programs(0) + group) * width, width)
+        dkv_ref[:, pl.ds(column, width)] = dv_ref[...].astype(jnp.bfloat16)
 
 
 def attention_setup(queries, keyval, query_labels, key_labels, bias, causal):
     rows, keys = queries.shape[0], keyval.shape[0]
     qb, kb = min(256, rows), min(256, keys)
-    spec = dict(qb=qb, kb=kb, causal=causal, bias=bias is not None)
+    skip = rows > qb
+    pairs = 1 if skip else 3
+    spec = dict(
+        qb=qb,
+        kb=kb,
+        causal=causal,
+        bias=bias is not None,
+        pairs=pairs,
+        tiles=keys // kb,
+        skip=skip,
+    )
     bounds = key_bounds(query_labels, key_labels, qb, kb)
     segq = query_labels[None, :]
     segk = jnp.broadcast_to(key_labels[:, None], (keys, TILE))
-    pairs = H // 2
-    in_specs = dict(
-        q=pl.BlockSpec((qb, 2 * HD), lambda pair, block, bounds: (block, pair)),
-        k=pl.BlockSpec((keys, 2 * HD), lambda pair, block, bounds: (0, pair)),
-        v=pl.BlockSpec((keys, 2 * HD), lambda pair, block, bounds: (0, pairs + pair)),
-        segq=pl.BlockSpec((1, qb), lambda pair, block, bounds: (0, block)),
-        segk=pl.BlockSpec((keys, TILE), lambda pair, block, bounds: (0, 0)),
-        lse=pl.BlockSpec((1, 2, qb), lambda pair, block, bounds: (pair, 0, block)),
+    groups = H // 2 // pairs
+    width = 2 * HD * pairs
+    specs = dict(
+        q=pl.BlockSpec((qb, width), lambda group, block, bounds: (block, group)),
+        k=pl.BlockSpec((keys, width), lambda group, block, bounds: (0, group)),
+        v=pl.BlockSpec((keys, width), lambda group, block, bounds: (0, groups + group)),
+        segq=pl.BlockSpec((1, qb), lambda group, block, bounds: (0, block)),
+        segk=pl.BlockSpec((keys, TILE), lambda group, block, bounds: (0, 0)),
+        lse=pl.BlockSpec((pairs, 2, qb), lambda group, block, bounds: (group, 0, block)),
         band=pl.BlockSpec(
-            (2, BAND, TILE, TILE), lambda pair, block, bounds: (pair, 0, 0, 0)
+            (2 * pairs, BAND, TILE, TILE), lambda group, block, bounds: (group, 0, 0, 0)
         ),
-        whole=pl.BlockSpec((keys, 4 * pairs * HD), lambda pair, block, bounds: (0, 0)),
-    )
-    return spec, bounds, segq, segk, in_specs, (pairs, rows // qb)
+        whole=pl.BlockSpec((keys, 2 * H * HD), lambda group, block, bounds: (0, 0)),
+    )
+    scores = pltpu.VMEM((2 * pairs, keys // kb, kb, qb), jnp.float32)
+    return spec, bounds, segq, segk, specs, (groups, rows // qb), scores
 
 
 def attend_forward(queries, keyval, query_labels, key_labels, bias, causal):
-    spec, bounds, segq, segk, specs, grid = attention_setup(
+    spec, bounds, segq, segk, specs, grid, scores = attention_setup(
         queries, keyval, query_labels, key_labels, bias, causal
     )
     rows, keys = queries.shape[0], keyval.shape[0]
@@ -319,8 +331,8 @@
             + extra[0],
             out_specs=[specs["q"], specs["lse"]],
             scratch_shapes=[
-                pltpu.VMEM((2, keys, spec["qb"]), jnp.float32),
-                pltpu.VMEM((2 * HD, keys), jnp.bfloat16),
+                scores,
+                pltpu.VMEM((2 * HD * spec["pairs"], keys), jnp.bfloat16),
             ],
         ),
         compiler_params=pltpu.CompilerParams(vmem_limit_bytes=40 << 20),
@@ -331,7 +343,7 @@
 
 
 def attend_backward(queries, keyval, query_labels, key_labels, bias, causal, lse, dmixture):
-    spec, bounds, segq, segk, specs, grid = attention_setup(
+    spec, bounds, segq, segk, specs, grid, scores = attention_setup(
         queries, keyval, query_labels, key_labels, bias, causal
     )
     rows, keys = queries.shape[0], keyval.shape[0]
@@ -362,11 +374,11 @@
             + extra[0],
             out_specs=[specs["q"], specs["whole"]] + extra[0],
             scratch_shapes=[
-                pltpu.VMEM((2, keys, spec["qb"]), jnp.float32),
-                pltpu.VMEM((2, keys, spec["qb"]), jnp.float32),
-                pltpu.VMEM((keys, 2 * HD), jnp.float32),
-                pltpu.VMEM((keys, 2 * HD), jnp.float32),
-                pltpu.VMEM((2 * HD, keys), jnp.bfloat16),
+                scores,
+                scores,
+                pltpu.VMEM((keys, 2 * HD * spec["pairs"]), jnp.float32),
+                pltpu.VMEM((keys, 2 * HD * spec["pairs"]), jnp.float32),
+                pltpu.VMEM((2 * HD * spec["pairs"], keys), jnp.bfloat16),
             ],
         ),
         compiler_params=pltpu.CompilerParams(vmem_limit_bytes=48 << 20),
@@ -459,10 +471,6 @@
     return devices.bit_length() - 1
 
 
-def swap_pairs(devices, bit):
-    return [(place, place ^ (1 << bit)) for place in range(devices)]
-
-
 class Links:
     def __init__(self, mesh):
         self.sizes = dict(mesh.shape)
@@ -470,10 +478,24 @@
         self.bits += [("dp", bit) for bit in range(index_bits(self.sizes["dp"]))]
 
     def side(self, axis, bit):
-        return (lax.axis_index(axis) >> bit) & 1
+        return lax.rem(lax.axis_index(axis) // (1 << bit), 2)
+
+    def partner(self, axis, bit):
+        return {axis: lax.axis_index(axis) + (1 - 2 * self.side(axis, bit)) * (1 << bit)}
+
+    def orders(self):
+        core, row = ("dp", 0), ("fsdp", 0)
+        rest = [key for key in self.bits if key not in (core, row)]
+        return ([core] + rest[:1] + [row] + rest[1:], [core, row] + rest)
 
     def swap(self, value, axis, bit):
-        return lax.ppermute(value, axis, swap_pairs(self.sizes[axis], bit))
+        pairs = [(place, place ^ (1 << bit)) for place in range(self.sizes[axis])]
+        return lax.ppermute(value, axis, pairs)
+
+    def total(self, value):
+        for key in self.bits:
+            value = value + self.swap(value, *key)
+        return value
 
     def gather(self, shard):
         rows, columns = shard.shape
@@ -495,28 +517,151 @@
             [jnp.where(first, shard, other), jnp.where(first, other, shard)], axis=0
         )
 
-    def scatter(self, value, order, kept=jnp.bfloat16):
-        rows, columns = value.shape
-        shape = (2,) * len(self.bits) + (rows >> len(self.bits), columns)
-        current = value.astype(kept).reshape(shape)
-        left = list(reversed(self.bits))
-        for step, key in enumerate(order):
-            spot = left.index(key)
-            side = self.side(*key)
-            send = lax.dynamic_index_in_dim(current, 1 - side, spot, keepdims=False)
-            mine = lax.dynamic_index_in_dim(current, side, spot, keepdims=False)
-            arrived = self.swap(send, *key)
-            current = mine.astype(jnp.float32) + arrived.astype(jnp.float32)
-            if step < len(order) - 1:
-                current = current.astype(kept)
+    def devices(self):
+        return self.sizes["dp"] * self.sizes["fsdp"]
+
+    def place(self):
+        return lax.axis_index("dp") * self.sizes["fsdp"] + lax.axis_index("fsdp")
+
+
+def pick(ref, lead, spot, count, side):
+    return ref.at[(lead,) + (slice(None),) * spot + (side,) + (slice(None),) * (count - spot - 1)]
+
+
+def reduce_kernel(links, pairs, g_ref, out_ref, own_ref, *rest):
+    stages = len(links.bits)
+    sums, (send_sem, recv_sem, own_sem) = rest[:stages], rest[stages:]
+    plans = []
+    for order in links.orders():
+        left = list(reversed(links.bits))
+        plan = []
+        for key in order:
+            plan.append((key, left.index(key), len(left)))
             left.remove(key)
-        return current
-
-    def orders(self):
-        core, row = ("dp", 0), ("fsdp", 0)
-        rest = [key for key in self.bits if key not in (core, row)]
-        across = rest[:1]
-        return ([core] + across + [row] + rest[1:], [core, row] + rest)
+        plans.append(plan)
+
+    barrier = pltpu.get_barrier_semaphore()
+    for key in links.bits:
+        pl.semaphore_signal(
+            barrier,
+            inc=1,
+            device_id=links.partner(*key),
+            device_id_type=pl.DeviceIdType.MESH,
+        )
+    pl.semaphore_wait(barrier, stages)
+
+    def source(stage, chunk, parity, away):
+        key, spot, count = plans[parity][stage]
+        side = links.side(*key)
+        ref = g_ref if stage == 0 else sums[stage - 1]
+        return pick(ref, chunk, spot, count, 1 - side if away else side)
+
+    def send(stage, chunk, parity):
+        key, _, _ = plans[parity][stage]
+        return pltpu.make_async_remote_copy(
+            src_ref=source(stage, chunk, parity, True),
+            dst_ref=sums[stage].at[chunk],
+            send_sem=send_sem.at[stage, chunk],
+            recv_sem=recv_sem.at[stage, chunk],
+            device_id=links.partner(*key),
+            device_id_type=pl.DeviceIdType.MESH,
+        )
+
+    def fetch(pair, parity):
+        slot = lax.rem(pair, 2)
+        return pltpu.make_async_copy(
+            source(0, 2 * pair + parity, parity, False),
+            own_ref.at[slot, parity],
+            own_sem.at[slot, parity],
+        )
+
+    def step(slot, carry):
+        @pl.when(slot < pairs)
+        def _():
+            for parity in range(2):
+                send(0, 2 * slot + parity, parity).start()
+                fetch(slot, parity).start()
+
+        for stage in range(stages):
+            pair = slot - 1 - stage
+
+            @pl.when((pair >= 0) & (pair < pairs))
+            def _():
+                for parity in range(2):
+                    chunk = 2 * pair + parity
+                    send(stage, chunk, parity).wait()
+                    if stage == 0:
+                        fetch(pair, parity).wait()
+                        mine = own_ref[lax.rem(pair, 2), parity]
+                    else:
+                        mine = source(stage, chunk, parity, False)[...]
+                    if stage < stages - 1:
+                        sums[stage][chunk] = sums[stage][chunk] + mine
+                        send(stage + 1, chunk, parity).start()
+                    else:
+                        out_ref[chunk] = sums[stage][chunk].astype(jnp.float32) + mine.astype(
+                            jnp.float32
+                        )
+
+        return carry
+
+    lax.fori_loop(0, pairs + stages, step, 0)
+
+
+def reduce_chunks(links, grads, collective_id):
+    chunks, _, rows, columns = grads.shape
+    stages = len(links.bits)
+    sums = [
+        pltpu.VMEM((chunks,) + (2,) * (stages - 1 - stage) + (rows, columns), jnp.bfloat16)
+        for stage in range(stages)
+    ]
+    return pl.pallas_call(
+        functools.partial(reduce_kernel, links, chunks // 2),
+        out_shape=jax.ShapeDtypeStruct((chunks, rows, columns), jnp.float32),
+        in_specs=[pl.BlockSpec(memory_space=pl.ANY)],
+        out_specs=pl.BlockSpec(memory_space=pltpu.VMEM),
+        scratch_shapes=[
+            pltpu.VMEM((2, 2) + (2,) * (stages - 1) + (rows, columns), jnp.bfloat16)
+        ]
+        + sums
+        + [
+            pltpu.SemaphoreType.DMA((stages, chunks)),
+            pltpu.SemaphoreType.DMA((stages, chunks)),
+            pltpu.SemaphoreType.DMA((2, 2)),
+        ],
+        compiler_params=pltpu.CompilerParams(
+            collective_id=collective_id, has_side_effects=True, vmem_limit_bytes=58 << 20
+        ),
+    )(grads.reshape((chunks,) + (2,) * stages + (rows, columns)))
+
+
+def fold_grad(grad, devices, width):
+    rows, columns = grad.shape
+    deep, wide = rows // width, columns // width
+    r = rows // devices // deep
+    grad = grad.astype(jnp.bfloat16).reshape(devices, deep, r, wide, 2, width // 2)
+    return grad.transpose(1, 3, 0, 4, 2, 5).reshape(deep * wide, devices, 2 * r, width // 2)
+
+
+def unfold_share(chunks, rows, columns):
+    count, folded, half = chunks.shape
+    deep, wide = rows * 2 // folded, columns // (2 * half)
+    chunks = chunks.reshape(deep, wide, 2, folded // 2, half)
+    return chunks.transpose(0, 3, 1, 2, 4).reshape(rows, columns)
+
+
+def reduce_grads(links, grads, collective_id):
+    devices = links.devices()
+    width = min(grad.shape[0] for grad in grads)
+    folded = [fold_grad(grad, devices, width) for grad in grads]
+    counts = [piece.shape[0] for piece in folded]
+    shares = reduce_chunks(links, jnp.concatenate(folded, axis=0), collective_id)
+    result, start = [], 0
+    for grad, count in zip(grads, counts):
+        rows, columns = grad.shape
+        result.append(unfold_share(shares[start : start + count], rows // devices, columns))
+        start += count
+    return result
 
 
 def body(
@@ -591,15 +736,12 @@
     )
     dec_final, dec_ffn = feed_forward(after_cross, dec_gains[:, 2], dinner, douter)
 
-    first, second = links.orders()
 
     dec_live = (dec_segments >= 0).astype(jnp.float32)[:, None]
     gradient = dec_upstream.astype(jnp.float32) * dec_live
     gradient, dgain_ffn, dinner_grad, douter_grad = feed_backward(
         after_cross, dec_gains[:, 2], dinner, douter, dec_ffn, gradient
     )
-    dinner_share = links.scatter(dinner_grad, first)
-    douter_share = links.scatter(douter_grad, second)
     gradient, dgain_cross, cquery_grad, ckeyval_grad, cproj_grad, _, memory_grad = (
         attention_backward(
             after_self,
@@ -613,9 +755,6 @@
             gradient,
         )
     )
-    cproj_share = links.scatter(cproj_grad, first)
-    cquery_share = links.scatter(cquery_grad, first)
-    ckeyval_share = links.scatter(ckeyval_grad, second)
     dec_gradient, dgain_self, dquery_grad, dkeyval_grad, dproj_grad, dec_band, _ = (
         attention_backward(
             dec_stream,
@@ -629,17 +768,12 @@
             gradient,
         )
     )
-    dproj_share = links.scatter(dproj_grad, first)
-    dquery_share = links.scatter(dquery_grad, first)
-    dkeyval_share = links.scatter(dkeyval_grad, second)
 
     enc_live = (enc_segments >= 0).astype(jnp.float32)[:, None]
     gradient = enc_upstream.astype(jnp.float32) * enc_live + memory_grad
     gradient, egain_ffn, einner_grad, eouter_grad = feed_backward(
         enc_middle, enc_gains[:, 1], einner, eouter, enc_ffn, gradient
     )
-    einner_share = links.scatter(einner_grad, first)
-    eouter_share = links.scatter(eouter_grad, second)
     enc_gradient, egain_self, equery_grad, ekeyval_grad, eproj_grad, enc_band, _ = (
         attention_backward(
             enc_stream,
@@ -653,26 +787,53 @@
             gradient,
         )
     )
-    eproj_share = links.scatter(eproj_grad, first)
-    equery_share = links.scatter(equery_grad, first)
-    ekeyval_share = links.scatter(ekeyval_grad, second)
-
-    table_grads = jnp.concatenate(
+
+    table_grads = [
+        band_table_grad(enc_band, encoder_bucket),
+        band_table_grad(dec_band, decoder_bucket),
+    ]
+    gain_grads = jnp.stack([egain_self, egain_ffn, dgain_self, dgain_cross, dgain_ffn])
+    flat = jnp.concatenate([gain_grads.reshape(-1)] + [grad.reshape(-1) for grad in table_grads])
+    flat = links.total(flat.reshape(-1, TILE)).reshape(-1)
+    width = gain_grads.shape[1]
+    tables_grad = flat[5 * width :].reshape(2, NB, H)
+    own = width // links.devices()
+    gains_share = lax.dynamic_slice_in_dim(
+        flat[: 5 * width].reshape(5, width), links.place() * own, own, 1
+    ).T
+    (
+        equery_share,
+        ekeyval_share,
+        eproj_share,
+        einner_share,
+        eouter_share,
+        dquery_share,
+        dkeyval_share,
+        dproj_share,
+        cquery_share,
+        ckeyval_share,
+        cproj_share,
+        dinner_share,
+        douter_share,
+    ) = reduce_grads(
+        links,
         [
-            band_table_grad(enc_band, encoder_bucket),
-            band_table_grad(dec_band, decoder_bucket),
+            equery_grad,
+            ekeyval_grad,
+            eproj_grad,
+            einner_grad,
+            eouter_grad,
+            dquery_grad,
+            dkeyval_grad,
+            dproj_grad,
+            cquery_grad,
+            ckeyval_grad,
+            cproj_grad,
+            dinner_grad,
+            douter_grad,
         ],
-        axis=0,
-    )
-    columns = jnp.stack([egain_self, egain_ffn, dgain_self, dgain_cross, dgain_ffn], axis=1)
-    wide = columns.shape[0]
-    packed = jnp.concatenate(
-        [columns, table_grads.reshape(wide, -1)], axis=1
-    )
-    packed = jnp.pad(packed, ((0, 0), (0, TILE - packed.shape[1])))
-    small_share = links.scatter(packed, second, jnp.float32)
-    tables_grad = lax.all_gather(small_share[:, 5:6], ("dp", "fsdp"), axis=0, tiled=True)
-    tables_grad = tables_grad.reshape(2, NB, H)
+        0,
+    )
     return (
         memory,
         dec_final.astype(jnp.bfloat16),
@@ -683,7 +844,7 @@
         eproj_share,
         einner_share,
         eouter_share,
-        small_share[:, 0:2],
+        gains_share[:, 0:2],
         tables_grad[0],
         dquery_share,
         dkeyval_share,
@@ -693,7 +854,7 @@
         cproj_share,
         dinner_share,
         douter_share,
-        small_share[:, 2:5],
+        gains_share[:, 2:5],
         tables_grad[1],
     )
 

time: 1010 us -> 899 us (0.89)
  waiting for transfers between devices: 320 us -> 87 us
  Pallas kernels: 143 us -> 276 us
  local copies, waits for them, and re-layouts: 157 us -> 281 us
  starting transfers between devices: 93.7 us -> 26.9 us
  blocking collectives: 40.9 us -> 0 us
  other arithmetic: 48.6 us -> 28.5 us
    ppermute x97 -> x32, waiting for transfers between devices: 320 us -> 87 us  [swap(): return lax.ppermute(value, axis, pairs)]
    pallas_call x0 -> x1, Pallas kernels: none -> 162 us  [reduce_chunks(): pl.pallas_call(functools.partial(reduce_kernel, links, chunks // 2), out_...]
    reshape x1 -> x40, local copies, waits for them, and re-layouts: 0.12 us -> 133 us  [the longest x26 125 us: fold_grad(): grad.astype(jnp.bfloat16).reshape(devices, deep, r, wide, 2, width // 2)]
    ppermute x97 -> x32, starting transfers between devices: 93.7 us -> 26.9 us  [swap(): return lax.ppermute(value, axis, pairs)]
    dynamic_slice x31 -> x0, local copies, waits for them, and re-layouts: 42.1 us -> none  [the longest x16 25.5 us: scatter(): mine = lax.dynamic_index_in_dim(current, side, spot, keepdims=False)]
    unnamed x1 -> x0, blocking collectives: 40.9 us -> none
    unnamed x333 -> x294, local copies, waits for them, and re-layouts: 36.8 us -> 58.2 us
    pallas_call x3, Pallas kernels: 86.2 us -> 69.7 us  [attend_backward(): pl.pallas_call(functools.partial(backward_kernel, spec), out_shape=[jax.S...]
  transfers between devices with their start and end apart: 97 -> 32, of which waited for: 58 -> 8; matrix products, arithmetic and copies ran while one was open for 24% -> 27% of each run, Pallas kernels for 6% -> 23%
where the time goes in v2:
time: 899 us; the launch traced here: 891 us
  local copies, waits for them, and re-layouts  281 us (31%)
  Pallas kernels  276 us (31%)
  matrix products  183 us (20%)
  waiting for transfers between devices  87 us (10%)
  other arithmetic  28.5 us (3%)
  starting transfers between devices  26.9 us (3%)
  between operations  9.44 us (1%)
    pallas_call x1, Pallas kernels, reduce_chunks(): pl.pallas_call(functools.partial(reduce_kernel, links, chunks // 2), out_...  162 us
    reshape x26, local copies, waits for them, and re-layouts, fold_grad(): grad.astype(jnp.bfloat16).reshape(devices, deep, r, wide, 2, width // 2)  125 us
    ppermute x32, waiting for transfers between devices, swap(): return lax.ppermute(value, axis, pairs)  87 us
    pallas_call x3, Pallas kernels, attend_backward(): pl.pallas_call(functools.partial(backward_kernel, spec), out_shape=[jax.S...  69.7 us
    unnamed x294, local copies, waits for them, and re-layouts  58.2 us
    dot_general x13, matrix products, product_transposed(): lax.dot_general(former, latter, (((1,), (1,)), ((), ())), preferred_eleme...  57.6 us
    dot_general x13, matrix products, transpose_product(): lax.dot_general(former, latter, (((0,), (0,)), ((), ())), preferred_eleme...  51.3 us
    dot_general x13, matrix products, product(): return jnp.dot(former, latter, preferred_element_type=jnp.float32)  45.4 us
  transfers between devices with their start and end apart: 32, of which 8 were waited for; matrix products, arithmetic and copies ran while one was open for 27% of the time, Pallas kernels for 23%

profile of v2, /device:TPU:0, one launch (start us, length us, event | category | flops | bytes accessed | tf_op | source)
XLA Modules:
  0.0 891.5 jit_solution(8712196330173875996)
XLA Ops:
  2.3 3.0 collective-permute-start
  64.1 2.8 broadcast.732.clone
  81.3 3.2 fusion.40
  84.4 4.0 fusion.37
  88.5 4.7 copy.255
  93.2 2.8 copy.196
  96.0 4.8 copy.256
  101.2 4.0 fusion.41
  105.3 3.4 fusion.43
  125.7 20.7 %collective-permute-done.13 = bf16[192,1536]{1,0:T(8,128)(2,1)S(1)} collective-permute-done((bf16[192,1536]{1,0:T(8,128)(2,1)S(1)}, bf16[192,1536]{1,0:T(8,128)(2,1)S(1)}, u32[]{:S(2)}, u32[]{:S(2)}) %collective-permute-start.13) | collective-permute-done | bytes 589856 | tf_op jit(solution)/shard_map/ppermute | solution.py:493
  148.5 10.6 %collective-permute-done.3 = bf16[192,1536]{1,0:T(8,128)(2,1)} collective-permute-done((bf16[192,1536]{1,0:T(8,128)(2,1)S(1)}, bf16[192,1536]{1,0:T(8,128)(2,1)}, u32[]{:S(2)}, u32[]{:S(2)}) %collective-permute-start.3) | collective-permute-done | bytes 589856 | tf_op jit(solution)/shard_map/ppermute | solution.py:493
  170.1 4.9 shard_map.383
  176.2 8.2 collective-permute-done.25
  184.4 25.3 %collective-permute-done.9 = bf16[768,768]{1,0:T(8,128)(2,1)} collective-permute-done((bf16[768,768]{1,0:T(8,128)(2,1)}, bf16[768,768]{1,0:T(8,128)(2,1)}, u32[]{:S(2)}, u32[]{:S(2)}) %collective-permute-start.9) | collective-permute-done | bytes 1179680 | tf_op jit(solution)/shard_map/ppermute | solution.py:493
  210.8 3.1 convolution_convert_fusion.5.k_ref.v_ref
  214.0 21.0 %collective-permute-done.23 = bf16[192,3072]{1,0:T(8,128)(2,1)} collective-permute-done((bf16[192,3072]{1,0:T(8,128)(2,1)S(1)}, bf16[192,3072]{1,0:T(8,128)(2,1)}, u32[]{:S(2)}, u32[]{:S(2)}) %collective-permute-start.23) | collective-permute-done | bytes 1179680 | tf_op jit(solution)/shard_map/ppermute | solution.py:493
  235.2 30.7 %shard_map.382 = (bf16[1024,768]{1,0:T(8,128)(2,1)S(1)}, f32[6,2,1024]{2,1,0:T(2,128)S(1)}) custom-call(s32[2,4]{1,0:T(2,128)S(1)} %pad_add_fusion.bounds_ref, bf16[1024,768]{1,0:T(8,128)(2,1)S(1)} %convolution_convert_fusion.11.q_ref, bf16[1024,1536]{1,0:T(8,128)(2,1)S(1)} %convolution_convert_fusion.5.k_ref.v_ref, ...), custom_call_target="tpu_custom_call" | custom-call | flops 12884901888 | bytes 8388608 | tf_op jit(solution)/shard_map/pallas_call | solution.py:321
  266.5 2.9 multiply_reduce_fusion.2
  283.2 10.8 %fusion.165 = f32[1024,3072]{1,0:T(8,128)} fusion(bf16[768,3072]{1,0:T(8,128)(2,1)} %constant_dynamic-update-slice_fusion.40, f32[1024,768]{0,1:T(8,128)S(1)} %get-tuple-element.182, f32[768]{0:T(1024)S(1)} %get-tuple-element.146, f32[1024]{0:T(1024)S(1)} %fusion.131), kind=kOutput, calls=%fused_computation.337 | convolution fusion | flops 4834197504 | bytes 20454400 | tf_op jit(solution)/shard_map/dot_general | solution.py:393
  296.4 10.3 %add_convert_fusion = bf16[1024,768]{0,1:T(8,128)(2,1)S(1)} fusion(f32[1024,768]{0,1:T(8,128)S(1)} %get-tuple-element.182, bf16[3072,768]{1,0:T(8,128)(2,1)} %constant_dynamic-update-slice_fusion.37, f32[1024,3072]{1,0:T(8,128)} %fusion.165), kind=kOutput, calls=%fused_computation.118 | convolution fusion | flops 4861722624 | bytes 22020096 | tf_op jit(solution)/shard_map/dot_general | solution.py:393
  306.8 5.2 convolution_convert_fusion.4.k_ref.v_ref
  312.0 8.6 shard_map.384
  325.3 5.3 fusion.91
  330.6 5.0 fusion.85
  338.0 15.3 %shard_map.385 = (bf16[256,768]{1,0:T(8,128)(2,1)S(1)}, bf16[1024,1536]{1,0:T(8,128)(2,1)S(1)}) custom-call(s32[2,1]{1,0:T(2,128)S(1)} %pad_add_fusion.2.bounds_ref, bf16[256,768]{1,0:T(8,128)(2,1)S(1)} %convolution_convert_fusion.20.q_ref, bf16[1024,1536]{1,0:T(8,128)(2,1)} %copy-done.4, bf16[1024,1536]{1,0:T(8,128)(2,1)} %copy-done.4, ...), custom_call_target="tpu_custom_call" | custom-call | flops 8053063680 | bytes 16777216 | tf_op jit(solution)/shard_map/pallas_call | solution.py:355
  360.8 8.0 shard_map.387
  373.7 4.4 convolution_convert_fusion.2
  378.2 4.0 convolution_convert_fusion.6
  382.2 5.9 fusion.90
  388.1 15.7 %fusion.6 = bf16[1024,3072]{1,0:T(8,128)(2,1)} fusion(f32[1024,3072]{1,0:T(8,128)} %fusion.165, bf16[1024,768]{0,1:T(8,128)(2,1)S(1)} %get-tuple-element.188, bf16[3072,768]{1,0:T(8,128)(2,1)} %constant_dynamic-update-slice_fusion.37), kind=kOutput, calls=%fused_computation.10 | convolution fusion | flops 4894752768 | bytes 25165824 | tf_op jit(solution)/shard_map/dot_general | solution.py:403
  403.8 13.2 %convolution_convert_fusion = bf16[3072,768]{1,0:T(8,128)(2,1)} fusion(bf16[1024,768]{0,1:T(8,128)(2,1)S(1)} %get-tuple-element.188, f32[1024,3072]{1,0:T(8,128)} %fusion.165), kind=kOutput, calls=%fused_computation.86 | convolution fusion | flops 4862509056 | bytes 18874368 | tf_op jit(solution)/shard_map/dot_general | solution.py:397
  417.1 9.8 %multiply_reduce_fusion = (f32[768]{0:T(1024)}, f32[1024]{0:T(1024)S(1)}, f32[1024,768]{0,1:T(8,128)S(1)}) fusion(f32[1024,768]{0,1:T(8,128)S(1)} %copy-done.15, f32[1024]{0:T(1024)S(1)} %fusion.131, f32[768]{0:T(1024)S(1)} %get-tuple-element.146, bf16[1024,3072]{1,0:T(8,128)(2,1)} %fusion.6, bf16[768,3072]{1,0:T(8,128)(2,1)} %constant_dynamic-update-slice_fusion.40), kind=kOutput, calls=%fused_computation.114 | convolution fusion | flops 4836554752 | bytes 17315840 | tf_op jit(solution)/shard_map/dot_general | solution.py:403
  426.8 7.2 convolution_convert_fusion.1
  439.2 46.4 %shard_map.386 = (bf16[1024,768]{1,0:T(8,128)(2,1)S(1)}, bf16[1024,1536]{1,0:T(8,128)(2,1)}, f32[12,5,128,128]{3,2,1,0:T(8,128)}) custom-call(s32[2,4]{1,0:T(2,128)S(1)} %pad_add_fusion.bounds_ref, bf16[1024,768]{1,0:T(8,128)(2,1)S(1)} %copy-done.7, bf16[1024,1536]{1,0:T(8,128)(2,1)} %copy-done.5, bf16[1024,1536]{1,0:T(8,128)(2,1)} %copy-done.5, ...), custom_call_target="tpu_custom_call" | custom-call | flops 32212254720 | bytes 16777216 | tf_op jit(solution)/shard_map/pallas_call | solution.py:355
  485.6 6.4 fusion.180
  492.1 4.2 convolution_convert_fusion.7
  496.3 3.7 convolution_convert_fusion.3
  504.9 11.6 %fusion.97 = f32[32,12]{1,0:T(8,128)} fusion(f32[12,5,128,128]{3,2,1,0:T(8,128)S(1)} %copy-done.122, s32[5]{0:T(128)S(1)} %copy-done.120), kind=kOutput, calls=%fused_computation.149 | convolution fusion | flops 511180800 | bytes 3933716 | tf_op jit(solution)/shard_map/dot_general | solution.py:54
  519.2 3.6 reshape.671
  525.2 3.6 reshape.672
  531.2 3.6 reshape.674
  537.2 3.6 reshape.669
  543.2 5.9 reshape.673
  549.1 3.5 copy.212
  552.6 5.9 reshape.670
  558.5 3.4 copy.209
  561.9 11.6 %reshape.667 = bf16[32,1,24,4,2,384]{5,4,3,2,0,1:T(2,128)(2,1)} reshape(bf16[768,3072]{1,0:T(8,128)(2,1)} %convolution_convert_fusion.1) | data formatting | bytes 9437184 | tf_op jit(solution)/shard_map/reshape | solution.py:642
  573.5 5.3 copy.206
  579.5 3.6 reshape.666
  585.5 10.2 %reshape.668 = bf16[32,4,24,1,2,384]{5,4,2,1,0,3:T(2,128)(2,1)} reshape(bf16[3072,768]{1,0:T(8,128)(2,1)} %convolution_convert_fusion) | data formatting | bytes 9437184 | tf_op jit(solution)/shard_map/reshape | solution.py:642
  595.8 5.5 copy.207
  601.3 9.6 %fusion.92 = f32[32,12]{1,0:T(8,128)} fusion(f32[12,5,128,128]{3,2,1,0:T(8,128)S(1)} %copy-done.126, s32[5]{0:T(128)S(1)} %copy-done.121), kind=kOutput, calls=%fused_computation.148 | convolution fusion | flops 456130560 | bytes 3933716 | tf_op jit(solution)/shard_map/dot_general | solution.py:54
  611.7 3.3 convolution_convert_fusion.17
  615.0 4.1 fusion.78
  619.1 3.8 reshape.664
  624.3 5.9 reshape.665
  630.3 3.5 copy.204
  635.9 11.6 %reshape.675 = bf16[32,1,24,4,2,384]{5,4,3,2,0,1:T(2,128)(2,1)} reshape(bf16[768,3072]{1,0:T(8,128)(2,1)} %convolution_convert_fusion.3) | data formatting | bytes 9437184 | tf_op jit(solution)/shard_map/reshape | solution.py:642
  647.5 3.3 copy.214
  659.6 2.9 constant_dynamic-update-slice_fusion.9
  675.3 2.7 constant_dynamic-update-slice_fusion.1
  678.0 10.3 %reshape.676 = bf16[32,4,24,1,2,384]{5,4,2,1,0,3:T(2,128)(2,1)} reshape(bf16[3072,768]{1,0:T(8,128)(2,1)} %convolution_convert_fusion.2) | data formatting | bytes 9437184 | tf_op jit(solution)/shard_map/reshape | solution.py:642
  688.3 3.1 copy.215
  694.2 161.9 %shard_map.388 = f32[28,48,384]{2,1,0:T(8,128)} custom-call(bf16[28,2,2,2,2,2,48,384]{7,6,5,4,3,2,1,0:T(8,128)(2,1)} %constant_dynamic-update-slice_fusion.g_ref), custom_call_target="tpu_custom_call" | custom-call | tf_op jit(solution)/shard_map/pallas_call | solution.py:618
  (534 shorter events, 225.4 us)
Async XLA Ops:
  0.7 34.9 %copy-start.11 = (bf16[256,768]{1,0:T(8,128)(2,1)S(1)}, bf16[256,768]{1,0:T(8,128)(2,1)}, u32[]{:S(2)}) copy-start(bf16[256,768]{1,0:T(8,128)(2,1)} %param.24) | copy-start | bytes 1179652
  2.3 98.5 %collective-permute-start = (bf16[384,6]{0,1:T(8,128)(2,1)S(1)}, bf16[384,6]{0,1:T(8,128)(2,1)S(1)}, u32[]{:S(2)}, u32[]{:S(2)}) collective-permute-start(bf16[384,6]{0,1:T(8,128)(2,1)S(1)} %pad_maximum_fusion.1), channel_id=1, source_target_pairs={{0,1},{1,0},{2,3},{3,2},{4,5},{5,4},{6,7},{7,6},{8,9},{9,8},{10,11... | collective-permute-start | bytes 13832 | tf_op jit(solution)/shard_map/ppermute | solution.py:493
  7.0 108.6 %collective-permute-start.21 = (bf16[192,768]{1,0:T(8,128)(2,1)}, bf16[192,768]{1,0:T(8,128)(2,1)}, u32[]{:S(2)}, u32[]{:S(2)}) collective-permute-start(bf16[192,768]{1,0:T(8,128)(2,1)} %constant_dynamic-slice_fusion.2), channel_id=1, source_target_pairs={{0,1},{1,0},{2,3},{3,2},{4,5},{5,4},{6,7},{7,6},{8,9},{9,8},{10,11... | collective-permute-start | bytes 884744 | tf_op jit(solution)/shard_map/ppermute | solution.py:493
  8.7 31.4 %copy-start.53 = (bf16[384,1536]{1,0:T(8,128)(2,1)S(1)}, bf16[384,1536]{1,0:T(8,128)(2,1)}, u32[]{:S(2)}) copy-start(bf16[384,1536]{1,0:T(8,128)(2,1)} %param.30) | copy-start | bytes 3538948
  8.7 114.9 %collective-permute-start.17 = (bf16[192,768]{1,0:T(8,128)(2,1)}, bf16[192,768]{1,0:T(8,128)(2,1)}, u32[]{:S(2)}, u32[]{:S(2)}) collective-permute-start(bf16[192,768]{1,0:T(8,128)(2,1)} %constant_dynamic-slice_fusion.4), channel_id=1, source_target_pairs={{0,1},{1,0},{2,3},{3,2},{4,5},{5,4},{6,7},{7,6},{8,9},{9,8},{10,11... | collective-permute-start | bytes 884744 | tf_op jit(solution)/shard_map/ppermute | solution.py:493
  12.4 99.0 %collective-permute-start.15 = (bf16[192,768]{1,0:T(8,128)(2,1)}, bf16[192,768]{1,0:T(8,128)(2,1)}, u32[]{:S(2)}, u32[]{:S(2)}) collective-permute-start(bf16[192,768]{1,0:T(8,128)(2,1)} %constant_dynamic-slice_fusion.5), channel_id=1, source_target_pairs={{0,1},{1,0},{2,3},{3,2},{4,5},{5,4},{6,7},{7,6},{8,9},{9,8},{10,11... | collective-permute-start | bytes 884744 | tf_op jit(solution)/shard_map/ppermute | solution.py:493
  14.2 26.8 %copy-start.51 = (bf16[384,1536]{1,0:T(8,128)(2,1)S(1)}, bf16[384,1536]{1,0:T(8,128)(2,1)}, u32[]{:S(2)}) copy-start(bf16[384,1536]{1,0:T(8,128)(2,1)} %param.37) | copy-start | bytes 3538948
  14.2 105.6 %collective-permute-start.11 = (bf16[192,768]{1,0:T(8,128)(2,1)}, bf16[192,768]{1,0:T(8,128)(2,1)}, u32[]{:S(2)}, u32[]{:S(2)}) collective-permute-start(bf16[192,768]{1,0:T(8,128)(2,1)} %constant_dynamic-slice_fusion.7), channel_id=1, source_target_pairs={{0,1},{1,0},{2,3},{3,2},{4,5},{5,4},{6,7},{7,6},{8,9},{9,8},{10,11... | collective-permute-start | bytes 884744 | tf_op jit(solution)/shard_map/ppermute | solution.py:493
  16.1 19.4 %copy-start.119 = (s32[5]{0:T(128)}, s32[5]{0:T(128)S(1)}, u32[]{:S(2)}) copy-start(s32[5]{0:T(128)S(1)} %add_multiply_fusion) | copy-start | bytes 64
  35.7 467.1 %copy-start.98 = (f32[256]{0:T(256)}, f32[256]{0:T(256)S(1)}, u32[]{:S(2)}) copy-start(f32[256]{0:T(256)S(1)} %fusion.136) | copy-start | bytes 3076
  57.3 209.2 %copy-start.12 = (bf16[1024,768]{0,1:T(8,128)(2,1)}, bf16[1024,768]{0,1:T(8,128)(2,1)S(1)}, u32[]{:S(2)}) copy-start(bf16[1024,768]{0,1:T(8,128)(2,1)S(1)} %copy.188) | copy-start | bytes 4718596
  57.7 153.1 %copy-start.103 = (f32[1024]{0:T(1024)}, f32[1024]{0:T(1024)S(1)}, u32[]{:S(2)}) copy-start(f32[1024]{0:T(1024)S(1)} %fusion.130) | copy-start | bytes 12292
  100.8 17.2 %collective-permute-start.1 = (bf16[192,768]{1,0:T(8,128)(2,1)S(1)}, bf16[192,768]{1,0:T(8,128)(2,1)}, u32[]{:S(2)}, u32[]{:S(2)}) collective-permute-start(bf16[192,768]{1,0:T(8,128)(2,1)S(1)} %copy-done.95), channel_id=1, source_target_pairs={{0,1},{1,0},{2,3},{3,2},{4,5},{5,4},{6,7},{7,6},{8,9},{9,8},{10,11... | collective-permute-start | bytes 884744 | tf_op jit(solution)/shard_map/ppermute | solution.py:493
  108.7 102.1 %copy-start.100 = (f32[768]{0:T(1024)}, f32[768]{0:T(1024)S(1)}, u32[]{:S(2)}) copy-start(f32[768]{0:T(1024)S(1)} %get-tuple-element.147) | copy-start | bytes 9220
  110.0 60.1 %copy-start = (f32[12,5,128,128]{3,2,1,0:T(8,128)}, f32[12,5,128,128]{3,2,1,0:T(8,128)S(1)}, u32[]{:S(2)}) copy-start(f32[12,5,128,128]{3,2,1,0:T(8,128)S(1)} %copy.195.rest_0_) | copy-start | bytes 11796484
  110.1 11.0 %copy-start.89 = (bf16[192,1536]{1,0:T(8,128)(2,1)S(1)}, bf16[192,1536]{1,0:T(8,128)(2,1)}, u32[]{:S(2)}) copy-start(bf16[192,1536]{1,0:T(8,128)(2,1)} %constant_dynamic-slice_fusion.12) | copy-start | bytes 1769476
  111.4 123.8 %copy-start.1 = (f32[12,5,128,128]{3,2,1,0:T(8,128)}, f32[12,5,128,128]{3,2,1,0:T(8,128)S(1)}, u32[]{:S(2)}) copy-start(f32[12,5,128,128]{3,2,1,0:T(8,128)S(1)} %copy.191.rest_0_) | copy-start | bytes 11796484
  111.4 35.0 %copy-start.58 = (bf16[768,1536]{1,0:T(8,128)(2,1)S(1)}, bf16[768,1536]{1,0:T(8,128)(2,1)}, u32[]{:S(2)}) copy-start(bf16[768,1536]{1,0:T(8,128)(2,1)} %copy-done.57) | copy-start | bytes 7077892
  111.4 9.7 %collective-permute-start.5 = (bf16[192,768]{1,0:T(8,128)(2,1)S(1)}, bf16[192,768]{1,0:T(8,128)(2,1)S(1)}, u32[]{:S(2)}, u32[]{:S(2)}) collective-permute-start(bf16[192,768]{1,0:T(8,128)(2,1)S(1)} %copy-done.94), channel_id=1, source_target_pairs={{0,1},{1,0},{2,3},{3,2},{4,5},{5,4},{6,7},{7,6},{8,9},{9,8},{10,11... | collective-permute-start | bytes 884744 | tf_op jit(solution)/shard_map/ppermute | solution.py:493
  115.6 44.6 %collective-permute-start.19 = (bf16[192,1536]{1,0:T(8,128)(2,1)S(1)}, bf16[192,1536]{1,0:T(8,128)(2,1)S(1)}, u32[]{:S(2)}, u32[]{:S(2)}) collective-permute-start(bf16[192,1536]{1,0:T(8,128)(2,1)S(1)} %copy-done.88), channel_id=1, source_target_pairs={{0,1},{1,0},{2,3},{3,2},{4,5},{5,4},{6,7},{7,6},{8,9},{9,8},{10,11... | collective-permute-start | bytes 1769480 | tf_op jit(solution)/shard_map/ppermute | solution.py:493
  118.0 28.4 %collective-permute-start.13 = (bf16[192,1536]{1,0:T(8,128)(2,1)S(1)}, bf16[192,1536]{1,0:T(8,128)(2,1)S(1)}, u32[]{:S(2)}, u32[]{:S(2)}) collective-permute-start(bf16[192,1536]{1,0:T(8,128)(2,1)S(1)} %copy-done.90), channel_id=1, source_target_pairs={{0,1},{1,0},{2,3},{3,2},{4,5},{5,4},{6,7},{7,6},{8,9},{9,8},{10,11... | collective-permute-start | bytes 1769480 | tf_op jit(solution)/shard_map/ppermute | solution.py:493
  119.8 5.8 collective-permute-start.2
  121.1 38.0 %collective-permute-start.3 = (bf16[192,1536]{1,0:T(8,128)(2,1)S(1)}, bf16[192,1536]{1,0:T(8,128)(2,1)}, u32[]{:S(2)}, u32[]{:S(2)}) collective-permute-start(bf16[192,1536]{1,0:T(8,128)(2,1)S(1)} %copy-done.89), channel_id=1, source_target_pairs={{0,1},{1,0},{2,3},{3,2},{4,5},{5,4},{6,7},{7,6},{8,9},{9,8},{10,11... | collective-permute-start | bytes 1769480 | tf_op jit(solution)/shard_map/ppermute | solution.py:493
  123.7 60.8 %collective-permute-start.25 = (bf16[768,768]{1,0:T(8,128)(2,1)}, bf16[768,768]{1,0:T(8,128)(2,1)}, u32[]{:S(2)}, u32[]{:S(2)}) collective-permute-start(bf16[768,768]{1,0:T(8,128)(2,1)} %constant_dynamic-slice_fusion), channel_id=1, source_target_pairs={{0,1},{1,0},{2,3},{3,2},{4,5},{5,4},{6,7},{7,6},{8,9},{9,8},{10,11... | collective-permute-start | bytes 3538952 | tf_op jit(solution)/shard_map/ppermute | solution.py:493
  125.6 36.1 %collective-permute-start.22 = (bf16[192,768]{1,0:T(8,128)(2,1)}, bf16[192,768]{1,0:T(8,128)(2,1)S(1)}, u32[]{:S(2)}, u32[]{:S(2)}) collective-permute-start(bf16[192,768]{1,0:T(8,128)(2,1)} %collective-permute-done.21), channel_id=1, source_target_pairs={{0,2},{2,0},{4,6},{6,4},{8,10},{10,8},{12,14},{14,12},{16,18},{18,... | collective-permute-start | bytes 884744 | tf_op jit(solution)/shard_map/ppermute | solution.py:493
  125.6 22.8 %copy-start.83 = (bf16[768,768]{1,0:T(8,128)(2,1)}, bf16[768,768]{1,0:T(8,128)(2,1)S(1)}, u32[]{:S(2)}) copy-start(bf16[768,768]{1,0:T(8,128)(2,1)S(1)} %constant_dynamic-update-slice_fusion.49) | copy-start | bytes 3538948
  146.4 17.1 %collective-permute-start.16 = (bf16[192,768]{1,0:T(8,128)(2,1)}, bf16[192,768]{1,0:T(8,128)(2,1)S(1)}, u32[]{:S(2)}, u32[]{:S(2)}) collective-permute-start(bf16[192,768]{1,0:T(8,128)(2,1)} %collective-permute-done.15), channel_id=1, source_target_pairs={{0,2},{2,0},{4,6},{6,4},{8,10},{10,8},{12,14},{14,12},{16,18},{18,... | collective-permute-start | bytes 884744 | tf_op jit(solution)/shard_map/ppermute | solution.py:493
  146.4 12.7 %copy-start.61 = (bf16[768,1536]{1,0:T(8,128)(2,1)S(1)}, bf16[768,1536]{1,0:T(8,128)(2,1)}, u32[]{:S(2)}) copy-start(bf16[768,1536]{1,0:T(8,128)(2,1)} %copy-done.60) | copy-start | bytes 7077892
  146.5 17.1 %copy-start.78 = (bf16[192,3072]{1,0:T(8,128)(2,1)S(1)}, bf16[192,3072]{1,0:T(8,128)(2,1)}, u32[]{:S(2)}) copy-start(bf16[192,3072]{1,0:T(8,128)(2,1)} %constant_dynamic-slice_fusion.1) | copy-start | bytes 3538948
  148.5 86.7 %copy-start.6 = (bf16[1024,768]{1,0:T(8,128)(2,1)}, bf16[1024,768]{1,0:T(8,128)(2,1)S(1)}, u32[]{:S(2)}) copy-start(bf16[1024,768]{1,0:T(8,128)(2,1)S(1)} %convolution_convert_fusion.11.q_ref) | copy-start | bytes 4718596
  159.1 4.7 collective-permute-start.12
  160.3 3.7 collective-permute-start.6
  161.7 48.0 %collective-permute-start.9 = (bf16[768,768]{1,0:T(8,128)(2,1)}, bf16[768,768]{1,0:T(8,128)(2,1)}, u32[]{:S(2)}, u32[]{:S(2)}) collective-permute-start(bf16[768,768]{1,0:T(8,128)(2,1)} %constant_dynamic-slice_fusion.8), channel_id=1, source_target_pairs={{0,1},{1,0},{2,3},{3,2},{4,5},{5,4},{6,7},{7,6},{8,9},{9,8},{10,11... | collective-permute-start | bytes 3538952 | tf_op jit(solution)/shard_map/ppermute | solution.py:493
  163.5 71.5 %collective-permute-start.23 = (bf16[192,3072]{1,0:T(8,128)(2,1)S(1)}, bf16[192,3072]{1,0:T(8,128)(2,1)}, u32[]{:S(2)}, u32[]{:S(2)}) collective-permute-start(bf16[192,3072]{1,0:T(8,128)(2,1)S(1)} %copy-done.78), channel_id=1, source_target_pairs={{0,1},{1,0},{2,3},{3,2},{4,5},{5,4},{6,7},{7,6},{8,9},{9,8},{10,11... | collective-permute-start | bytes 3538952 | tf_op jit(solution)/shard_map/ppermute | solution.py:493
  163.8 11.2 %copy-start.21 = (bf16[768,768]{1,0:T(8,128)(2,1)}, bf16[768,768]{1,0:T(8,128)(2,1)S(1)}, u32[]{:S(2)}) copy-start(bf16[768,768]{1,0:T(8,128)(2,1)S(1)} %get-tuple-element.197) | copy-start | bytes 3538948
  163.8 5.2 collective-permute-start.14
  163.9 2.6 collective-permute-start.18
  166.5 99.4 %collective-permute-start.7 = (bf16[192,3072]{1,0:T(8,128)(2,1)}, bf16[192,3072]{1,0:T(8,128)(2,1)}, u32[]{:S(2)}, u32[]{:S(2)}) collective-permute-start(bf16[192,3072]{1,0:T(8,128)(2,1)} %constant_dynamic-slice_fusion.9), channel_id=1, source_target_pairs={{0,1},{1,0},{2,3},{3,2},{4,5},{5,4},{6,7},{7,6},{8,9},{9,8},{10,11... | collective-permute-start | bytes 3538952 | tf_op jit(solution)/shard_map/ppermute | solution.py:493
  169.1 6.5 collective-permute-start.4
  175.6 145.1 %copy-start.9 = (f32[256,768]{1,0:T(8,128)}, f32[256,768]{1,0:T(8,128)S(1)}, u32[]{:S(2)}) copy-start(f32[256,768]{1,0:T(8,128)S(1)} %get-tuple-element.184) | copy-start | bytes 2359300
  175.6 93.8 %collective-permute-start.20 = (bf16[192,1536]{1,0:T(8,128)(2,1)S(1)}, bf16[192,1536]{1,0:T(8,128)(2,1)S(1)}, u32[]{:S(2)}, u32[]{:S(2)}) collective-permute-start(bf16[192,1536]{1,0:T(8,128)(2,1)S(1)} %collective-permute-done.19), channel_id=1, source_target_pairs={{0,2},{2,0},{4,6},{6,4},{8,10},{10,8},{12,14},{14,12},{16,18},{18,... | collective-permute-start | bytes 1769480 | tf_op jit(solution)/shard_map/ppermute | solution.py:493
  184.4 139.7 %collective-permute-start.26 = (bf16[768,768]{1,0:T(8,128)(2,1)}, bf16[768,768]{1,0:T(8,128)(2,1)S(1)}, u32[]{:S(2)}, u32[]{:S(2)}) collective-permute-start(bf16[768,768]{1,0:T(8,128)(2,1)} %collective-permute-done.25), channel_id=1, source_target_pairs={{0,2},{2,0},{4,6},{6,4},{8,10},{10,8},{12,14},{14,12},{16,18},{18,... | collective-permute-start | bytes 3538952 | tf_op jit(solution)/shard_map/ppermute | solution.py:493
  209.7 84.3 %collective-permute-start.10 = (bf16[768,768]{1,0:T(8,128)(2,1)}, bf16[768,768]{1,0:T(8,128)(2,1)}, u32[]{:S(2)}, u32[]{:S(2)}) collective-permute-start(bf16[768,768]{1,0:T(8,128)(2,1)} %collective-permute-done.9), channel_id=1, source_target_pairs={{0,2},{2,0},{4,6},{6,4},{8,10},{10,8},{12,14},{14,12},{16,18},{18,... | collective-permute-start | bytes 3538952 | tf_op jit(solution)/shard_map/ppermute | solution.py:493
  210.8 55.1 %copy-start.62 = (bf16[768,1536]{1,0:T(8,128)(2,1)}, bf16[768,1536]{1,0:T(8,128)(2,1)S(1)}, u32[]{:S(2)}) copy-start(bf16[768,1536]{1,0:T(8,128)(2,1)S(1)} %constant_dynamic-update-slice_fusion.46) | copy-start | bytes 7077892
  210.8 24.1 %copy-start.2 = (s32[1024]{0:T(1024)S(1)}, s32[1024]{0:T(1024)}, u32[]{:S(2)}) copy-start(s32[1024]{0:T(1024)} %param.25) | copy-start | bytes 12292
  214.0 51.9 %copy-start.5 = (bf16[1024,1536]{1,0:T(8,128)(2,1)}, bf16[1024,1536]{1,0:T(8,128)(2,1)S(1)}, u32[]{:S(2)}) copy-start(bf16[1024,1536]{1,0:T(8,128)(2,1)S(1)} %convolution_convert_fusion.5.k_ref.v_ref) | copy-start | bytes 9437188
  235.0 86.3 %collective-permute-start.24 = (bf16[192,3072]{1,0:T(8,128)(2,1)}, bf16[192,3072]{1,0:T(8,128)(2,1)}, u32[]{:S(2)}, u32[]{:S(2)}) collective-permute-start(bf16[192,3072]{1,0:T(8,128)(2,1)} %collective-permute-done.23), channel_id=1, source_target_pairs={{0,2},{2,0},{4,6},{6,4},{8,10},{10,8},{12,14},{14,12},{16,18},{18,... | collective-permute-start | bytes 3538952 | tf_op jit(solution)/shard_map/ppermute | solution.py:493
  265.9 16.1 %collective-permute-start.8 = (bf16[192,3072]{1,0:T(8,128)(2,1)}, bf16[192,3072]{1,0:T(8,128)(2,1)S(1)}, u32[]{:S(2)}, u32[]{:S(2)}) collective-permute-start(bf16[192,3072]{1,0:T(8,128)(2,1)} %collective-permute-done.7), channel_id=1, source_target_pairs={{0,2},{2,0},{4,6},{6,4},{8,10},{10,8},{12,14},{14,12},{16,18},{18,... | collective-permute-start | bytes 3538952 | tf_op jit(solution)/shard_map/ppermute | solution.py:493
  269.4 27.0 %copy-start.14 = (f32[1024,768]{0,1:T(8,128)}, f32[1024,768]{0,1:T(8,128)S(1)}, u32[]{:S(2)}) copy-start(f32[1024,768]{0,1:T(8,128)S(1)} %get-tuple-element.182) | copy-start | bytes 9437188
  306.8 71.4 %copy-start.66 = (bf16[1024,768]{0,1:T(8,128)(2,1)}, bf16[1024,768]{0,1:T(8,128)(2,1)S(1)}, u32[]{:S(2)}) copy-start(bf16[1024,768]{0,1:T(8,128)(2,1)S(1)} %add_convert_fusion) | copy-start | bytes 4718596
  306.8 14.4 %slice-start = ((s8[4718592]{0:T(1024)(128)(4,1)}), s8[4194304]{0:T(1024)(128)(4,1)S(1)}, s32[]{:S(2)}) async-start(s8[4718592]{0:T(1024)(128)(4,1)} %bitcast.232), calls=%async_computation | async-start | bytes 8388608
  338.0 15.3 %copy-start.10 = (f32[256,768]{1,0:T(8,128)S(1)}, f32[256,768]{1,0:T(8,128)}, u32[]{:S(2)}) copy-start(f32[256,768]{1,0:T(8,128)} %copy-done.9) | copy-start | bytes 2359300
  403.8 13.2 %copy-start.15 = (f32[1024,768]{0,1:T(8,128)S(1)}, f32[1024,768]{0,1:T(8,128)}, u32[]{:S(2)}) copy-start(f32[1024,768]{0,1:T(8,128)} %copy-done.14) | copy-start | bytes 9437188
  439.2 46.4 %copy-start.63 = (bf16[768,1536]{1,0:T(8,128)(2,1)S(1)}, bf16[768,1536]{1,0:T(8,128)(2,1)}, u32[]{:S(2)}) copy-start(bf16[768,1536]{1,0:T(8,128)(2,1)} %copy-done.62) | copy-start | bytes 7077892
  634.0 57.5 %collective-permute-start.27 = (f32[36,128]{1,0:T(8,128)S(1)}, f32[36,128]{1,0:T(8,128)S(1)}, u32[]{:S(2)}, u32[]{:S(2)}) collective-permute-start(f32[36,128]{1,0:T(8,128)S(1)} %maximum_bitcast_fusion), channel_id=1, source_target_pairs={{0,1},{1,0},{2,3},{3,2},{4,5},{5,4},{6,7},{7,6},{8,9},{9,8},{10,11... | collective-permute-start | bytes 55304 | tf_op jit(solution)/shard_map/ppermute | solution.py:493
  691.5 164.6 %collective-permute-start.28 = (f32[36,128]{1,0:T(8,128)S(1)}, f32[36,128]{1,0:T(8,128)S(1)}, u32[]{:S(2)}, u32[]{:S(2)}) collective-permute-start(f32[36,128]{1,0:T(8,128)S(1)} %fusion.163), channel_id=1, source_target_pairs={{0,2},{2,0},{4,6},{6,4},{8,10},{10,8},{12,14},{14,12},{16,18},{18,... | collective-permute-start | bytes 55304 | tf_op jit(solution)/shard_map/ppermute | solution.py:493
  856.1 13.8 %copy-start.16 = (f32[1024,768]{0,1:T(8,128)S(1)}, f32[1024,768]{0,1:T(8,128)}, u32[]{:S(2)}) copy-start(f32[1024,768]{0,1:T(8,128)} %fusion.87) | copy-start | bytes 9437188
  856.1 4.2 collective-permute-start.29
  860.4 3.8 collective-permute-start.30
  864.2 24.2 %collective-permute-start.31 = (f32[36,128]{1,0:T(8,128)S(1)}, f32[36,128]{1,0:T(8,128)S(1)}, u32[]{:S(2)}, u32[]{:S(2)}) collective-permute-start(f32[36,128]{1,0:T(8,128)S(1)} %add.576), channel_id=1, source_target_pairs={{0,16},{2,18},{4,20},{6,22},{8,24},{10,26},{12,28},{14,30},{16,0},... | collective-permute-start | bytes 55304 | tf_op jit(solution)/shard_map/ppermute | solution.py:493
  872.2 11.6 %copy-start.87 = (f32[2,48,384]{2,1,0:T(8,128)S(1)}, f32[2,48,384]{2,1,0:T(8,128)}, u32[]{:S(2)}) copy-start(f32[2,48,384]{2,1,0:T(8,128)} %get-tuple-element.166) | copy-start | bytes 442372
  872.2 12.4 %copy-start.86 = (f32[2,48,384]{2,1,0:T(8,128)S(1)}, f32[2,48,384]{2,1,0:T(8,128)}, u32[]{:S(2)}) copy-start(f32[2,48,384]{2,1,0:T(8,128)} %get-tuple-element.167) | copy-start | bytes 442372
  872.2 13.3 %copy-start.85 = (f32[2,48,384]{2,1,0:T(8,128)S(1)}, f32[2,48,384]{2,1,0:T(8,128)}, u32[]{:S(2)}) copy-start(f32[2,48,384]{2,1,0:T(8,128)} %get-tuple-element.168) | copy-start | bytes 442372
  872.2 14.2 %copy-start.76 = (f32[4,48,384]{2,1,0:T(8,128)S(1)}, f32[4,48,384]{2,1,0:T(8,128)}, u32[]{:S(2)}) copy-start(f32[4,48,384]{2,1,0:T(8,128)} %get-tuple-element.158) | copy-start | bytes 884740
  (101 other events, 414.1 us)

commit v3 on v2

--- a/solution.py
+++ b/solution.py
@@ -3,6 +3,7 @@
 
 import jax
 import jax.numpy as jnp
+import numpy as np
 from jax import lax
 from jax.experimental import pallas as pl
 from jax.experimental.pallas import tpu as pltpu
@@ -18,42 +19,66 @@
 ENC_EDGES = (12, 16, 23, 32, 46, 64, 91)
 DEC_EDGES = tuple((math.ceil(16 * 2 ** (3 * power / 16)) for power in range(1, 16)))
 PADDING_LABEL = 1 << 20
+SPAN = 2 * TILE
+FOLD = 8
+LAG = 2
+DELAY = 2
+HOLD = DELAY + 1
+OFFLOADED = ("dinner", "douter")
+NAMES = (
+    "equery",
+    "ekeyval",
+    "eproj",
+    "einner",
+    "eouter",
+    "dquery",
+    "dkeyval",
+    "dproj",
+    "cquery",
+    "ckeyval",
+    "cproj",
+    "dinner",
+    "douter",
+)
 
 
 def encoder_bucket(distance):
-    reach = jnp.abs(distance)
-    farther = 8 + sum(((reach >= threshold).astype(jnp.int32) for threshold in ENC_EDGES))
-    return jnp.where(reach < 8, reach, farther) + 16 * (distance < 0).astype(jnp.int32)
+    reach = np.abs(distance)
+    farther = 8 + sum((reach >= threshold).astype(np.int32) for threshold in ENC_EDGES)
+    return np.where(reach < 8, reach, farther) + 16 * (distance < 0).astype(np.int32)
 
 
 def decoder_bucket(distance):
-    ahead = jnp.maximum(distance, 0)
-    farther = 16 + sum(((ahead >= threshold).astype(jnp.int32) for threshold in DEC_EDGES))
-    return jnp.where(ahead < 16, ahead, farther)
-
-
-def band_onehot(bucket_of):
-    shape = (NB, BAND, TILE, TILE)
-    step = lax.broadcasted_iota(jnp.int32, shape, 1) - 2
-    key = lax.broadcasted_iota(jnp.int32, shape, 2)
-    query = lax.broadcasted_iota(jnp.int32, shape, 3)
-    bucket = bucket_of(step * TILE + query - key)
-    return (bucket == lax.broadcasted_iota(jnp.int32, shape, 0)).reshape(NB, BAND * TILE * TILE)
+    ahead = np.maximum(distance, 0)
+    farther = 16 + sum((ahead >= threshold).astype(np.int32) for threshold in DEC_EDGES)
+    return np.where(ahead < 16, ahead, farther)
+
+
+def band_distances(rows):
+    step = np.arange(BAND)[:, None, None] - 2
+    row = np.arange(rows)[None, :, None]
+    lane = np.arange(SPAN)[None, None, :]
+    lane = np.where(lane < TILE, lane, lane - SPAN)
+    return step * TILE + lane - row
+
+
+def bucket_onehot(bucket_of, rows, dtype):
+    bucket = jnp.asarray(bucket_of(band_distances(rows)).reshape(1, -1), jnp.int32)
+    return (bucket == lax.broadcasted_iota(jnp.int32, (NB, 1), 0)).astype(dtype)
 
 
 def band_bias(table, bucket_of):
-    onehot = band_onehot(bucket_of).astype(jnp.bfloat16)
+    onehot = bucket_onehot(bucket_of, 1, jnp.bfloat16)
     flat = lax.dot_general(
         table, onehot, (((0,), (0,)), ((), ())), preferred_element_type=jnp.float32
     )
-    return flat.reshape(H, BAND, TILE, TILE)
+    return flat.reshape(H, BAND, SPAN)
 
 
 def band_table_grad(band, bucket_of):
-    onehot = band_onehot(bucket_of).astype(jnp.float32)
     return lax.dot_general(
-        onehot,
-        band.reshape(H, BAND * TILE * TILE),
+        bucket_onehot(bucket_of, FOLD, jnp.float32),
+        band.reshape(H, BAND * FOLD * SPAN),
         (((1,), (1,)), ((), ())),
         precision=lax.Precision.HIGHEST,
         preferred_element_type=jnp.float32,
@@ -88,6 +113,30 @@
 
 def band_index(query_tile, key_tile):
     return jnp.clip(query_tile - key_tile, -2, 2) + 2
+
+
+def spread_bias(bias_ref, tiles_ref):
+    for head in range(tiles_ref.shape[0]):
+        for step in range(BAND):
+            row = bias_ref[head, step : step + 1, :]
+            if step in (0, BAND - 1):
+                tiles_ref[head, step] = jnp.broadcast_to(row[:, :TILE], (TILE, TILE))
+            else:
+                wide = jnp.broadcast_to(row, (TILE, SPAN))
+                wide = pltpu.roll(wide, 0, 1, stride=1, stride_axis=0)
+                tiles_ref[head, step] = wide[:, :TILE]
+
+
+def gather_diagonals(tiles_ref, band_ref):
+    for head in range(tiles_ref.shape[0]):
+        for step in range(BAND):
+            tile = tiles_ref[head, step]
+            tile = jnp.concatenate([tile, jnp.zeros_like(tile)], axis=1)
+            rows = TILE
+            while rows > FOLD:
+                rows //= 2
+                tile = tile[:rows] + pltpu.roll(tile[rows:], SPAN - rows, 1)
+            band_ref[head, step] = tile
 
 
 def tile_mask(spec, key_tile, query_block, segk_ref, segq_ref):
@@ -142,7 +191,8 @@
 
 def forward_kernel(spec, bounds_ref, q_ref, k_ref, v_ref, segq_ref, segk_ref, *rest):
     bias_ref, rest = (rest[0], rest[1:]) if spec["bias"] else (None, rest)
-    o_ref, lse_ref, score_ref, vt_ref = rest
+    o_ref, lse_ref, score_ref, vt_ref, rest = *rest[:4], rest[4:]
+    tiles_ref = rest[0] if spec["bias"] else None
     kb, qb, pairs = spec["kb"], spec["qb"], spec["pairs"]
     block = pl.program_id(1)
 
@@ -151,6 +201,8 @@
         for pair in range(pairs):
             span = slice(pair * 2 * HD, (pair + 1) * 2 * HD)
             vt_ref[span, :] = flip(v_ref[:, span]).astype(jnp.bfloat16)
+        if spec["bias"]:
+            spread_bias(bias_ref, tiles_ref)
 
     def run(first, count):
         starts = [(first + tile) * kb for tile in range(count)]
@@ -166,7 +218,7 @@
                 for tile in range(count):
                     s = dot_rows(k_ref[pl.ds(starts[tile], kb), span], parts[head])
                     if spec["bias"]:
-                        s = s + tile_bias(spec, number, first + tile, block, bias_ref)
+                        s = s + tile_bias(spec, number, first + tile, block, tiles_ref)
                     mask = tile_mask(spec, first + tile, block, segk_ref, segq_ref)
                     s = jnp.where(mask, s, MASKED)
                     score_ref[number, tile] = s
@@ -201,7 +253,8 @@
     bias_ref, rest = (rest[0], rest[1:]) if spec["bias"] else (None, rest)
     dq_ref, dkv_ref, rest = rest[0], rest[1], rest[2:]
     band_ref, rest = (rest[0], rest[1:]) if spec["bias"] else (None, rest)
-    p_ref, dp_ref, dk_ref, dv_ref, kt_ref = rest
+    p_ref, dp_ref, dk_ref, dv_ref, kt_ref, rest = *rest[:5], rest[5:]
+    tiles_ref, dtiles_ref = rest if spec["bias"] else (None, None)
     kb, qb, pairs = spec["kb"], spec["qb"], spec["pairs"]
     group, block = pl.program_id(0), pl.program_id(1)
 
@@ -213,7 +266,8 @@
         dk_ref[...] = jnp.zeros_like(dk_ref)
         dv_ref[...] = jnp.zeros_like(dv_ref)
         if spec["bias"]:
-            band_ref[...] = jnp.zeros_like(band_ref)
+            spread_bias(bias_ref, tiles_ref)
+            dtiles_ref[...] = jnp.zeros_like(dtiles_ref)
 
     def run(first, count):
         starts = [(first + tile) * kb for tile in range(count)]
@@ -224,7 +278,9 @@
             parts = head_parts(q_ref[:, span])
             dparts = head_parts(do_ref[:, span])
             lse = lse_ref[pair]
-            dquery = []
+            stacked = jnp.concatenate(parts, axis=0)
+            dstacked = jnp.concatenate(dparts, axis=0)
+            deltas = []
             for head in range(2):
                 number = 2 * pair + head
                 delta = None
@@ -232,7 +288,7 @@
                     here = pl.ds(starts[tile], kb)
                     s = dot_rows(k_ref[here, span], parts[head])
                     if spec["bias"]:
-                        s = s + tile_bias(spec, number, first + tile, block, bias_ref)
+                        s = s + tile_bias(spec, number, first + tile, block, tiles_ref)
                     mask = tile_mask(spec, first + tile, block, segk_ref, segq_ref)
                     p = jnp.exp(jnp.where(mask, s, MASKED) - lse[head : head + 1])
                     dp = dot_rows(v_ref[here, span], dparts[head])
@@ -240,12 +296,15 @@
                     dp_ref[number, tile] = dp
                     part = fold_rows(p * dp, jnp.add)
                     delta = part if delta is None else delta + part
-                    dv_ref[here, span] += dot_plain(p.astype(jnp.bfloat16), dparts[head])
-                delta = jnp.sum(delta, axis=0, keepdims=True)
-                mix = None
-                for tile in range(count):
-                    here = pl.ds(starts[tile], kb)
-                    ds = p_ref[number, tile] * (dp_ref[number, tile] - delta)
+                deltas.append(jnp.sum(delta, axis=0, keepdims=True))
+            dquery = [None, None]
+            for tile in range(count):
+                here = pl.ds(starts[tile], kb)
+                weights, lows = [], []
+                for head in range(2):
+                    number = 2 * pair + head
+                    p = p_ref[number, tile]
+                    ds = p * (dp_ref[number, tile] - deltas[head])
                     if spec["bias"]:
                         rows, lanes = kb // TILE, qb // TILE
                         for row in range(rows):
@@ -253,16 +312,18 @@
                                 index = band_index(
                                     block * lanes + lane, (first + tile) * rows + row
                                 )
-                                band_ref[number, index] += ds[
+                                dtiles_ref[number, index] += ds[
                                     row * TILE : (row + 1) * TILE,
                                     lane * TILE : (lane + 1) * TILE,
                                 ]
                     low = ds.astype(jnp.bfloat16)
-                    dk_ref[here, span] += dot_plain(low, parts[head])
+                    weights.append(p.astype(jnp.bfloat16))
+                    lows.append(low)
                     rows = slice(number * HD, (number + 1) * HD)
                     part = dot_plain(kt_ref[rows, here], low)
-                    mix = part if mix is None else mix + part
-                dquery.append(mix)
+                    dquery[head] = part if tile == 0 else dquery[head] + part
+                dv_ref[here, span] += dot_plain(jnp.concatenate(weights, axis=1), dstacked)
+                dk_ref[here, span] += dot_plain(jnp.concatenate(lows, axis=1), stacked)
             dq_ref[:, span] = flip(jnp.concatenate(dquery, axis=0)).astype(jnp.bfloat16)
 
     for_counts(spec, bounds_ref[0, block], bounds_ref[1, block], run)
@@ -274,13 +335,15 @@
         dkv_ref[:, pl.ds(column, width)] = dk_ref[...].astype(jnp.bfloat16)
         column = pl.multiple_of((pl.num_programs(0) + group) * width, width)
         dkv_ref[:, pl.ds(column, width)] = dv_ref[...].astype(jnp.bfloat16)
-
-
-def attention_setup(queries, keyval, query_labels, key_labels, bias, causal):
+        if spec["bias"]:
+            gather_diagonals(dtiles_ref, band_ref)
+
+
+def attention_setup(queries, keyval, query_labels, key_labels, bias, causal, pairs):
     rows, keys = queries.shape[0], keyval.shape[0]
     qb, kb = min(256, rows), min(256, keys)
     skip = rows > qb
-    pairs = 1 if skip else 3
+    pairs = pairs if skip else 3
     spec = dict(
         qb=qb,
         kb=kb,
@@ -290,7 +353,9 @@
         tiles=keys // kb,
         skip=skip,
     )
-    bounds = key_bounds(query_labels, key_labels, qb, kb)
+    bounds = jnp.zeros((2, 1), jnp.int32)
+    if skip:
+        bounds = key_bounds(query_labels, key_labels, qb, kb)
     segq = query_labels[None, :]
     segk = jnp.broadcast_to(key_labels[:, None], (keys, TILE))
     groups = H // 2 // pairs
@@ -302,8 +367,9 @@
         segq=pl.BlockSpec((1, qb), lambda group, block, bounds: (0, block)),
         segk=pl.BlockSpec((keys, TILE), lambda group, block, bounds: (0, 0)),
         lse=pl.BlockSpec((pairs, 2, qb), lambda group, block, bounds: (group, 0, block)),
+        bias=pl.BlockSpec((2 * pairs, BAND, SPAN), lambda group, block, bounds: (group, 0, 0)),
         band=pl.BlockSpec(
-            (2 * pairs, BAND, TILE, TILE), lambda group, block, bounds: (group, 0, 0, 0)
+            (2 * pairs, BAND, FOLD, SPAN), lambda group, block, bounds: (group, 0, 0, 0)
         ),
         whole=pl.BlockSpec((keys, 2 * H * HD), lambda group, block, bounds: (0, 0)),
     )
@@ -313,11 +379,12 @@
 
 def attend_forward(queries, keyval, query_labels, key_labels, bias, causal):
     spec, bounds, segq, segk, specs, grid, scores = attention_setup(
-        queries, keyval, query_labels, key_labels, bias, causal
+        queries, keyval, query_labels, key_labels, bias, causal, 2
     )
     rows, keys = queries.shape[0], keyval.shape[0]
     work = H * rows * keys
-    extra = ([specs["band"]], [bias]) if bias is not None else ([], [])
+    extra = ([specs["bias"]], [bias]) if bias is not None else ([], [])
+    tiles = [pltpu.VMEM((2 * spec["pairs"], BAND, TILE, TILE), jnp.float32)] * len(extra[0])
     return pl.pallas_call(
         functools.partial(forward_kernel, spec),
         out_shape=(
@@ -333,7 +400,8 @@
             scratch_shapes=[
                 scores,
                 pltpu.VMEM((2 * HD * spec["pairs"], keys), jnp.bfloat16),
-            ],
+            ]
+            + tiles,
         ),
         compiler_params=pltpu.CompilerParams(vmem_limit_bytes=40 << 20),
         cost_estimate=pl.CostEstimate(
@@ -344,13 +412,14 @@
 
 def attend_backward(queries, keyval, query_labels, key_labels, bias, causal, lse, dmixture):
     spec, bounds, segq, segk, specs, grid, scores = attention_setup(
-        queries, keyval, query_labels, key_labels, bias, causal
+        queries, keyval, query_labels, key_labels, bias, causal, 1
     )
     rows, keys = queries.shape[0], keyval.shape[0]
     work = H * rows * keys
-    extra = ([specs["band"]], [bias]) if bias is not None else ([], [])
+    extra = ([specs["bias"]], [bias]) if bias is not None else ([], [])
+    tiles = [pltpu.VMEM((2 * spec["pairs"], BAND, TILE, TILE), jnp.float32)] * len(extra[0])
     band = (
-        [jax.ShapeDtypeStruct((H, BAND, TILE, TILE), jnp.float32)] if bias is not None else []
+        [jax.ShapeDtypeStruct((H, BAND, FOLD, SPAN), jnp.float32)] if bias is not None else []
     )
     out = pl.pallas_call(
         functools.partial(backward_kernel, spec),
@@ -372,14 +441,16 @@
                 specs["segk"],
             ]
             + extra[0],
-            out_specs=[specs["q"], specs["whole"]] + extra[0],
+            out_specs=[specs["q"], specs["whole"]] + [specs["band"]] * len(band),
             scratch_shapes=[
                 scores,
                 scores,
                 pltpu.VMEM((keys, 2 * HD * spec["pairs"]), jnp.float32),
                 pltpu.VMEM((keys, 2 * HD * spec["pairs"]), jnp.float32),
                 pltpu.VMEM((2 * HD * spec["pairs"], keys), jnp.bfloat16),
-            ],
+            ]
+            + tiles
+            + tiles,
         ),
         compiler_params=pltpu.CompilerParams(vmem_limit_bytes=48 << 20),
         cost_estimate=pl.CostEstimate(
@@ -429,22 +500,24 @@
     return (stream + product(mixture, wproj), (normed, queries, keyval, mixture, logsum))
 
 
-def attention_backward(stream, norm_gain, wquery, wkeyval, wproj, layout, memory, stored, gradient):
+def attention_backward(
+    grads, names, stream, norm_gain, wquery, wkeyval, wproj, layout, memory, stored, gradient
+):
     normed, queries, keyval, mixture, logsum = stored
     gradient_low = gradient.astype(jnp.bfloat16)
-    project_grad = transpose_product(mixture, gradient_low)
+    grads.add(names[2], mixture, gradient_low)
     dmixture = product_transposed(gradient_low, wproj).astype(jnp.bfloat16)
     dquery_low, dkeyval_low, band = attend_backward(queries, keyval, *layout, logsum, dmixture)
     source = normed if memory is None else memory
-    query_grad = transpose_product(normed, dquery_low)
-    keyval_grad = transpose_product(source, dkeyval_low)
+    grads.add(names[0], normed, dquery_low)
+    grads.add(names[1], source, dkeyval_low)
     dnormed = product_transposed(dquery_low, wquery)
     dsource = product_transposed(dkeyval_low, wkeyval)
     if memory is None:
         dnormed = dnormed + dsource
         dsource = None
     dstream, dgain = norm_backward(stream, norm_gain, dnormed)
-    return (gradient + dstream, dgain, query_grad, keyval_grad, project_grad, band, dsource)
+    return (gradient + dstream, dgain, band, dsource)
 
 
 def feed_forward(stream, norm_gain, winner, wouter):
@@ -454,17 +527,17 @@
     return (stream + product(hidden, wouter), (normed, before, hidden))
 
 
-def feed_backward(stream, norm_gain, winner, wouter, stored, gradient):
+def feed_backward(grads, names, stream, norm_gain, winner, wouter, stored, gradient):
     normed, before, hidden = stored
     gradient_low = gradient.astype(jnp.bfloat16)
-    outer_grad = transpose_product(hidden, gradient_low)
+    grads.add(names[1], hidden, gradient_low)
     dhidden = product_transposed(gradient_low, wouter)
     gate_value, gate_pullback = jax.vjp(smooth_gate, before)
     dbefore = gate_pullback(dhidden)[0].astype(jnp.bfloat16)
-    inner_grad = transpose_product(normed, dbefore)
+    grads.add(names[0], normed, dbefore)
     dnormed = product_transposed(dbefore, winner)
     dstream, dgain = norm_backward(stream, norm_gain, dnormed)
-    return (gradient + dstream, dgain, inner_grad, outer_grad)
+    return (gradient + dstream, dgain)
 
 
 def index_bits(devices):
@@ -486,7 +559,8 @@
     def orders(self):
         core, row = ("dp", 0), ("fsdp", 0)
         rest = [key for key in self.bits if key not in (core, row)]
-        return ([core] + rest[:1] + [row] + rest[1:], [core, row] + rest)
+        third = [core] + rest[1:2] + rest[:1] + [row] + rest[2:]
+        return ([core] + rest[:1] + [row] + rest[1:], [core, row] + rest, third)
 
     def swap(self, value, axis, bit):
         pairs = [(place, place ^ (1 << bit)) for place in range(self.sizes[axis])]
@@ -496,19 +570,6 @@
         for key in self.bits:
             value = value + self.swap(value, *key)
         return value
-
-    def gather(self, shard):
-        rows, columns = shard.shape
-        half = rows // 2
-        core, place = self.side("dp", 0), lax.axis_index("fsdp")
-        part = lax.dynamic_slice_in_dim(shard, core * half, half, 0)
-        theirs = self.swap(part, "fsdp", 0)
-        mate = self.swap(theirs, "dp", 0)
-        whole = jnp.zeros((2 * rows, columns), shard.dtype)
-        other = (1 - place) * rows
-        whole = lax.dynamic_update_slice_in_dim(whole, shard, place * rows, 0)
-        whole = lax.dynamic_update_slice_in_dim(whole, theirs, other + core * half, 0)
-        return lax.dynamic_update_slice_in_dim(whole, mate, other + (1 - core) * half, 0)
 
     def gather_small(self, shard):
         other = self.swap(shard, "fsdp", 0)
@@ -528,7 +589,7 @@
     return ref.at[(lead,) + (slice(None),) * spot + (side,) + (slice(None),) * (count - spot - 1)]
 
 
-def reduce_kernel(links, pairs, g_ref, out_ref, own_ref, *rest):
+def reduce_kernel(links, chunks, g_ref, out_ref, own_ref, *rest):
     stages = len(links.bits)
     sums, (send_sem, recv_sem, own_sem) = rest[:stages], rest[stages:]
     plans = []
@@ -539,6 +600,7 @@
             plan.append((key, left.index(key), len(left)))
             left.remove(key)
         plans.append(plan)
+    kinds = len(plans)
 
     barrier = pltpu.get_barrier_semaphore()
     for key in links.bits:
@@ -550,16 +612,16 @@
         )
     pl.semaphore_wait(barrier, stages)
 
-    def source(stage, chunk, parity, away):
-        key, spot, count = plans[parity][stage]
+    def source(stage, chunk, kind, away):
+        key, spot, count = plans[kind][stage]
         side = links.side(*key)
         ref = g_ref if stage == 0 else sums[stage - 1]
         return pick(ref, chunk, spot, count, 1 - side if away else side)
 
-    def send(stage, chunk, parity):
-        key, _, _ = plans[parity][stage]
+    def send(stage, chunk, kind):
+        key, _, _ = plans[kind][stage]
         return pltpu.make_async_remote_copy(
-            src_ref=source(stage, chunk, parity, True),
+            src_ref=source(stage, chunk, kind, True),
             dst_ref=sums[stage].at[chunk],
             send_sem=send_sem.at[stage, chunk],
             recv_sem=recv_sem.at[stage, chunk],
@@ -567,37 +629,36 @@
             device_id_type=pl.DeviceIdType.MESH,
         )
 
-    def fetch(pair, parity):
-        slot = lax.rem(pair, 2)
+    def fetch(chunk, kind):
+        slot = lax.rem(chunk, HOLD)
         return pltpu.make_async_copy(
-            source(0, 2 * pair + parity, parity, False),
-            own_ref.at[slot, parity],
-            own_sem.at[slot, parity],
+            source(0, chunk, kind, False), own_ref.at[slot], own_sem.at[slot]
         )
 
-    def step(slot, carry):
-        @pl.when(slot < pairs)
-        def _():
-            for parity in range(2):
-                send(0, 2 * slot + parity, parity).start()
-                fetch(slot, parity).start()
-
-        for stage in range(stages):
-            pair = slot - 1 - stage
-
-            @pl.when((pair >= 0) & (pair < pairs))
+    def step(group, carry):
+        for turn in range(kinds):
+            now = group * kinds + turn
+
+            @pl.when(now < chunks)
             def _():
-                for parity in range(2):
-                    chunk = 2 * pair + parity
-                    send(stage, chunk, parity).wait()
+                send(0, now, turn).start()
+                fetch(now, turn).start()
+
+            for stage in range(stages):
+                chunk = now - DELAY * (stage + 1)
+                kind = (turn - DELAY * (stage + 1)) % kinds
+
+                @pl.when((chunk >= 0) & (chunk < chunks))
+                def _():
+                    send(stage, chunk, kind).wait()
                     if stage == 0:
-                        fetch(pair, parity).wait()
-                        mine = own_ref[lax.rem(pair, 2), parity]
+                        fetch(chunk, kind).wait()
+                        mine = own_ref[lax.rem(chunk, HOLD)]
                     else:
-                        mine = source(stage, chunk, parity, False)[...]
+                        mine = source(stage, chunk, kind, False)[...]
                     if stage < stages - 1:
                         sums[stage][chunk] = sums[stage][chunk] + mine
-                        send(stage + 1, chunk, parity).start()
+                        send(stage + 1, chunk, kind).start()
                     else:
                         out_ref[chunk] = sums[stage][chunk].astype(jnp.float32) + mine.astype(
                             jnp.float32
@@ -605,7 +666,8 @@
 
         return carry
 
-    lax.fori_loop(0, pairs + stages, step, 0)
+    slots = chunks + DELAY * stages
+    lax.fori_loop(0, (slots + kinds - 1) // kinds, step, 0)
 
 
 def reduce_chunks(links, grads, collective_id):
@@ -616,18 +678,18 @@
         for stage in range(stages)
     ]
     return pl.pallas_call(
-        functools.partial(reduce_kernel, links, chunks // 2),
+        functools.partial(reduce_kernel, links, chunks),
         out_shape=jax.ShapeDtypeStruct((chunks, rows, columns), jnp.float32),
-        in_specs=[pl.BlockSpec(memory_space=pl.ANY)],
+        in_specs=[pl.BlockSpec(memory_space=pltpu.HBM)],
         out_specs=pl.BlockSpec(memory_space=pltpu.VMEM),
         scratch_shapes=[
-            pltpu.VMEM((2, 2) + (2,) * (stages - 1) + (rows, columns), jnp.bfloat16)
+            pltpu.VMEM((HOLD,) + (2,) * (stages - 1) + (rows, columns), jnp.bfloat16)
         ]
         + sums
         + [
             pltpu.SemaphoreType.DMA((stages, chunks)),
             pltpu.SemaphoreType.DMA((stages, chunks)),
-            pltpu.SemaphoreType.DMA((2, 2)),
+            pltpu.SemaphoreType.DMA((HOLD,)),
         ],
         compiler_params=pltpu.CompilerParams(
             collective_id=collective_id, has_side_effects=True, vmem_limit_bytes=58 << 20
@@ -650,18 +712,222 @@
     return chunks.transpose(0, 3, 1, 2, 4).reshape(rows, columns)
 
 
-def reduce_grads(links, grads, collective_id):
-    devices = links.devices()
-    width = min(grad.shape[0] for grad in grads)
-    folded = [fold_grad(grad, devices, width) for grad in grads]
-    counts = [piece.shape[0] for piece in folded]
-    shares = reduce_chunks(links, jnp.concatenate(folded, axis=0), collective_id)
-    result, start = [], 0
-    for grad, count in zip(grads, counts):
-        rows, columns = grad.shape
-        result.append(unfold_share(shares[start : start + count], rows // devices, columns))
-        start += count
-    return result
+def gather_kernel(links, units, count, *refs):
+    shards, wholes, held = refs[:count], refs[count : 2 * count], refs[2 * count : 3 * count]
+    send_sem, recv_sem, local_sem = refs[3 * count :]
+    core, mesh_id = ("dp", 0), pl.DeviceIdType.MESH
+    keys = [("dp", 1), ("dp", 2), core]
+    orders = [[keys[0], keys[1], core], [keys[1], keys[0], core]]
+    row = ("fsdp", 0)
+    place = lax.axis_index("fsdp")
+
+    barrier = pltpu.get_barrier_semaphore()
+    for key in [row] + keys:
+        pl.semaphore_signal(
+            barrier, inc=1, device_id=links.partner(*key), device_id_type=mesh_id
+        )
+    pl.semaphore_wait(barrier, 1 + len(keys))
+
+    def piece(known):
+        return tuple(slice(None) if key in known else links.side(*key) for key in keys)
+
+    def send(stage, unit):
+        order = orders[unit % 2]
+        number, rows, columns = units[unit]
+        if stage == 0:
+            key, where = row, piece([])
+            src = shards[number].at[where + (rows, columns)]
+        else:
+            key, where = order[stage - 1], piece(order[: stage - 1])
+            src = wholes[number].at[(1 - place,) + where + (rows, columns)]
+        dst = wholes[number].at[
+            (place if stage == 0 else 1 - place,) + where + (rows, columns)
+        ]
+        return pltpu.make_async_remote_copy(
+            src_ref=src,
+            dst_ref=dst,
+            send_sem=send_sem.at[stage, unit],
+            recv_sem=recv_sem.at[stage, unit],
+            device_id=links.partner(*key),
+            device_id_type=mesh_id,
+        )
+
+    def load(number):
+        return pltpu.make_async_copy(shards[number], held[number], local_sem.at[0, number])
+
+    def keep(number):
+        return pltpu.make_async_copy(
+            held[number], wholes[number].at[place], local_sem.at[1, number]
+        )
+
+    stages = 1 + len(keys)
+    for unit in range(len(units)):
+        send(0, unit).start()
+    for number in range(count):
+        load(number).start()
+    for slot in range(len(units) + LAG * (stages - 1)):
+        for stage in range(stages):
+            unit = slot - LAG * stage
+            if 0 <= unit < len(units):
+                send(stage, unit).wait()
+                if stage + 1 < stages:
+                    send(stage + 1, unit).start()
+        if slot < count:
+            load(slot).wait()
+            keep(slot).start()
+    for number in range(count):
+        keep(number).wait()
+
+
+def gather_units(shards, width):
+    least = min(shard.shape[0] for shard in shards)
+    units = []
+    for number, shard in enumerate(shards):
+        deep, wide = shard.shape[0] // least, shard.shape[1] // width
+        rows = shard.shape[0] // 8 // deep
+        for part in range(deep):
+            for column in range(wide):
+                units.append(
+                    (
+                        number,
+                        slice(part * rows, (part + 1) * rows),
+                        slice(column * width, (column + 1) * width),
+                    )
+                )
+    return units
+
+
+def gather_weights(links, shards, collective_id):
+    count = len(shards)
+    units = gather_units(shards, shards[0].shape[1])
+    split = [
+        shard.reshape(2, 2, 2, shard.shape[0] // 8, shard.shape[1]) for shard in shards
+    ]
+    wholes = pl.pallas_call(
+        functools.partial(gather_kernel, links, units, count),
+        out_shape=[jax.ShapeDtypeStruct((2,) + piece.shape, piece.dtype) for piece in split],
+        in_specs=[pl.BlockSpec(memory_space=pltpu.HBM)] * count,
+        out_specs=[pl.BlockSpec(memory_space=pltpu.HBM)] * count,
+        scratch_shapes=[pltpu.VMEM(piece.shape, piece.dtype) for piece in split]
+        + [
+            pltpu.SemaphoreType.DMA((4, len(units))),
+            pltpu.SemaphoreType.DMA((4, len(units))),
+            pltpu.SemaphoreType.DMA((2, count)),
+        ],
+        compiler_params=pltpu.CompilerParams(
+            collective_id=collective_id, has_side_effects=True, vmem_limit_bytes=60 << 20
+        ),
+    )(*split)
+    return [
+        whole.reshape(2 * shard.shape[0], shard.shape[1]) for whole, shard in zip(wholes, shards)
+    ]
+
+
+def weight_kernel(deep, x_ref, dy_ref, *rest):
+    out_ref = rest[-1]
+    total = lax.dot_general(
+        x_ref[...], dy_ref[...], (((0,), (0,)), ((), ())), preferred_element_type=jnp.float32
+    )
+    half = total.shape[1] // 2
+    rows = out_ref.shape[2] // 2
+    total = total.reshape(out_ref.shape[1], deep, rows, 2 * half)
+    for part in range(deep):
+        piece = total[:, part]
+        piece = jnp.concatenate([piece[:, :, :half], piece[:, :, half:]], axis=1)
+        out_ref[part] = piece.astype(jnp.bfloat16)
+
+
+def weight_chunks(x, dy, chunks, start, count, devices, width):
+    rows, deep, wide = x.shape[0], x.shape[1] // width, dy.shape[1] // width
+    r = width // devices
+    if deep == 1:
+        specs = [
+            pl.BlockSpec((rows, width), lambda w: (0, 0)),
+            pl.BlockSpec((rows, width), lambda w: (0, w)),
+        ]
+        out_spec = pl.BlockSpec((1, devices, 2 * r, width // 2), lambda w: (start + w, 0, 0, 0))
+    else:
+        specs = [
+            pl.BlockSpec((rows, width), lambda w: (0, w)),
+            pl.BlockSpec((rows, width), lambda w: (0, 0)),
+        ]
+        out_spec = pl.BlockSpec(
+            (deep, devices // deep, 2 * r, width // 2), lambda w: (start // deep, w, 0, 0)
+        )
+    extra = [] if chunks is None else [chunks]
+    return pl.pallas_call(
+        functools.partial(weight_kernel, deep),
+        out_shape=jax.ShapeDtypeStruct((count, devices, 2 * r, width // 2), jnp.bfloat16),
+        grid=(max(deep, wide),),
+        in_specs=specs + [pl.BlockSpec(memory_space=pltpu.HBM)] * len(extra),
+        out_specs=out_spec,
+        input_output_aliases={2: 0} if extra else {},
+        compiler_params=pltpu.CompilerParams(vmem_limit_bytes=40 << 20),
+        cost_estimate=pl.CostEstimate(
+            flops=2 * rows * x.shape[1] * dy.shape[1],
+            transcendentals=0,
+            bytes_accessed=2 * (x.size + dy.size + x.shape[1] * dy.shape[1]),
+        ),
+    )(x, dy, *extra)
+
+
+class Gradients:
+    def __init__(self, links, width, shapes):
+        self.links, self.width, self.shapes = links, width, shapes
+        self.starts, self.count, self.scattered = {}, 0, {}
+        for name, (rows, columns) in shapes.items():
+            self.starts[name] = self.count
+            self.count += rows // width * (columns // width)
+        self.chunks = None
+
+    def scatter(self, name, x, dy):
+        grad = transpose_product(x, dy).astype(jnp.bfloat16)
+        share = lax.psum_scatter(grad, ("dp", "fsdp"), scatter_dimension=0, tiled=True)
+        self.scattered[name] = share.astype(jnp.float32)
+
+    def add(self, name, x, dy):
+        if name in OFFLOADED:
+            self.scatter(name, x, dy)
+            return
+        devices, start = self.links.devices(), self.starts[name]
+        if self.width // devices % 8 == 0:
+            self.chunks = weight_chunks(
+                x, dy, self.chunks, start, self.count, devices, self.width
+            )
+            return
+        fresh = fold_grad(transpose_product(x, dy), devices, self.width)
+        if self.chunks is None:
+            self.chunks = jnp.zeros((self.count,) + fresh.shape[1:], fresh.dtype)
+        self.chunks = lax.dynamic_update_slice_in_dim(self.chunks, fresh, start, 0)
+
+    def shares(self, collective_id):
+        shares = reduce_chunks(self.links, self.chunks, collective_id)
+        devices = self.links.devices()
+        shapes = [(rows // devices, columns) for rows, columns in self.shapes.values()]
+        if self.width // devices % 8 == 0:
+            result = pl.pallas_call(
+                functools.partial(unfold_kernel, self.width),
+                out_shape=[jax.ShapeDtypeStruct(shape, jnp.float32) for shape in shapes],
+            )(shares)
+            return dict(zip(self.shapes, result)) | self.scattered
+        result = dict(self.scattered)
+        for (name, (rows, columns)), shape in zip(self.shapes.items(), shapes):
+            start = self.starts[name]
+            count = rows // self.width * (columns // self.width)
+            result[name] = unfold_share(shares[start : start + count], *shape)
+        return result
+
+
+def unfold_kernel(width, shares_ref, *out_refs):
+    chunk, r, half = 0, shares_ref.shape[1] // 2, width // 2
+    for out_ref in out_refs:
+        for row in range(0, out_ref.shape[0], r):
+            for column in range(0, out_ref.shape[1], width):
+                for part in range(2):
+                    out_ref[
+                        row : row + r, column + part * half : column + (part + 1) * half
+                    ] = shares_ref[chunk, part * r : (part + 1) * r, :]
+                chunk += 1
 
 
 def body(
@@ -706,15 +972,47 @@
     enc_bias = band_bias(tables[:, 0].reshape(NB, H), encoder_bucket)
     dec_bias = band_bias(tables[:, 1].reshape(NB, H), decoder_bucket)
 
-    equery, ekeyval, eproj = (
-        links.gather(w) for w in (encoder_query, encoder_keyval, encoder_proj)
-    )
-    einner, eouter = (links.gather(w) for w in (encoder_inner, encoder_outer))
-    dquery, dkeyval, dproj = (
-        links.gather(w) for w in (decoder_query, decoder_keyval, decoder_proj)
-    )
-    cquery, ckeyval, cproj = (links.gather(w) for w in (cross_query, cross_keyval, cross_proj))
-    dinner, douter = (links.gather(w) for w in (decoder_inner, decoder_outer))
+    shards = [
+        encoder_query,
+        encoder_keyval,
+        encoder_proj,
+        encoder_inner,
+        encoder_outer,
+        decoder_query,
+        decoder_keyval,
+        decoder_proj,
+        cross_query,
+        cross_keyval,
+        cross_proj,
+        decoder_inner,
+        decoder_outer,
+    ]
+    shards = dict(zip(NAMES, shards))
+    later = [shards.pop(name) for name in OFFLOADED]
+    weights = dict(zip(shards, gather_weights(links, list(shards.values()), 1)))
+    weights["equery"], *later = lax.optimization_barrier((weights["equery"], *later))
+    for name, shard in zip(OFFLOADED, later):
+        weights[name] = lax.all_gather(shard, "fsdp", axis=0, tiled=True)
+    order = [
+        "dinner",
+        "douter",
+        "einner",
+        "eouter",
+        "cproj",
+        "cquery",
+        "ckeyval",
+        "dproj",
+        "dquery",
+        "dkeyval",
+        "eproj",
+        "equery",
+        "ekeyval",
+    ]
+    grads = Gradients(
+        links,
+        encoder_query.shape[1],
+        {name: weights[name].shape for name in order if name not in OFFLOADED},
+    )
 
     enc_layout = (enc_segments, enc_segments, enc_bias, False)
     dec_layout = (dec_segments, dec_segments, dec_bias, True)
@@ -722,46 +1020,50 @@
 
     enc_stream = enc_tokens.astype(jnp.float32)
     enc_middle, enc_self = attention_forward(
-        enc_stream, enc_gains[:, 0], equery, ekeyval, eproj, enc_layout, None
-    )
-    enc_final, enc_ffn = feed_forward(enc_middle, enc_gains[:, 1], einner, eouter)
+        enc_stream, enc_gains[:, 0], weights["equery"], weights["ekeyval"], weights["eproj"], enc_layout, None
+    )
+    enc_final, enc_ffn = feed_forward(enc_middle, enc_gains[:, 1], weights["einner"], weights["eouter"])
     memory = enc_final.astype(jnp.bfloat16)
 
     dec_stream = dec_tokens.astype(jnp.float32)
     after_self, dec_self = attention_forward(
-        dec_stream, dec_gains[:, 0], dquery, dkeyval, dproj, dec_layout, None
+        dec_stream, dec_gains[:, 0], weights["dquery"], weights["dkeyval"], weights["dproj"], dec_layout, None
     )
     after_cross, dec_cross = attention_forward(
-        after_self, dec_gains[:, 1], cquery, ckeyval, cproj, cross_layout, memory
-    )
-    dec_final, dec_ffn = feed_forward(after_cross, dec_gains[:, 2], dinner, douter)
+        after_self, dec_gains[:, 1], weights["cquery"], weights["ckeyval"], weights["cproj"], cross_layout, memory
+    )
+    dec_final, dec_ffn = feed_forward(after_cross, dec_gains[:, 2], weights["dinner"], weights["douter"])
 
 
     dec_live = (dec_segments >= 0).astype(jnp.float32)[:, None]
     gradient = dec_upstream.astype(jnp.float32) * dec_live
-    gradient, dgain_ffn, dinner_grad, douter_grad = feed_backward(
-        after_cross, dec_gains[:, 2], dinner, douter, dec_ffn, gradient
-    )
-    gradient, dgain_cross, cquery_grad, ckeyval_grad, cproj_grad, _, memory_grad = (
+    gradient, dgain_ffn = feed_backward(
+        grads, ("dinner", "douter"), after_cross, dec_gains[:, 2], weights["dinner"], weights["douter"], dec_ffn, gradient
+    )
+    gradient, dgain_cross, _, memory_grad = (
         attention_backward(
+            grads,
+            ("cquery", "ckeyval", "cproj"),
             after_self,
             dec_gains[:, 1],
-            cquery,
-            ckeyval,
-            cproj,
+            weights["cquery"],
+            weights["ckeyval"],
+            weights["cproj"],
             cross_layout,
             memory,
             dec_cross,
             gradient,
         )
     )
-    dec_gradient, dgain_self, dquery_grad, dkeyval_grad, dproj_grad, dec_band, _ = (
+    dec_gradient, dgain_self, dec_band, _ = (
         attention_backward(
+            grads,
+            ("dquery", "dkeyval", "dproj"),
             dec_stream,
             dec_gains[:, 0],
-            dquery,
-            dkeyval,
-            dproj,
+            weights["dquery"],
+            weights["dkeyval"],
+            weights["dproj"],
             dec_layout,
             None,
             dec_self,
@@ -771,16 +1073,18 @@
 
     enc_live = (enc_segments >= 0).astype(jnp.float32)[:, None]
     gradient = enc_upstream.astype(jnp.float32) * enc_live + memory_grad
-    gradient, egain_ffn, einner_grad, eouter_grad = feed_backward(
-        enc_middle, enc_gains[:, 1], einner, eouter, enc_ffn, gradient
-    )
-    enc_gradient, egain_self, equery_grad, ekeyval_grad, eproj_grad, enc_band, _ = (
+    gradient, egain_ffn = feed_backward(
+        grads, ("einner", "eouter"), enc_middle, enc_gains[:, 1], weights["einner"], weights["eouter"], enc_ffn, gradient
+    )
+    enc_gradient, egain_self, enc_band, _ = (
         attention_backward(
+            grads,
+            ("equery", "ekeyval", "eproj"),
             enc_stream,
             enc_gains[:, 0],
-            equery,
-            ekeyval,
-            eproj,
+            weights["equery"],
+            weights["ekeyval"],
+            weights["eproj"],
             enc_layout,
             None,
             enc_self,
@@ -796,64 +1100,33 @@
     flat = jnp.concatenate([gain_grads.reshape(-1)] + [grad.reshape(-1) for grad in table_grads])
     flat = links.total(flat.reshape(-1, TILE)).reshape(-1)
     width = gain_grads.shape[1]
+    flat, grads.chunks = lax.optimization_barrier((flat, grads.chunks))
     tables_grad = flat[5 * width :].reshape(2, NB, H)
     own = width // links.devices()
     gains_share = lax.dynamic_slice_in_dim(
         flat[: 5 * width].reshape(5, width), links.place() * own, own, 1
     ).T
-    (
-        equery_share,
-        ekeyval_share,
-        eproj_share,
-        einner_share,
-        eouter_share,
-        dquery_share,
-        dkeyval_share,
-        dproj_share,
-        cquery_share,
-        ckeyval_share,
-        cproj_share,
-        dinner_share,
-        douter_share,
-    ) = reduce_grads(
-        links,
-        [
-            equery_grad,
-            ekeyval_grad,
-            eproj_grad,
-            einner_grad,
-            eouter_grad,
-            dquery_grad,
-            dkeyval_grad,
-            dproj_grad,
-            cquery_grad,
-            ckeyval_grad,
-            cproj_grad,
-            dinner_grad,
-            douter_grad,
-        ],
-        0,
-    )
+    shares = grads.shares(0)
     return (
         memory,
         dec_final.astype(jnp.bfloat16),
         enc_gradient,
         dec_gradient,
-        equery_share,
-        ekeyval_share,
-        eproj_share,
-        einner_share,
-        eouter_share,
+        shares["equery"],
+        shares["ekeyval"],
+        shares["eproj"],
+        shares["einner"],
+        shares["eouter"],
         gains_share[:, 0:2],
         tables_grad[0],
-        dquery_share,
-        dkeyval_share,
-        dproj_share,
-        cquery_share,
-        ckeyval_share,
-        cproj_share,
-        dinner_share,
-        douter_share,
+        shares["dquery"],
+        shares["dkeyval"],
+        shares["dproj"],
+        shares["cquery"],
+        shares["ckeyval"],
+        shares["cproj"],
+        shares["dinner"],
+        shares["douter"],
         gains_share[:, 2:5],
         tables_grad[1],
     )

time: 899 us -> 537 us (0.60)
  local copies, waits for them, and re-layouts: 281 us -> 20.1 us
  matrix products: 183 us -> 109 us
  Pallas kernels: 276 us -> 331 us
  waiting for transfers between devices: 87 us -> 33 us
  starting transfers between devices: 26.9 us -> 9.34 us
  other arithmetic: 28.5 us -> 14.7 us
    reshape x32 -> x0, local copies, waits for them, and re-layouts: 129 us -> none  [the longest x26 125 us: fold_grad(): grad.astype(jnp.bfloat16).reshape(devices, deep, r, wide, 2, width // 2)]
    ppermute x32 -> x6, waiting for transfers between devices: 87 us -> 1.45 us  [swap(): return lax.ppermute(value, axis, pairs)]
    pallas_call x1 -> x14, Pallas kernels: 162 us -> 223 us  [the longest x1 117 us: reduce_chunks(): pl.pallas_call(functools.partial(reduce_kernel, links, chunks), out_shape...]
    unnamed x294 -> x268, local copies, waits for them, and re-layouts: 58.2 us -> 14.1 us
    dot_general x13 -> x2, matrix products: 51.3 us -> 8.08 us  [transpose_product(): lax.dot_general(former, latter, (((0,), (0,)), ((), ())), preferred_eleme...]
    dynamic_update_slice x38 -> x0, local copies, waits for them, and re-layouts: 36.8 us -> none  [the longest x13 19.5 us: gather(): lax.dynamic_update_slice_in_dim(whole, theirs, other + core * half, 0)]
    all_gather x0 -> x2, waiting for transfers between devices: none -> 31.5 us  [body(): weights[name] = lax.all_gather(shard, 'fsdp', axis=0, tiled=True)]
    dynamic_slice x13 -> x0, local copies, waits for them, and re-layouts: 21.4 us -> none  [gather(): part = lax.dynamic_slice_in_dim(shard, core * half, half, 0)]
  transfers between devices with their start and end apart: 32 -> 10, of which waited for: 8 -> 3; matrix products, arithmetic and copies ran while one was open for 27% -> 21% of each run, Pallas kernels for 23% -> 45%
where the time goes in v3:
time: 537 us; the launch traced here: 533 us
  Pallas kernels  331 us (62%)
  matrix products  109 us (20%)
  waiting for transfers between devices  33 us (6%)
  local copies, waits for them, and re-layouts  20.1 us (4%)
  between operations  16.2 us (3%)
  other arithmetic  14.7 us (3%)
  starting transfers between devices  9.34 us (2%)
    pallas_call x1, Pallas kernels, reduce_chunks(): pl.pallas_call(functools.partial(reduce_kernel, links, chunks), out_shape...  117 us
    pallas_call x3, Pallas kernels, attend_backward(): pl.pallas_call(functools.partial(backward_kernel, spec), out_shape=[jax.S...  66.4 us
    pallas_call x1, Pallas kernels, gather_weights(): pl.pallas_call(functools.partial(gather_kernel, links, units, count), out...  66.4 us
    dot_general x13, matrix products, product_transposed(): lax.dot_general(former, latter, (((1,), (1,)), ((), ())), preferred_eleme...  57.6 us
    pallas_call x3, Pallas kernels, attend_forward(): pl.pallas_call(functools.partial(forward_kernel, spec), out_shape=(jax.Sh...  41.7 us
    dot_general x13, matrix products, product(): return jnp.dot(former, latter, preferred_element_type=jnp.float32)  40.4 us
    pallas_call x11, Pallas kernels, weight_chunks(): pl.pallas_call(functools.partial(weight_kernel, deep), out_shape=jax.Shap...  36.6 us
    all_gather x2, waiting for transfers between devices, body(): weights[name] = lax.all_gather(shard, 'fsdp', axis=0, tiled=True)  31.5 us
  transfers between devices with their start and end apart: 10, of which 3 were waited for; matrix products, arithmetic and copies ran while one was open for 21% of the time, Pallas kernels for 45%

profile of v3, /device:TPU:0, one launch (start us, length us, event | category | flops | bytes accessed | tf_op | source)
XLA Modules:
  0.0 533.4 jit_solution(3764314213371530401)
XLA Ops:
  7.3 66.4 %shard_map.418 = (bf16[2,2,2,2,48,768]{5,4,3,2,1,0:T(8,128)(2,1)}, bf16[2,2,2,2,48,1536]{5,4,3,2,1,0:T(8,128)(2,1)}, bf16[2,2,2,2,48,768]{5,4,3,2,1,0:T(8,128)(2...) custom-call(bf16[2,2,2,48,768]{4,3,2,1,0:T(8,128)(2,1)} %bitcast.157, ...), custom_call_target="tpu_custom_call" | custom-call | tf_op jit(solution)/shard_map/pallas_call | solution.py:806
  78.7 2.3 convolution_convert_fusion.10.q_ref
  81.0 0.8 convolution_convert_fusion.4.k_ref.v_ref
  82.0 5.5 %shard_map.420 = (bf16[256,768]{1,0:T(8,128)(2,1)S(1)}, f32[6,2,256]{2,1,0:T(2,128)S(1)}) custom-call(s32[2,1]{1,0:T(2,128)S(1)} %broadcast_28_bounds_ref.2.bounds_ref, bf16[256,768]{1,0:T(8,128)(2,1)S(1)} %convolution_convert_fusion.10.q_ref, bf16[256,1536]{1,0:T(8,128)(2,1)S(1)} %convolution_convert_fusion.4.k_ref.v_ref, ...), custom_call_target="tpu_custom_call" | custom-call | flops 805306368 | bytes 8388608 | tf_op jit(solution)/shard_map/pallas_call | solution.py:388
  88.8 1.4 convolution_convert_fusion.6.q_ref
  90.3 0.8 copy-done.115
  91.1 2.8 convolution_convert_fusion.3.k_ref.v_ref
  94.2 27.7 %shard_map.419 = (bf16[1024,768]{1,0:T(8,128)(2,1)S(1)}, f32[6,2,1024]{2,1,0:T(2,128)S(1)}) custom-call(s32[2,4]{1,0:T(2,128)S(1)} %pad_add_fusion.bounds_ref, bf16[1024,768]{1,0:T(8,128)(2,1)S(1)} %convolution_convert_fusion.6.q_ref, bf16[1024,1536]{1,0:T(8,128)(2,1)S(1)} %convolution_convert_fusion.3.k_ref.v_ref, ...), custom_call_target="tpu_custom_call" | custom-call | flops 12884901888 | bytes 8388608 | tf_op jit(solution)/shard_map/pallas_call | solution.py:388
  122.0 1.5 multiply_reduce_fusion.2
  125.0 9.8 %multiply_convert_fusion = (bf16[1024,3072]{1,0:T(8,128)(2,1)S(1)}, f32[1024,3072]{1,0:T(8,128)}) fusion(bf16[1024,768]{1,0:T(8,128)(2,1)S(1)} %multiply_convert_fusion.2.x_ref, bf16[768,3072]{1,0:T(8,128)(2,1)S(1)} %bitcast.170), kind=kOutput, calls=%fused_computation.9 | convolution fusion | flops 4860149760 | bytes 25165824 | tf_op jit(solution)/shard_map/dot_general | solution.py:464
  134.8 9.7 %add_convert_fusion.x_ref = bf16[1024,768]{1,0:T(8,128)(2,1)S(1)} fusion(f32[1024,768]{1,0:T(8,128)S(1)} %get-tuple-element.200, bf16[1024,3072]{1,0:T(8,128)(2,1)S(1)} %get-tuple-element.201.x_ref, bf16[3072,768]{1,0:T(8,128)(2,1)} %bitcast.171), kind=kOutput, calls=%fused_computation.42 | convolution fusion | flops 4833411072 | bytes 15728640 | tf_op jit(solution)/shard_map/dot_general | solution.py:464
  144.6 2.8 convolution_convert_fusion.2.k_ref.v_ref
  147.4 1.1 copy-done.17
  148.5 8.5 %shard_map.421 = (bf16[256,768]{1,0:T(8,128)(2,1)S(1)}, f32[6,2,256]{2,1,0:T(2,128)S(1)}) custom-call(s32[2,1]{1,0:T(2,128)S(1)} %broadcast_28_bounds_ref.2.bounds_ref, bf16[256,768]{1,0:T(8,128)(2,1)S(1)} %convolution_convert_fusion.9.q_ref, bf16[1024,1536]{1,0:T(8,128)(2,1)S(1)} %convolution_convert_fusion.2.k_ref.v_ref, ...), custom_call_target="tpu_custom_call" | custom-call | flops 3221225472 | bytes 8388608 | tf_op jit(solution)/shard_map/pallas_call | solution.py:388
  157.1 1.4 multiply_reduce_fusion.7
  158.5 4.1 fusion.59
  162.6 1.7 copy-done.63
  164.3 4.5 convolution_convert_fusion
  168.8 31.5 %all-gather.5.cloned.1.call-done = bf16[3072,768]{1,0:T(8,128)(2,1)} async-done(((bf16[1536,768]{1,0:T(8,128)(2,1)}), bf16[3072,768]{1,0:T(8,128)(2,1)}) %all-gather.5.cloned.1.call-update) | async-done | bytes 4718608 | tf_op jit(solution)/shard_map/all_gather | solution.py:995
  200.2 6.7 %fusion.17 = bf16[256,3072]{1,0:T(8,128)(2,1)S(1)} fusion(f32[256,3072]{1,0:T(8,128)} %copy-done.63, bf16[3072,768]{1,0:T(8,128)(2,1)} %all-gather.5.cloned.1.call-done, bf16[256,768]{1,0:T(8,128)(2,1)S(1)} %copy-done.71, f32[256]{0:T(256)S(1)} %copy-done.110), kind=kOutput, calls=%fused_computation.33 | convolution fusion | flops 1224278016 | bytes 9831424 | tf_op jit(solution)/shard_map/dot_general | solution.py:474
  206.9 4.5 multiply_reduce_fusion.3
  213.3 12.0 %shard_map.422 = (bf16[256,768]{1,0:T(8,128)(2,1)S(1)}, bf16[1024,1536]{1,0:T(8,128)(2,1)S(1)}) custom-call(s32[2,1]{1,0:T(2,128)S(1)} %broadcast_28_bounds_ref.2.bounds_ref, bf16[256,768]{1,0:T(8,128)(2,1)S(1)} %convolution_convert_fusion.9.q_ref, bf16[1024,1536]{1,0:T(8,128)(2,1)} %copy-done.35, bf16[1024,1536]{1,0:T(8,128)(2,1)} %copy-done.35, ...), custom_call_target="tpu_custom_call" | custom-call | flops 8053063680 | bytes 16777216 | tf_op jit(solution)/shard_map/pallas_call | solution.py:424
  226.6 1.1 fusion.60
  228.3 11.9 %shard_map.424 = (bf16[256,768]{1,0:T(8,128)(2,1)S(1)}, bf16[256,1536]{1,0:T(8,128)(2,1)S(1)}, f32[12,5,8,256]{3,2,1,0:T(8,128)S(1)}) custom-call(s32[2,1]{1,0:T(2,128)S(1)} %broadcast_28_bounds_ref.2.bounds_ref, bf16[256,768]{1,0:T(8,128)(2,1)S(1)} %convolution_convert_fusion.10.q_ref, bf16[256,1536]{1,0:T(8,128)(2,1)S(1)} %copy-done.34, ...), custom_call_target="tpu_custom_call" | custom-call | flops 2013265920 | bytes 16777216 | tf_op jit(solution)/shard_map/pallas_call | solution.py:424
  240.8 2.4 fusion.29
  244.0 0.8 fusion.24
  245.6 5.7 %fusion.22 = (bf16[1024,768]{1,0:T(8,128)(2,1)S(1)}, f32[1024,768]{1,0:T(8,128)S(1)}) fusion(bf16[1024,768]{1,0:T(8,128)(2,1)} %param.31, f32[1024]{0:T(1024)S(1)} %copy-done.92, bf16[1024,1536]{1,0:T(8,128)(2,1)} %copy-done.12, bf16[768,1536]{1,0:T(8,128)(2,1)} %bitcast.175), kind=kOutput, calls=%fused_computation.46 | convolution fusion | flops 2419064832 | bytes 11800576 | tf_op jit(solution)/shard_map/dot_general | solution.py:474
  251.3 15.0 %fusion.6.dy_ref = bf16[1024,3072]{1,0:T(8,128)(2,1)S(1)} fusion(f32[1024,3072]{1,0:T(8,128)} %get-tuple-element.202, bf16[1024,768]{1,0:T(8,128)(2,1)S(1)} %get-tuple-element.207.dy_ref, bf16[3072,768]{1,0:T(8,128)(2,1)} %bitcast.172), kind=kOutput, calls=%fused_computation.8 | convolution fusion | flops 4894752768 | bytes 25165824 | tf_op jit(solution)/shard_map/dot_general | solution.py:474
  266.4 10.2 %multiply_reduce_fusion = (f32[768]{0:T(1024)S(1)}, f32[1024]{0:T(1024)S(1)}, f32[1024,768]{1,0:T(8,128)S(1)}) fusion(f32[1024,768]{1,0:T(8,128)S(1)} %copy-done.51, f32[1024]{0:T(1024)S(1)} %copy-done.84, f32[768]{0:T(1024)S(1)} %copy-done.79, bf16[1024,3072]{1,0:T(8,128)(2,1)S(1)} %fusion.6.dy_ref, bf16[768,3072]{1,0:T(8,128)(2,1)} %bitcast.167), kind=kOutput, calls=%fused_computation.38 | convolution fusion | flops 4836554752 | bytes 17315840 | tf_op jit(solution)/shard_map/dot_general | solution.py:474
  277.2 2.5 fusion.62
  279.7 1.4 convolution_convert_fusion.5.do_ref
  281.9 42.5 %shard_map.423 = (bf16[1024,768]{1,0:T(8,128)(2,1)S(1)}, bf16[1024,1536]{1,0:T(8,128)(2,1)}, f32[12,5,8,256]{3,2,1,0:T(8,128)S(1)}) custom-call(s32[2,4]{1,0:T(2,128)S(1)} %pad_add_fusion.bounds_ref, bf16[1024,768]{1,0:T(8,128)(2,1)S(1)} %copy-done.37, bf16[1024,1536]{1,0:T(8,128)(2,1)} %copy-done.38, bf16[1024,1536]{1,0:T(8,128)(2,1)} %copy-done.38, ...), custom_call_target="tpu_custom_call" | custom-call | flops 32212254720 | bytes 16777216 | tf_op jit(solution)/shard_map/pallas_call | solution.py:424
  324.5 1.1 copy.103
  326.1 0.8 copy-done.69
  326.9 3.6 convolution_convert_fusion.1
  330.5 1.9 fusion.23
  333.1 5.4 %fusion.68 = f32[1024,768]{1,0:T(8,128)S(1)} fusion(bf16[1024,1536]{1,0:T(8,128)(2,1)} %get-tuple-element.83.dy_ref, bf16[768,1536]{1,0:T(8,128)(2,1)} %bitcast.173), kind=kOutput, calls=%fused_computation.156 | convolution fusion | flops 2415919104 | bytes 8650752 | tf_op jit(solution)/shard_map/dot_general | solution.py:474
  338.6 4.2 fusion.10
  342.8 0.7 maximum_bitcast_fusion
  343.9 1.5 shard_map.425.rest_0_
  345.4 1.6 shard_map.426.rest_0_
  347.0 0.7 copy-done.13
  348.2 4.4 shard_map.427.rest_0_
  352.6 1.5 shard_map.428.rest_0_
  354.1 1.6 shard_map.429.rest_0_
  355.7 2.2 shard_map.430.rest_0_
  357.9 0.8 slice-done.1
  359.2 7.2 %shard_map.431.rest_0_ = bf16[20,32,48,384]{3,2,1,0:T(8,128)(2,1)} custom-call(bf16[1024,3072]{1,0:T(8,128)(2,1)S(1)} %bitcast.128, bf16[1024,768]{1,0:T(8,128)(2,1)S(1)} %copy-done.24, bf16[20,32,48,384]{3,2,1,0:T(8,128)(2,1)} %shard_map.430.rest_0_), custom_call_target="tpu_custom_call", output_to_operand_aliasing={{}: (2, {})} | custom-call | flops 4831838208 | bytes 12582912 | tf_op jit(solution)/shard_map/pallas_call | solution.py:858
  366.5 7.3 %shard_map.432.rest_0_ = bf16[20,32,48,384]{3,2,1,0:T(8,128)(2,1)} custom-call(bf16[1024,768]{1,0:T(8,128)(2,1)S(1)} %copy-done.9, bf16[1024,3072]{1,0:T(8,128)(2,1)S(1)} %bitcast.130, bf16[20,32,48,384]{3,2,1,0:T(8,128)(2,1)} %shard_map.431.rest_0_), custom_call_target="tpu_custom_call", output_to_operand_aliasing={{}: (2, {})} | custom-call | flops 4831838208 | bytes 12582912 | tf_op jit(solution)/shard_map/pallas_call | solution.py:858
  373.8 2.4 fusion.19
  376.3 0.9 copy-done.64
  377.2 2.7 fusion.25
  380.0 4.1 collective-permute-start.2
  384.1 1.1 fusion.32
  385.4 2.5 shard_map.433.rest_0_
  387.8 1.3 collective-permute-done.3
  389.2 1.4 collective-permute-start.4
  390.6 2.5 shard_map.434.rest_0_
  393.1 2.7 collective-permute-start.5
  395.8 4.4 shard_map.435
  401.5 117.5 %shard_map.436.shares_ref = f32[20,48,384]{2,1,0:T(8,128)} custom-call(bf16[20,2,2,2,2,2,48,384]{7,6,5,4,3,2,1,0:T(8,128)(2,1)} %bitcast.139), custom_call_target="tpu_custom_call" | custom-call | tf_op jit(solution)/shard_map/pallas_call | solution.py:680
  519.0 2.5 shard_map.437
  523.0 1.6 convert_element_type.161
  524.7 1.6 convert_element_type.159
  (353 shorter events, 20.6 us)
Async XLA Ops:
  7.2 151.3 %all-gather.3.cloned.1.call-start = ((), (), s32[]{:S(2)}) async-start(), calls=%async_computation.2 | async-start | bytes 7077888 | tf_op jit(solution)/shard_map/all_gather | solution.py:995
  7.2 66.6 %copy-start.112 = (bf16[16,12]{1,0:T(8,128)(2,1)S(1)}, bf16[16,12]{1,0:T(8,128)(2,1)}, u32[]{:S(2)}) copy-start(bf16[16,12]{1,0:T(8,128)(2,1)} %param.49) | copy-start | bytes 1156
  7.3 66.6 %copy-start.113 = (bf16[16,12]{1,0:T(8,128)(2,1)S(1)}, bf16[16,12]{1,0:T(8,128)(2,1)}, u32[]{:S(2)}) copy-start(bf16[16,12]{1,0:T(8,128)(2,1)} %param.39) | copy-start | bytes 1156
  7.3 66.7 %copy-start.99 = (bf16[384,3]{0,1:T(4,128)(2,1)S(1)}, bf16[384,3]{0,1:T(4,128)(2,1)}, u32[]{:S(2)}) copy-start(bf16[384,3]{0,1:T(4,128)(2,1)} %param.48) | copy-start | bytes 6916
  7.3 66.7 %copy-start.109 = (bf16[384,2]{0,1:T(2,128)(2,1)S(1)}, bf16[384,2]{0,1:T(2,128)(2,1)}, u32[]{:S(2)}) copy-start(bf16[384,2]{0,1:T(2,128)(2,1)} %param.38) | copy-start | bytes 4612
  73.8 126.5 %all-gather.5.cloned.1.call-start = ((), (), s32[]{:S(2)}) async-start(), calls=%async_computation.3 | async-start | bytes 7077888 | tf_op jit(solution)/shard_map/all_gather | solution.py:995
  74.0 3.7 collective-permute-start
  74.6 448.4 %reduce-scatter.5.cloned.1.call-start = ((), (), s32[]{:S(2)}) async-start(), calls=%async_computation.5 | async-start | bytes 4866048 | tf_op jit(solution)/shard_map/reduce_scatter | solution.py:885
  77.0 11.1 %copy-start.80 = (f32[1024]{0:T(1024)}, f32[1024]{0:T(1024)S(1)}, u32[]{:S(2)}) copy-start(f32[1024]{0:T(1024)S(1)} %fusion.51) | copy-start | bytes 12292
  77.8 10.2 %copy-start.75 = (f32[768]{0:T(1024)}, f32[768]{0:T(1024)S(1)}, u32[]{:S(2)}) copy-start(f32[768]{0:T(1024)S(1)} %get-tuple-element.180) | copy-start | bytes 9220
  77.9 46.8 %copy-start.78 = (f32[768]{0:T(1024)}, f32[768]{0:T(1024)S(1)}, u32[]{:S(2)}) copy-start(f32[768]{0:T(1024)S(1)} %get-tuple-element.179) | copy-start | bytes 9220
  78.2 15.9 %copy-start.29 = (f32[12,5,256]{2,1,0:T(8,128)}, f32[12,5,256]{2,1,0:T(8,128)S(1)}, u32[]{:S(2)}) copy-start(f32[12,5,256]{2,1,0:T(8,128)S(1)} %copy.88.rest_0_) | copy-start | bytes 184324
  88.0 69.0 %copy-start.44 = (f32[256,768]{1,0:T(8,128)}, f32[256,768]{1,0:T(8,128)S(1)}, u32[]{:S(2)}) copy-start(f32[256,768]{1,0:T(8,128)S(1)} %get-tuple-element.198) | copy-start | bytes 2359300
  91.1 33.9 %slice-start.6 = ((s8[4718592]{0:T(1024)(128)(4,1)}), s8[4194304]{0:T(1024)(128)(4,1)S(1)}, s32[]{:S(2)}) async-start(s8[4718592]{0:T(1024)(128)(4,1)} %bitcast.168), calls=%async_computation.12 | async-start | bytes 8388608
  93.9 28.0 %copy-start.38 = (bf16[1024,1536]{1,0:T(8,128)(2,1)}, bf16[1024,1536]{1,0:T(8,128)(2,1)S(1)}, u32[]{:S(2)}) copy-start(bf16[1024,1536]{1,0:T(8,128)(2,1)S(1)} %convolution_convert_fusion.3.k_ref.v_ref) | copy-start | bytes 9437188
  94.1 119.1 %copy-start.27 = (s32[1024,128]{1,0:T(8,128)}, s32[1024,128]{1,0:T(8,128)S(1)}, u32[]{:S(2)}) copy-start(s32[1024,128]{1,0:T(8,128)S(1)} %broadcast_in_dim.27.segk_ref) | copy-start | bytes 1572868
  94.1 27.8 %copy-start.47 = (bf16[1024,768]{1,0:T(8,128)(2,1)S(1)}, bf16[1024,768]{1,0:T(8,128)(2,1)}, u32[]{:S(2)}) copy-start(bf16[1024,768]{1,0:T(8,128)(2,1)} %param.27) | copy-start | bytes 4718596
  94.2 27.8 %copy-start.121 = (bf16[2,2,2,2,48,768]{5,4,3,2,1,0:T(8,128)(2,1)S(1)}, bf16[2,2,2,2,48,768]{5,4,3,2,1,0:T(8,128)(2,1)}, u32[]{:S(2)}) copy-start(bf16[2,2,2,2,48,768]{5,4,3,2,1,0:T(8,128)(2,1)} %get-tuple-element.66) | copy-start | bytes 3538948
  94.2 30.8 %slice-start.7 = ((s8[4718592]{0:T(1024)(128)(4,1)}), s8[524288]{0:T(1024)(128)(4,1)S(1)}, s32[]{:S(2)}) async-start(s8[4718592]{0:T(1024)(128)(4,1)} %bitcast.168), calls=%async_computation.13 | async-start | bytes 1048576
  123.5 11.3 %copy-start.50 = (f32[1024,768]{1,0:T(8,128)}, f32[1024,768]{1,0:T(8,128)S(1)}, u32[]{:S(2)}) copy-start(f32[1024,768]{1,0:T(8,128)S(1)} %get-tuple-element.200) | copy-start | bytes 9437188
  125.0 9.8 %copy-start.8 = (bf16[1024,768]{1,0:T(8,128)(2,1)}, bf16[1024,768]{1,0:T(8,128)(2,1)S(1)}, u32[]{:S(2)}) copy-start(bf16[1024,768]{1,0:T(8,128)(2,1)S(1)} %multiply_convert_fusion.2.x_ref) | copy-start | bytes 4718596
  134.8 9.7 %copy-start.6 = (bf16[1024,3072]{1,0:T(8,128)(2,1)}, bf16[1024,3072]{1,0:T(8,128)(2,1)S(1)}, u32[]{:S(2)}) copy-start(bf16[1024,3072]{1,0:T(8,128)(2,1)S(1)} %get-tuple-element.201.x_ref) | copy-start | bytes 18874372
  134.8 9.7 %copy-start.116 = (bf16[2,2,2,2,48,1536]{5,4,3,2,1,0:T(8,128)(2,1)S(1)}, bf16[2,2,2,2,48,1536]{5,4,3,2,1,0:T(8,128)(2,1)}, u32[]{:S(2)}) copy-start(bf16[2,2,2,2,48,1536]{5,4,3,2,1,0:T(8,128)(2,1)} %get-tuple-element.74) | copy-start | bytes 7077892
  148.5 8.5 %copy-start.35 = (bf16[1024,1536]{1,0:T(8,128)(2,1)}, bf16[1024,1536]{1,0:T(8,128)(2,1)S(1)}, u32[]{:S(2)}) copy-start(bf16[1024,1536]{1,0:T(8,128)(2,1)S(1)} %convolution_convert_fusion.2.k_ref.v_ref) | copy-start | bytes 9437188
  148.5 8.5 %copy-start.59 = (bf16[2,2,2,2,48,768]{5,4,3,2,1,0:T(8,128)(2,1)S(1)}, bf16[2,2,2,2,48,768]{5,4,3,2,1,0:T(8,128)(2,1)}, u32[]{:S(2)}) copy-start(bf16[2,2,2,2,48,768]{5,4,3,2,1,0:T(8,128)(2,1)} %get-tuple-element.76) | copy-start | bytes 3538948
  158.5 53.6 %copy-start.73 = (f32[256]{0:T(256)}, f32[256]{0:T(256)S(1)}, u32[]{:S(2)}) copy-start(f32[256]{0:T(256)S(1)} %fusion.57) | copy-start | bytes 3076
  213.3 12.0 %copy-start.45 = (f32[256,768]{1,0:T(8,128)S(1)}, f32[256,768]{1,0:T(8,128)}, u32[]{:S(2)}) copy-start(f32[256,768]{1,0:T(8,128)} %copy-done.44) | copy-start | bytes 2359300
  213.3 12.0 %copy-start.62 = (bf16[2,2,2,2,48,768]{5,4,3,2,1,0:T(8,128)(2,1)S(1)}, bf16[2,2,2,2,48,768]{5,4,3,2,1,0:T(8,128)(2,1)}, u32[]{:S(2)}) copy-start(bf16[2,2,2,2,48,768]{5,4,3,2,1,0:T(8,128)(2,1)} %get-tuple-element.73) | copy-start | bytes 3538948
  228.2 12.0 %copy-start.58 = (bf16[2,2,2,2,48,768]{5,4,3,2,1,0:T(8,128)(2,1)S(1)}, bf16[2,2,2,2,48,768]{5,4,3,2,1,0:T(8,128)(2,1)}, u32[]{:S(2)}) copy-start(bf16[2,2,2,2,48,768]{5,4,3,2,1,0:T(8,128)(2,1)} %get-tuple-element.69) | copy-start | bytes 3538948
  228.2 12.5 %copy-start.54 = (bf16[256,768]{1,0:T(8,128)(2,1)S(1)}, bf16[256,768]{1,0:T(8,128)(2,1)}, u32[]{:S(2)}) copy-start(bf16[256,768]{1,0:T(8,128)(2,1)} %param.28) | copy-start | bytes 1179652
  228.3 12.5 %copy-start.86 = (f32[768]{0:T(1024)S(1)}, f32[768]{0:T(1024)}, u32[]{:S(2)}) copy-start(f32[768]{0:T(1024)} %copy-done.85) | copy-start | bytes 9220
  228.3 12.5 %copy-start.103 = (f32[256]{0:T(256)S(1)}, f32[256]{0:T(256)}, u32[]{:S(2)}) copy-start(f32[256]{0:T(256)} %copy-done.102) | copy-start | bytes 3076
  228.3 12.5 %copy-start.118 = (bf16[2,2,2,2,48,1536]{5,4,3,2,1,0:T(8,128)(2,1)S(1)}, bf16[2,2,2,2,48,1536]{5,4,3,2,1,0:T(8,128)(2,1)}, u32[]{:S(2)}) copy-start(bf16[2,2,2,2,48,1536]{5,4,3,2,1,0:T(8,128)(2,1)} %get-tuple-element.70) | copy-start | bytes 7077892
  245.5 279.1 %reduce-scatter.3.cloned.1.call-start = ((), (), s32[]{:S(2)}) async-start(), calls=%async_computation.4 | async-start | bytes 4866048 | tf_op jit(solution)/shard_map/reduce_scatter | solution.py:885
  251.3 15.1 %copy-start.23 = (bf16[1024,768]{1,0:T(8,128)(2,1)}, bf16[1024,768]{1,0:T(8,128)(2,1)S(1)}, u32[]{:S(2)}) copy-start(bf16[1024,768]{1,0:T(8,128)(2,1)S(1)} %get-tuple-element.207.dy_ref) | copy-start | bytes 4718596
  251.3 15.1 %copy-start.51 = (f32[1024,768]{1,0:T(8,128)S(1)}, f32[1024,768]{1,0:T(8,128)}, u32[]{:S(2)}) copy-start(f32[1024,768]{1,0:T(8,128)} %copy-done.50) | copy-start | bytes 9437188
  251.3 15.1 %copy-start.79 = (f32[768]{0:T(1024)S(1)}, f32[768]{0:T(1024)}, u32[]{:S(2)}) copy-start(f32[768]{0:T(1024)} %copy-done.78) | copy-start | bytes 9220
  251.3 15.1 %copy-start.84 = (f32[1024]{0:T(1024)S(1)}, f32[1024]{0:T(1024)}, u32[]{:S(2)}) copy-start(f32[1024]{0:T(1024)} %copy-done.83) | copy-start | bytes 12292
  266.4 10.2 %copy-start.7 = (bf16[1024,3072]{1,0:T(8,128)(2,1)}, bf16[1024,3072]{1,0:T(8,128)(2,1)S(1)}, u32[]{:S(2)}) copy-start(bf16[1024,3072]{1,0:T(8,128)(2,1)S(1)} %fusion.6.dy_ref) | copy-start | bytes 18874372
  266.4 10.8 %copy-start.94 = (f32[1024]{0:T(1024)S(1)}, f32[1024]{0:T(1024)}, u32[]{:S(2)}) copy-start(f32[1024]{0:T(1024)} %copy-done.93) | copy-start | bytes 12292
  266.4 10.8 %copy-start.67 = (bf16[1024,768]{1,0:T(8,128)(2,1)S(1)}, bf16[1024,768]{1,0:T(8,128)(2,1)}, u32[]{:S(2)}) copy-start(bf16[1024,768]{1,0:T(8,128)(2,1)} %param.31) | copy-start | bytes 4718596
  281.9 43.6 %copy-start.74 = (f32[256]{0:T(256)S(1)}, f32[256]{0:T(256)}, u32[]{:S(2)}) copy-start(f32[256]{0:T(256)} %copy-done.73) | copy-start | bytes 3076
  324.4 14.1 %copy-start.21 = (bf16[1024,768]{1,0:T(8,128)(2,1)}, bf16[1024,768]{1,0:T(8,128)(2,1)S(1)}, u32[]{:S(2)}) copy-start(bf16[1024,768]{1,0:T(8,128)(2,1)S(1)} %get-tuple-element.82.dy_ref) | copy-start | bytes 4718596
  343.6 36.4 %collective-permute-start.1 = (f32[36,128]{1,0:T(8,128)S(1)}, f32[36,128]{1,0:T(8,128)S(1)}, u32[]{:S(2)}, u32[]{:S(2)}) collective-permute-start(f32[36,128]{1,0:T(8,128)S(1)} %maximum_bitcast_fusion), channel_id=1, source_target_pairs={{0,1},{1,0},{2,3},{3,2},{4,5},{5,4},{6,7},{7,6},{8,9},{9,8},{10,11... | collective-permute-start | bytes 55304 | tf_op jit(solution)/shard_map/ppermute | solution.py:567
  355.7 10.7 %slice-start.2 = ((s8[6291456]{0:T(1024)(128)(4,1)}), s8[4194304]{0:T(1024)(128)(4,1)S(1)}, s32[]{:S(2)}) async-start(s8[6291456]{0:T(1024)(128)(4,1)} %bitcast.129), calls=%async_computation.8 | async-start | bytes 8388608
  359.2 7.3 %slice-start.3 = ((s8[6291456]{0:T(1024)(128)(4,1)}), s8[2097152]{0:T(1024)(128)(4,1)S(1)}, s32[]{:S(2)}) async-start(s8[6291456]{0:T(1024)(128)(4,1)} %bitcast.129), calls=%async_computation.9 | async-start | bytes 4194304
  359.2 7.3 %copy-start.9 = (bf16[1024,768]{1,0:T(8,128)(2,1)S(1)}, bf16[1024,768]{1,0:T(8,128)(2,1)}, u32[]{:S(2)}) copy-start(bf16[1024,768]{1,0:T(8,128)(2,1)} %copy-done.8) | copy-start | bytes 4718596
  359.2 17.1 %slice-start.4 = ((s8[4718592]{0:T(1024)(128)(4,1)}), s8[4194304]{0:T(1024)(128)(4,1)S(1)}, s32[]{:S(2)}) async-start(s8[4718592]{0:T(1024)(128)(4,1)} %bitcast.165), calls=%async_computation.10 | async-start | bytes 8388608
  366.5 7.3 %copy-start.49 = (bf16[1024,768]{1,0:T(8,128)(2,1)S(1)}, bf16[1024,768]{1,0:T(8,128)(2,1)}, u32[]{:S(2)}) copy-start(bf16[1024,768]{1,0:T(8,128)(2,1)} %param.27) | copy-start | bytes 4718596
  366.5 7.3 %copy-start.52 = (f32[1024,768]{1,0:T(8,128)S(1)}, f32[1024,768]{1,0:T(8,128)}, u32[]{:S(2)}) copy-start(f32[1024,768]{1,0:T(8,128)} %get-tuple-element.188) | copy-start | bytes 9437188
  366.5 7.3 %copy-start.65 = (f32[1024,768]{1,0:T(8,128)S(1)}, f32[1024,768]{1,0:T(8,128)}, u32[]{:S(2)}) copy-start(f32[1024,768]{1,0:T(8,128)} %get-tuple-element.210) | copy-start | bytes 9437188
  366.5 7.3 %copy-start.77 = (f32[768]{0:T(1024)S(1)}, f32[768]{0:T(1024)}, u32[]{:S(2)}) copy-start(f32[768]{0:T(1024)} %copy-done.75) | copy-start | bytes 9220
  366.5 7.3 %copy-start.82 = (f32[1024]{0:T(1024)S(1)}, f32[1024]{0:T(1024)}, u32[]{:S(2)}) copy-start(f32[1024]{0:T(1024)} %copy-done.80) | copy-start | bytes 12292
  366.5 9.8 %slice-start.5 = ((s8[4718592]{0:T(1024)(128)(4,1)}), s8[524288]{0:T(1024)(128)(4,1)S(1)}, s32[]{:S(2)}) async-start(s8[4718592]{0:T(1024)(128)(4,1)} %bitcast.165), calls=%async_computation.11 | async-start | bytes 1048576
  377.2 6.9 %copy-start.55 = (bf16[256,768]{1,0:T(8,128)(2,1)S(1)}, bf16[256,768]{1,0:T(8,128)(2,1)}, u32[]{:S(2)}) copy-start(bf16[256,768]{1,0:T(8,128)(2,1)} %param.28) | copy-start | bytes 1179652
  377.2 6.9 %copy-start.66 = (f32[256,768]{1,0:T(8,128)S(1)}, f32[256,768]{1,0:T(8,128)}, u32[]{:S(2)}) copy-start(f32[256,768]{1,0:T(8,128)} %get-tuple-element.186) | copy-start | bytes 2359300
  377.2 6.9 %copy-start.70 = (f32[256,768]{1,0:T(8,128)S(1)}, f32[256,768]{1,0:T(8,128)}, u32[]{:S(2)}) copy-start(f32[256,768]{1,0:T(8,128)} %get-tuple-element.211) | copy-start | bytes 2359300
  377.2 6.9 %copy-start.87 = (f32[768]{0:T(1024)S(1)}, f32[768]{0:T(1024)}, u32[]{:S(2)}) copy-start(f32[768]{0:T(1024)} %copy-done.85) | copy-start | bytes 9220
  377.2 6.9 %copy-start.104 = (f32[256]{0:T(256)S(1)}, f32[256]{0:T(256)}, u32[]{:S(2)}) copy-start(f32[256]{0:T(256)} %copy-done.102) | copy-start | bytes 3076
  377.2 8.1 %copy-start.20 = (bf16[1024,768]{1,0:T(8,128)(2,1)S(1)}, bf16[1024,768]{1,0:T(8,128)(2,1)}, u32[]{:S(2)}) copy-start(bf16[1024,768]{1,0:T(8,128)(2,1)} %copy-done.19) | copy-start | bytes 4718596
  380.0 5.2 collective-permute-start.2
  385.3 3.8 collective-permute-start.3
  389.2 3.9 collective-permute-start.4
  393.1 7.1 %collective-permute-start.5 = (f32[36,128]{1,0:T(8,128)S(1)}, f32[36,128]{1,0:T(8,128)S(1)}, u32[]{:S(2)}, u32[]{:S(2)}) collective-permute-start(f32[36,128]{1,0:T(8,128)S(1)} %add.192), channel_id=1, source_target_pairs={{0,16},{2,18},{4,20},{6,22},{8,24},{10,26},{12,28},{14,30},{16,0},... | collective-permute-start | bytes 55304 | tf_op jit(solution)/shard_map/ppermute | solution.py:567
  (77 other events, 234.5 us)
Sparse Core Ops, SparseCore 0:
  73.9 62.0 all-gather.2
  137.5 62.6 all-gather.4
  245.7 107.0 reduce-scatter.4
  359.0 124.6 reduce-scatter.2

commit v4 on v3

--- a/solution.py
+++ b/solution.py
@@ -21,10 +21,11 @@
 PADDING_LABEL = 1 << 20
 SPAN = 2 * TILE
 FOLD = 8
-LAG = 2
+LAG = 3
 DELAY = 2
 HOLD = DELAY + 1
 OFFLOADED = ("dinner", "douter")
+LATER = ("dinner",)
 NAMES = (
     "equery",
     "ekeyval",
@@ -343,7 +344,8 @@
     rows, keys = queries.shape[0], keyval.shape[0]
     qb, kb = min(256, rows), min(256, keys)
     skip = rows > qb
-    pairs = pairs if skip else 3
+    kb = TILE if skip else kb
+    pairs = pairs if skip else 2
     spec = dict(
         qb=qb,
         kb=kb,
@@ -589,18 +591,29 @@
     return ref.at[(lead,) + (slice(None),) * spot + (side,) + (slice(None),) * (count - spot - 1)]
 
 
-def reduce_kernel(links, chunks, g_ref, out_ref, own_ref, *rest):
-    stages = len(links.bits)
-    sums, (send_sem, recv_sem, own_sem) = rest[:stages], rest[stages:]
-    plans = []
+def fold_product(x, dy, devices):
+    total = lax.dot_general(x, dy, (((0,), (0,)), ((), ())), preferred_element_type=jnp.float32)
+    rows, columns = total.shape
+    total = total.reshape(devices, rows // devices, columns)
+    half = columns // 2
+    total = jnp.concatenate([total[:, :, :half], total[:, :, half:]], axis=1)
+    return total.astype(jnp.bfloat16)
+
+
+def reduce_kernel(links, plan, count, *refs):
+    stages, chunks = len(links.bits), len(plan)
+    sources, (out_ref, ring_ref, x_ref, y_ref) = refs[:count], refs[count : count + 4]
+    rest = refs[count + 4 :]
+    sums, (send_sem, recv_sem, load_sem) = rest[:stages], rest[stages:]
+    halvings = []
     for order in links.orders():
         left = list(reversed(links.bits))
-        plan = []
+        halving = []
         for key in order:
-            plan.append((key, left.index(key), len(left)))
+            halving.append((key, left.index(key), len(left)))
             left.remove(key)
-        plans.append(plan)
-    kinds = len(plans)
+        halvings.append(halving)
+    kinds = len(halvings)
 
     barrier = pltpu.get_barrier_semaphore()
     for key in links.bits:
@@ -613,13 +626,13 @@
     pl.semaphore_wait(barrier, stages)
 
     def source(stage, chunk, kind, away):
-        key, spot, count = plans[kind][stage]
+        key, spot, width = halvings[kind][stage]
         side = links.side(*key)
-        ref = g_ref if stage == 0 else sums[stage - 1]
-        return pick(ref, chunk, spot, count, 1 - side if away else side)
+        ref, lead = (ring_ref, lax.rem(chunk, HOLD)) if stage == 0 else (sums[stage - 1], chunk)
+        return pick(ref, lead, spot, width, 1 - side if away else side)
 
     def send(stage, chunk, kind):
-        key, _, _ = plans[kind][stage]
+        key, _, _ = halvings[kind][stage]
         return pltpu.make_async_remote_copy(
             src_ref=source(stage, chunk, kind, True),
             dst_ref=sums[stage].at[chunk],
@@ -629,21 +642,36 @@
             device_id_type=pl.DeviceIdType.MESH,
         )
 
-    def fetch(chunk, kind):
-        slot = lax.rem(chunk, HOLD)
-        return pltpu.make_async_copy(
-            source(0, chunk, kind, False), own_ref.at[slot], own_sem.at[slot]
-        )
+    def loads(chunk):
+        item = plan[chunk]
+        if item[0] == "chunk":
+            _, which, index = item
+            return [
+                pltpu.make_async_copy(
+                    sources[which].at[index], ring_ref.at[chunk % HOLD], load_sem.at[chunk % 2, 0]
+                )
+            ]
+        _, rows, *operands = item
+        slot = chunk % 2
+        result = []
+        for place, (which, column) in enumerate(operands):
+            buffer = (x_ref, y_ref)[place]
+            width = buffer.shape[2]
+            result.append(
+                pltpu.make_async_copy(
+                    sources[which].at[:, column * width : (column + 1) * width],
+                    buffer.at[slot, :rows],
+                    load_sem.at[slot, place],
+                )
+            )
+        return result
+
+    sizes = sorted({item[1] for item in plan if item[0] == "product"})
 
     def step(group, carry):
         for turn in range(kinds):
             now = group * kinds + turn
 
-            @pl.when(now < chunks)
-            def _():
-                send(0, now, turn).start()
-                fetch(now, turn).start()
-
             for stage in range(stages):
                 chunk = now - DELAY * (stage + 1)
                 kind = (turn - DELAY * (stage + 1)) % kinds
@@ -651,11 +679,7 @@
                 @pl.when((chunk >= 0) & (chunk < chunks))
                 def _():
                     send(stage, chunk, kind).wait()
-                    if stage == 0:
-                        fetch(chunk, kind).wait()
-                        mine = own_ref[lax.rem(chunk, HOLD)]
-                    else:
-                        mine = source(stage, chunk, kind, False)[...]
+                    mine = source(stage, chunk, kind, False)[...]
                     if stage < stages - 1:
                         sums[stage][chunk] = sums[stage][chunk] + mine
                         send(stage + 1, chunk, kind).start()
@@ -664,37 +688,68 @@
                             jnp.float32
                         )
 
+            for chunk in range(turn, chunks, kinds):
+
+                @pl.when(now == chunk)
+                def _():
+                    for load in loads(chunk):
+                        load.wait()
+
+            for rows in sizes:
+                spots = [spot for spot, item in enumerate(plan) if item[:2] == ("product", rows)]
+
+                @pl.when((now >= spots[0]) & (now <= spots[-1]))
+                def _():
+                    slot = lax.rem(now, 2)
+                    made = fold_product(x_ref[slot, :rows], y_ref[slot, :rows], links.devices())
+                    ring_ref[lax.rem(now, HOLD)] = made.reshape(ring_ref.shape[1:])
+
+            @pl.when(now < chunks)
+            def _():
+                send(0, now, turn).start()
+
+            for chunk in range((turn + 1) % kinds, chunks, kinds):
+
+                @pl.when(now + 1 == chunk)
+                def _():
+                    for load in loads(chunk):
+                        load.start()
+
         return carry
 
+    for load in loads(0):
+        load.start()
     slots = chunks + DELAY * stages
     lax.fori_loop(0, (slots + kinds - 1) // kinds, step, 0)
 
 
-def reduce_chunks(links, grads, collective_id):
-    chunks, _, rows, columns = grads.shape
-    stages = len(links.bits)
+def reduce_chunks(links, plan, sources, shape, width, collective_id):
+    stages, chunks = len(links.bits), len(plan)
     sums = [
-        pltpu.VMEM((chunks,) + (2,) * (stages - 1 - stage) + (rows, columns), jnp.bfloat16)
+        pltpu.VMEM((chunks,) + (2,) * (stages - 1 - stage) + shape, jnp.bfloat16)
         for stage in range(stages)
     ]
+    rows = max([item[1] for item in plan if item[0] == "product"] + [16])
     return pl.pallas_call(
-        functools.partial(reduce_kernel, links, chunks),
-        out_shape=jax.ShapeDtypeStruct((chunks, rows, columns), jnp.float32),
-        in_specs=[pl.BlockSpec(memory_space=pltpu.HBM)],
+        functools.partial(reduce_kernel, links, plan, len(sources)),
+        out_shape=jax.ShapeDtypeStruct((chunks,) + shape, jnp.float32),
+        in_specs=[pl.BlockSpec(memory_space=pltpu.HBM)] * len(sources),
         out_specs=pl.BlockSpec(memory_space=pltpu.VMEM),
         scratch_shapes=[
-            pltpu.VMEM((HOLD,) + (2,) * (stages - 1) + (rows, columns), jnp.bfloat16)
+            pltpu.VMEM((HOLD,) + (2,) * stages + shape, jnp.bfloat16),
+            pltpu.VMEM((2, rows, width), jnp.bfloat16),
+            pltpu.VMEM((2, rows, width), jnp.bfloat16),
         ]
         + sums
         + [
             pltpu.SemaphoreType.DMA((stages, chunks)),
             pltpu.SemaphoreType.DMA((stages, chunks)),
-            pltpu.SemaphoreType.DMA((HOLD,)),
+            pltpu.SemaphoreType.DMA((2, 2)),
         ],
         compiler_params=pltpu.CompilerParams(
-            collective_id=collective_id, has_side_effects=True, vmem_limit_bytes=58 << 20
+            collective_id=collective_id, has_side_effects=True, vmem_limit_bytes=60 << 20
         ),
-    )(grads.reshape((chunks,) + (2,) * stages + (rows, columns)))
+    )(*sources)
 
 
 def fold_grad(grad, devices, width):
@@ -872,53 +927,79 @@
 
 
 class Gradients:
-    def __init__(self, links, width, shapes):
-        self.links, self.width, self.shapes = links, width, shapes
-        self.starts, self.count, self.scattered = {}, 0, {}
-        for name, (rows, columns) in shapes.items():
-            self.starts[name] = self.count
-            self.count += rows // width * (columns // width)
-        self.chunks = None
-
-    def scatter(self, name, x, dy):
-        grad = transpose_product(x, dy).astype(jnp.bfloat16)
-        share = lax.psum_scatter(grad, ("dp", "fsdp"), scatter_dimension=0, tiled=True)
-        self.scattered[name] = share.astype(jnp.float32)
+    def __init__(self, links, width):
+        self.links, self.width = links, width
+        self.products, self.scattered = {}, {}
 
     def add(self, name, x, dy):
         if name in OFFLOADED:
-            self.scatter(name, x, dy)
-            return
-        devices, start = self.links.devices(), self.starts[name]
-        if self.width // devices % 8 == 0:
-            self.chunks = weight_chunks(
-                x, dy, self.chunks, start, self.count, devices, self.width
+            grad = transpose_product(x, dy).astype(jnp.bfloat16)
+            self.scattered[name] = lax.psum_scatter(
+                grad, ("dp", "fsdp"), scatter_dimension=0, tiled=True
             )
-            return
-        fresh = fold_grad(transpose_product(x, dy), devices, self.width)
-        if self.chunks is None:
-            self.chunks = jnp.zeros((self.count,) + fresh.shape[1:], fresh.dtype)
-        self.chunks = lax.dynamic_update_slice_in_dim(self.chunks, fresh, start, 0)
-
-    def shares(self, collective_id):
-        shares = reduce_chunks(self.links, self.chunks, collective_id)
-        devices = self.links.devices()
-        shapes = [(rows // devices, columns) for rows, columns in self.shapes.values()]
-        if self.width // devices % 8 == 0:
+        else:
+            self.products[name] = (x, dy)
+
+    def shares(self, collective_id, before):
+        width, devices = self.width, self.links.devices()
+        r = width // devices
+        aligned = r % 8 == 0
+        names = list(self.products)
+        size = {name: self.products[name][0].shape for name in names}
+        deep = {name: size[name][1] // width for name in names}
+        names.sort(key=lambda name: (deep[name] == 1, size[name][0]))
+        plan, sources, known = [], [], {}
+
+        def number(array):
+            if id(array) not in known:
+                known[id(array)] = len(sources)
+                sources.append(array)
+            return known[id(array)]
+
+        shapes = {}
+        for name in names:
+            x, dy = self.products[name]
+            shapes[name] = (x.shape[1] // devices, dy.shape[1])
+            wide = dy.shape[1] // width
+            if aligned and deep[name] == 1:
+                for part in range(wide):
+                    plan.append(("product", x.shape[0], (number(x), 0), (number(dy), part)))
+                continue
+            count = deep[name] * wide
+            if aligned:
+                made = weight_chunks(x, dy, None, 0, count, devices, width)
+            else:
+                made = fold_grad(transpose_product(x, dy), devices, width)
+            made = made.reshape((count,) + (2,) * len(self.links.bits) + made.shape[2:])
+            for part in range(count):
+                plan.append(("chunk", number(made), part))
+        before, sources[0] = lax.optimization_barrier((before, sources[0]))
+        shares = reduce_chunks(
+            self.links, plan, sources, (2 * r, width // 2), width, collective_id
+        )
+        if aligned:
+            scattered = list(self.scattered.values())
             result = pl.pallas_call(
-                functools.partial(unfold_kernel, self.width),
-                out_shape=[jax.ShapeDtypeStruct(shape, jnp.float32) for shape in shapes],
-            )(shares)
-            return dict(zip(self.shapes, result)) | self.scattered
-        result = dict(self.scattered)
-        for (name, (rows, columns)), shape in zip(self.shapes.items(), shapes):
-            start = self.starts[name]
-            count = rows // self.width * (columns // self.width)
+                functools.partial(unfold_kernel, width, len(scattered)),
+                out_shape=[jax.ShapeDtypeStruct(shape, jnp.float32) for shape in shapes.values()]
+                + [jax.ShapeDtypeStruct(share.shape, jnp.float32) for share in scattered],
+            )(shares, *scattered)
+            return dict(zip(list(shapes) + list(self.scattered), result)), before
+        result = {name: share.astype(jnp.float32) for name, share in self.scattered.items()}
+        start = 0
+        for name, shape in shapes.items():
+            count = deep[name] * shape[1] // width
             result[name] = unfold_share(shares[start : start + count], *shape)
-        return result
-
-
-def unfold_kernel(width, shares_ref, *out_refs):
+            start += count
+        return result, before
+
+
+def unfold_kernel(width, count, shares_ref, *refs):
+    scattered, out_refs = refs[:count], refs[count:]
+    if count:
+        for scattered_ref, out_ref in zip(scattered, out_refs[-count:]):
+            out_ref[...] = scattered_ref[...].astype(jnp.float32)
+        out_refs = out_refs[:-count]
     chunk, r, half = 0, shares_ref.shape[1] // 2, width // 2
     for out_ref in out_refs:
         for row in range(0, out_ref.shape[0], r):
@@ -988,31 +1069,12 @@
         decoder_outer,
     ]
     shards = dict(zip(NAMES, shards))
-    later = [shards.pop(name) for name in OFFLOADED]
+    later = [shards.pop(name) for name in LATER]
     weights = dict(zip(shards, gather_weights(links, list(shards.values()), 1)))
     weights["equery"], *later = lax.optimization_barrier((weights["equery"], *later))
-    for name, shard in zip(OFFLOADED, later):
+    for name, shard in zip(LATER, later):
         weights[name] = lax.all_gather(shard, "fsdp", axis=0, tiled=True)
-    order = [
-        "dinner",
-        "douter",
-        "einner",
-        "eouter",
-        "cproj",
-        "cquery",
-        "ckeyval",
-        "dproj",
-        "dquery",
-        "dkeyval",
-        "eproj",
-        "equery",
-        "ekeyval",
-    ]
-    grads = Gradients(
-        links,
-        encoder_query.shape[1],
-        {name: weights[name].shape for name in order if name not in OFFLOADED},
-    )
+    grads = Gradients(links, encoder_query.shape[1])
 
     enc_layout = (enc_segments, enc_segments, enc_bias, False)
     dec_layout = (dec_segments, dec_segments, dec_bias, True)
@@ -1100,13 +1162,12 @@
     flat = jnp.concatenate([gain_grads.reshape(-1)] + [grad.reshape(-1) for grad in table_grads])
     flat = links.total(flat.reshape(-1, TILE)).reshape(-1)
     width = gain_grads.shape[1]
-    flat, grads.chunks = lax.optimization_barrier((flat, grads.chunks))
+    shares, flat = grads.shares(0, flat)
     tables_grad = flat[5 * width :].reshape(2, NB, H)
     own = width // links.devices()
     gains_share = lax.dynamic_slice_in_dim(
         flat[: 5 * width].reshape(5, width), links.place() * own, own, 1
     ).T
-    shares = grads.shares(0)
     return (
         memory,
         dec_final.astype(jnp.bfloat16),

time: 537 us -> 499 us (0.929); the launches traced: 533 us -> 490 us
  Pallas kernels: 331 us -> 301 us
  waiting for transfers between devices: 33 us -> 7.34 us
  local copies, waits for them, and re-layouts: 20.1 us -> 29.3 us
  starting transfers between devices: 9.34 us -> 18.2 us
    all_gather x2 -> x1, waiting for transfers between devices: 31.5 us -> 0.02 us  [body(): weights[name] = lax.all_gather(shard, 'fsdp', axis=0, tiled=True)]
    pallas_call x11 -> x1, Pallas kernels: 36.6 us -> 6.7 us  [weight_chunks(): pl.pallas_call(functools.partial(weight_kernel, deep), out_shape=jax.Shap...]
    unnamed x268 -> x278, local copies, waits for them, and re-layouts: 14.1 us -> 23.2 us
    ppermute x6, starting transfers between devices: 9.18 us -> 17.7 us  [swap(): return lax.ppermute(value, axis, pairs)]
    ppermute x6, waiting for transfers between devices: 1.45 us -> 7.27 us  [swap(): return lax.ppermute(value, axis, pairs)]
  transfers between devices with their start and end apart: 10 -> 9, of which waited for: 3 -> 2; matrix products, arithmetic and copies ran while one was open for 21% -> 20% of each run, Pallas kernels for 45% -> 58%
where the time goes in v4:
time: 499 us; the launch traced here: 490 us
  Pallas kernels  301 us (60%)
  matrix products  105 us (21%)
  local copies, waits for them, and re-layouts  29.3 us (6%)
  starting transfers between devices  18.2 us (4%)
  between operations  16.2 us (3%)
  other arithmetic  12.8 us (3%)
  waiting for transfers between devices  7.34 us (1%)
    pallas_call x1, Pallas kernels, reduce_chunks(): pl.pallas_call(functools.partial(reduce_kernel, links, plan, len(sources)...  118 us
    pallas_call x1, Pallas kernels, gather_weights(): pl.pallas_call(functools.partial(gather_kernel, links, units, count), out...  71 us
    pallas_call x3, Pallas kernels, attend_backward(): pl.pallas_call(functools.partial(backward_kernel, spec), out_shape=[jax.S...  62.7 us
    dot_general x13, matrix products, product_transposed(): lax.dot_general(former, latter, (((1,), (1,)), ((), ())), preferred_eleme...  58.5 us
    pallas_call x3, Pallas kernels, attend_forward(): pl.pallas_call(functools.partial(forward_kernel, spec), out_shape=(jax.Sh...  39.3 us
    dot_general x13, matrix products, product(): return jnp.dot(former, latter, preferred_element_type=jnp.float32)  36.6 us
    unnamed x278, local copies, waits for them, and re-layouts  23.2 us
    ppermute x6, starting transfers between devices, swap(): return lax.ppermute(value, axis, pairs)  17.7 us
  transfers between devices with their start and end apart: 9, of which 2 were waited for; matrix products, arithmetic and copies ran while one was open for 20% of the time, Pallas kernels for 58%

profile of v4, /device:TPU:0, one launch (start us, length us, event | category | flops | bytes accessed | tf_op | source)
XLA Modules:
  0.0 489.9 jit_solution(8264433586857113070)
XLA Ops:
  7.2 0.7 pad_maximum_fusion
  8.1 0.7 pad_maximum_fusion.1
  8.8 3.0 collective-permute-start
  11.8 71.0 %shard_map.418 = (bf16[2,2,2,2,48,768]{5,4,3,2,1,0:T(8,128)(2,1)}, bf16[2,2,2,2,48,1536]{5,4,3,2,1,0:T(8,128)(2,1)}, bf16[2,2,2,2,48,768]{5,4,3,2,1,0:T(8,128)(2...) custom-call(bf16[2,2,2,48,768]{4,3,2,1,0:T(8,128)(2,1)} %bitcast.156, ...), custom_call_target="tpu_custom_call" | custom-call | tf_op jit(solution)/shard_map/pallas_call | solution.py:861
  83.0 0.6 compare_convert_fusion
  86.7 0.7 copy-done.125
  87.3 0.8 convolution_convert_fusion.4.k_ref.v_ref
  88.3 5.2 %shard_map.420 = (bf16[256,768]{1,0:T(8,128)(2,1)S(1)}, f32[6,2,256]{2,1,0:T(2,128)S(1)}) custom-call(s32[2,1]{1,0:T(2,128)S(1)} %broadcast_28_bounds_ref.2.bounds_ref, bf16[256,768]{1,0:T(8,128)(2,1)S(1)} %convolution_convert_fusion.10.q_ref, bf16[256,1536]{1,0:T(8,128)(2,1)S(1)} %convolution_convert_fusion.4.k_ref.v_ref, ...), custom_call_target="tpu_custom_call" | custom-call | flops 805306368 | bytes 8388608 | tf_op jit(solution)/shard_map/pallas_call | solution.py:390
  95.0 1.4 convolution_convert_fusion.6.q_ref
  96.5 0.8 copy-done.124
  97.3 2.8 convolution_convert_fusion.3.k_ref.v_ref
  100.8 1.2 copy-done.68
  102.2 25.3 %shard_map.419 = (bf16[1024,768]{1,0:T(8,128)(2,1)S(1)}, f32[6,2,1024]{2,1,0:T(2,128)S(1)}) custom-call(s32[2,4]{1,0:T(2,128)S(1)} %pad_add_fusion.bounds_ref, bf16[1024,768]{1,0:T(8,128)(2,1)S(1)} %convolution_convert_fusion.6.q_ref, bf16[1024,1536]{1,0:T(8,128)(2,1)S(1)} %convolution_convert_fusion.3.k_ref.v_ref, ...), custom_call_target="tpu_custom_call" | custom-call | flops 12884901888 | bytes 8388608 | tf_op jit(solution)/shard_map/pallas_call | solution.py:390
  127.6 1.5 multiply_reduce_fusion.2
  129.6 1.3 slice-done
  131.5 9.8 %multiply_convert_fusion = (bf16[1024,3072]{1,0:T(8,128)(2,1)S(1)}, f32[1024,3072]{1,0:T(8,128)}) fusion(bf16[1024,768]{1,0:T(8,128)(2,1)S(1)} %multiply_convert_fusion.2.refs_12_, bf16[768,3072]{1,0:T(8,128)(2,1)S(1)} %bitcast.169), kind=kOutput, calls=%fused_computation.9 | convolution fusion | flops 4860149760 | bytes 25165824 | tf_op jit(solution)/shard_map/dot_general | solution.py:466
  141.4 5.1 %add_convert_fusion.refs_10_ = bf16[1024,768]{1,0:T(8,128)(2,1)S(1)} fusion(f32[1024,768]{1,0:T(8,128)S(1)} %get-tuple-element.204, bf16[1024,3072]{1,0:T(8,128)(2,1)S(1)} %get-tuple-element.205.x_ref, bf16[3072,768]{1,0:T(8,128)(2,1)S(1)} %bitcast.173), kind=kOutput, calls=%fused_computation.42 | convolution fusion | flops 4833411072 | bytes 15728640 | tf_op jit(solution)/shard_map/dot_general | solution.py:466
  146.5 1.1 copy-done.74
  147.7 2.8 convolution_convert_fusion.2.k_ref.v_ref
  150.5 8.8 %shard_map.421 = (bf16[256,768]{1,0:T(8,128)(2,1)S(1)}, f32[6,2,256]{2,1,0:T(2,128)S(1)}) custom-call(s32[2,1]{1,0:T(2,128)S(1)} %broadcast_28_bounds_ref.2.bounds_ref, bf16[256,768]{1,0:T(8,128)(2,1)S(1)} %convolution_convert_fusion.9.q_ref, bf16[1024,1536]{1,0:T(8,128)(2,1)S(1)} %convolution_convert_fusion.2.k_ref.v_ref, ...), custom_call_target="tpu_custom_call" | custom-call | flops 3221225472 | bytes 8388608 | tf_op jit(solution)/shard_map/pallas_call | solution.py:390
  160.6 4.0 fusion.59
  164.7 1.7 copy-done.70
  166.4 4.5 convolution_convert_fusion.1
  170.8 6.6 %fusion.17 = bf16[256,3072]{1,0:T(8,128)(2,1)S(1)} fusion(f32[256,3072]{1,0:T(8,128)} %copy-done.70, bf16[3072,768]{1,0:T(8,128)(2,1)} %bitcast.164, bf16[256,768]{1,0:T(8,128)(2,1)S(1)} %copy-done.81, f32[256]{0:T(256)S(1)} %compare_convert_fusion.1), kind=kOutput, calls=%fused_computation.33 | convolution fusion | flops 1224278016 | bytes 9831424 | tf_op jit(solution)/shard_map/dot_general | solution.py:476
  177.5 4.4 multiply_reduce_fusion.3
  181.9 0.6 reshape.469
  182.6 1.2 fusion.64
  184.6 11.8 %shard_map.422 = (bf16[256,768]{1,0:T(8,128)(2,1)S(1)}, bf16[1024,1536]{1,0:T(8,128)(2,1)S(1)}) custom-call(s32[2,1]{1,0:T(2,128)S(1)} %broadcast_28_bounds_ref.2.bounds_ref, bf16[256,768]{1,0:T(8,128)(2,1)S(1)} %copy-done.15, bf16[1024,1536]{1,0:T(8,128)(2,1)} %copy-done.28, bf16[1024,1536]{1,0:T(8,128)(2,1)} %copy-done.28, ...), custom_call_target="tpu_custom_call" | custom-call | flops 8053063680 | bytes 16777216 | tf_op jit(solution)/shard_map/pallas_call | solution.py:426
  196.5 1.9 multiply_reduce_fusion.4
  200.1 4.8 fusion.22
  204.9 14.6 %fusion.6.refs_13_ = bf16[1024,3072]{1,0:T(8,128)(2,1)S(1)} fusion(f32[1024,3072]{1,0:T(8,128)} %get-tuple-element.206, bf16[1024,768]{1,0:T(8,128)(2,1)S(1)} %get-tuple-element.211.dy_ref, bf16[3072,768]{1,0:T(8,128)(2,1)} %bitcast.170), kind=kOutput, calls=%fused_computation.8 | convolution fusion | flops 4894752768 | bytes 25165824 | tf_op jit(solution)/shard_map/dot_general | solution.py:476
  219.6 10.2 %multiply_reduce_fusion = (f32[768]{0:T(1024)S(1)}, f32[1024]{0:T(1024)S(1)}, f32[1024,768]{1,0:T(8,128)S(1)}) fusion(f32[1024,768]{1,0:T(8,128)S(1)} %copy-done.51, f32[1024]{0:T(1024)S(1)} %copy-done.96, f32[768]{0:T(1024)S(1)} %copy-done.92, bf16[1024,3072]{1,0:T(8,128)(2,1)S(1)} %fusion.6.refs_13_, bf16[768,3072]{1,0:T(8,128)(2,1)} %bitcast.166), kind=kOutput, calls=%fused_computation.38 | convolution fusion | flops 4836554752 | bytes 17315840 | tf_op jit(solution)/shard_map/dot_general | solution.py:476
  229.8 2.5 fusion.62
  232.3 1.2 copy-done.53
  233.5 2.6 convolution_convert_fusion.5.do_ref
  236.1 3.6 convolution_convert_fusion
  239.8 1.0 copy-done.11
  240.8 1.4 copy-done.30
  242.2 1.4 copy-done.34
  243.7 39.3 %shard_map.423 = (bf16[1024,768]{1,0:T(8,128)(2,1)S(1)}, bf16[1024,1536]{1,0:T(8,128)(2,1)}, f32[12,5,8,256]{3,2,1,0:T(8,128)S(1)}) custom-call(s32[2,4]{1,0:T(2,128)S(1)} %pad_add_fusion.bounds_ref, bf16[1024,768]{1,0:T(8,128)(2,1)S(1)} %copy-done.30, bf16[1024,1536]{1,0:T(8,128)(2,1)} %copy-done.33, bf16[1024,1536]{1,0:T(8,128)(2,1)} %copy-done.33, ...), custom_call_target="tpu_custom_call" | custom-call | flops 32212254720 | bytes 16777216 | tf_op jit(solution)/shard_map/pallas_call | solution.py:426
  283.3 1.6 copy-done.60
  285.6 11.6 %shard_map.424 = (bf16[256,768]{1,0:T(8,128)(2,1)S(1)}, bf16[256,1536]{1,0:T(8,128)(2,1)S(1)}, f32[12,5,8,256]{3,2,1,0:T(8,128)S(1)}) custom-call(s32[2,1]{1,0:T(2,128)S(1)} %broadcast_28_bounds_ref.2.bounds_ref, bf16[256,768]{1,0:T(8,128)(2,1)S(1)} %copy-done.13, bf16[256,1536]{1,0:T(8,128)(2,1)S(1)} %copy-done.25, bf16[256,1536]{1,0:T(8,128)(2,1)S(1)} %copy-done.25, ...), custom_call_target="tpu_custom_call" | custom-call | flops 2013265920 | bytes 16777216 | tf_op jit(solution)/shard_map/pallas_call | solution.py:426
  297.8 2.3 fusion.29
  301.0 0.8 fusion.24
  302.8 0.8 fusion.23
  303.6 0.7 reshape.472
  304.3 5.4 %fusion.68 = f32[1024,768]{1,0:T(8,128)S(1)} fusion(bf16[1024,1536]{1,0:T(8,128)(2,1)} %get-tuple-element.85.refs_18_, bf16[768,1536]{1,0:T(8,128)(2,1)} %bitcast.174), kind=kOutput, calls=%fused_computation.156 | convolution fusion | flops 2415919104 | bytes 8650752 | tf_op jit(solution)/shard_map/dot_general | solution.py:476
  309.7 4.0 fusion.10
  313.8 0.8 stack.5
  314.6 0.7 maximum_bitcast_fusion
  315.3 2.5 collective-permute-start.1
  317.8 6.1 %fusion.25 = bf16[256,768]{1,0:T(8,128)(2,1)} fusion(f32[256,768]{1,0:T(8,128)S(1)} %copy-done.43, bf16[3072,768]{1,0:T(8,128)(2,1)} %bitcast.165, f32[256,3072]{1,0:T(8,128)} %copy-done.70), kind=kOutput, calls=%fused_computation.62 | convolution fusion | flops 1215430656 | bytes 9043968 | tf_op jit(solution)/shard_map/dot_general | solution.py:466
  324.0 12.0 %collective-permute-start.2 = (f32[36,128]{1,0:T(8,128)S(1)}, f32[36,128]{1,0:T(8,128)S(1)}, u32[]{:S(2)}, u32[]{:S(2)}) collective-permute-start(f32[36,128]{1,0:T(8,128)S(1)} %fusion.58), channel_id=1, source_target_pairs={{0,2},{2,0},{4,6},{6,4},{8,10},{10,8},{12,14},{14,12},{16,18},{18,... | collective-permute-start | bytes 55304 | tf_op jit(solution)/shard_map/ppermute | solution.py:569
  336.0 2.4 fusion.19
  338.6 2.9 copy-done.27
  341.5 6.7 %shard_map.425 = bf16[4,32,48,384]{3,2,1,0:T(8,128)(2,1)S(1)} custom-call(bf16[1024,3072]{1,0:T(8,128)(2,1)S(1)} %copy-done.27, bf16[1024,768]{1,0:T(8,128)(2,1)S(1)} %copy-done.32), custom_call_target="tpu_custom_call" | custom-call | flops 4831838208 | bytes 12582912 | tf_op jit(solution)/shard_map/pallas_call | solution.py:913
  348.2 2.1 copy-done
  350.4 3.7 collective-permute-done.4
  354.2 1.1 fusion.32
  355.3 3.5 collective-permute-done.5
  360.1 118.4 %shard_map.426.shares_ref = f32[20,48,384]{2,1,0:T(8,128)} custom-call(bf16[4,2,2,2,2,2,48,384]{7,6,5,4,3,2,1,0:T(8,128)(2,1)} %bitcast.129, bf16[256,768]{1,0:T(8,128)(2,1)} %copy-done.4, bf16[256,768]{1,0:T(8,128)(2,1)} %copy-done.66, bf16[256,768]{1,0:T(8,128)(2,1)} %copy-done.68, bf16[256,768]{1,0:T(8,128)(2,1)} %copy-done.5, ...), custom_call_target="tpu_custom_call" | custom-call | tf_op jit(solution)/shard_map/pallas_call | solution.py:733
  478.7 0.7 copy.87
  479.4 0.7 copy.86
  480.1 2.8 shard_map.427
  (346 shorter events, 15.0 us)
Async XLA Ops:
  7.2 153.4 %all-gather.2.cloned.1.call-start = ((), (), s32[]{:S(2)}) async-start(), calls=%async_computation.2 | async-start | bytes 7077888 | tf_op jit(solution)/shard_map/all_gather | solution.py:1076
  8.8 76.3 %collective-permute-start = (bf16[384,6]{0,1:T(8,128)(2,1)S(1)}, bf16[384,6]{0,1:T(8,128)(2,1)S(1)}, u32[]{:S(2)}, u32[]{:S(2)}) collective-permute-start(bf16[384,6]{0,1:T(8,128)(2,1)S(1)} %pad_maximum_fusion.1), channel_id=1, source_target_pairs={{0,1},{1,0},{2,3},{3,2},{4,5},{5,4},{6,7},{7,6},{8,9},{9,8},{10,11... | collective-permute-start | bytes 13832 | tf_op jit(solution)/shard_map/ppermute | solution.py:569
  11.8 71.1 %copy-start.22 = (s32[1024]{0:T(1024)S(1)}, s32[1024]{0:T(1024)}, u32[]{:S(2)}) copy-start(s32[1024]{0:T(1024)} %param.29) | copy-start | bytes 12292
  11.8 71.8 %copy-start.23 = (s32[256]{0:T(256)S(1)}, s32[256]{0:T(256)}, u32[]{:S(2)}) copy-start(s32[256]{0:T(256)} %param.30) | copy-start | bytes 3076
  11.8 71.8 %copy-start.56 = (bf16[256,768]{1,0:T(8,128)(2,1)S(1)}, bf16[256,768]{1,0:T(8,128)(2,1)}, u32[]{:S(2)}) copy-start(bf16[256,768]{1,0:T(8,128)(2,1)} %param.28) | copy-start | bytes 1179652
  82.9 397.2 %reduce-scatter.3.cloned.1.call-start = ((), (), s32[]{:S(2)}) async-start(), calls=%async_computation.3 | async-start | bytes 4866048 | tf_op jit(solution)/shard_map/reduce_scatter | solution.py:937
  84.6 9.5 %copy-start.93 = (f32[1024]{0:T(1024)}, f32[1024]{0:T(1024)S(1)}, u32[]{:S(2)}) copy-start(f32[1024]{0:T(1024)S(1)} %fusion.51) | copy-start | bytes 12292
  85.3 14.9 %copy-start.82 = (f32[768]{0:T(1024)}, f32[768]{0:T(1024)S(1)}, u32[]{:S(2)}) copy-start(f32[768]{0:T(1024)S(1)} %get-tuple-element.182) | copy-start | bytes 9220
  85.3 97.3 %copy-start.79 = (f32[768]{0:T(1024)}, f32[768]{0:T(1024)S(1)}, u32[]{:S(2)}) copy-start(f32[768]{0:T(1024)S(1)} %get-tuple-element.180) | copy-start | bytes 9220
  85.3 43.9 %copy-start.91 = (f32[768]{0:T(1024)}, f32[768]{0:T(1024)S(1)}, u32[]{:S(2)}) copy-start(f32[768]{0:T(1024)S(1)} %get-tuple-element.183) | copy-start | bytes 9220
  85.7 16.5 %copy-start.20 = (f32[12,5,256]{2,1,0:T(8,128)}, f32[12,5,256]{2,1,0:T(8,128)S(1)}, u32[]{:S(2)}) copy-start(f32[12,5,256]{2,1,0:T(8,128)S(1)} %copy.78.rest_0_) | copy-start | bytes 184324
  94.1 65.9 %copy-start.44 = (f32[256,768]{1,0:T(8,128)}, f32[256,768]{1,0:T(8,128)S(1)}, u32[]{:S(2)}) copy-start(f32[256,768]{1,0:T(8,128)S(1)} %get-tuple-element.202) | copy-start | bytes 2359300
  100.2 27.4 %copy-start.33 = (bf16[1024,1536]{1,0:T(8,128)(2,1)}, bf16[1024,1536]{1,0:T(8,128)(2,1)S(1)}, u32[]{:S(2)}) copy-start(bf16[1024,1536]{1,0:T(8,128)(2,1)S(1)} %convolution_convert_fusion.3.k_ref.v_ref) | copy-start | bytes 9437188
  102.0 48.5 %copy-start.14 = (bf16[256,768]{1,0:T(8,128)(2,1)}, bf16[256,768]{1,0:T(8,128)(2,1)S(1)}, u32[]{:S(2)}) copy-start(bf16[256,768]{1,0:T(8,128)(2,1)S(1)} %convolution_convert_fusion.9.q_ref) | copy-start | bytes 1179652
  102.2 48.3 %copy-start.9 = (s32[1024,128]{1,0:T(8,128)}, s32[1024,128]{1,0:T(8,128)S(1)}, u32[]{:S(2)}) copy-start(s32[1024,128]{1,0:T(8,128)S(1)} %broadcast_in_dim.27.segk_ref) | copy-start | bytes 1572868
  102.2 25.4 %copy-start.130 = (bf16[2,2,2,2,48,768]{5,4,3,2,1,0:T(8,128)(2,1)S(1)}, bf16[2,2,2,2,48,768]{5,4,3,2,1,0:T(8,128)(2,1)}, u32[]{:S(2)}) copy-start(bf16[2,2,2,2,48,768]{5,4,3,2,1,0:T(8,128)(2,1)} %get-tuple-element.68) | copy-start | bytes 3538948
  129.2 12.1 %copy-start.105 = (f32[1024]{0:T(1024)}, f32[1024]{0:T(1024)S(1)}, u32[]{:S(2)}) copy-start(f32[1024]{0:T(1024)S(1)} %get-tuple-element.203) | copy-start | bytes 12292
  129.2 12.1 %copy-start.50 = (f32[1024,768]{1,0:T(8,128)}, f32[1024,768]{1,0:T(8,128)S(1)}, u32[]{:S(2)}) copy-start(f32[1024,768]{1,0:T(8,128)S(1)} %get-tuple-element.204) | copy-start | bytes 9437188
  129.2 12.1 %copy-start.95 = (f32[1024]{0:T(1024)}, f32[1024]{0:T(1024)S(1)}, u32[]{:S(2)}) copy-start(f32[1024]{0:T(1024)S(1)} %fusion.52) | copy-start | bytes 12292
  129.3 12.1 %slice-start.2 = ((s8[4718592]{0:T(1024)(128)(4,1)}), s8[4194304]{0:T(1024)(128)(4,1)S(1)}, s32[]{:S(2)}) async-start(s8[4718592]{0:T(1024)(128)(4,1)} %bitcast.171), calls=%async_computation.7 | async-start | bytes 8388608
  129.6 11.7 %copy-start.55 = (bf16[1024,768]{1,0:T(8,128)(2,1)}, bf16[1024,768]{1,0:T(8,128)(2,1)S(1)}, u32[]{:S(2)}) copy-start(bf16[1024,768]{1,0:T(8,128)(2,1)S(1)} %multiply_convert_fusion.2.refs_12_) | copy-start | bytes 4718596
  131.5 9.9 %slice-start.3 = ((s8[4718592]{0:T(1024)(128)(4,1)}), s8[524288]{0:T(1024)(128)(4,1)S(1)}, s32[]{:S(2)}) async-start(s8[4718592]{0:T(1024)(128)(4,1)} %bitcast.171), calls=%async_computation.8 | async-start | bytes 1048576
  150.5 9.5 %copy-start.63 = (bf16[2,2,2,2,48,768]{5,4,3,2,1,0:T(8,128)(2,1)S(1)}, bf16[2,2,2,2,48,768]{5,4,3,2,1,0:T(8,128)(2,1)}, u32[]{:S(2)}) copy-start(bf16[2,2,2,2,48,768]{5,4,3,2,1,0:T(8,128)(2,1)} %get-tuple-element.78) | copy-start | bytes 3538948
  160.6 22.0 %copy-start.41 = (f32[256,768]{1,0:T(8,128)}, f32[256,768]{1,0:T(8,128)S(1)}, u32[]{:S(2)}) copy-start(f32[256,768]{1,0:T(8,128)S(1)} %get-tuple-element.208) | copy-start | bytes 2359300
  160.6 22.0 %copy-start.87 = (f32[256]{0:T(256)}, f32[256]{0:T(256)S(1)}, u32[]{:S(2)}) copy-start(f32[256]{0:T(256)S(1)} %fusion.57) | copy-start | bytes 3076
  184.6 11.9 %copy-start.45 = (f32[256,768]{1,0:T(8,128)S(1)}, f32[256,768]{1,0:T(8,128)}, u32[]{:S(2)}) copy-start(f32[256,768]{1,0:T(8,128)} %copy-done.44) | copy-start | bytes 2359300
  184.6 11.9 %copy-start.65 = (bf16[2,2,2,2,48,768]{5,4,3,2,1,0:T(8,128)(2,1)S(1)}, bf16[2,2,2,2,48,768]{5,4,3,2,1,0:T(8,128)(2,1)}, u32[]{:S(2)}) copy-start(bf16[2,2,2,2,48,768]{5,4,3,2,1,0:T(8,128)(2,1)} %get-tuple-element.75) | copy-start | bytes 3538948
  184.6 11.9 %copy-start.83 = (f32[768]{0:T(1024)S(1)}, f32[768]{0:T(1024)}, u32[]{:S(2)}) copy-start(f32[768]{0:T(1024)} %copy-done.82) | copy-start | bytes 9220
  184.6 11.9 %copy-start.108 = (f32[256]{0:T(256)S(1)}, f32[256]{0:T(256)}, u32[]{:S(2)}) copy-start(f32[256]{0:T(256)} %copy-done.107) | copy-start | bytes 3076
  199.6 280.5 %reduce-scatter.5.cloned.1.call-start = ((), (), s32[]{:S(2)}) async-start(), calls=%async_computation.4 | async-start | bytes 4866048 | tf_op jit(solution)/shard_map/reduce_scatter | solution.py:937
  204.9 14.6 %copy-start.31 = (bf16[1024,768]{1,0:T(8,128)(2,1)}, bf16[1024,768]{1,0:T(8,128)(2,1)S(1)}, u32[]{:S(2)}) copy-start(bf16[1024,768]{1,0:T(8,128)(2,1)S(1)} %get-tuple-element.211.dy_ref) | copy-start | bytes 4718596
  204.9 14.6 %copy-start.51 = (f32[1024,768]{1,0:T(8,128)S(1)}, f32[1024,768]{1,0:T(8,128)}, u32[]{:S(2)}) copy-start(f32[1024,768]{1,0:T(8,128)} %copy-done.50) | copy-start | bytes 9437188
  204.9 14.6 %copy-start.92 = (f32[768]{0:T(1024)S(1)}, f32[768]{0:T(1024)}, u32[]{:S(2)}) copy-start(f32[768]{0:T(1024)} %copy-done.91) | copy-start | bytes 9220
  204.9 14.6 %copy-start.96 = (f32[1024]{0:T(1024)S(1)}, f32[1024]{0:T(1024)}, u32[]{:S(2)}) copy-start(f32[1024]{0:T(1024)} %copy-done.95) | copy-start | bytes 12292
  219.5 10.2 %copy-start.58 = (bf16[1024,3072]{1,0:T(8,128)(2,1)}, bf16[1024,3072]{1,0:T(8,128)(2,1)S(1)}, u32[]{:S(2)}) copy-start(bf16[1024,3072]{1,0:T(8,128)(2,1)S(1)} %fusion.6.refs_13_) | copy-start | bytes 18874372
  219.6 10.2 %copy-start.106 = (f32[1024]{0:T(1024)S(1)}, f32[1024]{0:T(1024)}, u32[]{:S(2)}) copy-start(f32[1024]{0:T(1024)} %copy-done.105) | copy-start | bytes 12292
  219.6 10.2 %copy-start.75 = (bf16[1024,768]{1,0:T(8,128)(2,1)S(1)}, bf16[1024,768]{1,0:T(8,128)(2,1)}, u32[]{:S(2)}) copy-start(bf16[1024,768]{1,0:T(8,128)(2,1)} %param.31) | copy-start | bytes 4718596
  219.6 10.2 %copy-start.104 = (f32[1024]{0:T(1024)S(1)}, f32[1024]{0:T(1024)}, u32[]{:S(2)}) copy-start(f32[1024]{0:T(1024)} %compare_convert_fusion) | copy-start | bytes 12292
  243.6 39.4 %copy-start.46 = (f32[256,768]{1,0:T(8,128)S(1)}, f32[256,768]{1,0:T(8,128)}, u32[]{:S(2)}) copy-start(f32[256,768]{1,0:T(8,128)} %copy-done.44) | copy-start | bytes 2359300
  243.7 39.4 %copy-start.72 = (f32[256,768]{1,0:T(8,128)S(1)}, f32[256,768]{1,0:T(8,128)}, u32[]{:S(2)}) copy-start(f32[256,768]{1,0:T(8,128)} %get-tuple-element.194) | copy-start | bytes 2359300
  243.7 39.4 %copy-start.73 = (f32[256,768]{1,0:T(8,128)S(1)}, f32[256,768]{1,0:T(8,128)}, u32[]{:S(2)}) copy-start(f32[256,768]{1,0:T(8,128)} %get-tuple-element.210) | copy-start | bytes 2359300
  243.7 39.4 %copy-start.84 = (f32[768]{0:T(1024)S(1)}, f32[768]{0:T(1024)}, u32[]{:S(2)}) copy-start(f32[768]{0:T(1024)} %copy-done.82) | copy-start | bytes 9220
  243.7 39.4 %copy-start.109 = (f32[256]{0:T(256)S(1)}, f32[256]{0:T(256)}, u32[]{:S(2)}) copy-start(f32[256]{0:T(256)} %copy-done.107) | copy-start | bytes 3076
  243.7 39.4 %copy-start.122 = (f32[256]{0:T(256)S(1)}, f32[256]{0:T(256)}, u32[]{:S(2)}) copy-start(f32[256]{0:T(256)} %multiply_multiply_fusion.7) | copy-start | bytes 3076
  283.0 26.7 %copy-start.7 = (bf16[1024,768]{1,0:T(8,128)(2,1)}, bf16[1024,768]{1,0:T(8,128)(2,1)S(1)}, u32[]{:S(2)}) copy-start(bf16[1024,768]{1,0:T(8,128)(2,1)S(1)} %get-tuple-element.84.refs_17_) | copy-start | bytes 4718596
  283.3 13.9 %copy-start.69 = (bf16[256,768]{1,0:T(8,128)(2,1)}, bf16[256,768]{1,0:T(8,128)(2,1)S(1)}, u32[]{:S(2)}) copy-start(bf16[256,768]{1,0:T(8,128)(2,1)S(1)} %get-tuple-element.189.refs_6_) | copy-start | bytes 1179652
  285.5 11.7 %copy-start.62 = (bf16[2,2,2,2,48,768]{5,4,3,2,1,0:T(8,128)(2,1)S(1)}, bf16[2,2,2,2,48,768]{5,4,3,2,1,0:T(8,128)(2,1)}, u32[]{:S(2)}) copy-start(bf16[2,2,2,2,48,768]{5,4,3,2,1,0:T(8,128)(2,1)} %get-tuple-element.71) | copy-start | bytes 3538948
  285.5 12.2 %copy-start.57 = (bf16[256,768]{1,0:T(8,128)(2,1)S(1)}, bf16[256,768]{1,0:T(8,128)(2,1)}, u32[]{:S(2)}) copy-start(bf16[256,768]{1,0:T(8,128)(2,1)} %param.28) | copy-start | bytes 1179652
  285.5 12.2 %copy-start.98 = (f32[768]{0:T(1024)S(1)}, f32[768]{0:T(1024)}, u32[]{:S(2)}) copy-start(f32[768]{0:T(1024)} %copy-done.97) | copy-start | bytes 9220
  285.6 12.2 %copy-start.114 = (f32[256]{0:T(256)S(1)}, f32[256]{0:T(256)}, u32[]{:S(2)}) copy-start(f32[256]{0:T(256)} %copy-done.113) | copy-start | bytes 3076
  285.6 12.2 %copy-start.126 = (bf16[2,2,2,2,48,1536]{5,4,3,2,1,0:T(8,128)(2,1)S(1)}, bf16[2,2,2,2,48,1536]{5,4,3,2,1,0:T(8,128)(2,1)}, u32[]{:S(2)}) copy-start(bf16[2,2,2,2,48,1536]{5,4,3,2,1,0:T(8,128)(2,1)} %get-tuple-element.72) | copy-start | bytes 7077892
  301.9 12.7 %copy-start.101 = (f32[384]{0:T(512)}, f32[384]{0:T(512)S(1)}, u32[]{:S(2)}) copy-start(f32[384]{0:T(512)S(1)} %reshape.474) | copy-start | bytes 4612
  315.3 20.7 %copy-start.49 = (bf16[1024,768]{1,0:T(8,128)(2,1)S(1)}, bf16[1024,768]{1,0:T(8,128)(2,1)}, u32[]{:S(2)}) copy-start(bf16[1024,768]{1,0:T(8,128)(2,1)} %param.27) | copy-start | bytes 4718596
  315.3 20.7 %copy-start.52 = (f32[1024,768]{1,0:T(8,128)S(1)}, f32[1024,768]{1,0:T(8,128)}, u32[]{:S(2)}) copy-start(f32[1024,768]{1,0:T(8,128)} %get-tuple-element.192) | copy-start | bytes 9437188
  315.3 20.7 %copy-start.71 = (f32[1024,768]{1,0:T(8,128)S(1)}, f32[1024,768]{1,0:T(8,128)}, u32[]{:S(2)}) copy-start(f32[1024,768]{1,0:T(8,128)} %get-tuple-element.214) | copy-start | bytes 9437188
  315.3 8.7 %collective-permute-start.1 = (f32[36,128]{1,0:T(8,128)S(1)}, f32[36,128]{1,0:T(8,128)S(1)}, u32[]{:S(2)}, u32[]{:S(2)}) collective-permute-start(f32[36,128]{1,0:T(8,128)S(1)} %maximum_bitcast_fusion), channel_id=1, source_target_pairs={{0,1},{1,0},{2,3},{3,2},{4,5},{5,4},{6,7},{7,6},{8,9},{9,8},{10,11... | collective-permute-start | bytes 55304 | tf_op jit(solution)/shard_map/ppermute | solution.py:569
  324.0 14.4 %collective-permute-start.2 = (f32[36,128]{1,0:T(8,128)S(1)}, f32[36,128]{1,0:T(8,128)S(1)}, u32[]{:S(2)}, u32[]{:S(2)}) collective-permute-start(f32[36,128]{1,0:T(8,128)S(1)} %fusion.58), channel_id=1, source_target_pairs={{0,2},{2,0},{4,6},{6,4},{8,10},{10,8},{12,14},{14,12},{16,18},{18,... | collective-permute-start | bytes 55304 | tf_op jit(solution)/shard_map/ppermute | solution.py:569
  338.5 11.8 %collective-permute-start.3 = (f32[36,128]{1,0:T(8,128)S(1)}, f32[36,128]{1,0:T(8,128)S(1)}, u32[]{:S(2)}, u32[]{:S(2)}) collective-permute-start(f32[36,128]{1,0:T(8,128)S(1)} %fusion.124), channel_id=1, source_target_pairs={{0,4},{2,6},{4,0},{6,2},{8,12},{10,14},{12,8},{14,10},{16,20},{18,... | collective-permute-start | bytes 55304 | tf_op jit(solution)/shard_map/ppermute | solution.py:569
  341.5 8.9 %copy-start.117 = (f32[256]{0:T(256)S(1)}, f32[256]{0:T(256)}, u32[]{:S(2)}) copy-start(f32[256]{0:T(256)} %copy-done.116) | copy-start | bytes 3076
  341.5 8.9 %copy-start.123 = (f32[256]{0:T(256)S(1)}, f32[256]{0:T(256)}, u32[]{:S(2)}) copy-start(f32[256]{0:T(256)} %get-tuple-element.179) | copy-start | bytes 3076
  341.5 12.7 %copy-start.78 = (f32[256,768]{1,0:T(8,128)S(1)}, f32[256,768]{1,0:T(8,128)}, u32[]{:S(2)}) copy-start(f32[256,768]{1,0:T(8,128)} %get-tuple-element.215) | copy-start | bytes 2359300
  341.5 12.7 %copy-start.115 = (f32[256]{0:T(256)S(1)}, f32[256]{0:T(256)}, u32[]{:S(2)}) copy-start(f32[256]{0:T(256)} %copy-done.113) | copy-start | bytes 3076
  350.3 3.8 collective-permute-start.4
  354.2 4.7 collective-permute-start.5
  (81 other events, 286.2 us)
Sparse Core Ops, SparseCore 0:
  83.0 62.0 all-gather.1
  199.7 107.7 reduce-scatter.2
  313.9 120.7 reduce-scatter.4

commit v5 on v4

--- a/solution.py
+++ b/solution.py
@@ -24,7 +24,7 @@
 LAG = 3
 DELAY = 2
 HOLD = DELAY + 1
-OFFLOADED = ("dinner", "douter")
+OFFLOADED = ("douter",)
 LATER = ("dinner",)
 NAMES = (
     "equery",
@@ -529,17 +529,79 @@
     return (stream + product(hidden, wouter), (normed, before, hidden))
 
 
+def feed_backward_kernel(g_ref, v_ref, gain_ref, pre_ref, wi_ref, wf_ref, *outs):
+    out_ref, dpre_ref, low_ref, dgain_ref = outs
+    gradient = g_ref[...]
+    low = gradient.astype(jnp.bfloat16)
+    low_ref[...] = low
+    features, hidden = wi_ref.shape
+    curve, bend = math.sqrt(2 / math.pi), 0.044715
+    dnormed = None
+    for start in range(0, hidden, features):
+        span = slice(start, start + features)
+        dhidden = dot_rows(low, wf_ref[span, :])
+        value = pre_ref[:, span]
+        square = value * value
+        bent = jnp.tanh(value * (curve + curve * bend * square))
+        slope = 0.5 * (1.0 + bent) + (0.5 * value) * (1.0 - bent * bent) * (
+            curve + 3 * curve * bend * square
+        )
+        dpre = (dhidden * slope).astype(jnp.bfloat16)
+        dpre_ref[:, span] = dpre
+        part = dot_rows(dpre, wi_ref[:, span])
+        dnormed = part if dnormed is None else dnormed + part
+    value = v_ref[...]
+    scale = lax.rsqrt(jnp.mean(value * value, axis=1, keepdims=True) + EPSILON)
+    pulled = dnormed * gain_ref[...]
+    inner = jnp.mean(pulled * value, axis=1, keepdims=True)
+    out_ref[...] = gradient + scale * pulled - value * (scale * scale * scale * inner)
+    dgain = fold_rows(dnormed * value * scale, jnp.add)
+
+    @pl.when(pl.program_id(0) == 0)
+    def _():
+        dgain_ref[...] = dgain
+
+    @pl.when(pl.program_id(0) > 0)
+    def _():
+        dgain_ref[...] += dgain
+
+
 def feed_backward(grads, names, stream, norm_gain, winner, wouter, stored, gradient):
     normed, before, hidden = stored
-    gradient_low = gradient.astype(jnp.bfloat16)
-    grads.add(names[1], hidden, gradient_low)
-    dhidden = product_transposed(gradient_low, wouter)
-    gate_value, gate_pullback = jax.vjp(smooth_gate, before)
-    dbefore = gate_pullback(dhidden)[0].astype(jnp.bfloat16)
-    grads.add(names[0], normed, dbefore)
-    dnormed = product_transposed(dbefore, winner)
-    dstream, dgain = norm_backward(stream, norm_gain, dnormed)
-    return (gradient + dstream, dgain)
+    rows, features = stream.shape
+    wide = before.shape[1]
+    block = min(256, rows)
+    row = pl.BlockSpec((block, features), lambda step: (step, 0))
+    row_wide = pl.BlockSpec((block, wide), lambda step: (step, 0))
+    once = pl.Buffered(1)
+    dstream, dbefore, low, dgain = pl.pallas_call(
+        feed_backward_kernel,
+        out_shape=[
+            jax.ShapeDtypeStruct((rows, features), jnp.float32),
+            jax.ShapeDtypeStruct((rows, wide), jnp.bfloat16),
+            jax.ShapeDtypeStruct((rows, features), jnp.bfloat16),
+            jax.ShapeDtypeStruct((8, features), jnp.float32),
+        ],
+        grid=(rows // block,),
+        in_specs=[
+            row,
+            row,
+            pl.BlockSpec((1, features), lambda step: (0, 0)),
+            row_wide,
+            pl.BlockSpec((features, wide), lambda step: (0, 0), pipeline_mode=once),
+            pl.BlockSpec((wide, features), lambda step: (0, 0), pipeline_mode=once),
+        ],
+        out_specs=[row, row_wide, row, pl.BlockSpec((8, features), lambda step: (0, 0))],
+        compiler_params=pltpu.CompilerParams(vmem_limit_bytes=48 << 20),
+        cost_estimate=pl.CostEstimate(
+            flops=4 * rows * features * wide,
+            transcendentals=rows * wide,
+            bytes_accessed=rows * wide * 6 + 4 * features * wide + rows * features * 14,
+        ),
+    )(gradient, stream, norm_gain[None, :], before, winner, wouter)
+    dstream = grads.add(names[1], hidden, low, dstream)
+    dstream = grads.add(names[0], normed, dbefore, dstream)
+    return (dstream, jnp.sum(dgain, axis=0))
 
 
 def index_bits(devices):
@@ -567,11 +629,6 @@
     def swap(self, value, axis, bit):
         pairs = [(place, place ^ (1 << bit)) for place in range(self.sizes[axis])]
         return lax.ppermute(value, axis, pairs)
-
-    def total(self, value):
-        for key in self.bits:
-            value = value + self.swap(value, *key)
-        return value
 
     def gather_small(self, shard):
         other = self.swap(shard, "fsdp", 0)
@@ -600,11 +657,14 @@
     return total.astype(jnp.bfloat16)
 
 
-def reduce_kernel(links, plan, count, *refs):
+def reduce_kernel(links, plan, sides, count, *refs):
     stages, chunks = len(links.bits), len(plan)
-    sources, (out_ref, ring_ref, x_ref, y_ref) = refs[:count], refs[count : count + 4]
-    rest = refs[count + 4 :]
-    sums, (send_sem, recv_sem, load_sem) = rest[:stages], rest[stages:]
+    sources, (value_ref, out_ref, total_ref) = refs[:count], refs[count : count + 3]
+    ring_ref, x_ref, y_ref, part_ref, come_ref = refs[count + 3 : count + 8]
+    deep_ref, side_x_ref, side_y_ref = refs[count + 8 : count + 11]
+    rest = refs[count + 11 :]
+    sums, rest = rest[:stages], rest[stages:]
+    send_sem, recv_sem, load_sem, part_sem, come_sem, side_sem = rest
     halvings = []
     for order in links.orders():
         left = list(reversed(links.bits))
@@ -642,6 +702,16 @@
             device_id_type=pl.DeviceIdType.MESH,
         )
 
+    def trade(stage):
+        return pltpu.make_async_remote_copy(
+            src_ref=part_ref.at[stage],
+            dst_ref=come_ref.at[stage],
+            send_sem=part_sem.at[stage],
+            recv_sem=come_sem.at[stage],
+            device_id=links.partner(*links.bits[stage]),
+            device_id_type=pl.DeviceIdType.MESH,
+        )
+
     def loads(chunk):
         item = plan[chunk]
         if item[0] == "chunk":
@@ -649,6 +719,12 @@
             return [
                 pltpu.make_async_copy(
                     sources[which].at[index], ring_ref.at[chunk % HOLD], load_sem.at[chunk % 2, 0]
+                )
+            ]
+        if item[0] == "kept":
+            return [
+                pltpu.make_async_copy(
+                    deep_ref.at[item[1]], ring_ref.at[chunk % HOLD], load_sem.at[chunk % 2, 0]
                 )
             ]
         _, rows, *operands = item
@@ -666,9 +742,52 @@
             )
         return result
 
+    def side_loads(side):
+        width = x_ref.shape[2]
+        return [
+            pltpu.make_async_copy(
+                sources[which].at[:, column * width : (column + 1) * width],
+                (side_x_ref, side_y_ref)[place],
+                side_sem.at[place],
+            )
+            for place, (which, column) in enumerate(sides[side])
+        ]
+
+    def make_side(side):
+        deep = len(sides)
+        total = lax.dot_general(
+            side_x_ref[...],
+            side_y_ref[...],
+            (((0,), (0,)), ((), ())),
+            preferred_element_type=jnp.float32,
+        )
+        rows, columns = total.shape
+        half, r = columns // 2, ring_ref.shape[-2] // 2
+        total = total.reshape(rows // deep // r, deep, r, columns)
+        spot = tuple((side >> bit) & 1 for bit in reversed(range(index_bits(deep))))
+        for part in range(deep):
+            piece = total[:, part]
+            piece = jnp.concatenate([piece[:, :, :half], piece[:, :, half:]], axis=1)
+            target = (part,) + spot
+            deep_ref[target] = piece.astype(jnp.bfloat16).reshape(
+                deep_ref.shape[len(target) :]
+            )
+
     sizes = sorted({item[1] for item in plan if item[0] == "product"})
 
     def step(group, carry):
+        for stage in range(stages):
+
+            @pl.when(group == stage + 1)
+            def _():
+                trade(stage).wait()
+                total = part_ref[stage] + come_ref[stage]
+                if stage < stages - 1:
+                    part_ref[stage + 1] = total
+                    trade(stage + 1).start()
+                else:
+                    total_ref[...] = total
+
         for turn in range(kinds):
             now = group * kinds + turn
 
@@ -708,6 +827,24 @@
             def _():
                 send(0, now, turn).start()
 
+            for side in range(len(sides)):
+                spot = 2 * side + 2
+
+                if (spot - 1) % kinds == turn:
+
+                    @pl.when(now == spot - 1)
+                    def _():
+                        for load in side_loads(side):
+                            load.start()
+
+                if spot % kinds == turn:
+
+                    @pl.when(now == spot)
+                    def _():
+                        for load in side_loads(side):
+                            load.wait()
+                        make_side(side)
+
             for chunk in range((turn + 1) % kinds, chunks, kinds):
 
                 @pl.when(now + 1 == chunk)
@@ -719,11 +856,13 @@
 
     for load in loads(0):
         load.start()
+    part_ref[0] = value_ref[...]
+    trade(0).start()
     slots = chunks + DELAY * stages
     lax.fori_loop(0, (slots + kinds - 1) // kinds, step, 0)
 
 
-def reduce_chunks(links, plan, sources, shape, width, collective_id):
+def reduce_chunks(links, plan, sides, sources, value, shape, width, collective_id):
     stages, chunks = len(links.bits), len(plan)
     sums = [
         pltpu.VMEM((chunks,) + (2,) * (stages - 1 - stage) + shape, jnp.bfloat16)
@@ -731,25 +870,37 @@
     ]
     rows = max([item[1] for item in plan if item[0] == "product"] + [16])
     return pl.pallas_call(
-        functools.partial(reduce_kernel, links, plan, len(sources)),
-        out_shape=jax.ShapeDtypeStruct((chunks,) + shape, jnp.float32),
-        in_specs=[pl.BlockSpec(memory_space=pltpu.HBM)] * len(sources),
-        out_specs=pl.BlockSpec(memory_space=pltpu.VMEM),
+        functools.partial(reduce_kernel, links, plan, sides, len(sources)),
+        out_shape=[
+            jax.ShapeDtypeStruct((chunks,) + shape, jnp.float32),
+            jax.ShapeDtypeStruct(value.shape, jnp.float32),
+        ],
+        in_specs=[pl.BlockSpec(memory_space=pltpu.HBM)] * len(sources)
+        + [pl.BlockSpec(memory_space=pltpu.VMEM)],
+        out_specs=[pl.BlockSpec(memory_space=pltpu.VMEM)] * 2,
         scratch_shapes=[
             pltpu.VMEM((HOLD,) + (2,) * stages + shape, jnp.bfloat16),
             pltpu.VMEM((2, rows, width), jnp.bfloat16),
             pltpu.VMEM((2, rows, width), jnp.bfloat16),
+            pltpu.VMEM((stages,) + value.shape, jnp.float32),
+            pltpu.VMEM((stages,) + value.shape, jnp.float32),
+            pltpu.VMEM((max(1, len(sides)),) + (2,) * stages + shape, jnp.bfloat16),
+            pltpu.VMEM((rows, width), jnp.bfloat16),
+            pltpu.VMEM((rows, width), jnp.bfloat16),
         ]
         + sums
         + [
             pltpu.SemaphoreType.DMA((stages, chunks)),
             pltpu.SemaphoreType.DMA((stages, chunks)),
             pltpu.SemaphoreType.DMA((2, 2)),
+            pltpu.SemaphoreType.DMA((stages,)),
+            pltpu.SemaphoreType.DMA((stages,)),
+            pltpu.SemaphoreType.DMA((2,)),
         ],
         compiler_params=pltpu.CompilerParams(
             collective_id=collective_id, has_side_effects=True, vmem_limit_bytes=60 << 20
         ),
-    )(*sources)
+    )(*sources, value)
 
 
 def fold_grad(grad, devices, width):
@@ -931,23 +1082,31 @@
         self.links, self.width = links, width
         self.products, self.scattered = {}, {}
 
-    def add(self, name, x, dy):
+    def add(self, name, x, dy, carry=None):
         if name in OFFLOADED:
             grad = transpose_product(x, dy).astype(jnp.bfloat16)
+            if carry is not None:
+                grad, carry = lax.optimization_barrier((grad, carry))
             self.scattered[name] = lax.psum_scatter(
                 grad, ("dp", "fsdp"), scatter_dimension=0, tiled=True
             )
         else:
             self.products[name] = (x, dy)
-
-    def shares(self, collective_id, before):
+        return carry
+
+    def shares(self, collective_id, value):
         width, devices = self.width, self.links.devices()
         r = width // devices
         aligned = r % 8 == 0
         names = list(self.products)
         size = {name: self.products[name][0].shape for name in names}
         deep = {name: size[name][1] // width for name in names}
-        names.sort(key=lambda name: (deep[name] == 1, size[name][0]))
+        tallest = max(rows for rows, _ in size.values())
+        split = [name for name in names if deep[name] > 1 and size[name][0] == tallest][:1]
+        if not aligned or 2 * max(deep.values()) + 2 > len(names) + 4:
+            split = []
+        names.sort(key=lambda name: (name in split, deep[name] == 1, size[name][0]))
+        sides = []
         plan, sources, known = [], [], {}
 
         def number(array):
@@ -966,6 +1125,10 @@
                     plan.append(("product", x.shape[0], (number(x), 0), (number(dy), part)))
                 continue
             count = deep[name] * wide
+            if name in split:
+                sides += [((number(x), part), (number(dy), 0)) for part in range(count)]
+                plan += [("kept", part) for part in range(count)]
+                continue
             if aligned:
                 made = weight_chunks(x, dy, None, 0, count, devices, width)
             else:
@@ -973,9 +1136,8 @@
             made = made.reshape((count,) + (2,) * len(self.links.bits) + made.shape[2:])
             for part in range(count):
                 plan.append(("chunk", number(made), part))
-        before, sources[0] = lax.optimization_barrier((before, sources[0]))
-        shares = reduce_chunks(
-            self.links, plan, sources, (2 * r, width // 2), width, collective_id
+        shares, total = reduce_chunks(
+            self.links, plan, sides, sources, value, (2 * r, width // 2), width, collective_id
         )
         if aligned:
             scattered = list(self.scattered.values())
@@ -984,14 +1146,14 @@
                 out_shape=[jax.ShapeDtypeStruct(shape, jnp.float32) for shape in shapes.values()]
                 + [jax.ShapeDtypeStruct(share.shape, jnp.float32) for share in scattered],
             )(shares, *scattered)
-            return dict(zip(list(shapes) + list(self.scattered), result)), before
+            return dict(zip(list(shapes) + list(self.scattered), result)), total
         result = {name: share.astype(jnp.float32) for name, share in self.scattered.items()}
         start = 0
         for name, shape in shapes.items():
             count = deep[name] * shape[1] // width
             result[name] = unfold_share(shares[start : start + count], *shape)
             start += count
-        return result, before
+        return result, total
 
 
 def unfold_kernel(width, count, shares_ref, *refs):
@@ -1160,10 +1322,12 @@
     ]
     gain_grads = jnp.stack([egain_self, egain_ffn, dgain_self, dgain_cross, dgain_ffn])
     flat = jnp.concatenate([gain_grads.reshape(-1)] + [grad.reshape(-1) for grad in table_grads])
-    flat = links.total(flat.reshape(-1, TILE)).reshape(-1)
+    count = flat.shape[0]
+    flat = jnp.pad(flat, (0, -count % (8 * TILE)))
+    shares, flat = grads.shares(0, flat.reshape(-1, TILE))
+    flat = flat.reshape(-1)
     width = gain_grads.shape[1]
-    shares, flat = grads.shares(0, flat)
-    tables_grad = flat[5 * width :].reshape(2, NB, H)
+    tables_grad = flat[5 * width : count].reshape(2, NB, H)
     own = width // links.devices()
     gains_share = lax.dynamic_slice_in_dim(
         flat[: 5 * width].reshape(5, width), links.place() * own, own, 1

time: 499 us -> 474 us (0.950)
  Pallas kernels: 301 us -> 341 us
  matrix products: 105 us -> 68.5 us
  starting transfers between devices: 18.2 us -> 3.11 us
  waiting for transfers between devices: 7.34 us -> 0.06 us
  local copies, waits for them, and re-layouts: 29.3 us -> 23.2 us
    pallas_call x2 -> x3, Pallas kernels: 125 us -> 163 us  [the longest x1 134 us: reduce_chunks(): pl.pallas_call(functools.partial(reduce_kernel, links, plan, sides, len(s...]
    dot_general x13 -> x9, matrix products: 58.5 us -> 21.5 us  [product_transposed(): lax.dot_general(former, latter, (((1,), (1,)), ((), ())), preferred_eleme...]
    ppermute x6 -> x1, starting transfers between devices: 17.7 us -> 3.03 us  [swap(): return lax.ppermute(value, axis, pairs)]
    unnamed x278 -> x220, local copies, waits for them, and re-layouts: 23.2 us -> 14.8 us
    ppermute x6 -> x1, waiting for transfers between devices: 7.27 us -> 0.01 us  [swap(): return lax.ppermute(value, axis, pairs)]
  transfers between devices with their start and end apart: 9 -> 3, of which waited for: 2 -> 0; matrix products, arithmetic and copies ran while one was open for 20% -> 17% of each run, Pallas kernels for 58% -> 71%
where the time goes in v5:
time: 474 us; the launch traced here: 467 us
  Pallas kernels  341 us (72%)
  matrix products  68.5 us (14%)
  local copies, waits for them, and re-layouts  23.2 us (5%)
  between operations  16 us (3%)
  other arithmetic  14.8 us (3%)
    pallas_call x1, Pallas kernels, reduce_chunks(): pl.pallas_call(functools.partial(reduce_kernel, links, plan, sides, len(s...  134 us
    pallas_call x1, Pallas kernels, gather_weights(): pl.pallas_call(functools.partial(gather_kernel, links, units, count), out...  71 us
    pallas_call x3, Pallas kernels, attend_backward(): pl.pallas_call(functools.partial(backward_kernel, spec), out_shape=[jax.S...  64.8 us
    pallas_call x3, Pallas kernels, attend_forward(): pl.pallas_call(functools.partial(forward_kernel, spec), out_shape=(jax.Sh...  40.1 us
    dot_general x13, matrix products, product(): return jnp.dot(former, latter, preferred_element_type=jnp.float32)  38.8 us
    pallas_call x2, Pallas kernels, feed_backward(): pl.pallas_call(feed_backward_kernel, out_shape=[jax.ShapeDtypeStruct((row...  29.2 us
    dot_general x9, matrix products, product_transposed(): lax.dot_general(former, latter, (((1,), (1,)), ((), ())), preferred_eleme...  21.5 us
    unnamed x220, local copies, waits for them, and re-layouts  14.8 us
  transfers between devices with their start and end apart: 3, of which 0 were waited for; matrix products, arithmetic and copies ran while one was open for 17% of the time, Pallas kernels for 71%

profile of v5, /device:TPU:0, one launch (start us, length us, event | category | flops | bytes accessed | tf_op | source)
XLA Modules:
  0.0 466.9 jit_solution(11716692710969290580)
XLA Ops:
  7.2 0.7 pad_maximum_fusion
  8.1 0.7 pad_maximum_fusion.1
  8.8 3.0 collective-permute-start
  11.8 71.0 %shard_map.418 = (bf16[2,2,2,2,48,768]{5,4,3,2,1,0:T(8,128)(2,1)}, bf16[2,2,2,2,48,1536]{5,4,3,2,1,0:T(8,128)(2,1)}, bf16[2,2,2,2,48,768]{5,4,3,2,1,0:T(8,128)(2...) custom-call(bf16[2,2,2,48,768]{4,3,2,1,0:T(8,128)(2,1)} %bitcast.148, ...), custom_call_target="tpu_custom_call" | custom-call | tf_op jit(solution)/shard_map/pallas_call | solution.py:1012
  83.0 0.6 compare_convert_fusion
  86.3 2.0 convolution_convert_fusion.9.q_ref
  88.3 0.8 convolution_convert_fusion.3.k_ref.v_ref
  89.3 5.2 %shard_map.420 = (bf16[256,768]{1,0:T(8,128)(2,1)S(1)}, f32[6,2,256]{2,1,0:T(2,128)S(1)}) custom-call(s32[2,1]{1,0:T(2,128)S(1)} %broadcast_14_bounds_ref.2.bounds_ref, bf16[256,768]{1,0:T(8,128)(2,1)S(1)} %convolution_convert_fusion.9.q_ref, bf16[256,1536]{1,0:T(8,128)(2,1)S(1)} %convolution_convert_fusion.3.k_ref.v_ref, ...), custom_call_target="tpu_custom_call" | custom-call | flops 805306368 | bytes 8388608 | tf_op jit(solution)/shard_map/pallas_call | solution.py:390
  94.5 0.6 multiply_reduce_fusion.4
  96.0 1.4 convolution_convert_fusion.5.q_ref
  97.5 0.8 copy-done.95
  98.2 2.8 convolution_convert_fusion.2.k_ref.v_ref
  101.3 26.1 %shard_map.419 = (bf16[1024,768]{1,0:T(8,128)(2,1)S(1)}, f32[6,2,1024]{2,1,0:T(2,128)S(1)}) custom-call(s32[2,4]{1,0:T(2,128)S(1)} %pad_add_fusion.bounds_ref, bf16[1024,768]{1,0:T(8,128)(2,1)S(1)} %convolution_convert_fusion.5.q_ref, bf16[1024,1536]{1,0:T(8,128)(2,1)S(1)} %convolution_convert_fusion.2.k_ref.v_ref, ...), custom_call_target="tpu_custom_call" | custom-call | flops 12884901888 | bytes 8388608 | tf_op jit(solution)/shard_map/pallas_call | solution.py:390
  127.5 1.5 multiply_reduce_fusion
  129.6 1.6 copy-done.60
  131.8 9.9 %fusion.7 = (bf16[1024,3072]{1,0:T(8,128)(2,1)S(1)}, f32[1024,3072]{1,0:T(8,128)}) fusion(bf16[1024,768]{1,0:T(8,128)(2,1)S(1)} %multiply_convert_fusion.refs_13_, bf16[768,3072]{1,0:T(8,128)(2,1)S(1)} %bitcast.159), kind=kOutput, calls=%fused_computation.8 | convolution fusion | flops 4860149760 | bytes 25165824 | tf_op jit(solution)/shard_map/dot_general | solution.py:466
  141.7 5.1 %add_convert_fusion.refs_11_ = bf16[1024,768]{1,0:T(8,128)(2,1)S(1)} fusion(f32[1024,768]{1,0:T(8,128)S(1)} %get-tuple-element.241.v_ref, bf16[1024,3072]{1,0:T(8,128)(2,1)S(1)} %get-tuple-element.242.refs_20_, bf16[3072,768]{1,0:T(8,128)(2,1)S(1)} %bitcast.163), kind=kOutput, calls=%fused_computation.35 | convolution fusion | flops 4833411072 | bytes 15728640 | tf_op jit(solution)/shard_map/dot_general | solution.py:466
  146.9 1.1 copy-done.69
  148.0 2.8 convolution_convert_fusion.1.k_ref.v_ref
  150.9 8.8 %shard_map.421 = (bf16[256,768]{1,0:T(8,128)(2,1)S(1)}, f32[6,2,256]{2,1,0:T(2,128)S(1)}) custom-call(s32[2,1]{1,0:T(2,128)S(1)} %broadcast_14_bounds_ref.2.bounds_ref, bf16[256,768]{1,0:T(8,128)(2,1)S(1)} %convolution_convert_fusion.8.q_ref, bf16[1024,1536]{1,0:T(8,128)(2,1)S(1)} %convolution_convert_fusion.1.k_ref.v_ref, ...), custom_call_target="tpu_custom_call" | custom-call | flops 3221225472 | bytes 8388608 | tf_op jit(solution)/shard_map/pallas_call | solution.py:390
  159.7 0.7 copy-done.7
  160.4 0.6 multiply_reduce_fusion.3
  161.2 5.7 %fusion.57.pre_ref = f32[256,3072]{1,0:T(8,128)} fusion(bf16[256,768]{1,0:T(8,128)(2,1)S(1)} %multiply_convert_fusion.1.refs_0_, bf16[768,3072]{1,0:T(8,128)(2,1)} %all-gather.2.cloned.1.call-done.wi_ref), kind=kOutput, calls=%fused_computation.137 | convolution fusion | flops 1207959552 | bytes 8257536 | tf_op jit(solution)/shard_map/dot_general | solution.py:466
  166.9 8.2 %shard_map.422 = (f32[256,768]{1,0:T(8,128)S(1)}, bf16[256,3072]{1,0:T(8,128)(2,1)S(1)}, bf16[256,768]{1,0:T(8,128)(2,1)S(1)}, f32[8,768]{1,0:T(8,128)S(1)}) custom-call(f32[256,768]{1,0:T(8,128)S(1)} %convert_multiply_fusion.8.g_ref, f32[256,768]{1,0:T(8,128)S(1)} %get-tuple-element.245.v_ref, f32[1,768]{1,0:T(1,128)S(1)} %bitcast.123, ...), custom_call_target="tpu_custom_call" | custom-call | flops 2415919104 | bytes 16908288 | tf_op jit(solution)/shard_map/pallas_call | solution.py:577
  175.1 1.1 copy-done.10
  176.3 0.6 stack.10
  176.9 6.3 %convolution_convert_fusion = bf16[3072,768]{1,0:T(8,128)(2,1)} fusion(bf16[256,768]{1,0:T(8,128)(2,1)S(1)} %get-tuple-element.91, f32[256,3072]{1,0:T(8,128)} %fusion.57.pre_ref), kind=kOutput, calls=%fused_computation.14 | convolution fusion | flops 1217396736 | bytes 8257536 | tf_op jit(solution)/shard_map/dot_general | solution.py:470
  183.3 1.2 copy-done.59
  185.3 11.8 %shard_map.423 = (bf16[256,768]{1,0:T(8,128)(2,1)S(1)}, bf16[1024,1536]{1,0:T(8,128)(2,1)S(1)}) custom-call(s32[2,1]{1,0:T(2,128)S(1)} %copy-done.29, bf16[256,768]{1,0:T(8,128)(2,1)S(1)} %convolution_convert_fusion.8.q_ref, bf16[1024,1536]{1,0:T(8,128)(2,1)} %copy-done.32, bf16[1024,1536]{1,0:T(8,128)(2,1)} %copy-done.32, ...), custom_call_target="tpu_custom_call" | custom-call | flops 8053063680 | bytes 16777216 | tf_op jit(solution)/shard_map/pallas_call | solution.py:426
  197.2 0.6 multiply_reduce_fusion.1
  197.9 0.6 reshape.414
  198.9 1.1 fusion.51
  200.9 11.4 %shard_map.426 = (bf16[256,768]{1,0:T(8,128)(2,1)S(1)}, bf16[256,1536]{1,0:T(8,128)(2,1)S(1)}, f32[12,5,8,256]{3,2,1,0:T(8,128)S(1)}) custom-call(s32[2,1]{1,0:T(2,128)S(1)} %copy-done.29, bf16[256,768]{1,0:T(8,128)(2,1)S(1)} %copy-done.19, bf16[256,1536]{1,0:T(8,128)(2,1)S(1)} %copy-done.31, bf16[256,1536]{1,0:T(8,128)(2,1)S(1)} %copy-done.31, ...), custom_call_target="tpu_custom_call" | custom-call | flops 2013265920 | bytes 16777216 | tf_op jit(solution)/shard_map/pallas_call | solution.py:426
  212.9 2.3 fusion.29
  215.5 0.8 fusion.24
  216.4 6.0 %multiply_add_fusion.g_ref = f32[1024,768]{1,0:T(8,128)} fusion(bf16[1024,768]{1,0:T(8,128)(2,1)} %param.31, bf16[1024,1536]{1,0:T(8,128)(2,1)S(1)} %get-tuple-element.95.refs_12_, bf16[768,1536]{1,0:T(8,128)(2,1)} %bitcast.166, f32[1024]{0:T(1024)} %compare_convert_fusion), kind=kOutput, calls=%fused_computation.34 | convolution fusion | flops 2418278400 | bytes 10227712 | tf_op jit(solution)/shard_map/dot_general | solution.py:476
  222.4 21.0 %shard_map.424 = (f32[1024,768]{1,0:T(8,128)S(1)}, bf16[1024,3072]{1,0:T(8,128)(2,1)}, bf16[1024,768]{1,0:T(8,128)(2,1)S(1)}, f32[8,768]{1,0:T(8,128)S(1)}) custom-call(f32[1024,768]{1,0:T(8,128)} %multiply_add_fusion.g_ref, f32[1024,768]{1,0:T(8,128)} %copy-done.66, f32[1,768]{1,0:T(1,128)S(1)} %get-tuple-element.237.gain_ref, ...), custom_call_target="tpu_custom_call" | custom-call | flops 9663676416 | bytes 39321600 | tf_op jit(solution)/shard_map/pallas_call | solution.py:577
  243.4 1.1 copy-done.11
  244.8 1.1 copy-done.102
  245.9 1.4 convolution_convert_fusion.4.do_ref
  247.3 0.7 copy-done.34
  248.1 41.6 %shard_map.425 = (bf16[1024,768]{1,0:T(8,128)(2,1)S(1)}, bf16[1024,1536]{1,0:T(8,128)(2,1)}, f32[12,5,8,256]{3,2,1,0:T(8,128)S(1)}) custom-call(s32[2,4]{1,0:T(2,128)S(1)} %pad_add_fusion.bounds_ref, bf16[1024,768]{1,0:T(8,128)(2,1)S(1)} %copy-done.34, bf16[1024,1536]{1,0:T(8,128)(2,1)} %copy-done.35, bf16[1024,1536]{1,0:T(8,128)(2,1)} %copy-done.35, ...), custom_call_target="tpu_custom_call" | custom-call | flops 32212254720 | bytes 16777216 | tf_op jit(solution)/shard_map/pallas_call | solution.py:426
  289.7 1.2 copy-done.12
  291.1 0.8 fusion.23
  292.0 5.4 %fusion.58 = f32[1024,768]{1,0:T(8,128)S(1)} fusion(bf16[1024,1536]{1,0:T(8,128)(2,1)} %get-tuple-element.99.refs_19_, bf16[768,1536]{1,0:T(8,128)(2,1)} %bitcast.164), kind=kOutput, calls=%fused_computation.138 | convolution fusion | flops 2415919104 | bytes 8650752 | tf_op jit(solution)/shard_map/dot_general | solution.py:476
  297.5 4.1 fusion.11
  301.7 0.6 fusion.44.refs_22_
  302.4 133.5 %shard_map.427 = (f32[24,48,384]{2,1,0:T(8,128)}, f32[40,128]{1,0:T(8,128)}) custom-call(bf16[256,768]{1,0:T(8,128)(2,1)} %copy-done.68, bf16[256,3072]{1,0:T(8,128)(2,1)} %copy-done.10, bf16[256,768]{1,0:T(8,128)(2,1)} %copy-done.7, bf16[256,768]{1,0:T(8,128)(2,1)} %copy-done.64, bf16[256,768]{1,0:T(8,128)(2,1)} %copy-done.63, bf16[256,768]{1,0:T(8,128)(2,1)} %copy-done.8, ...), custom_call_target="tpu_custom_call" | custom-call | tf_op jit(solution)/shard_map/pallas_call | solution.py:872
  435.9 0.7 slice.77
  436.6 0.6 reshape.421
  437.2 0.8 dynamic-slice_bitcast_fusion
  438.0 0.6 slice.78
  438.6 0.6 slice.80
  439.1 1.4 fusion.55
  440.5 0.8 squeeze.7
  441.3 0.7 copy.89
  442.0 0.8 squeeze.6
  442.7 0.7 copy.88
  443.4 0.8 multiply_multiply_fusion.3
  444.2 0.7 multiply_multiply_fusion.2
  445.0 2.5 fusion.31
  447.5 4.5 fusion.20
  452.0 5.1 %fusion.25 = bf16[256,768]{1,0:T(8,128)(2,1)} fusion(f32[256,768]{1,0:T(8,128)S(1)} %copy-done.1, bf16[3072,768]{1,0:T(8,128)(2,1)} %bitcast.137, f32[256,3072]{1,0:T(8,128)S(1)} %copy-done.67), kind=kOutput, calls=%fused_computation.54 | convolution fusion | flops 1215430656 | bytes 9043968 | tf_op jit(solution)/shard_map/dot_general | solution.py:466
  457.1 2.8 shard_map.428
  (268 shorter events, 8.8 us)
Async XLA Ops:
  7.2 154.0 %all-gather.2.cloned.1.call-start = ((), (), s32[]{:S(2)}) async-start(), calls=%async_computation.1 | async-start | bytes 7077888 | tf_op jit(solution)/shard_map/all_gather | solution.py:1238
  8.8 76.5 %collective-permute-start = (bf16[384,6]{0,1:T(8,128)(2,1)S(1)}, bf16[384,6]{0,1:T(8,128)(2,1)S(1)}, u32[]{:S(2)}, u32[]{:S(2)}) collective-permute-start(bf16[384,6]{0,1:T(8,128)(2,1)S(1)} %pad_maximum_fusion.1), channel_id=1, source_target_pairs={{0,1},{1,0},{2,3},{3,2},{4,5},{5,4},{6,7},{7,6},{8,9},{9,8},{10,11... | collective-permute-start | bytes 13832 | tf_op jit(solution)/shard_map/ppermute | solution.py:631
  11.8 71.2 %copy-start.26 = (s32[1024]{0:T(1024)S(1)}, s32[1024]{0:T(1024)}, u32[]{:S(2)}) copy-start(s32[1024]{0:T(1024)} %param.29) | copy-start | bytes 12292
  11.8 71.8 %copy-start.51 = (bf16[256,768]{1,0:T(8,128)(2,1)S(1)}, bf16[256,768]{1,0:T(8,128)(2,1)}, u32[]{:S(2)}) copy-start(bf16[256,768]{1,0:T(8,128)(2,1)} %param.28) | copy-start | bytes 1179652
  11.8 71.9 %copy-start.27 = (s32[256]{0:T(256)S(1)}, s32[256]{0:T(256)}, u32[]{:S(2)}) copy-start(s32[256]{0:T(256)} %param.30) | copy-start | bytes 3076
  82.9 374.2 %reduce-scatter.2.cloned.1.call-start = ((), (), s32[]{:S(2)}) async-start(), calls=%async_computation.2 | async-start | bytes 4866048 | tf_op jit(solution)/shard_map/reduce_scatter | solution.py:1090
  83.8 4.5 copy-start.89
  84.6 4.5 copy-start.81
  84.6 10.5 %copy-start.79 = (f32[1024]{0:T(1024)}, f32[1024]{0:T(1024)S(1)}, u32[]{:S(2)}) copy-start(f32[1024]{0:T(1024)S(1)} %fusion.45) | copy-start | bytes 12292
  85.4 3.7 copy-start.77
  85.4 43.7 %copy-start.71 = (f32[768]{0:T(1024)}, f32[768]{0:T(1024)S(1)}, u32[]{:S(2)}) copy-start(f32[768]{0:T(1024)S(1)} %get-tuple-element.234) | copy-start | bytes 9220
  85.5 9.7 %copy-start.75 = (f32[768]{0:T(1024)}, f32[768]{0:T(1024)S(1)}, u32[]{:S(2)}) copy-start(f32[768]{0:T(1024)S(1)} %get-tuple-element.220) | copy-start | bytes 9220
  85.8 15.4 %copy-start.22 = (f32[12,5,256]{2,1,0:T(8,128)}, f32[12,5,256]{2,1,0:T(8,128)S(1)}, u32[]{:S(2)}) copy-start(f32[12,5,256]{2,1,0:T(8,128)S(1)} %copy.80.rest_0_) | copy-start | bytes 184324
  86.1 3.2 copy-start.24
  88.3 6.2 %copy-start.18 = (bf16[256,768]{1,0:T(8,128)(2,1)}, bf16[256,768]{1,0:T(8,128)(2,1)S(1)}, u32[]{:S(2)}) copy-start(bf16[256,768]{1,0:T(8,128)(2,1)S(1)} %convolution_convert_fusion.9.q_ref) | copy-start | bytes 1179652
  88.3 6.2 %copy-start.55 = (bf16[2,2,2,2,48,768]{5,4,3,2,1,0:T(8,128)(2,1)S(1)}, bf16[2,2,2,2,48,768]{5,4,3,2,1,0:T(8,128)(2,1)}, u32[]{:S(2)}) copy-start(bf16[2,2,2,2,48,768]{5,4,3,2,1,0:T(8,128)(2,1)} %get-tuple-element.84) | copy-start | bytes 3538948
  89.1 6.5 %copy-start.30 = (bf16[256,1536]{1,0:T(8,128)(2,1)}, bf16[256,1536]{1,0:T(8,128)(2,1)S(1)}, u32[]{:S(2)}) copy-start(bf16[256,1536]{1,0:T(8,128)(2,1)S(1)} %convolution_convert_fusion.3.k_ref.v_ref) | copy-start | bytes 2359300
  89.1 6.0 %copy-start.45 = (bf16[1024,768]{1,0:T(8,128)(2,1)S(1)}, bf16[1024,768]{1,0:T(8,128)(2,1)}, u32[]{:S(2)}) copy-start(bf16[1024,768]{1,0:T(8,128)(2,1)} %param.27) | copy-start | bytes 4718596
  89.2 6.3 %copy-start.20 = (s32[256,128]{1,0:T(8,128)}, s32[256,128]{1,0:T(8,128)S(1)}, u32[]{:S(2)}) copy-start(s32[256,128]{1,0:T(8,128)S(1)} %broadcast_in_dim.25.segk_ref) | copy-start | bytes 393220
  89.3 61.5 %copy-start.28 = (s32[2,1]{1,0:T(2,128)}, s32[2,1]{1,0:T(2,128)S(1)}, u32[]{:S(2)}) copy-start(s32[2,1]{1,0:T(2,128)S(1)} %broadcast_14_bounds_ref.2.bounds_ref) | copy-start | bytes 28
  95.1 64.6 %copy-start.42 = (f32[256,768]{1,0:T(8,128)}, f32[256,768]{1,0:T(8,128)S(1)}, u32[]{:S(2)}) copy-start(f32[256,768]{1,0:T(8,128)S(1)} %get-tuple-element.239) | copy-start | bytes 2359300
  95.1 34.0 %copy-start.82 = (f32[256]{0:T(256)}, f32[256]{0:T(256)S(1)}, u32[]{:S(2)}) copy-start(f32[256]{0:T(256)S(1)} %fusion.48) | copy-start | bytes 3076
  97.4 3.9 copy-start.33
  98.2 33.5 %slice-start = ((s8[4718592]{0:T(1024)(128)(4,1)}), s8[4194304]{0:T(1024)(128)(4,1)S(1)}, s32[]{:S(2)}) async-start(s8[4718592]{0:T(1024)(128)(4,1)} %bitcast.157), calls=%async_computation.3 | async-start | bytes 8388608
  101.1 26.4 %copy-start.35 = (bf16[1024,1536]{1,0:T(8,128)(2,1)}, bf16[1024,1536]{1,0:T(8,128)(2,1)S(1)}, u32[]{:S(2)}) copy-start(bf16[1024,1536]{1,0:T(8,128)(2,1)S(1)} %convolution_convert_fusion.2.k_ref.v_ref) | copy-start | bytes 9437188
  101.3 49.5 %copy-start.15 = (s32[1024,128]{1,0:T(8,128)}, s32[1024,128]{1,0:T(8,128)S(1)}, u32[]{:S(2)}) copy-start(s32[1024,128]{1,0:T(8,128)S(1)} %broadcast_in_dim.23.segk_ref) | copy-start | bytes 1572868
  101.3 26.2 %copy-start.101 = (bf16[2,2,2,2,48,768]{5,4,3,2,1,0:T(8,128)(2,1)S(1)}, bf16[2,2,2,2,48,768]{5,4,3,2,1,0:T(8,128)(2,1)}, u32[]{:S(2)}) copy-start(bf16[2,2,2,2,48,768]{5,4,3,2,1,0:T(8,128)(2,1)} %get-tuple-element.78) | copy-start | bytes 3538948
  101.3 30.4 %slice-start.1 = ((s8[4718592]{0:T(1024)(128)(4,1)}), s8[524288]{0:T(1024)(128)(4,1)S(1)}, s32[]{:S(2)}) async-start(s8[4718592]{0:T(1024)(128)(4,1)} %bitcast.157), calls=%async_computation.4 | async-start | bytes 1048576
  129.1 12.6 %copy-start.66 = (f32[1024,768]{1,0:T(8,128)}, f32[1024,768]{1,0:T(8,128)S(1)}, u32[]{:S(2)}) copy-start(f32[1024,768]{1,0:T(8,128)S(1)} %get-tuple-element.241.v_ref) | copy-start | bytes 9437188
  129.6 12.1 %copy-start.49 = (bf16[1024,768]{1,0:T(8,128)(2,1)}, bf16[1024,768]{1,0:T(8,128)(2,1)S(1)}, u32[]{:S(2)}) copy-start(bf16[1024,768]{1,0:T(8,128)(2,1)S(1)} %multiply_convert_fusion.refs_13_) | copy-start | bytes 4718596
  131.2 10.5 %slice-start.2 = ((s8[4718592]{0:T(1024)(128)(4,1)}), s8[4194304]{0:T(1024)(128)(4,1)S(1)}, s32[]{:S(2)}) async-start(s8[4718592]{0:T(1024)(128)(4,1)} %bitcast.161), calls=%async_computation.5 | async-start | bytes 8388608
  131.8 9.9 %slice-start.3 = ((s8[4718592]{0:T(1024)(128)(4,1)}), s8[524288]{0:T(1024)(128)(4,1)S(1)}, s32[]{:S(2)}) async-start(s8[4718592]{0:T(1024)(128)(4,1)} %bitcast.161), calls=%async_computation.6 | async-start | bytes 1048576
  141.7 5.2 %copy-start.54 = (bf16[1024,3072]{1,0:T(8,128)(2,1)}, bf16[1024,3072]{1,0:T(8,128)(2,1)S(1)}, u32[]{:S(2)}) copy-start(bf16[1024,3072]{1,0:T(8,128)(2,1)S(1)} %get-tuple-element.242.refs_20_) | copy-start | bytes 18874372
  141.7 6.3 %copy-start.96 = (bf16[2,2,2,2,48,1536]{5,4,3,2,1,0:T(8,128)(2,1)S(1)}, bf16[2,2,2,2,48,1536]{5,4,3,2,1,0:T(8,128)(2,1)}, u32[]{:S(2)}) copy-start(bf16[2,2,2,2,48,1536]{5,4,3,2,1,0:T(8,128)(2,1)} %get-tuple-element.86) | copy-start | bytes 7077892
  150.8 8.8 %copy-start.32 = (bf16[1024,1536]{1,0:T(8,128)(2,1)}, bf16[1024,1536]{1,0:T(8,128)(2,1)S(1)}, u32[]{:S(2)}) copy-start(bf16[1024,1536]{1,0:T(8,128)(2,1)S(1)} %convolution_convert_fusion.1.k_ref.v_ref) | copy-start | bytes 9437188
  150.8 9.6 %copy-start.58 = (bf16[2,2,2,2,48,768]{5,4,3,2,1,0:T(8,128)(2,1)S(1)}, bf16[2,2,2,2,48,768]{5,4,3,2,1,0:T(8,128)(2,1)}, u32[]{:S(2)}) copy-start(bf16[2,2,2,2,48,768]{5,4,3,2,1,0:T(8,128)(2,1)} %get-tuple-element.88) | copy-start | bytes 3538948
  159.7 7.2 %copy-start.38 = (f32[6,2,256]{2,1,0:T(2,128)}, f32[6,2,256]{2,1,0:T(2,128)S(1)}, u32[]{:S(2)}) copy-start(f32[6,2,256]{2,1,0:T(2,128)S(1)} %get-tuple-element.94.lse_ref) | copy-start | bytes 36868
  161.0 5.9 %copy-start = (f32[256,768]{1,0:T(8,128)}, f32[256,768]{1,0:T(8,128)S(1)}, u32[]{:S(2)}) copy-start(f32[256,768]{1,0:T(8,128)S(1)} %get-tuple-element.245.v_ref) | copy-start | bytes 2359300
  161.1 5.8 %copy-start.68 = (bf16[256,768]{1,0:T(8,128)(2,1)}, bf16[256,768]{1,0:T(8,128)(2,1)S(1)}, u32[]{:S(2)}) copy-start(bf16[256,768]{1,0:T(8,128)(2,1)S(1)} %multiply_convert_fusion.1.refs_0_) | copy-start | bytes 1179652
  176.3 6.9 %copy-start.3 = (f32[256,768]{1,0:T(8,128)}, f32[256,768]{1,0:T(8,128)S(1)}, u32[]{:S(2)}) copy-start(f32[256,768]{1,0:T(8,128)S(1)} %get-tuple-element.93) | copy-start | bytes 2359300
  185.2 11.9 %copy-start.43 = (f32[256,768]{1,0:T(8,128)S(1)}, f32[256,768]{1,0:T(8,128)}, u32[]{:S(2)}) copy-start(f32[256,768]{1,0:T(8,128)} %copy-done.42) | copy-start | bytes 2359300
  185.2 11.9 %copy-start.61 = (bf16[2,2,2,2,48,768]{5,4,3,2,1,0:T(8,128)(2,1)S(1)}, bf16[2,2,2,2,48,768]{5,4,3,2,1,0:T(8,128)(2,1)}, u32[]{:S(2)}) copy-start(bf16[2,2,2,2,48,768]{5,4,3,2,1,0:T(8,128)(2,1)} %get-tuple-element.85) | copy-start | bytes 3538948
  185.3 11.9 %copy-start.72 = (f32[768]{0:T(1024)S(1)}, f32[768]{0:T(1024)}, u32[]{:S(2)}) copy-start(f32[768]{0:T(1024)} %copy-done.71) | copy-start | bytes 9220
  185.3 11.9 %copy-start.83 = (f32[256]{0:T(256)S(1)}, f32[256]{0:T(256)}, u32[]{:S(2)}) copy-start(f32[256]{0:T(256)} %copy-done.82) | copy-start | bytes 3076
  197.1 3.0 copy-start.8
  197.1 19.3 %copy-start.2 = (bf16[1024,1536]{1,0:T(8,128)(2,1)}, bf16[1024,1536]{1,0:T(8,128)(2,1)S(1)}, u32[]{:S(2)}) copy-start(bf16[1024,1536]{1,0:T(8,128)(2,1)S(1)} %get-tuple-element.95.refs_12_) | copy-start | bytes 9437188
  197.8 3.0 copy-start.19
  200.8 11.5 %copy-start.57 = (bf16[2,2,2,2,48,768]{5,4,3,2,1,0:T(8,128)(2,1)S(1)}, bf16[2,2,2,2,48,768]{5,4,3,2,1,0:T(8,128)(2,1)}, u32[]{:S(2)}) copy-start(bf16[2,2,2,2,48,768]{5,4,3,2,1,0:T(8,128)(2,1)} %get-tuple-element.81) | copy-start | bytes 3538948
  200.8 12.0 %copy-start.52 = (bf16[256,768]{1,0:T(8,128)(2,1)S(1)}, bf16[256,768]{1,0:T(8,128)(2,1)}, u32[]{:S(2)}) copy-start(bf16[256,768]{1,0:T(8,128)(2,1)} %param.28) | copy-start | bytes 1179652
  200.9 12.0 %copy-start.78 = (f32[768]{0:T(1024)S(1)}, f32[768]{0:T(1024)}, u32[]{:S(2)}) copy-start(f32[768]{0:T(1024)} %copy-done.77) | copy-start | bytes 9220
  200.9 12.0 %copy-start.90 = (f32[256]{0:T(256)S(1)}, f32[256]{0:T(256)}, u32[]{:S(2)}) copy-start(f32[256]{0:T(256)} %copy-done.89) | copy-start | bytes 3076
  200.9 12.0 %copy-start.98 = (bf16[2,2,2,2,48,1536]{5,4,3,2,1,0:T(8,128)(2,1)S(1)}, bf16[2,2,2,2,48,1536]{5,4,3,2,1,0:T(8,128)(2,1)}, u32[]{:S(2)}) copy-start(bf16[2,2,2,2,48,1536]{5,4,3,2,1,0:T(8,128)(2,1)} %get-tuple-element.82) | copy-start | bytes 7077892
  248.1 43.0 %copy-start.73 = (s32[10240]{0:T(1024)S(1)}, s32[10240]{0:T(1024)}, u32[]{:S(2)}) copy-start(s32[10240]{0:T(1024)} %constant.99) | copy-start | bytes 122884
  292.0 5.5 %copy-start.13 = (bf16[1024,768]{1,0:T(8,128)(2,1)S(1)}, bf16[1024,768]{1,0:T(8,128)(2,1)}, u32[]{:S(2)}) copy-start(bf16[1024,768]{1,0:T(8,128)(2,1)} %copy-done.12) | copy-start | bytes 4718596
  292.0 5.5 %copy-start.46 = (bf16[1024,768]{1,0:T(8,128)(2,1)S(1)}, bf16[1024,768]{1,0:T(8,128)(2,1)}, u32[]{:S(2)}) copy-start(bf16[1024,768]{1,0:T(8,128)(2,1)} %param.27) | copy-start | bytes 4718596
  292.0 5.5 %copy-start.76 = (f32[768]{0:T(1024)S(1)}, f32[768]{0:T(1024)}, u32[]{:S(2)}) copy-start(f32[768]{0:T(1024)} %copy-done.75) | copy-start | bytes 9220
  292.0 5.5 %copy-start.80 = (f32[1024]{0:T(1024)S(1)}, f32[1024]{0:T(1024)}, u32[]{:S(2)}) copy-start(f32[1024]{0:T(1024)} %copy-done.79) | copy-start | bytes 12292
  292.0 5.5 %copy-start.100 = (bf16[2,2,2,2,48,768]{5,4,3,2,1,0:T(8,128)(2,1)S(1)}, bf16[2,2,2,2,48,768]{5,4,3,2,1,0:T(8,128)(2,1)}, u32[]{:S(2)}) copy-start(bf16[2,2,2,2,48,768]{5,4,3,2,1,0:T(8,128)(2,1)} %get-tuple-element.74) | copy-start | bytes 3538948
  297.5 4.2 copy-start.84
  297.5 4.2 copy-start.85
  302.3 142.6 %copy-start.53 = (bf16[256,768]{1,0:T(8,128)(2,1)S(1)}, bf16[256,768]{1,0:T(8,128)(2,1)}, u32[]{:S(2)}) copy-start(bf16[256,768]{1,0:T(8,128)(2,1)} %param.28) | copy-start | bytes 1179652
  443.4 4.0 copy-start.47
  447.5 4.5 copy-start.1
  447.5 4.5 copy-start.67
  (46 other events, 92.8 us)
Sparse Core Ops, SparseCore 0:
  83.0 62.0 all-gather.1
  183.3 109.6 reduce-scatter.1

commit v6 on v5

--- a/solution.py
+++ b/solution.py
@@ -488,11 +488,6 @@
     )
 
 
-def norm_backward(stream, norm_gain, gradient):
-    outcome, pullback = jax.vjp(norm_forward, stream, norm_gain)
-    return pullback(gradient)
-
-
 def attention_forward(stream, norm_gain, wquery, wkeyval, wproj, layout, memory):
     normed = norm_forward(stream, norm_gain).astype(jnp.bfloat16)
     queries = product(normed, wquery).astype(jnp.bfloat16)
@@ -513,13 +508,74 @@
     source = normed if memory is None else memory
     grads.add(names[0], normed, dquery_low)
     grads.add(names[1], source, dkeyval_low)
-    dnormed = product_transposed(dquery_low, wquery)
-    dsource = product_transposed(dkeyval_low, wkeyval)
+    pulls, dsource = [(dquery_low, wquery)], None
     if memory is None:
-        dnormed = dnormed + dsource
-        dsource = None
-    dstream, dgain = norm_backward(stream, norm_gain, dnormed)
-    return (gradient + dstream, dgain, band, dsource)
+        pulls.append((dkeyval_low, wkeyval))
+    else:
+        dsource = product_transposed(dkeyval_low, wkeyval)
+    dstream, dgain = pull_norm(stream, norm_gain, pulls, gradient)
+    return (dstream, dgain, band, dsource)
+
+
+def norm_pull(gradient, value, gain, dnormed):
+    scale = lax.rsqrt(jnp.mean(value * value, axis=1, keepdims=True) + EPSILON)
+    pulled = dnormed * gain
+    inner = jnp.mean(pulled * value, axis=1, keepdims=True)
+    result = gradient + scale * pulled - value * (scale * scale * scale * inner)
+    return result, fold_rows(dnormed * value * scale, jnp.add)
+
+
+def add_gain(dgain_ref, dgain):
+    @pl.when(pl.program_id(0) == 0)
+    def _():
+        dgain_ref[...] = dgain
+
+    @pl.when(pl.program_id(0) > 0)
+    def _():
+        dgain_ref[...] += dgain
+
+
+def pull_norm_kernel(g_ref, v_ref, gain_ref, *refs):
+    *pulls, out_ref, dgain_ref = refs
+    dnormed = None
+    for low_ref, weight_ref in zip(pulls[::2], pulls[1::2]):
+        part = dot_rows(low_ref[...], weight_ref[...])
+        dnormed = part if dnormed is None else dnormed + part
+    out_ref[...], dgain = norm_pull(
+        g_ref[...], v_ref[...].astype(jnp.float32), gain_ref[...], dnormed
+    )
+    add_gain(dgain_ref, dgain)
+
+
+def pull_norm(stream, norm_gain, pulls, gradient):
+    rows, features = stream.shape
+    block = min(256, rows)
+    row = pl.BlockSpec((block, features), lambda step: (step, 0))
+    specs, operands = [], []
+    for low, weight in pulls:
+        specs.append(pl.BlockSpec((block, low.shape[1]), lambda step: (step, 0)))
+        specs.append(
+            pl.BlockSpec(weight.shape, lambda step: (0, 0), pipeline_mode=pl.Buffered(1))
+        )
+        operands += [low, weight]
+    dstream, dgain = pl.pallas_call(
+        pull_norm_kernel,
+        out_shape=[
+            jax.ShapeDtypeStruct((rows, features), jnp.float32),
+            jax.ShapeDtypeStruct((8, features), jnp.float32),
+        ],
+        grid=(rows // block,),
+        in_specs=[row, row, pl.BlockSpec((1, features), lambda step: (0, 0))] + specs,
+        out_specs=[row, pl.BlockSpec((8, features), lambda step: (0, 0))],
+        compiler_params=pltpu.CompilerParams(vmem_limit_bytes=40 << 20),
+        cost_estimate=pl.CostEstimate(
+            flops=sum(2 * rows * weight.size for _, weight in pulls),
+            transcendentals=rows,
+            bytes_accessed=rows * features * 12
+            + sum(2 * (low.size + weight.size) for low, weight in pulls),
+        ),
+    )(gradient, stream, norm_gain[None, :], *operands)
+    return dstream, jnp.sum(dgain, axis=0)
 
 
 def feed_forward(stream, norm_gain, winner, wouter):
@@ -550,20 +606,8 @@
         dpre_ref[:, span] = dpre
         part = dot_rows(dpre, wi_ref[:, span])
         dnormed = part if dnormed is None else dnormed + part
-    value = v_ref[...]
-    scale = lax.rsqrt(jnp.mean(value * value, axis=1, keepdims=True) + EPSILON)
-    pulled = dnormed * gain_ref[...]
-    inner = jnp.mean(pulled * value, axis=1, keepdims=True)
-    out_ref[...] = gradient + scale * pulled - value * (scale * scale * scale * inner)
-    dgain = fold_rows(dnormed * value * scale, jnp.add)
-
-    @pl.when(pl.program_id(0) == 0)
-    def _():
-        dgain_ref[...] = dgain
-
-    @pl.when(pl.program_id(0) > 0)
-    def _():
-        dgain_ref[...] += dgain
+    out_ref[...], dgain = norm_pull(gradient, v_ref[...], gain_ref[...], dnormed)
+    add_gain(dgain_ref, dgain)
 
 
 def feed_backward(grads, names, stream, norm_gain, winner, wouter, stored, gradient):
@@ -626,17 +670,6 @@
         third = [core] + rest[1:2] + rest[:1] + [row] + rest[2:]
         return ([core] + rest[:1] + [row] + rest[1:], [core, row] + rest, third)
 
-    def swap(self, value, axis, bit):
-        pairs = [(place, place ^ (1 << bit)) for place in range(self.sizes[axis])]
-        return lax.ppermute(value, axis, pairs)
-
-    def gather_small(self, shard):
-        other = self.swap(shard, "fsdp", 0)
-        first = lax.axis_index("fsdp") == 0
-        return jnp.concatenate(
-            [jnp.where(first, shard, other), jnp.where(first, other, shard)], axis=0
-        )
-
     def devices(self):
         return self.sizes["dp"] * self.sizes["fsdp"]
 
@@ -659,10 +692,11 @@
 
 def reduce_kernel(links, plan, sides, count, *refs):
     stages, chunks = len(links.bits), len(plan)
-    sources, (value_ref, out_ref, total_ref) = refs[:count], refs[count : count + 3]
-    ring_ref, x_ref, y_ref, part_ref, come_ref = refs[count + 3 : count + 8]
-    deep_ref, side_x_ref, side_y_ref = refs[count + 8 : count + 11]
-    rest = refs[count + 11 :]
+    sources, refs = refs[:count], refs[count:]
+    gains_ref, tables_ref, out_ref, gains_out_ref, tables_out_ref, *refs = refs
+    ring_ref, x_ref, y_ref, part_ref, come_ref, deep_ref, side_x_ref, side_y_ref, *rest = refs
+    gain_rows, lanes = gains_ref.shape[0], tables_ref.shape[1]
+    blocks = gains_ref.shape[1] // lanes
     sums, rest = rest[:stages], rest[stages:]
     send_sem, recv_sem, load_sem, part_sem, come_sem, side_sem = rest
     halvings = []
@@ -786,7 +820,11 @@
                     part_ref[stage + 1] = total
                     trade(stage + 1).start()
                 else:
-                    total_ref[...] = total
+                    for block in range(blocks):
+                        gains_out_ref[:, block * lanes : (block + 1) * lanes] = total[
+                            block * gain_rows : (block + 1) * gain_rows
+                        ]
+                    tables_out_ref[...] = total[blocks * gain_rows :]
 
         for turn in range(kinds):
             now = group * kinds + turn
@@ -856,13 +894,19 @@
 
     for load in loads(0):
         load.start()
-    part_ref[0] = value_ref[...]
+    part_ref[0] = jnp.concatenate(
+        [gains_ref[:, block * lanes : (block + 1) * lanes] for block in range(blocks)]
+        + [tables_ref[...]],
+        axis=0,
+    )
     trade(0).start()
     slots = chunks + DELAY * stages
     lax.fori_loop(0, (slots + kinds - 1) // kinds, step, 0)
 
 
-def reduce_chunks(links, plan, sides, sources, value, shape, width, collective_id):
+def reduce_chunks(links, plan, sides, sources, small, shape, width, collective_id):
+    gains, tables = small
+    value = (gains.size // tables.shape[1] + tables.shape[0], tables.shape[1])
     stages, chunks = len(links.bits), len(plan)
     sums = [
         pltpu.VMEM((chunks,) + (2,) * (stages - 1 - stage) + shape, jnp.bfloat16)
@@ -873,17 +917,18 @@
         functools.partial(reduce_kernel, links, plan, sides, len(sources)),
         out_shape=[
             jax.ShapeDtypeStruct((chunks,) + shape, jnp.float32),
-            jax.ShapeDtypeStruct(value.shape, jnp.float32),
+            jax.ShapeDtypeStruct(gains.shape, jnp.float32),
+            jax.ShapeDtypeStruct(tables.shape, jnp.float32),
         ],
         in_specs=[pl.BlockSpec(memory_space=pltpu.HBM)] * len(sources)
-        + [pl.BlockSpec(memory_space=pltpu.VMEM)],
-        out_specs=[pl.BlockSpec(memory_space=pltpu.VMEM)] * 2,
+        + [pl.BlockSpec(memory_space=pltpu.VMEM)] * 2,
+        out_specs=[pl.BlockSpec(memory_space=pltpu.VMEM)] * 3,
         scratch_shapes=[
             pltpu.VMEM((HOLD,) + (2,) * stages + shape, jnp.bfloat16),
             pltpu.VMEM((2, rows, width), jnp.bfloat16),
             pltpu.VMEM((2, rows, width), jnp.bfloat16),
-            pltpu.VMEM((stages,) + value.shape, jnp.float32),
-            pltpu.VMEM((stages,) + value.shape, jnp.float32),
+            pltpu.VMEM((stages,) + value, jnp.float32),
+            pltpu.VMEM((stages,) + value, jnp.float32),
             pltpu.VMEM((max(1, len(sides)),) + (2,) * stages + shape, jnp.bfloat16),
             pltpu.VMEM((rows, width), jnp.bfloat16),
             pltpu.VMEM((rows, width), jnp.bfloat16),
@@ -900,7 +945,7 @@
         compiler_params=pltpu.CompilerParams(
             collective_id=collective_id, has_side_effects=True, vmem_limit_bytes=60 << 20
         ),
-    )(*sources, value)
+    )(*sources, gains, tables)
 
 
 def fold_grad(grad, devices, width):
@@ -919,8 +964,9 @@
 
 
 def gather_kernel(links, units, count, *refs):
-    shards, wholes, held = refs[:count], refs[count : 2 * count], refs[2 * count : 3 * count]
-    send_sem, recv_sem, local_sem = refs[3 * count :]
+    shards, small_ref, refs = refs[:count], refs[count], refs[count + 1 :]
+    wholes, other_ref, refs = refs[:count], refs[count], refs[count + 1 :]
+    held, (send_sem, recv_sem, local_sem, small_sem) = refs[:count], refs[count:]
     core, mesh_id = ("dp", 0), pl.DeviceIdType.MESH
     keys = [("dp", 1), ("dp", 2), core]
     orders = [[keys[0], keys[1], core], [keys[1], keys[0], core]]
@@ -966,11 +1012,20 @@
             held[number], wholes[number].at[place], local_sem.at[1, number]
         )
 
+    trade = pltpu.make_async_remote_copy(
+        src_ref=small_ref,
+        dst_ref=other_ref,
+        send_sem=small_sem.at[0],
+        recv_sem=small_sem.at[1],
+        device_id=links.partner(*row),
+        device_id_type=mesh_id,
+    )
     stages = 1 + len(keys)
     for unit in range(len(units)):
         send(0, unit).start()
     for number in range(count):
         load(number).start()
+    trade.start()
     for slot in range(len(units) + LAG * (stages - 1)):
         for stage in range(stages):
             unit = slot - LAG * stage
@@ -983,6 +1038,7 @@
             keep(slot).start()
     for number in range(count):
         keep(number).wait()
+    trade.wait()
 
 
 def gather_units(shards, width):
@@ -1003,30 +1059,35 @@
     return units
 
 
-def gather_weights(links, shards, collective_id):
+def gather_weights(links, shards, small, collective_id):
     count = len(shards)
     units = gather_units(shards, shards[0].shape[1])
     split = [
         shard.reshape(2, 2, 2, shard.shape[0] // 8, shard.shape[1]) for shard in shards
     ]
-    wholes = pl.pallas_call(
+    *wholes, other = pl.pallas_call(
         functools.partial(gather_kernel, links, units, count),
-        out_shape=[jax.ShapeDtypeStruct((2,) + piece.shape, piece.dtype) for piece in split],
-        in_specs=[pl.BlockSpec(memory_space=pltpu.HBM)] * count,
-        out_specs=[pl.BlockSpec(memory_space=pltpu.HBM)] * count,
+        out_shape=[jax.ShapeDtypeStruct((2,) + piece.shape, piece.dtype) for piece in split]
+        + [jax.ShapeDtypeStruct(small.shape, small.dtype)],
+        in_specs=[pl.BlockSpec(memory_space=pltpu.HBM)] * (count + 1),
+        out_specs=[pl.BlockSpec(memory_space=pltpu.HBM)] * (count + 1),
         scratch_shapes=[pltpu.VMEM(piece.shape, piece.dtype) for piece in split]
         + [
             pltpu.SemaphoreType.DMA((4, len(units))),
             pltpu.SemaphoreType.DMA((4, len(units))),
             pltpu.SemaphoreType.DMA((2, count)),
+            pltpu.SemaphoreType.DMA((2,)),
         ],
         compiler_params=pltpu.CompilerParams(
             collective_id=collective_id, has_side_effects=True, vmem_limit_bytes=60 << 20
         ),
-    )(*split)
-    return [
+    )(*split, small)
+    wholes = [
         whole.reshape(2 * shard.shape[0], shard.shape[1]) for whole, shard in zip(wholes, shards)
     ]
+    first = lax.axis_index("fsdp") == 0
+    small = jnp.concatenate([jnp.where(first, small, other), jnp.where(first, other, small)])
+    return wholes, small
 
 
 def weight_kernel(deep, x_ref, dy_ref, *rest):
@@ -1094,7 +1155,7 @@
             self.products[name] = (x, dy)
         return carry
 
-    def shares(self, collective_id, value):
+    def shares(self, collective_id, small):
         width, devices = self.width, self.links.devices()
         r = width // devices
         aligned = r % 8 == 0
@@ -1136,8 +1197,8 @@
             made = made.reshape((count,) + (2,) * len(self.links.bits) + made.shape[2:])
             for part in range(count):
                 plan.append(("chunk", number(made), part))
-        shares, total = reduce_chunks(
-            self.links, plan, sides, sources, value, (2 * r, width // 2), width, collective_id
+        shares, *total = reduce_chunks(
+            self.links, plan, sides, sources, small, (2 * r, width // 2), width, collective_id
         )
         if aligned:
             scattered = list(self.scattered.values())
@@ -1208,13 +1269,6 @@
         ],
         axis=1,
     )
-    small = links.gather_small(small)
-    enc_gains = small[:, 0:2].astype(jnp.float32)
-    dec_gains = small[:, 2:5].astype(jnp.float32)
-    tables = small[:, 5:].reshape(2, 2, NB // 2, H)
-    enc_bias = band_bias(tables[:, 0].reshape(NB, H), encoder_bucket)
-    dec_bias = band_bias(tables[:, 1].reshape(NB, H), decoder_bucket)
-
     shards = [
         encoder_query,
         encoder_keyval,
@@ -1232,7 +1286,14 @@
     ]
     shards = dict(zip(NAMES, shards))
     later = [shards.pop(name) for name in LATER]
-    weights = dict(zip(shards, gather_weights(links, list(shards.values()), 1)))
+    wholes, small = gather_weights(links, list(shards.values()), small, 1)
+    weights = dict(zip(shards, wholes))
+    enc_gains = small[:, 0:2].astype(jnp.float32)
+    dec_gains = small[:, 2:5].astype(jnp.float32)
+    tables = small[:, 5:].reshape(2, 2, NB // 2, H)
+    enc_bias = band_bias(tables[:, 0].reshape(NB, H), encoder_bucket)
+    dec_bias = band_bias(tables[:, 1].reshape(NB, H), decoder_bucket)
+
     weights["equery"], *later = lax.optimization_barrier((weights["equery"], *later))
     for name, shard in zip(LATER, later):
         weights[name] = lax.all_gather(shard, "fsdp", axis=0, tiled=True)
@@ -1283,7 +1344,7 @@
         attention_backward(
             grads,
             ("dquery", "dkeyval", "dproj"),
-            dec_stream,
+            dec_tokens,
             dec_gains[:, 0],
             weights["dquery"],
             weights["dkeyval"],
@@ -1304,7 +1365,7 @@
         attention_backward(
             grads,
             ("equery", "ekeyval", "eproj"),
-            enc_stream,
+            enc_tokens,
             enc_gains[:, 0],
             weights["equery"],
             weights["ekeyval"],
@@ -1316,22 +1377,22 @@
         )
     )
 
-    table_grads = [
-        band_table_grad(enc_band, encoder_bucket),
-        band_table_grad(dec_band, decoder_bucket),
-    ]
-    gain_grads = jnp.stack([egain_self, egain_ffn, dgain_self, dgain_cross, dgain_ffn])
-    flat = jnp.concatenate([gain_grads.reshape(-1)] + [grad.reshape(-1) for grad in table_grads])
-    count = flat.shape[0]
-    flat = jnp.pad(flat, (0, -count % (8 * TILE)))
-    shares, flat = grads.shares(0, flat.reshape(-1, TILE))
-    flat = flat.reshape(-1)
-    width = gain_grads.shape[1]
-    tables_grad = flat[5 * width : count].reshape(2, NB, H)
-    own = width // links.devices()
-    gains_share = lax.dynamic_slice_in_dim(
-        flat[: 5 * width].reshape(5, width), links.place() * own, own, 1
-    ).T
+    table_grads = jnp.concatenate(
+        [
+            band_table_grad(enc_band, encoder_bucket),
+            band_table_grad(dec_band, decoder_bucket),
+        ],
+        axis=0,
+    )
+    table_grads = jnp.pad(table_grads, ((0, 0), (0, TILE - H)))
+    none = jnp.zeros_like(egain_self)
+    gain_grads = jnp.stack(
+        [egain_self, egain_ffn, dgain_self, dgain_cross, dgain_ffn, none, none, none]
+    )
+    shares, (gain_grads, table_grads) = grads.shares(0, (gain_grads, table_grads))
+    own = gain_grads.shape[1] // links.devices()
+    gains_share = lax.dynamic_slice_in_dim(gain_grads, links.place() * own, own, 1).T
+    tables_grad = (table_grads[:NB, :H], table_grads[NB:, :H])
     return (
         memory,
         dec_final.astype(jnp.bfloat16),

time: 474 us -> 472 us (level)
  Pallas kernels: 341 us -> 352 us
  matrix products: 68.5 us -> 59.5 us
    dot_general x9 -> x4, matrix products: 21.5 us -> 8.11 us  [product_transposed(): lax.dot_general(former, latter, (((1,), (1,)), ((), ())), preferred_eleme...]
    pallas_call x0 -> x3, Pallas kernels: none -> 9.2 us  [pull_norm(): pl.pallas_call(pull_norm_kernel, out_shape=[jax.ShapeDtypeStruct((rows, f...]
    add x2 -> x0, other arithmetic: 7.03 us -> none  [attention_backward(): return (gradient + dstream, dgain, band, dsource)]
    dot_general x13, matrix products: 38.8 us -> 44.1 us  [product(): return jnp.dot(former, latter, preferred_element_type=jnp.float32)]
    unnamed x220 -> x214, local copies, waits for them, and re-layouts: 14.8 us -> 18.2 us
  transfers between devices with their start and end apart: 3 -> 2, of which waited for: 0 -> 0; matrix products, arithmetic and copies ran while one was open for 17% -> 15% of each run, Pallas kernels for 71% -> 57%
where the time goes in v6:
time: 472 us; the launch traced here: 466 us
  Pallas kernels  352 us (75%)
  matrix products  59.5 us (13%)
  local copies, waits for them, and re-layouts  25.8 us (5%)
  between operations  16 us (3%)
  other arithmetic  12.9 us (3%)
    pallas_call x1, Pallas kernels, reduce_chunks(): pl.pallas_call(functools.partial(reduce_kernel, links, plan, sides, len(s...  138 us
    pallas_call x1, Pallas kernels, gather_weights(): pl.pallas_call(functools.partial(gather_kernel, links, units, count), out...  72.9 us
    pallas_call x3, Pallas kernels, attend_backward(): pl.pallas_call(functools.partial(backward_kernel, spec), out_shape=[jax.S...  61.1 us
    dot_general x13, matrix products, product(): return jnp.dot(former, latter, preferred_element_type=jnp.float32)  44.1 us
    pallas_call x3, Pallas kernels, attend_forward(): pl.pallas_call(functools.partial(forward_kernel, spec), out_shape=(jax.Sh...  38.9 us
    pallas_call x2, Pallas kernels, feed_backward(): pl.pallas_call(feed_backward_kernel, out_shape=[jax.ShapeDtypeStruct((row...  29.4 us
    unnamed x214, local copies, waits for them, and re-layouts  18.2 us
  transfers between devices with their start and end apart: 2, of which 0 were waited for; matrix products, arithmetic and copies ran while one was open for 15% of the time, Pallas kernels for 57%

profile of v6, /device:TPU:0, one launch (start us, length us, event | category | flops | bytes accessed | tf_op | source)
XLA Modules:
  0.0 466.3 jit_solution(5641785359005836758)
XLA Ops:
  7.2 0.7 pad_maximum_fusion
  8.1 0.7 pad_maximum_fusion.2
  8.8 0.8 copy.105.refs_12_
  9.6 72.9 %shard_map.418 = (bf16[2,2,2,2,48,768]{5,4,3,2,1,0:T(8,128)(2,1)}, bf16[2,2,2,2,48,1536]{5,4,3,2,1,0:T(8,128)(2,1)}, bf16[2,2,2,2,48,768]{5,4,3,2,1,0:T(8,128)(2...) custom-call(bf16[2,2,2,48,768]{4,3,2,1,0:T(8,128)(2,1)} %bitcast.148, ...), custom_call_target="tpu_custom_call" | custom-call | tf_op jit(solution)/shard_map/pallas_call | solution.py:1068
  82.7 1.1 broadcast_select_fusion.1
  84.0 0.6 fusion.38
  85.4 0.7 slice_reduce_fusion.1
  86.5 0.6 add_rsqrt_fusion.1
  87.1 1.2 slice_bitcast_fusion.1
  88.9 0.6 convert_reduce_fusion.2
  90.5 0.8 convolution_convert_fusion.3.k_ref.v_ref
  91.4 5.2 %shard_map.420 = (bf16[256,768]{1,0:T(8,128)(2,1)S(1)}, f32[6,2,256]{2,1,0:T(2,128)S(1)}) custom-call(s32[2,1]{1,0:T(2,128)S(1)} %broadcast_12_bounds_ref.2.bounds_ref, bf16[256,768]{1,0:T(8,128)(2,1)S(1)} %convolution_convert_fusion.9.q_ref, bf16[256,1536]{1,0:T(8,128)(2,1)S(1)} %convolution_convert_fusion.3.k_ref.v_ref, ...), custom_call_target="tpu_custom_call" | custom-call | flops 805306368 | bytes 8388608 | tf_op jit(solution)/shard_map/pallas_call | solution.py:390
  96.6 0.6 copy-done.60
  98.6 1.4 convolution_convert_fusion.5.q_ref
  100.1 0.8 copy-done.48
  100.9 2.8 convolution_convert_fusion.2.k_ref.v_ref
  104.2 24.8 %shard_map.419 = (bf16[1024,768]{1,0:T(8,128)(2,1)S(1)}, f32[6,2,1024]{2,1,0:T(2,128)S(1)}) custom-call(s32[2,4]{1,0:T(2,128)S(1)} %pad_add_fusion.bounds_ref, bf16[1024,768]{1,0:T(8,128)(2,1)S(1)} %convolution_convert_fusion.5.q_ref, bf16[1024,1536]{1,0:T(8,128)(2,1)S(1)} %convolution_convert_fusion.2.k_ref.v_ref, ...), custom_call_target="tpu_custom_call" | custom-call | flops 12884901888 | bytes 8388608 | tf_op jit(solution)/shard_map/pallas_call | solution.py:390
  129.1 3.1 multiply_reduce_fusion
  132.4 2.0 convolution_convert_fusion.8.q_ref
  135.0 13.0 %fusion.7 = (bf16[1024,3072]{1,0:T(8,128)(2,1)S(1)}, f32[1024,3072]{1,0:T(8,128)}) fusion(bf16[1024,768]{1,0:T(8,128)(2,1)S(1)} %multiply_convert_fusion.refs_13_, bf16[768,3072]{1,0:T(8,128)(2,1)} %bitcast.156), kind=kOutput, calls=%fused_computation.8 | convolution fusion | flops 4860149760 | bytes 25165824 | tf_op jit(solution)/shard_map/dot_general | solution.py:466
  148.0 5.1 %add_convert_fusion.refs_11_ = bf16[1024,768]{1,0:T(8,128)(2,1)S(1)} fusion(f32[1024,768]{1,0:T(8,128)S(1)} %copy-done.77, bf16[1024,3072]{1,0:T(8,128)(2,1)S(1)} %get-tuple-element.277.refs_20_, bf16[3072,768]{1,0:T(8,128)(2,1)S(1)} %bitcast.161), kind=kOutput, calls=%fused_computation.28 | convolution fusion | flops 4833411072 | bytes 15728640 | tf_op jit(solution)/shard_map/dot_general | solution.py:466
  153.1 1.1 copy-done.79
  154.2 2.8 convolution_convert_fusion.1.k_ref.v_ref
  157.1 8.9 %shard_map.421 = (bf16[256,768]{1,0:T(8,128)(2,1)S(1)}, f32[6,2,256]{2,1,0:T(2,128)S(1)}) custom-call(s32[2,1]{1,0:T(2,128)S(1)} %broadcast_12_bounds_ref.2.bounds_ref, bf16[256,768]{1,0:T(8,128)(2,1)S(1)} %convolution_convert_fusion.8.q_ref, bf16[1024,1536]{1,0:T(8,128)(2,1)S(1)} %convolution_convert_fusion.1.k_ref.v_ref, ...), custom_call_target="tpu_custom_call" | custom-call | flops 3221225472 | bytes 8388608 | tf_op jit(solution)/shard_map/pallas_call | solution.py:390
  166.0 0.6 copy-done.62
  166.6 0.8 copy-done.18
  168.0 0.6 compare_convert_fusion
  168.6 1.0 convert_multiply_fusion.4.g_ref
  169.6 0.9 multiply_convert_fusion.1.refs_0_
  170.5 5.6 %fusion.42.pre_ref = f32[256,3072]{1,0:T(8,128)} fusion(bf16[256,768]{1,0:T(8,128)(2,1)} %multiply_convert_fusion.1.refs_0_, bf16[768,3072]{1,0:T(8,128)(2,1)} %all-gather.2.cloned.1.call-done.wi_ref), kind=kOutput, calls=%fused_computation.112 | convolution fusion | flops 1207959552 | bytes 8257536 | tf_op jit(solution)/shard_map/dot_general | solution.py:466
  176.1 8.3 %shard_map.422 = (f32[256,768]{1,0:T(8,128)S(1)}, bf16[256,3072]{1,0:T(8,128)(2,1)S(1)}, bf16[256,768]{1,0:T(8,128)(2,1)S(1)}, f32[8,768]{1,0:T(8,128)S(1)}) custom-call(f32[256,768]{1,0:T(8,128)S(1)} %copy-done.10, f32[256,768]{1,0:T(8,128)S(1)} %get-tuple-element.280.v_ref, f32[1,768]{1,0:T(1,128)S(1)} %bitcast.123, f32[256,3072]{1,0:T(8,128)} %fusion.42.pre_ref, ...), custom_call_target="tpu_custom_call" | custom-call | flops 2415919104 | bytes 16908288 | tf_op jit(solution)/shard_map/pallas_call | solution.py:621
  184.5 0.9 copy-done.7
  185.3 1.1 copy-done.20
  186.5 0.6 copy-done.37
  187.1 4.4 convolution_convert_fusion
  191.5 1.2 convert_element_type.130.refs_3_
  192.8 1.9 convolution_convert_fusion.7.do_ref
  194.8 11.7 %shard_map.423 = (bf16[256,768]{1,0:T(8,128)(2,1)S(1)}, bf16[1024,1536]{1,0:T(8,128)(2,1)S(1)}) custom-call(s32[2,1]{1,0:T(2,128)S(1)} %copy-done.53, bf16[256,768]{1,0:T(8,128)(2,1)S(1)} %copy-done.29, bf16[1024,1536]{1,0:T(8,128)(2,1)} %copy-done.56, bf16[1024,1536]{1,0:T(8,128)(2,1)} %copy-done.56, bf16[256,768]{1,0:T(8,128)(2,1)S(1)} %convolution_convert_fusion.7.do_ref, ...), custom_call_target="tpu_custom_call" | custom-call | flops 8053063680 | bytes 16777216 | tf_op jit(solution)/shard_map/pallas_call | solution.py:426
  206.7 0.7 shard_map.427
  207.4 1.4 copy-done.71
  209.6 11.4 %shard_map.428 = (bf16[256,768]{1,0:T(8,128)(2,1)S(1)}, bf16[256,1536]{1,0:T(8,128)(2,1)S(1)}, f32[12,5,8,256]{3,2,1,0:T(8,128)S(1)}) custom-call(s32[2,1]{1,0:T(2,128)S(1)} %copy-done.53, bf16[256,768]{1,0:T(8,128)(2,1)S(1)} %copy-done.27, bf16[256,1536]{1,0:T(8,128)(2,1)S(1)} %copy-done.55, bf16[256,1536]{1,0:T(8,128)(2,1)S(1)} %copy-done.55, ...), custom_call_target="tpu_custom_call" | custom-call | flops 2013265920 | bytes 16777216 | tf_op jit(solution)/shard_map/pallas_call | solution.py:426
  221.1 4.3 multiply_add_fusion.g_ref
  225.4 2.2 shard_map.429
  227.7 1.0 copy.123
  228.8 21.1 %shard_map.424 = (f32[1024,768]{1,0:T(8,128)S(1)}, bf16[1024,3072]{1,0:T(8,128)(2,1)}, bf16[1024,768]{1,0:T(8,128)(2,1)S(1)}, f32[8,768]{1,0:T(8,128)S(1)}) custom-call(f32[1024,768]{1,0:T(8,128)} %multiply_add_fusion.g_ref, f32[1024,768]{1,0:T(8,128)} %get-tuple-element.276.v_ref, f32[1,768]{1,0:T(1,128)S(1)} %copy-done.45, ...), custom_call_target="tpu_custom_call" | custom-call | flops 9663676416 | bytes 39321600 | tf_op jit(solution)/shard_map/pallas_call | solution.py:621
  249.9 1.7 copy-done.5
  251.6 1.1 copy-done.21
  252.8 2.2 convert_element_type.132.refs_16_
  255.0 1.4 convolution_convert_fusion.4.do_ref
  256.5 0.7 copy-done.58
  257.3 37.9 %shard_map.425 = (bf16[1024,768]{1,0:T(8,128)(2,1)S(1)}, bf16[1024,1536]{1,0:T(8,128)(2,1)}, f32[12,5,8,256]{3,2,1,0:T(8,128)S(1)}) custom-call(s32[2,4]{1,0:T(2,128)S(1)} %copy-done.47, bf16[1024,768]{1,0:T(8,128)(2,1)S(1)} %copy-done.58, bf16[1024,1536]{1,0:T(8,128)(2,1)} %copy-done.59, bf16[1024,1536]{1,0:T(8,128)(2,1)} %copy-done.59, ...), custom_call_target="tpu_custom_call" | custom-call | flops 32212254720 | bytes 16777216 | tf_op jit(solution)/shard_map/pallas_call | solution.py:426
  295.2 2.5 copy-done.12
  297.7 6.3 %shard_map.426 = (f32[1024,768]{1,0:T(8,128)}, f32[8,768]{1,0:T(8,128)S(1)}) custom-call(f32[1024,768]{1,0:T(8,128)S(1)} %copy-done.6, bf16[1024,768]{1,0:T(8,128)(2,1)S(1)} %copy-done, f32[1,768]{1,0:T(1,128)S(1)} %copy-done.44, bf16[1024,768]{1,0:T(8,128)(2,1)S(1)} %get-tuple-element.107.refs_0_.refs_18_, bf16[768,768]{1,0:T(8,128)(2,1)S(1)} %bitcast.131, ...), custom_call_target="tpu_custom_call" | custom-call | flops 3623878656 | bytes 17694720 | tf_op jit(solution)/shard_map/pallas_call | solution.py:561
  304.4 1.9 fusion.20
  306.3 0.8 fusion.19
  307.2 0.6 pad.4.refs_23_
  307.9 0.6 stack.36.refs_22_
  308.5 137.6 %shard_map.430 = (f32[24,48,384]{2,1,0:T(8,128)}, f32[8,768]{1,0:T(8,128)}, f32[64,128]{1,0:T(8,128)}) custom-call(bf16[256,768]{1,0:T(8,128)(2,1)} %multiply_convert_fusion.1.refs_0_, bf16[256,3072]{1,0:T(8,128)(2,1)} %copy-done.20, bf16[256,768]{1,0:T(8,128)(2,1)} %copy-done.18, bf16[256,768]{1,0:T(8,128)(2,1)} %copy-done.75, bf16[256,768]{1,0:T(8,128)(2,1)} %copy-done.74, ...), custom_call_target="tpu_custom_call" | custom-call | tf_op jit(solution)/shard_map/pallas_call | solution.py:916
  446.1 0.8 dynamic-slice_bitcast_fusion
  448.1 0.7 fusion.40
  448.8 0.7 copy.118
  449.5 0.7 copy.117
  450.1 6.0 %fusion.21 = bf16[256,768]{1,0:T(8,128)(2,1)} fusion(f32[256,768]{1,0:T(8,128)S(1)} %get-tuple-element.280.v_ref, bf16[3072,768]{1,0:T(8,128)(2,1)} %bitcast.137, f32[256,3072]{1,0:T(8,128)} %fusion.42.pre_ref), kind=kOutput, calls=%fused_computation.41 | convolution fusion | flops 1215430656 | bytes 9043968 | tf_op jit(solution)/shard_map/dot_general | solution.py:466
  456.1 2.8 shard_map.431
  (256 shorter events, 9.2 us)
Async XLA Ops:
  7.2 163.3 %all-gather.2.cloned.1.call-start = ((), (), s32[]{:S(2)}) async-start(), calls=%async_computation.1 | async-start | bytes 7077888 | tf_op jit(solution)/shard_map/all_gather | solution.py:1299
  9.6 73.1 %copy-start.80 = (bf16[384,6]{1,0:T(8,128)(2,1)S(1)}, bf16[384,6]{1,0:T(8,128)(2,1)}, u32[]{:S(2)}) copy-start(bf16[384,6]{1,0:T(8,128)(2,1)} %copy.105.refs_12_) | copy-start | bytes 13828
  9.6 75.1 %copy-start.41 = (s32[256]{0:T(256)S(1)}, s32[256]{0:T(256)}, u32[]{:S(2)}) copy-start(s32[256]{0:T(256)} %param.30) | copy-start | bytes 3076
  82.6 3.6 copy-start
  82.6 5.9 %copy-start.92 = (s32[5,256]{1,0:T(8,128)S(1)}, s32[5,256]{1,0:T(8,128)}, u32[]{:S(2)}) copy-start(s32[5,256]{1,0:T(8,128)} %constant.93) | copy-start | bytes 15364
  82.6 6.1 %copy-start.91 = (s32[5,256]{1,0:T(8,128)S(1)}, s32[5,256]{1,0:T(8,128)}, u32[]{:S(2)}) copy-start(s32[5,256]{1,0:T(8,128)} %constant.94) | copy-start | bytes 15364
  82.6 7.1 %copy-start.3 = (bf16[2,2,2,2,48,768]{5,4,3,2,1,0:T(8,128)(2,1)S(1)}, bf16[2,2,2,2,48,768]{5,4,3,2,1,0:T(8,128)(2,1)}, u32[]{:S(2)}) copy-start(bf16[2,2,2,2,48,768]{5,4,3,2,1,0:T(8,128)(2,1)} %get-tuple-element.90) | copy-start | bytes 3538948
  82.6 373.5 %reduce-scatter.2.cloned.1.call-start = ((), (), s32[]{:S(2)}) async-start(), calls=%async_computation.2 | async-start | bytes 4866048 | tf_op jit(solution)/shard_map/reduce_scatter | solution.py:1151
  88.7 15.5 %copy-start.32 = (f32[12,5,256]{2,1,0:T(8,128)}, f32[12,5,256]{2,1,0:T(8,128)S(1)}, u32[]{:S(2)}) copy-start(f32[12,5,256]{2,1,0:T(8,128)S(1)} %copy.110.rest_0_) | copy-start | bytes 184324
  89.7 6.9 %copy-start.73 = (bf16[256,768]{1,0:T(8,128)(2,1)}, bf16[256,768]{1,0:T(8,128)(2,1)S(1)}, u32[]{:S(2)}) copy-start(bf16[256,768]{1,0:T(8,128)(2,1)S(1)} %fusion.24.refs_8_) | copy-start | bytes 1179652
  90.2 6.4 %copy-start.26 = (bf16[256,768]{1,0:T(8,128)(2,1)}, bf16[256,768]{1,0:T(8,128)(2,1)S(1)}, u32[]{:S(2)}) copy-start(bf16[256,768]{1,0:T(8,128)(2,1)S(1)} %convolution_convert_fusion.9.q_ref) | copy-start | bytes 1179652
  90.5 6.7 %copy-start.70 = (bf16[2,2,2,2,48,768]{5,4,3,2,1,0:T(8,128)(2,1)S(1)}, bf16[2,2,2,2,48,768]{5,4,3,2,1,0:T(8,128)(2,1)}, u32[]{:S(2)}) copy-start(bf16[2,2,2,2,48,768]{5,4,3,2,1,0:T(8,128)(2,1)} %get-tuple-element.93) | copy-start | bytes 3538948
  91.3 7.0 %copy-start.54 = (bf16[256,1536]{1,0:T(8,128)(2,1)}, bf16[256,1536]{1,0:T(8,128)(2,1)S(1)}, u32[]{:S(2)}) copy-start(bf16[256,1536]{1,0:T(8,128)(2,1)S(1)} %convolution_convert_fusion.3.k_ref.v_ref) | copy-start | bytes 2359300
  91.3 6.5 %copy-start.89 = (f32[768]{0:T(1024)S(1)}, f32[768]{0:T(1024)}, u32[]{:S(2)}) copy-start(f32[768]{0:T(1024)} %get-tuple-element.271) | copy-start | bytes 9220
  91.3 6.5 %copy-start.90 = (f32[1024]{0:T(1024)S(1)}, f32[1024]{0:T(1024)}, u32[]{:S(2)}) copy-start(f32[1024]{0:T(1024)} %add_rsqrt_fusion.1) | copy-start | bytes 12292
  91.4 6.9 %copy-start.30 = (s32[256,128]{1,0:T(8,128)}, s32[256,128]{1,0:T(8,128)S(1)}, u32[]{:S(2)}) copy-start(s32[256,128]{1,0:T(8,128)S(1)} %broadcast_in_dim.19.segk_ref) | copy-start | bytes 393220
  91.4 65.6 %copy-start.52 = (s32[2,1]{1,0:T(2,128)}, s32[2,1]{1,0:T(2,128)S(1)}, u32[]{:S(2)}) copy-start(s32[2,1]{1,0:T(2,128)S(1)} %broadcast_12_bounds_ref.2.bounds_ref) | copy-start | bytes 28
  100.0 4.2 copy-start.57
  103.7 25.3 %copy-start.59 = (bf16[1024,1536]{1,0:T(8,128)(2,1)}, bf16[1024,1536]{1,0:T(8,128)(2,1)S(1)}, u32[]{:S(2)}) copy-start(bf16[1024,1536]{1,0:T(8,128)(2,1)S(1)} %convolution_convert_fusion.2.k_ref.v_ref) | copy-start | bytes 9437188
  104.0 25.1 %copy-start.46 = (s32[2,4]{1,0:T(2,128)}, s32[2,4]{1,0:T(2,128)S(1)}, u32[]{:S(2)}) copy-start(s32[2,4]{1,0:T(2,128)S(1)} %pad_add_fusion.bounds_ref) | copy-start | bytes 100
  104.2 52.8 %copy-start.23 = (s32[1024,128]{1,0:T(8,128)}, s32[1024,128]{1,0:T(8,128)S(1)}, u32[]{:S(2)}) copy-start(s32[1024,128]{1,0:T(8,128)S(1)} %broadcast_in_dim.17.segk_ref) | copy-start | bytes 1572868
  104.2 24.9 %copy-start.100 = (bf16[2,2,2,2,48,768]{5,4,3,2,1,0:T(8,128)(2,1)S(1)}, bf16[2,2,2,2,48,768]{5,4,3,2,1,0:T(8,128)(2,1)}, u32[]{:S(2)}) copy-start(bf16[2,2,2,2,48,768]{5,4,3,2,1,0:T(8,128)(2,1)} %get-tuple-element.87) | copy-start | bytes 3538948
  129.1 3.1 copy-start.19
  129.1 3.1 copy-start.64
  129.1 3.1 copy-start.88
  134.4 22.7 %copy-start.28 = (bf16[256,768]{1,0:T(8,128)(2,1)}, bf16[256,768]{1,0:T(8,128)(2,1)S(1)}, u32[]{:S(2)}) copy-start(bf16[256,768]{1,0:T(8,128)(2,1)S(1)} %convolution_convert_fusion.8.q_ref) | copy-start | bytes 1179652
  134.6 13.3 %slice-start = ((s8[4718592]{0:T(1024)(128)(4,1)}), s8[4194304]{0:T(1024)(128)(4,1)S(1)}, s32[]{:S(2)}) async-start(s8[4718592]{0:T(1024)(128)(4,1)} %bitcast.159), calls=%async_computation.3 | async-start | bytes 8388608
  134.9 13.0 %copy-start.68 = (bf16[1024,768]{1,0:T(8,128)(2,1)}, bf16[1024,768]{1,0:T(8,128)(2,1)S(1)}, u32[]{:S(2)}) copy-start(bf16[1024,768]{1,0:T(8,128)(2,1)S(1)} %multiply_convert_fusion.refs_13_) | copy-start | bytes 4718596
  134.9 13.0 %slice-start.1 = ((s8[4718592]{0:T(1024)(128)(4,1)}), s8[524288]{0:T(1024)(128)(4,1)S(1)}, s32[]{:S(2)}) async-start(s8[4718592]{0:T(1024)(128)(4,1)} %bitcast.159), calls=%async_computation.4 | async-start | bytes 1048576
  147.9 5.1 %copy-start.66 = (bf16[1024,3072]{1,0:T(8,128)(2,1)}, bf16[1024,3072]{1,0:T(8,128)(2,1)S(1)}, u32[]{:S(2)}) copy-start(bf16[1024,3072]{1,0:T(8,128)(2,1)S(1)} %get-tuple-element.277.refs_20_) | copy-start | bytes 18874372
  148.0 6.2 %copy-start.97 = (bf16[2,2,2,2,48,1536]{5,4,3,2,1,0:T(8,128)(2,1)S(1)}, bf16[2,2,2,2,48,1536]{5,4,3,2,1,0:T(8,128)(2,1)}, u32[]{:S(2)}) copy-start(bf16[2,2,2,2,48,1536]{5,4,3,2,1,0:T(8,128)(2,1)} %get-tuple-element.95) | copy-start | bytes 7077892
  157.0 9.0 %copy-start.56 = (bf16[1024,1536]{1,0:T(8,128)(2,1)}, bf16[1024,1536]{1,0:T(8,128)(2,1)S(1)}, u32[]{:S(2)}) copy-start(bf16[1024,1536]{1,0:T(8,128)(2,1)S(1)} %convolution_convert_fusion.1.k_ref.v_ref) | copy-start | bytes 9437188
  157.1 10.4 %copy-start.72 = (bf16[2,2,2,2,48,768]{5,4,3,2,1,0:T(8,128)(2,1)S(1)}, bf16[2,2,2,2,48,768]{5,4,3,2,1,0:T(8,128)(2,1)}, u32[]{:S(2)}) copy-start(bf16[2,2,2,2,48,768]{5,4,3,2,1,0:T(8,128)(2,1)} %get-tuple-element.97) | copy-start | bytes 3538948
  166.6 3.0 copy-start.86
  170.5 5.6 %copy-start.10 = (f32[256,768]{1,0:T(8,128)S(1)}, f32[256,768]{1,0:T(8,128)}, u32[]{:S(2)}) copy-start(f32[256,768]{1,0:T(8,128)} %convert_multiply_fusion.4.g_ref) | copy-start | bytes 2359300
  176.1 11.0 %copy-start.78 = (f32[256,3072]{1,0:T(8,128)S(1)}, f32[256,3072]{1,0:T(8,128)}, u32[]{:S(2)}) copy-start(f32[256,3072]{1,0:T(8,128)} %fusion.42.pre_ref) | copy-start | bytes 9437188
  191.5 3.3 copy-start.43
  191.5 3.3 copy-start.24
  191.5 3.3 copy-start.29
  191.5 3.3 copy-start.53
  191.5 3.3 copy-start.63
  194.8 11.8 %copy-start.2 = (bf16[2,2,2,2,48,768]{5,4,3,2,1,0:T(8,128)(2,1)S(1)}, bf16[2,2,2,2,48,768]{5,4,3,2,1,0:T(8,128)(2,1)}, u32[]{:S(2)}) copy-start(bf16[2,2,2,2,48,768]{5,4,3,2,1,0:T(8,128)(2,1)} %get-tuple-element.94) | copy-start | bytes 3538948
  194.8 11.8 %copy-start.8 = (f32[256,768]{1,0:T(8,128)S(1)}, f32[256,768]{1,0:T(8,128)}, u32[]{:S(2)}) copy-start(f32[256,768]{1,0:T(8,128)} %copy-done.7) | copy-start | bytes 2359300
  206.6 14.5 %copy-start.11 = (bf16[1024,1536]{1,0:T(8,128)(2,1)}, bf16[1024,1536]{1,0:T(8,128)(2,1)S(1)}, u32[]{:S(2)}) copy-start(bf16[1024,1536]{1,0:T(8,128)(2,1)S(1)} %get-tuple-element.104.refs_12_) | copy-start | bytes 9437188
  206.6 3.0 copy-start.27
  206.6 3.0 copy-start.31
  206.6 3.0 copy-start.35
  206.6 3.0 copy-start.55
  206.6 3.0 copy-start.61
  207.4 13.7 %copy-start.39 = (f32[8,768]{1,0:T(8,128)}, f32[8,768]{1,0:T(8,128)S(1)}, u32[]{:S(2)}) copy-start(f32[8,768]{1,0:T(8,128)S(1)} %get-tuple-element.122) | copy-start | bytes 73732
  209.6 11.4 %copy-start.93 = (f32[1024]{0:T(1024)S(1)}, f32[1024]{0:T(1024)}, u32[]{:S(2)}) copy-start(f32[1024]{0:T(1024)} %compare_convert_fusion) | copy-start | bytes 12292
  209.6 11.5 %copy-start.98 = (bf16[2,2,2,2,48,1536]{5,4,3,2,1,0:T(8,128)(2,1)S(1)}, bf16[2,2,2,2,48,1536]{5,4,3,2,1,0:T(8,128)(2,1)}, u32[]{:S(2)}) copy-start(bf16[2,2,2,2,48,1536]{5,4,3,2,1,0:T(8,128)(2,1)} %get-tuple-element.95) | copy-start | bytes 7077892
  209.6 11.5 %copy-start.99 = (bf16[1024,768]{1,0:T(8,128)(2,1)S(1)}, bf16[1024,768]{1,0:T(8,128)(2,1)}, u32[]{:S(2)}) copy-start(bf16[1024,768]{1,0:T(8,128)(2,1)} %param.31) | copy-start | bytes 4718596
  221.0 4.4 copy-start.9
  221.0 4.3 copy-start.17
  221.1 4.3 copy-start.4
  221.1 4.3 copy-start.14
  225.4 3.4 copy-start.45
  257.2 38.0 %copy-start.6 = (f32[1024,768]{1,0:T(8,128)S(1)}, f32[1024,768]{1,0:T(8,128)}, u32[]{:S(2)}) copy-start(f32[1024,768]{1,0:T(8,128)} %copy-done.5) | copy-start | bytes 9437188
  257.3 38.0 %copy-start.44 = (f32[1,768]{1,0:T(1,128)S(1)}, f32[1,768]{1,0:T(1,128)}, u32[]{:S(2)}) copy-start(f32[1,768]{1,0:T(1,128)} %get-tuple-element.269.gain_ref) | copy-start | bytes 9220
  257.3 38.0 %copy-start.49 = (bf16[2,2,2,2,48,1536]{5,4,3,2,1,0:T(8,128)(2,1)S(1)}, bf16[2,2,2,2,48,1536]{5,4,3,2,1,0:T(8,128)(2,1)}, u32[]{:S(2)}) copy-start(bf16[2,2,2,2,48,1536]{5,4,3,2,1,0:T(8,128)(2,1)} %get-tuple-element.85) | copy-start | bytes 7077892
  257.3 38.0 %copy-start.51 = (bf16[2,2,2,2,48,768]{5,4,3,2,1,0:T(8,128)(2,1)S(1)}, bf16[2,2,2,2,48,768]{5,4,3,2,1,0:T(8,128)(2,1)}, u32[]{:S(2)}) copy-start(bf16[2,2,2,2,48,768]{5,4,3,2,1,0:T(8,128)(2,1)} %get-tuple-element.83) | copy-start | bytes 3538948
  295.2 8.9 %copy-start.22 = (bf16[1024,768]{1,0:T(8,128)(2,1)}, bf16[1024,768]{1,0:T(8,128)(2,1)S(1)}, u32[]{:S(2)}) copy-start(bf16[1024,768]{1,0:T(8,128)(2,1)S(1)} %get-tuple-element.107.refs_0_.refs_18_) | copy-start | bytes 4718596
  297.7 6.7 %copy-start.83 = (s32[10240]{0:T(1024)S(1)}, s32[10240]{0:T(1024)}, u32[]{:S(2)}) copy-start(s32[10240]{0:T(1024)} %constant.96) | copy-start | bytes 122884
  (42 other events, 81.4 us)
Sparse Core Ops, SparseCore 0:
  82.7 62.1 all-gather.1
  191.6 109.3 reduce-scatter.1
